TPU v7x, 32 devices: a whole 2x2x4 slice. The times are simulated.
32 devices in a mesh: group: 2 (over x), shard: 16 (over z, y, core).
Axes of the slice: x: 2, y: 2, z: 4, core: 2. Of those that a mesh axis runs over, the one named last changes fastest.
Arguments:
- tokens_in: bfloat16 [16384, 1024], P(('group', 'shard')), may hold values from -6 to 6
- out_grad: bfloat16 [16384, 1024], P(('group', 'shard')), may hold values from -6 to 6
- deal_order: int32 [32, 512], P(('group', 'shard')), may hold values from 0 to 511, each once within a row
- seq_lengths: int32 [2, 3], P('group'), may hold values from 1024 to 4096, as said below
- value_routes: int32 [16384, 4, 2], P(('group', 'shard')), may hold values from 0 to 4, all different within a row
- output_routes: int32 [16384, 4, 2], P(('group', 'shard')), may hold values from 0 to 4, all different within a row
- ffn_routes: int32 [16384, 16], P(('group', 'shard')), may hold values from 0 to 63, all different within a row; in each aligned block of 512 rows (0 to 511, 512 to 1023, ...) at most 192 rows name the same one
- norm1_gain: bfloat16 [1024], P(('group', 'shard')), may hold values from 0.5 to 1.5
- norm1_bias: bfloat16 [1024], P(('group', 'shard')), may hold values from -0.59765625 to 0.59765625
- norm2_gain: bfloat16 [1024], P(('group', 'shard')), may hold values from 0.5 to 1.5
- norm2_bias: bfloat16 [1024], P(('group', 'shard')), may hold values from -0.59765625 to 0.59765625
- query_weight: bfloat16 [1024, 512], P(('group', 'shard')), may hold values from -0.1875 to 0.1875
- key_weight: bfloat16 [1024, 512], P(('group', 'shard')), may hold values from -0.1875 to 0.1875
- value_weight: bfloat16 [1024, 2560], P(('group', 'shard')), may hold values from -0.1875 to 0.1875
- output_weight: bfloat16 [1024, 2560], P(('group', 'shard')), may hold values from -4 to 4
- value_router: bfloat16 [1024, 20], P(('group', 'shard')), may hold values from -0.125 to 0.125
- output_router: bfloat16 [1024, 20], P(('group', 'shard')), may hold values from -0.125 to 0.125
- ffn_router: bfloat16 [1024, 64], P(('group', 'shard')), may hold values from -0.09375 to 0.09375
- ffn_in: bfloat16 [1024, 8192], P('group', 'shard'), may hold values from -0.1875 to 0.1875
- ffn_out: bfloat16 [1024, 8192], P('group', 'shard'), may hold values from -0.5 to 0.5
Outputs:
- layer_out: bfloat16 [16384, 1024], P(('group', 'shard'))
- input_grad: float32 [16384, 1024], P(('group', 'shard'))
- norm1_gain_grad: float32 [1024], P(('group', 'shard'))
- norm1_bias_grad: float32 [1024], P(('group', 'shard'))
- norm2_gain_grad: float32 [1024], P(('group', 'shard'))
- norm2_bias_grad: float32 [1024], P(('group', 'shard'))
- query_weight_grad: float32 [1024, 512], P(('group', 'shard'))
- key_weight_grad: float32 [1024, 512], P(('group', 'shard'))
- value_weight_grad: float32 [1024, 2560], P(('group', 'shard'))
- output_weight_grad: float32 [1024, 2560], P(('group', 'shard'))
- value_router_grad: float32 [1024, 20], P(('group', 'shard'))
- output_router_grad: float32 [1024, 20], P(('group', 'shard'))
- ffn_router_grad: float32 [1024, 64], P(('group', 'shard'))
- ffn_in_grad: float32 [1024, 8192], P('group', 'shard')
- ffn_out_grad: float32 [1024, 8192], P('group', 'shard')
Inputs may be any that keep to these rules, and one draw needn't show every extreme that they name: `deal_order`: each row is a permutation of 0 to 511. `seq_lengths`: each group's lengths add up to its tokens, 512 on each of its devices. `value_routes`: the two entries of a token and head differ. `output_routes`: the two entries of a token and head differ. `ffn_routes`: a token's 16 entries differ; within the rows of one device no expert is named by more than 192 rows.
All inputs are finite; a program needn't handle non-finite values.
Results may differ from a plain program's by a relative error of at most 0.015.
Values may be sent and summed in bfloat16 or wider, within the bound.
A program may use at most 576 MiB of HBM per device.

v0:
```python
import jax
import jax.numpy as jnp
from jax import lax
from jax.sharding import PartitionSpec as P

HEADS = 4
DH = 128
VEXP = 5
FH = 128
FTOP = 16
LMAX = 4096


def passed_along(value, axis, by):
    count = lax.axis_size(axis)
    pairs = [(i, i + by) for i in range(count) if 0 <= i + by < count]
    return lax.ppermute(value, axis, pairs)


def matmul(left_side, right_side):
    return jnp.dot(left_side, right_side, preferred_element_type=jnp.float32)


def transposed(left_side, right_side):
    return lax.dot_general(
        left_side, right_side, (((1,), (1,)), ((), ())), preferred_element_type=jnp.float32
    )


def contract_rows(left_side, right_side):
    return lax.dot_general(
        left_side, right_side, (((0,), (0,)), ((), ())), preferred_element_type=jnp.float32
    )


def layer_norm(inputs, gain_vec, bias_vec):
    centred = inputs - jnp.mean(inputs, axis=-1, keepdims=True)
    inverse = lax.rsqrt(jnp.mean(centred * centred, axis=-1, keepdims=True) + 1e-05)
    scaled = centred * inverse
    return (scaled * gain_vec + bias_vec, scaled, inverse)


def norm_back(grad_normed, gain_vec, scaled, inverse):
    inner_grad = grad_normed * gain_vec
    return inverse * (
        inner_grad
        - jnp.mean(inner_grad, axis=-1, keepdims=True)
        - scaled * jnp.mean(inner_grad * scaled, axis=-1, keepdims=True)
    )


def silu_slope(pre_act):
    sig = jax.nn.sigmoid(pre_act)
    return sig * (1.0 + pre_act * (1.0 - sig))


def choose(routes, options):
    return jnp.sum(
        (routes[..., None] == jnp.arange(options, dtype=jnp.int32)).astype(jnp.float32), axis=-2
    )


def segment_of(seq_ends, positions):
    return jnp.sum((seq_ends[None, :] <= positions[:, None]).astype(jnp.int32), axis=1)


def body(
    tokens_in,
    out_grad,
    deal_order,
    seq_lengths,
    value_routes,
    output_routes,
    ffn_routes,
    norm1_gain,
    norm1_bias,
    norm2_gain,
    norm2_bias,
    query_weight,
    key_weight,
    value_weight,
    output_weight,
    value_router,
    output_router,
    ffn_router,
    ffn_in,
    ffn_out,
):
    weights = (
        lax.all_gather(norm1_gain, ("group", "shard"), axis=0, tiled=True),
        lax.all_gather(norm1_bias, ("group", "shard"), axis=0, tiled=True),
        lax.all_gather(norm2_gain, ("group", "shard"), axis=0, tiled=True),
        lax.all_gather(norm2_bias, ("group", "shard"), axis=0, tiled=True),
        lax.all_gather(query_weight, ("group", "shard"), axis=0, tiled=True),
        lax.all_gather(key_weight, ("group", "shard"), axis=0, tiled=True),
        lax.all_gather(value_weight, ("group", "shard"), axis=0, tiled=True),
        lax.all_gather(output_weight, ("group", "shard"), axis=0, tiled=True),
        lax.all_gather(value_router, ("group", "shard"), axis=0, tiled=True),
        lax.all_gather(output_router, ("group", "shard"), axis=0, tiled=True),
        lax.all_gather(ffn_router, ("group", "shard"), axis=0, tiled=True),
    )
    (
        gain_one,
        bias_one,
        gain_two,
        bias_two,
        w_query,
        w_key,
        w_value,
        w_output,
        r_value,
        r_output,
        r_ffn,
    ) = weights
    ffn_rows = (
        lax.all_gather(ffn_in, "group", axis=0, tiled=True),
        lax.all_gather(ffn_out, "group", axis=0, tiled=True),
    )
    local_rows = tokens_in.shape[0]
    slot_rows = deal_order[0]
    arrived = lax.all_to_all(tokens_in, "shard", split_axis=0, concat_axis=0, tiled=True)
    worker_in = arrived[slot_rows]
    inputs_f = worker_in.astype(jnp.float32)
    normed, scaled_one, inverse_one = layer_norm(
        inputs_f, gain_one.astype(jnp.float32), bias_one.astype(jnp.float32)
    )
    normed_one = normed.astype(jnp.bfloat16)
    queries = matmul(normed_one, w_query).astype(jnp.bfloat16)
    key_rows = matmul(normed_one, w_key).astype(jnp.bfloat16)
    projected = matmul(worker_in, w_value)
    per_expert = projected.reshape(local_rows, HEADS, VEXP, DH)
    value_sig = jax.nn.sigmoid(matmul(normed_one, r_value)).reshape(local_rows, HEADS, VEXP)
    value_mask = choose(value_routes, VEXP)
    value_gate = value_sig * value_mask
    values = (
        jnp.sum(value_gate[..., None] * per_expert, axis=2)
        .reshape(local_rows, HEADS * DH)
        .astype(jnp.bfloat16)
    )
    reach_back = LMAX // local_rows
    window_keys = [key_rows]
    window_values = [values]
    for distance in range(1, reach_back + 1):
        earlier = passed_along((key_rows, values), "shard", distance)
        window_keys.insert(0, earlier[0])
        window_values.insert(0, earlier[1])
    key_span = (reach_back + 1) * local_rows
    keys_three = jnp.concatenate(window_keys, axis=0).reshape(key_span, HEADS, DH)
    values_three = jnp.concatenate(window_values, axis=0).reshape(key_span, HEADS, DH)
    worker = lax.axis_index("shard")
    seq_ends = jnp.cumsum(seq_lengths[0])
    pos_query = worker * local_rows + jnp.arange(local_rows, dtype=jnp.int32)
    pos_key = (worker - reach_back) * local_rows + jnp.arange(key_span, dtype=jnp.int32)
    seg_query = segment_of(seq_ends, pos_query)
    seg_key = segment_of(seq_ends, pos_key)
    block_rows = min(512, local_rows)
    blocks = local_rows // block_rows
    score_scale = DH ** (-0.5)
    query_three = queries.reshape(blocks, block_rows, HEADS, DH)

    def allowed():
        return (
            (seg_key[None, :] == seg_query[:, None])
            & (pos_key[None, :] <= pos_query[:, None])
            & (pos_key[None, :] >= 0)
        )

    def forward_block(block_index):
        query_block = lax.dynamic_index_in_dim(query_three, block_index, 0, keepdims=False)
        scores = (
            jnp.einsum("qhd,khd->hqk", query_block, keys_three, preferred_element_type=jnp.float32)
            * score_scale
        )
        scores = jnp.where(allowed()[None], scores, -1e30)
        row_max = jnp.max(scores, axis=-1, keepdims=True)
        exponent = jnp.exp(scores - row_max)
        row_total = jnp.sum(exponent, axis=-1, keepdims=True)
        soft_low = (exponent / row_total).astype(jnp.bfloat16)
        result = jnp.einsum(
            "hqk,khd->qhd", soft_low, values_three, preferred_element_type=jnp.float32
        )
        return (result, (row_max + jnp.log(row_total))[..., 0])

    attended, log_total = lax.map(forward_block, jnp.arange(blocks, dtype=jnp.int32))
    attended = attended.reshape(local_rows, HEADS, DH)
    out_sig = jax.nn.sigmoid(matmul(normed_one, r_output)).reshape(local_rows, HEADS, VEXP)
    out_mask = choose(output_routes, VEXP)
    out_gate = out_sig * out_mask
    mixed_rows = (
        (out_gate[..., None] * attended[:, :, None, :])
        .reshape(local_rows, HEADS * VEXP * DH)
        .astype(jnp.bfloat16)
    )
    branch = transposed(mixed_rows, w_output).astype(jnp.bfloat16)
    placed = jnp.zeros_like(branch).at[slot_rows].set(branch)
    branch_home = lax.all_to_all(placed, "shard", split_axis=0, concat_axis=0, tiled=True)
    middle = tokens_in.astype(jnp.float32) + branch_home.astype(jnp.float32)
    normed_mid, scaled_two, inverse_two = layer_norm(
        middle, gain_two.astype(jnp.float32), bias_two.astype(jnp.float32)
    )
    normed_two = normed_mid.astype(jnp.bfloat16)
    ffn_sig = jax.nn.sigmoid(matmul(normed_two, r_ffn))
    expert_count = r_ffn.shape[1]
    capacity = local_rows * FTOP * 3 // (2 * expert_count)
    member = choose(ffn_routes, expert_count)
    ffn_gate = ffn_sig * member
    ranking = jnp.cumsum(member.astype(jnp.int32), axis=0) - 1
    slot_index = jnp.take_along_axis(ranking, ffn_routes, axis=1)
    row_ids = jnp.broadcast_to(jnp.arange(local_rows, dtype=jnp.int32)[:, None], ffn_routes.shape)
    slot_table = (
        jnp.full((expert_count, capacity), local_rows, jnp.int32)
        .at[ffn_routes.reshape(-1), slot_index.reshape(-1)]
        .set(row_ids.reshape(-1))
    )
    expert_cols = jnp.arange(expert_count, dtype=jnp.int32)[:, None]
    gate_pad = jnp.concatenate([ffn_gate, jnp.zeros((1, expert_count), jnp.float32)], axis=0)
    gate_table = gate_pad[slot_table, expert_cols]
    width = middle.shape[1]
    hidden_pad = jnp.concatenate(
        [middle.astype(jnp.bfloat16), jnp.zeros((1, width), jnp.bfloat16)], axis=0
    )
    grad_pad = jnp.concatenate([out_grad, jnp.zeros((1, width), jnp.bfloat16)], axis=0)
    w_in, w_out = (
        lax.all_gather(ffn_rows[0], "shard", axis=1, tiled=True),
        lax.all_gather(ffn_rows[1], "shard", axis=1, tiled=True),
    )
    group_size = 8
    rounds = expert_count // group_size

    def expert_slices(round_index):
        first_expert = round_index * group_size
        group_rows = lax.dynamic_slice_in_dim(slot_table, first_expert, group_size, 0)
        group_gates = lax.dynamic_slice_in_dim(gate_table, first_expert, group_size, 0)
        group_in = lax.dynamic_slice_in_dim(
            w_in.reshape(width, expert_count, FH), first_expert, group_size, 1
        )
        group_out = lax.dynamic_slice_in_dim(
            w_out.reshape(width, expert_count, FH), first_expert, group_size, 1
        )
        return (first_expert, group_rows, group_gates, group_in, group_out)

    def ffn_step(running, round_index):
        first_expert, group_rows, group_gates, group_in, group_out = expert_slices(round_index)
        group_inputs = hidden_pad[group_rows]
        pre_act = jnp.einsum(
            "ecd,def->ecf", group_inputs, group_in, preferred_element_type=jnp.float32
        )
        active = (jax.nn.silu(pre_act) * group_gates[..., None]).astype(jnp.bfloat16)
        produced = jnp.einsum("ecf,def->ecd", active, group_out, preferred_element_type=jnp.float32)
        return (running.at[group_rows].add(produced), None)

    feed = lax.scan(
        ffn_step,
        jnp.zeros((local_rows + 1, width), jnp.float32),
        jnp.arange(rounds, dtype=jnp.int32),
    )[0]

    def ffn_back(running, round_index):
        grad_rows, gate_grads, grad_in3, grad_out3 = running
        first_expert, group_rows, group_gates, group_in, group_out = expert_slices(round_index)
        group_inputs = hidden_pad[group_rows]
        pre_act = jnp.einsum(
            "ecd,def->ecf", group_inputs, group_in, preferred_element_type=jnp.float32
        )
        act_pre = jax.nn.silu(pre_act)
        active = (act_pre * group_gates[..., None]).astype(jnp.bfloat16)
        group_grads = grad_pad[group_rows]
        grad_out3 = lax.dynamic_update_slice_in_dim(
            grad_out3,
            jnp.einsum("ecf,ecd->def", active, group_grads, preferred_element_type=jnp.float32),
            first_expert,
            1,
        )
        grad_active = jnp.einsum(
            "ecd,def->ecf", group_grads, group_out, preferred_element_type=jnp.float32
        )
        grad_gate_group = jnp.sum(grad_active * act_pre, axis=-1)
        grad_pre = (grad_active * group_gates[..., None] * silu_slope(pre_act)).astype(jnp.bfloat16)
        grad_in3 = lax.dynamic_update_slice_in_dim(
            grad_in3,
            jnp.einsum("ecd,ecf->def", group_inputs, grad_pre, preferred_element_type=jnp.float32),
            first_expert,
            1,
        )
        grad_rows = grad_rows.at[group_rows].add(
            jnp.einsum("ecf,def->ecd", grad_pre, group_in, preferred_element_type=jnp.float32)
        )
        round_cols = first_expert + jnp.arange(group_size, dtype=jnp.int32)[:, None]
        gate_grads = gate_grads.at[group_rows, round_cols].add(grad_gate_group)
        return ((grad_rows, gate_grads, grad_in3, grad_out3), None)

    start_state = (
        jnp.zeros((local_rows + 1, width), jnp.float32),
        jnp.zeros((local_rows + 1, expert_count), jnp.float32),
        jnp.zeros((width, expert_count, FH), jnp.float32),
        jnp.zeros((width, expert_count, FH), jnp.float32),
    )
    grad_ffn_rows, gate_grads, grad_in3, grad_out3 = lax.scan(
        ffn_back, start_state, jnp.arange(rounds, dtype=jnp.int32)
    )[0]
    local_ffn = (
        lax.psum_scatter(
            grad_in3.reshape(width, expert_count * FH).astype(jnp.bfloat16),
            "shard",
            scatter_dimension=1,
            tiled=True,
        ).astype(jnp.float32),
        lax.psum_scatter(
            grad_out3.reshape(width, expert_count * FH).astype(jnp.bfloat16),
            "shard",
            scatter_dimension=1,
            tiled=True,
        ).astype(jnp.float32),
    )
    ffn_grads = (
        lax.psum_scatter(
            local_ffn[0].astype(jnp.bfloat16), "group", scatter_dimension=0, tiled=True
        ).astype(jnp.float32),
        lax.psum_scatter(
            local_ffn[1].astype(jnp.bfloat16), "group", scatter_dimension=0, tiled=True
        ).astype(jnp.float32),
    )
    layer_out = (middle + feed[:local_rows]).astype(jnp.bfloat16)
    grad_ffn_logit = (gate_grads[:local_rows] * ffn_sig * (1.0 - ffn_sig) * member).astype(
        jnp.bfloat16
    )
    grad_second = transposed(grad_ffn_logit, r_ffn)
    grad_r_ffn = contract_rows(normed_two, grad_ffn_logit)
    grad_gain_two = jnp.sum(grad_second * scaled_two, axis=0)
    grad_bias_two = jnp.sum(grad_second, axis=0)
    grad_middle = (
        out_grad.astype(jnp.float32)
        + grad_ffn_rows[:local_rows]
        + norm_back(grad_second, gain_two.astype(jnp.float32), scaled_two, inverse_two)
    )
    back_rows = lax.all_to_all(
        grad_middle.astype(jnp.bfloat16), "shard", split_axis=0, concat_axis=0, tiled=True
    )
    grad_branch = back_rows[slot_rows]
    grad_mixed = matmul(grad_branch, w_output).reshape(local_rows, HEADS, VEXP, DH)
    grad_w_output = contract_rows(grad_branch, mixed_rows)
    grad_out_gate = jnp.sum(grad_mixed * attended[:, :, None, :], axis=-1)
    grad_attended = jnp.sum(grad_mixed * out_gate[..., None], axis=2).astype(jnp.bfloat16)
    grad_out_logit = (
        (grad_out_gate * out_sig * (1.0 - out_sig) * out_mask)
        .reshape(local_rows, HEADS * VEXP)
        .astype(jnp.bfloat16)
    )
    grad_three = grad_attended.reshape(blocks, block_rows, HEADS, DH)

    def backward_block(running, block_index):
        key_grad, value_grad = running
        query_block = lax.dynamic_index_in_dim(query_three, block_index, 0, keepdims=False)
        grad_block = lax.dynamic_index_in_dim(grad_three, block_index, 0, keepdims=False)
        log_block = lax.dynamic_index_in_dim(log_total, block_index, 0, keepdims=False)
        scores = (
            jnp.einsum("qhd,khd->hqk", query_block, keys_three, preferred_element_type=jnp.float32)
            * score_scale
        )
        scores = jnp.where(allowed()[None], scores, -1e30)
        soft = jnp.exp(scores - log_block[..., None])
        grad_soft = jnp.einsum(
            "qhd,khd->hqk", grad_block, values_three, preferred_element_type=jnp.float32
        )
        row_inner = jnp.sum(soft * grad_soft, axis=-1, keepdims=True)
        grad_scores = (soft * (grad_soft - row_inner)).astype(jnp.bfloat16)
        grad_query = (
            jnp.einsum("hqk,khd->qhd", grad_scores, keys_three, preferred_element_type=jnp.float32)
            * score_scale
        )
        key_grad = (
            key_grad
            + jnp.einsum(
                "hqk,qhd->khd", grad_scores, query_block, preferred_element_type=jnp.float32
            )
            * score_scale
        )
        value_grad = value_grad + jnp.einsum(
            "hqk,qhd->khd",
            soft.astype(jnp.bfloat16),
            grad_block,
            preferred_element_type=jnp.float32,
        )
        return ((key_grad, value_grad), grad_query)

    zero_window = jnp.zeros((key_span, HEADS, DH), jnp.float32)
    window_grads, grad_queries = lax.scan(
        backward_block, (zero_window, zero_window), jnp.arange(blocks, dtype=jnp.int32)
    )
    key_window = window_grads[0].reshape(reach_back + 1, local_rows, HEADS * DH)
    value_window = window_grads[1].reshape(reach_back + 1, local_rows, HEADS * DH)
    own_key = key_window[reach_back]
    own_value = value_window[reach_back]
    for distance in range(1, reach_back + 1):
        came_back = (
            passed_along(
                key_window[reach_back - distance].astype(jnp.bfloat16), "shard", -distance
            ).astype(jnp.float32),
            passed_along(
                value_window[reach_back - distance].astype(jnp.bfloat16), "shard", -distance
            ).astype(jnp.float32),
        )
        own_key = own_key + came_back[0]
        own_value = own_value + came_back[1]
    grad_queries = grad_queries.reshape(local_rows, HEADS * DH).astype(jnp.bfloat16)
    grad_keys = own_key.astype(jnp.bfloat16)
    grad_values = own_value.reshape(local_rows, HEADS, DH)
    grad_projected = (
        (value_gate[..., None] * grad_values[:, :, None, :])
        .reshape(local_rows, HEADS * VEXP * DH)
        .astype(jnp.bfloat16)
    )
    grad_value_gate = jnp.sum(grad_values[:, :, None, :] * per_expert, axis=-1)
    grad_value_logit = (
        (grad_value_gate * value_sig * (1.0 - value_sig) * value_mask)
        .reshape(local_rows, HEADS * VEXP)
        .astype(jnp.bfloat16)
    )
    grad_first = (
        transposed(grad_queries, w_query)
        + transposed(grad_keys, w_key)
        + transposed(grad_value_logit, r_value)
        + transposed(grad_out_logit, r_output)
    )
    grad_w_query = contract_rows(normed_one, grad_queries)
    grad_w_key = contract_rows(normed_one, grad_keys)
    grad_r_value = contract_rows(normed_one, grad_value_logit)
    grad_r_output = contract_rows(normed_one, grad_out_logit)
    grad_w_value = contract_rows(worker_in, grad_projected)
    grad_gain_one = jnp.sum(grad_first * scaled_one, axis=0)
    grad_bias_one = jnp.sum(grad_first, axis=0)
    grad_worker = norm_back(
        grad_first, gain_one.astype(jnp.float32), scaled_one, inverse_one
    ) + transposed(grad_projected, w_value)
    placed_grad = jnp.zeros_like(grad_worker).at[slot_rows].set(grad_worker)
    grad_home = lax.all_to_all(
        placed_grad.astype(jnp.bfloat16), "shard", split_axis=0, concat_axis=0, tiled=True
    ).astype(placed_grad.dtype)
    input_grad = grad_middle + grad_home
    summed = (
        lax.psum_scatter(grad_gain_one, ("group", "shard"), scatter_dimension=0, tiled=True),
        lax.psum_scatter(grad_bias_one, ("group", "shard"), scatter_dimension=0, tiled=True),
        lax.psum_scatter(grad_gain_two, ("group", "shard"), scatter_dimension=0, tiled=True),
        lax.psum_scatter(grad_bias_two, ("group", "shard"), scatter_dimension=0, tiled=True),
        lax.psum_scatter(grad_w_query, ("group", "shard"), scatter_dimension=0, tiled=True),
        lax.psum_scatter(grad_w_key, ("group", "shard"), scatter_dimension=0, tiled=True),
        lax.psum_scatter(grad_w_value, ("group", "shard"), scatter_dimension=0, tiled=True),
        lax.psum_scatter(grad_w_output, ("group", "shard"), scatter_dimension=0, tiled=True),
        lax.psum_scatter(grad_r_value, ("group", "shard"), scatter_dimension=0, tiled=True),
        lax.psum_scatter(grad_r_output, ("group", "shard"), scatter_dimension=0, tiled=True),
        lax.psum_scatter(grad_r_ffn, ("group", "shard"), scatter_dimension=0, tiled=True),
    )
    return (
        layer_out,
        input_grad,
        summed[0],
        summed[1],
        summed[2],
        summed[3],
        summed[4],
        summed[5],
        summed[6],
        summed[7],
        summed[8],
        summed[9],
        summed[10],
        ffn_grads[0],
        ffn_grads[1],
    )


def solution(mesh):
    placed = (
        P(("group", "shard"), None),
        P(("group", "shard"), None),
        P(("group", "shard"), None),
        P("group", None),
        P(("group", "shard"), None, None),
        P(("group", "shard"), None, None),
        P(("group", "shard"), None),
        P(("group", "shard")),
        P(("group", "shard")),
        P(("group", "shard")),
        P(("group", "shard")),
        P(("group", "shard"), None),
        P(("group", "shard"), None),
        P(("group", "shard"), None),
        P(("group", "shard"), None),
        P(("group", "shard"), None),
        P(("group", "shard"), None),
        P(("group", "shard"), None),
        P("group", "shard"),
        P("group", "shard"),
    )
    return jax.shard_map(
        body,
        mesh=mesh,
        in_specs=placed,
        out_specs=(
            P(("group", "shard"), None),
            P(("group", "shard"), None),
            P(("group", "shard")),
            P(("group", "shard")),
            P(("group", "shard")),
            P(("group", "shard")),
            P(("group", "shard"), None),
            P(("group", "shard"), None),
            P(("group", "shard"), None),
            P(("group", "shard"), None),
            P(("group", "shard"), None),
            P(("group", "shard"), None),
            P(("group", "shard"), None),
            P("group", "shard"),
            P("group", "shard"),
        ),
        check_vma=False,
    )
```

profile of v0, /device:TPU:8, one launch (start us, length us, event | category | flops | bytes accessed | tf_op | source)
XLA Modules:
  0.0 2985.4 jit_solution(2006838743225628253)
XLA Ops:
  32.8 23.4 all-gather.23.cloned.1.call-done
  63.3 43.6 %all-reduce.12 = (bf16[1024]{0:T(1024)(128)(2,1)S(1)}, bf16[1024]{0:T(1024)(128)(2,1)S(1)}, bf16[1024]{0:T(1024)(128)(2,1)S(1)}, bf16[1024]{0:T(1024)(128)(2,1)S(1)}) all-reduce(bf16[1024]{0:T(1024)(128)(2,1)S(1)} %dynamic-update-slice.1, ...), channel_id=1, replica_groups=mesh['group'=2,'shard'=16] {'group','shard'}, use_global_device_ids=true, to_apply=%add.4 | all-reduce | flops 4096 | bytes 16384
  106.8 39.7 %all-gather.1 = bf16[32,32,20]{1,2,0:T(8,128)(2,1)S(1)} all-gather(bf16[1,32,20]{1,2,0:T(8,128)(2,1)S(1)} %bitcast.323), channel_id=1, replica_groups=mesh['group'=2,'shard'=16] {'group','shard'}, dimensions={0}, use_global_device_ids=true | all-gather | bytes 42240 | tf_op jit(solution)/shard_map/all_gather | solution.py:98
  146.8 37.3 %all-gather = bf16[32,32,20]{1,2,0:T(8,128)(2,1)S(1)} all-gather(bf16[1,32,20]{1,2,0:T(8,128)(2,1)S(1)} %bitcast.324), channel_id=1, replica_groups=mesh['group'=2,'shard'=16] {'group','shard'}, dimensions={0}, use_global_device_ids=true | all-gather | bytes 42240 | tf_op jit(solution)/shard_map/all_gather | solution.py:99
  210.6 24.2 collective-permute-done.8
  234.8 28.1 collective-permute-start.13
  264.8 21.4 collective-permute-start.14
  340.9 23.7 collective-permute-start
  419.0 30.4 %collective-permute-start.5 = (bf16[512,512]{0,1:T(8,128)(2,1)S(1)}, bf16[512,512]{0,1:T(8,128)(2,1)S(1)}, u32[]{:S(2)}, u32[]{:S(2)}) collective-permute-start(bf16[512,512]{0,1:T(8,128)(2,1)S(1)} %bitcast.303), channel_id=1, source_target_pairs={{0,3},{1,4},{2,5},{3,6},{4,7},{5,8},{6,9},{7,10},{8,11},{9,12},{10... | collective-permute-start | bytes 1572872 | tf_op jit(solution)/shard_map/ppermute | solution.py:17
  455.1 20.4 collective-permute-start.7
  475.6 23.6 collective-permute-done.4
  543.6 93.9 %all-to-all-start.1 = ((bf16[16,32,1024]{2,1,0:T(8,128)(2,1)}), bf16[16,32,1024]{2,1,0:T(8,128)(2,1)S(1)}, u32[]{:S(2)}, u32[]{:S(2)}) async-start(bf16[16,32,1024]{2,1,0:T(8,128)(2,1)} %bitcast.30), calls=%async_computation.1 | async-start | bytes 2097152 | tf_op jit(solution)/shard_map/all_to_all | solution.py:196
  639.3 79.4 %all_gather.57 = bf16[1024,64]{1,0:T(8,128)(2,1)S(1)} all-gather(bf16[32,64]{1,0:T(8,128)(2,1)S(1)} %copy-done.84), channel_id=1, replica_groups=mesh['group'=2,'shard'=16] {'group','shard'}, dimensions={0}, use_global_device_ids=true | all-gather | bytes 135168 | tf_op jit(solution)/shard_map/all_gather | solution.py:100
  728.8 65.5 %gather_fusion.6 = s32[8192]{0:T(1024)S(1)} fusion(s32[512,64]{0,1:T(8,128)S(1)} %bitcast_bitcast_fusion, s32[8192]{0:T(1024)S(1)} %reshape.551), kind=kCustom, calls=%fused_computation.6 | custom fusion | bytes 131072 | tf_op jit(solution)/shard_map/jit(take_along_axis)/gather | solution.py:208
  795.3 30.5 %scatter_custom_fusion.5 = s32[12288]{0:T(1024)S(1)} fusion(s32[8192]{0:T(1024)S(1)} %broadcast_select_fusion.1, s32[8192]{0:T(1024)S(1)} %reshape.597, s32[]{:T(128)} %constant.95.clone.1), kind=kCustom, calls=%fused_computation.205 | custom fusion | bytes 49156
  826.1 98.1 %gather_fusion.4 = f32[12288]{0:T(1024)S(1)} fusion(f32[513,64]{0,1:T(8,128)S(1)} %concatenate.28, s32[12288]{0:T(1024)S(1)} %reshape.537), kind=kCustom, calls=%fused_computation.4 | custom fusion | bytes 196608 | tf_op jit(solution)/shard_map/gather | solution.py:217
  937.4 530.7 %while.5 = (s32[]{:T(128)}, f32[513,1024]{1,0:T(8,128)S(1)}, f32[513,64]{0,1:T(8,128)S(1)}, bf16[1024,64,128]{0,2,1:T(8,128)(2,1)}, bf16[1024,64,128]{2,0,1:T(8,...) while((s32[]{:T(128)}, f32[513,1024]{1,0:T(8,128)S(1)}, ...), condition=%wide.region_24.25_spmd, body=%wide.region_20.24_spmd.sunk | while | flops 2018608640 | bytes 86972896 | solution.py:298
  1468.1 21.3 copy.180
  1522.2 44.7 %all-to-all-done.2 = bf16[16,32,1024]{2,1,0:T(8,128)(2,1)S(1)} async-done(((bf16[16,32,1024]{2,1,0:T(8,128)(2,1)}), bf16[16,32,1024]{2,1,0:T(8,128)(2,1)S(1)}, u32[]{:S(2)}, u32[]{:S(2)}) %all-to-all-start.2) | async-done | bytes 1048608 | tf_op jit(solution)/shard_map/all_to_all | solution.py:336
  1575.5 21.6 fusion.110
  1624.4 43.9 %collective-permute-start.26 = (bf16[512,512]{0,1:T(8,128)(2,1)}, bf16[512,512]{0,1:T(8,128)(2,1)}, u32[]{:S(2)}, u32[]{:S(2)}) collective-permute-start(bf16[512,512]{0,1:T(8,128)(2,1)} %bitcast.55), channel_id=1, source_target_pairs={{3,0},{4,1},{5,2},{6,3},{7,4},{8,5},{9,6},{10,7},{11,8},{12,9},{13... | collective-permute-start | bytes 1572872 | tf_op jit(solution)/shard_map/ppermute | solution.py:17
  1725.5 46.3 %reduce-scatter.26.cloned.1.call-done = bf16[1024,512]{1,0:T(8,128)(2,1)} async-done(((bf16[1024,8192]{1,0:T(8,128)(2,1)}), bf16[1024,512]{1,0:T(8,128)(2,1)}) %reduce-scatter.26.cloned.1.call-update) | async-done | bytes 1048592 | tf_op jit(solution)/shard_map/reduce_scatter | solution.py:302
  1771.8 181.0 %reduce-scatter.30.cloned.1.call-done = bf16[1024,512]{1,0:T(8,128)(2,1)} async-done(((bf16[1024,8192]{1,0:T(8,128)(2,1)}), bf16[1024,512]{1,0:T(8,128)(2,1)}) %reduce-scatter.30.cloned.1.call-update) | async-done | bytes 1048592 | tf_op jit(solution)/shard_map/reduce_scatter | solution.py:308
  1954.2 30.0 %multiply_reduce_fusion.1 = (f32[4,512]{1,0:T(4,128)S(1)}, f32[4,512,4608]{2,1,0:T(8,128)}) fusion(f32[4,512,4608]{2,1,0:T(8,128)} %get-tuple-element.341, f32[4,512]{1,0:T(4,128)S(1)} %log_add_fusion, bf16[512,4,128]{0,2,1:T(8,128)(2,1)} %copy-done.15, bf16[4608,4,128]{0,2,1:T(8,128)(2,1)} %bitcast.286), kind=kOutput, calls=%fused_computation.56 | convolution fusion | flops 2444228608 | bytes 80756736 | tf_op jit(solution)/shard_map/while/body/eval_jaxpr/qhd,khd->hqk/dot_general | solution.py:362
  1984.3 30.6 %multiply_convert_fusion.4 = bf16[4,512,4608]{2,1,0:T(8,128)(2,1)} fusion(f32[4,512,4608]{2,1,0:T(8,128)} %get-tuple-element.346, f32[4,512,4608]{2,1,0:T(8,128)} %get-tuple-element.341, f32[4,512]{1,0:T(4,128)S(1)} %get-tuple-element.345, f32[4,512]{1,0:T(4,128)S(1)} %log_add_fusion), kind=kLoop, calls=%fused_computation.55 | loop fusion | flops 37748736 | bytes 94388224 | tf_op jit(solution)/shard_map/while/body/eval_jaxpr/convert_element_type | solution.py:366
  2055.6 42.1 %collective-permute-start.18 = (bf16[512,512]{0,1:T(8,128)(2,1)S(1)}, bf16[512,512]{0,1:T(8,128)(2,1)S(1)}, u32[]{:S(2)}, u32[]{:S(2)}) collective-permute-start(bf16[512,512]{0,1:T(8,128)(2,1)S(1)} %bitcast.310), channel_id=1, source_target_pairs={{3,0},{4,1},{5,2},{6,3},{7,4},{8,5},{9,6},{10,7},{11,8},{12,9},{13... | collective-permute-start | bytes 1572872 | tf_op jit(solution)/shard_map/ppermute | solution.py:17
  2183.9 28.0 all-to-all-start.3
  2212.2 253.4 %while.4 = (s32[]{:T(128)}, f32[513,1024]{1,0:T(8,128)S(1)}, s32[8]{0:T(128)S(1)}, s32[64,192]{1,0:T(8,128)}, bf16[513,1024]{1,0:T(8,128)(2,1)S(1)}, /*index=5*/...) while((s32[]{:T(128)}, f32[513,1024]{1,0:T(8,128)S(1)}, ...), condition=%wide.region_19.20_spmd, body=%wide.region_17.19_spmd.sunk | while | flops 808065536 | bytes 38868160 | solution.py:252
  2470.1 40.9 %all-reduce.11 = (f32[1024]{0:T(1024)S(1)}, f32[1024]{0:T(1024)S(1)}, f32[1024]{0:T(1024)S(1)}, f32[1024]{0:T(1024)S(1)}) all-reduce(f32[1024]{0:T(1024)S(1)} %copy-done.74, f32[1024]{0:T(1024)S(1)} %copy-done.75, f32[1024]{0:T(1024)S(1)} %copy-done.80, ...), channel_id=2, replica_groups=mesh['group'=2,'shard'=16] {'group','shard'}, use_global_device_ids=true, to_apply=%region_35.36.clone | all-reduce | flops 4096 | bytes 32768
  2536.9 135.8 %reduce-scatter.18.cloned.1.call-done = f32[32,512]{1,0:T(8,128)} async-done(((f32[1024,512]{1,0:T(8,128)}), f32[32,512]{1,0:T(8,128)}) %reduce-scatter.18.cloned.1.call-update) | async-done | bytes 65552 | tf_op jit(solution)/shard_map/reduce_scatter | solution.py:446
  2672.7 152.5 %reduce-scatter.22.cloned.1.call-done = f32[32,2560]{1,0:T(8,128)} async-done(((f32[1024,2560]{1,0:T(8,128)}), f32[32,2560]{1,0:T(8,128)}) %reduce-scatter.22.cloned.1.call-update) | async-done | bytes 327696 | tf_op jit(solution)/shard_map/reduce_scatter | solution.py:448
  2825.2 153.5 %reduce-scatter.20.cloned.1.call-done = f32[32,2560]{1,0:T(8,128)} async-done(((f32[1024,2560]{1,0:T(8,128)}), f32[32,2560]{1,0:T(8,128)}) %reduce-scatter.20.cloned.1.call-update) | async-done | bytes 327696 | tf_op jit(solution)/shard_map/reduce_scatter | solution.py:447
  (810 shorter events, 1301.9 us)
Async XLA Ops:
  11.5 181.9 %all-gather.15.cloned.1.call-start = ((), (), s32[]{:S(2)}) async-start(), calls=%async_computation.17 | async-start | bytes 1081344 | tf_op jit(solution)/shard_map/all_gather | solution.py:95
  12.2 196.3 %all-gather.13.cloned.1.call-start = ((), (), s32[]{:S(2)}) async-start(), calls=%async_computation.16 | async-start | bytes 1081344 | tf_op jit(solution)/shard_map/all_gather | solution.py:94
  12.8 322.2 %all-gather.11.cloned.1.call-start = ((), (), s32[]{:S(2)}) async-start(), calls=%async_computation.15 | async-start | bytes 5406720 | tf_op jit(solution)/shard_map/all_gather | solution.py:96
  13.4 518.0 %all-gather.17.cloned.1.call-start = ((), (), s32[]{:S(2)}) async-start(), calls=%async_computation.18 | async-start | bytes 5406720 | tf_op jit(solution)/shard_map/all_gather | solution.py:97
  14.0 911.0 %all-gather.21.cloned.1.call-start = ((), (), s32[]{:S(2)}) async-start(), calls=%async_computation.20 | async-start | bytes 17825792 | tf_op jit(solution)/shard_map/all_gather | solution.py:224
  32.7 892.3 %all-gather.25.cloned.1.call-start = ((), (), s32[]{:S(2)}) async-start(), calls=%async_computation.22 | async-start | bytes 17825792 | tf_op jit(solution)/shard_map/all_gather | solution.py:225
  56.2 132.3 %all-to-all-start = ((bf16[16,32,1024]{2,1,0:T(8,128)(2,1)}), bf16[16,32,1024]{2,1,0:T(8,128)(2,1)S(1)}, u32[]{:S(2)}, u32[]{:S(2)}) async-start(bf16[16,32,1024]{2,1,0:T(8,128)(2,1)} %bitcast.18), calls=%async_computation | async-start | bytes 2097152 | tf_op jit(solution)/shard_map/all_to_all | solution.py:121
  201.7 86.4 %collective-permute-start.10 = (bf16[512,512]{1,0:T(8,128)(2,1)S(1)}, bf16[512,512]{1,0:T(8,128)(2,1)}, u32[]{:S(2)}, u32[]{:S(2)}) collective-permute-start(bf16[512,512]{1,0:T(8,128)(2,1)S(1)} %convolution_convert_fusion.1), channel_id=1, source_target_pairs={{0,6},{1,7},{2,8},{3,9},{4,10},{5,11},{6,12},{7,13},{8,14},{9,15},... | collective-permute-start | bytes 1572872 | tf_op jit(solution)/shard_map/ppermute | solution.py:17
  203.8 88.3 %collective-permute-start.11 = (bf16[512,512]{1,0:T(8,128)(2,1)S(1)}, bf16[512,512]{1,0:T(8,128)(2,1)}, u32[]{:S(2)}, u32[]{:S(2)}) collective-permute-start(bf16[512,512]{1,0:T(8,128)(2,1)S(1)} %convolution_convert_fusion.1), channel_id=1, source_target_pairs={{0,5},{1,6},{2,7},{3,8},{4,9},{5,10},{6,11},{7,12},{8,13},{9,14},{... | collective-permute-start | bytes 1572872 | tf_op jit(solution)/shard_map/ppermute | solution.py:17
  206.5 87.5 %collective-permute-start.12 = (bf16[512,512]{1,0:T(8,128)(2,1)S(1)}, bf16[512,512]{1,0:T(8,128)(2,1)}, u32[]{:S(2)}, u32[]{:S(2)}) collective-permute-start(bf16[512,512]{1,0:T(8,128)(2,1)S(1)} %convolution_convert_fusion.1), channel_id=1, source_target_pairs={{0,4},{1,5},{2,6},{3,7},{4,8},{5,9},{6,10},{7,11},{8,12},{9,13},{1... | collective-permute-start | bytes 1572872 | tf_op jit(solution)/shard_map/ppermute | solution.py:17
  366.0 89.1 %collective-permute-start.2 = (bf16[512,512]{0,1:T(8,128)(2,1)S(1)}, bf16[512,512]{0,1:T(8,128)(2,1)S(1)}, u32[]{:S(2)}, u32[]{:S(2)}) collective-permute-start(bf16[512,512]{0,1:T(8,128)(2,1)S(1)} %bitcast.300), channel_id=1, source_target_pairs={{0,6},{1,7},{2,8},{3,9},{4,10},{5,11},{6,12},{7,13},{8,14},{9,15},... | collective-permute-start | bytes 1572872 | tf_op jit(solution)/shard_map/ppermute | solution.py:17
  374.9 100.7 %collective-permute-start.3 = (bf16[512,512]{0,1:T(8,128)(2,1)S(1)}, bf16[512,512]{0,1:T(8,128)(2,1)S(1)}, u32[]{:S(2)}, u32[]{:S(2)}) collective-permute-start(bf16[512,512]{0,1:T(8,128)(2,1)S(1)} %bitcast.301), channel_id=1, source_target_pairs={{0,5},{1,6},{2,7},{3,8},{4,9},{5,10},{6,11},{7,12},{8,13},{9,14},{... | collective-permute-start | bytes 1572872 | tf_op jit(solution)/shard_map/ppermute | solution.py:17
  393.5 105.7 %collective-permute-start.4 = (bf16[512,512]{0,1:T(8,128)(2,1)S(1)}, bf16[512,512]{0,1:T(8,128)(2,1)S(1)}, u32[]{:S(2)}, u32[]{:S(2)}) collective-permute-start(bf16[512,512]{0,1:T(8,128)(2,1)S(1)} %bitcast.302), channel_id=1, source_target_pairs={{0,4},{1,5},{2,6},{3,7},{4,8},{5,9},{6,10},{7,11},{8,12},{9,13},{1... | collective-permute-start | bytes 1572872 | tf_op jit(solution)/shard_map/ppermute | solution.py:17
  543.6 175.3 %all-to-all-start.1 = ((bf16[16,32,1024]{2,1,0:T(8,128)(2,1)}), bf16[16,32,1024]{2,1,0:T(8,128)(2,1)S(1)}, u32[]{:S(2)}, u32[]{:S(2)}) async-start(bf16[16,32,1024]{2,1,0:T(8,128)(2,1)} %bitcast.30), calls=%async_computation.1 | async-start | bytes 2097152 | tf_op jit(solution)/shard_map/all_to_all | solution.py:196
  637.4 1134.3 %reduce-scatter.26.cloned.1.call-start = ((), (), s32[]{:S(2)}) async-start(), calls=%async_computation.28 | async-start | bytes 17825792 | tf_op jit(solution)/shard_map/reduce_scatter | solution.py:302
  1489.4 463.4 %reduce-scatter.30.cloned.1.call-start = ((), (), s32[]{:S(2)}) async-start(), calls=%async_computation.30 | async-start | bytes 17825792 | tf_op jit(solution)/shard_map/reduce_scatter | solution.py:308
  1522.1 946.5 %reduce-scatter.36.cloned.1.call-start = ((), (), s32[]{:S(2)}) async-start(), calls=%async_computation.33 | async-start | bytes 540672
  1604.9 94.2 %collective-permute-start.28 = (bf16[512,512]{0,1:T(8,128)(2,1)}, bf16[512,512]{0,1:T(8,128)(2,1)}, u32[]{:S(2)}, u32[]{:S(2)}) collective-permute-start(bf16[512,512]{0,1:T(8,128)(2,1)} %bitcast.57), channel_id=1, source_target_pairs={{5,0},{6,1},{7,2},{8,3},{9,4},{10,5},{11,6},{12,7},{13,8},{14,9},{... | collective-permute-start | bytes 1572872 | tf_op jit(solution)/shard_map/ppermute | solution.py:17
  1606.2 104.6 %collective-permute-start.27 = (bf16[512,512]{0,1:T(8,128)(2,1)}, bf16[512,512]{0,1:T(8,128)(2,1)}, u32[]{:S(2)}, u32[]{:S(2)}) collective-permute-start(bf16[512,512]{0,1:T(8,128)(2,1)} %bitcast.56), channel_id=1, source_target_pairs={{4,0},{5,1},{6,2},{7,3},{8,4},{9,5},{10,6},{11,7},{12,8},{13,9},{1... | collective-permute-start | bytes 1572872 | tf_op jit(solution)/shard_map/ppermute | solution.py:17
  1624.4 86.4 %collective-permute-start.26 = (bf16[512,512]{0,1:T(8,128)(2,1)}, bf16[512,512]{0,1:T(8,128)(2,1)}, u32[]{:S(2)}, u32[]{:S(2)}) collective-permute-start(bf16[512,512]{0,1:T(8,128)(2,1)} %bitcast.55), channel_id=1, source_target_pairs={{3,0},{4,1},{5,2},{6,3},{7,4},{8,5},{9,6},{10,7},{11,8},{12,9},{13... | collective-permute-start | bytes 1572872 | tf_op jit(solution)/shard_map/ppermute | solution.py:17
  1695.3 818.0 %reduce-scatter.34.cloned.1.call-start = ((), (), s32[]{:S(2)}) async-start(), calls=%async_computation.32 | async-start | bytes 540672
  1725.4 792.9 %reduce-scatter.28.cloned.1.call-start = ((), (), s32[]{:S(2)}) async-start(), calls=%async_computation.29 | async-start | bytes 1572864 | tf_op jit(solution)/shard_map/reduce_scatter | solution.py:316
  1771.7 748.7 %reduce-scatter.32.cloned.1.call-start = ((), (), s32[]{:S(2)}) async-start(), calls=%async_computation.31 | async-start | bytes 1572864 | tf_op jit(solution)/shard_map/reduce_scatter | solution.py:319
  1952.8 569.8 %reduce-scatter.24.cloned.1.call-start = ((), (), s32[]{:S(2)}) async-start(), calls=%async_computation.27 | async-start | bytes 540672 | tf_op jit(solution)/shard_map/reduce_scatter | solution.py:451
  1954.2 582.7 %reduce-scatter.16.cloned.1.call-start = ((), (), s32[]{:S(2)}) async-start(), calls=%async_computation.23 | async-start | bytes 2162688 | tf_op jit(solution)/shard_map/reduce_scatter | solution.py:445
  2029.5 643.2 %reduce-scatter.18.cloned.1.call-start = ((), (), s32[]{:S(2)}) async-start(), calls=%async_computation.24 | async-start | bytes 2162688 | tf_op jit(solution)/shard_map/reduce_scatter | solution.py:446
  2041.9 87.1 %collective-permute-start.20 = (bf16[512,512]{0,1:T(8,128)(2,1)S(1)}, bf16[512,512]{0,1:T(8,128)(2,1)S(1)}, u32[]{:S(2)}, u32[]{:S(2)}) collective-permute-start(bf16[512,512]{0,1:T(8,128)(2,1)S(1)} %bitcast.312), channel_id=1, source_target_pairs={{5,0},{6,1},{7,2},{8,3},{9,4},{10,5},{11,6},{12,7},{13,8},{14,9},{... | collective-permute-start | bytes 1572872 | tf_op jit(solution)/shard_map/ppermute | solution.py:17
  2043.2 97.5 %collective-permute-start.19 = (bf16[512,512]{0,1:T(8,128)(2,1)S(1)}, bf16[512,512]{0,1:T(8,128)(2,1)S(1)}, u32[]{:S(2)}, u32[]{:S(2)}) collective-permute-start(bf16[512,512]{0,1:T(8,128)(2,1)S(1)} %bitcast.311), channel_id=1, source_target_pairs={{4,0},{5,1},{6,2},{7,3},{8,4},{9,5},{10,6},{11,7},{12,8},{13,9},{1... | collective-permute-start | bytes 1572872 | tf_op jit(solution)/shard_map/ppermute | solution.py:17
  2055.6 85.1 %collective-permute-start.18 = (bf16[512,512]{0,1:T(8,128)(2,1)S(1)}, bf16[512,512]{0,1:T(8,128)(2,1)S(1)}, u32[]{:S(2)}, u32[]{:S(2)}) collective-permute-start(bf16[512,512]{0,1:T(8,128)(2,1)S(1)} %bitcast.310), channel_id=1, source_target_pairs={{3,0},{4,1},{5,2},{6,3},{7,4},{8,5},{9,6},{10,7},{11,8},{12,9},{13... | collective-permute-start | bytes 1572872 | tf_op jit(solution)/shard_map/ppermute | solution.py:17
  2149.0 676.2 %reduce-scatter.22.cloned.1.call-start = ((), (), s32[]{:S(2)}) async-start(), calls=%async_computation.26 | async-start | bytes 10813440 | tf_op jit(solution)/shard_map/reduce_scatter | solution.py:448
  2156.5 822.2 %reduce-scatter.20.cloned.1.call-start = ((), (), s32[]{:S(2)}) async-start(), calls=%async_computation.25 | async-start | bytes 10813440 | tf_op jit(solution)/shard_map/reduce_scatter | solution.py:447
  2183.9 330.8 %all-to-all-start.3 = ((bf16[16,32,1024]{2,1,0:T(8,128)(2,1)}), bf16[16,32,1024]{2,1,0:T(8,128)(2,1)}, u32[]{:S(2)}, u32[]{:S(2)}) async-start(bf16[16,32,1024]{2,1,0:T(8,128)(2,1)} %bitcast.63), calls=%async_computation.3 | async-start | bytes 2097152 | tf_op jit(solution)/shard_map/all_to_all | solution.py:436
  (158 other events, 6278.4 us)
Sparse Core Ops, SparseCore 0:
  10.2 22.4 all-gather.18
  34.8 21.2 all-gather.22
  59.1 57.3 all-gather.14
  119.3 52.8 all-gather.12
  174.8 108.9 all-gather.10
  286.5 89.8 all-gather.16
  378.6 190.4 all-gather.20
  571.3 155.9 all-gather.24
  1489.5 282.1 reduce-scatter.25
  1775.7 177.0 reduce-scatter.29
  1955.1 128.6 reduce-scatter.35
  2086.0 135.1 reduce-scatter.33
  2223.4 28.0 reduce-scatter.27
  2253.7 20.3 reduce-scatter.31
  2276.7 124.2 reduce-scatter.23
  2403.8 133.1 reduce-scatter.15
  2539.6 133.0 reduce-scatter.17
  2675.6 149.5 reduce-scatter.21
  2828.2 150.4 reduce-scatter.19
where the time goes:
time: 3010 us; the launch traced here: 2990 us
  waiting for transfers between devices  914 us (30%)
  local copies, waits for them, and re-layouts  494 us (16%)
  starting transfers between devices  470 us (16%)
  other arithmetic  443 us (15%)
  matrix products  396 us (13%)
  blocking collectives  241 us (8%)
    ppermute x32, starting transfers between devices, passed_along(): return lax.ppermute(value, axis, pairs)  332 us
    reduce_scatter x1, waiting for transfers between devices, body(): lax.psum_scatter(grad_out3.reshape(width, expert_count * FH).astype(jnp.b...  181 us
    reduce_scatter x1, waiting for transfers between devices, body(): lax.psum_scatter(grad_w_value, ('group', 'shard'), scatter_dimension=0, t...  153 us
    reduce_scatter x1, waiting for transfers between devices, body(): lax.psum_scatter(grad_w_output, ('group', 'shard'), scatter_dimension=0,...  152 us
    ppermute x32, waiting for transfers between devices, passed_along(): return lax.ppermute(value, axis, pairs)  141 us
    reduce_scatter x1, waiting for transfers between devices, body(): lax.psum_scatter(grad_w_key, ('group', 'shard'), scatter_dimension=0, til...  136 us
    scatter-add x8, other arithmetic, ffn_back(): grad_rows.at[group_rows]  123 us
    scatter-add x8, other arithmetic, ffn_step(): return (running.at[group_rows].add(produced), None)  123 us
  transfers between devices with their start and end apart: 55, of which 24 were waited for; matrix products, arithmetic and copies ran while one was open for 26% of the time, Pallas kernels for 0%

commit v1 on v0

v1 whole, which is shorter than its diff:
```python
import functools

import jax
import jax.numpy as jnp
from jax import lax
from jax.experimental import pallas as pl
from jax.experimental.pallas import tpu as pltpu
from jax.sharding import Mesh, PartitionSpec as P

HEADS = 4
DH = 128
VEXP = 5
FH = 128
LMAX = 4096

TOK = ("group", "level", "head")


def matmul(left_side, right_side):
    return jnp.dot(left_side, right_side, preferred_element_type=jnp.float32)


def transposed(left_side, right_side):
    return lax.dot_general(
        left_side, right_side, (((1,), (1,)), ((), ())), preferred_element_type=jnp.float32
    )


def contract_rows(left_side, right_side):
    return lax.dot_general(
        left_side, right_side, (((0,), (0,)), ((), ())), preferred_element_type=jnp.float32
    )


def low(value):
    return value.astype(jnp.bfloat16)


def layer_norm(inputs, gain_vec, bias_vec):
    centred = inputs - jnp.mean(inputs, axis=-1, keepdims=True)
    inverse = lax.rsqrt(jnp.mean(centred * centred, axis=-1, keepdims=True) + 1e-05)
    scaled = centred * inverse
    return (scaled * gain_vec + bias_vec, scaled, inverse)


def norm_back(grad_normed, gain_vec, scaled, inverse):
    inner_grad = grad_normed * gain_vec
    return inverse * (
        inner_grad
        - jnp.mean(inner_grad, axis=-1, keepdims=True)
        - scaled * jnp.mean(inner_grad * scaled, axis=-1, keepdims=True)
    )


def silu_slope(pre_act, sig):
    return sig * (1.0 + pre_act * (1.0 - sig))


def to_workers(rows):
    levels = lax.axis_size("level")
    count = rows.shape[0]
    came = lax.all_to_all(
        rows.reshape(levels, count // levels, -1), "level", split_axis=0, concat_axis=0, tiled=True
    )
    came = came.reshape(levels, HEADS, count // levels // HEADS, -1)
    return came.transpose(1, 0, 2, 3).reshape(count, -1)


def to_home(rows):
    levels = lax.axis_size("level")
    count = rows.shape[0]
    out = rows.reshape(HEADS, levels, count // levels // HEADS, -1).transpose(1, 0, 2, 3)
    back = lax.all_to_all(
        out.reshape(levels, count // levels, -1), "level", split_axis=0, concat_axis=0, tiled=True
    )
    return back.reshape(count, -1)


MESH = pl.DeviceIdType.MESH


def partners(head):
    near = head + 1 - 2 * lax.rem(head, 2)
    far = lax.rem(head + 2, HEADS)
    return near, far


def greet(near, far):
    barrier = pltpu.get_barrier_semaphore()
    for peer in (near, far):
        pl.semaphore_signal(barrier, inc=1, device_id={"head": peer}, device_id_type=MESH)
    pl.semaphore_wait(barrier, 2)


def gather_kernel(own, out, local_sem, near_send, near_recv, far_send, far_recv, pass_send, pass_recv):
    head = lax.axis_index("head")
    near, far = partners(head)
    greet(near, far)

    def remote(src, dst, send, recv, peer):
        return pltpu.make_async_remote_copy(
            src_ref=src,
            dst_ref=dst,
            send_sem=send,
            recv_sem=recv,
            device_id={"head": peer},
            device_id_type=MESH,
        )

    to_far = [
        remote(own.at[i], out.at[i, head], far_send.at[i], far_recv.at[i], far)
        for i in range(HEADS)
    ]
    to_near = [
        remote(own.at[i], out.at[i, head], near_send.at[i], near_recv.at[i], near)
        for i in range(HEADS)
    ]
    passed = [
        remote(out.at[i, far], out.at[i, far], pass_send.at[i], pass_recv.at[i], near)
        for i in range(HEADS)
    ]
    kept = [
        pltpu.make_async_copy(own.at[i], out.at[i, head], local_sem.at[i]) for i in range(HEADS)
    ]
    for copy in to_far + to_near + kept:
        copy.start()
    for i in range(HEADS):
        to_far[i].wait_recv()
        passed[i].start()
    for i in range(HEADS):
        to_near[i].wait_recv()
        passed[i].wait_recv()
        kept[i].wait()
        to_far[i].wait_send()
        to_near[i].wait_send()
        passed[i].wait_send()


def level_gather(rows, collective_id):
    count, width = rows.shape
    sems = [pltpu.SemaphoreType.DMA((HEADS,))] * 7
    whole = pl.pallas_call(
        gather_kernel,
        out_shape=jax.ShapeDtypeStruct((HEADS, HEADS, count // HEADS, width), rows.dtype),
        in_specs=[pl.BlockSpec(memory_space=pl.ANY)],
        out_specs=pl.BlockSpec(memory_space=pl.ANY),
        scratch_shapes=sems,
        compiler_params=pltpu.CompilerParams(collective_id=collective_id, has_side_effects=True),
        name="level_gather",
    )(rows.reshape(HEADS, count // HEADS, width))
    return whole.reshape(HEADS * count, width)


def scatter_kernel(part, out, near_buf, send_buf, far_buf, near_send, near_recv, far_send, far_recv):
    head = lax.axis_index("head")
    near, far = partners(head)
    greet(near, far)
    across = HEADS - 1 - head

    def to_near(slot, i, dest):
        return pltpu.make_async_remote_copy(
            src_ref=part.at[i, dest],
            dst_ref=near_buf.at[slot, i],
            send_sem=near_send.at[slot, i],
            recv_sem=near_recv.at[slot, i],
            device_id={"head": near},
            device_id_type=MESH,
        )

    first = [to_near(0, i, across) for i in range(HEADS)]
    second = [to_near(1, i, near) for i in range(HEADS)]
    onward = [
        pltpu.make_async_remote_copy(
            src_ref=send_buf.at[i],
            dst_ref=far_buf.at[i],
            send_sem=far_send.at[i],
            recv_sem=far_recv.at[i],
            device_id={"head": far},
            device_id_type=MESH,
        )
        for i in range(HEADS)
    ]
    for copy in first + second:
        copy.start()
    for i in range(HEADS):
        first[i].wait_recv()
        both = part[i, far].astype(jnp.float32) + near_buf[0, i].astype(jnp.float32)
        send_buf[i] = both.astype(jnp.bfloat16)
        onward[i].start()
    for i in range(HEADS):
        second[i].wait_recv()
        out[i] = part[i, head].astype(jnp.float32) + near_buf[1, i].astype(jnp.float32)
    for i in range(HEADS):
        onward[i].wait_recv()
        out[i] = out[i] + far_buf[i].astype(jnp.float32)
    for i in range(HEADS):
        first[i].wait_send()
        second[i].wait_send()
        onward[i].wait_send()


def level_scatter(rows, collective_id):
    total, width = rows.shape
    piece = total // (HEADS * HEADS)
    low_type = jnp.bfloat16
    mine = pl.pallas_call(
        scatter_kernel,
        out_shape=jax.ShapeDtypeStruct((HEADS, piece, width), jnp.float32),
        in_specs=[pl.BlockSpec(memory_space=pltpu.VMEM)],
        out_specs=pl.BlockSpec(memory_space=pltpu.VMEM),
        scratch_shapes=[
            pltpu.VMEM((2, HEADS, piece, width), low_type),
            pltpu.VMEM((HEADS, piece, width), low_type),
            pltpu.VMEM((HEADS, piece, width), low_type),
            pltpu.SemaphoreType.DMA((2, HEADS)),
            pltpu.SemaphoreType.DMA((2, HEADS)),
            pltpu.SemaphoreType.DMA((HEADS,)),
            pltpu.SemaphoreType.DMA((HEADS,)),
        ],
        compiler_params=pltpu.CompilerParams(
            collective_id=collective_id, has_side_effects=True, vmem_limit_bytes=32 * 2**20
        ),
        name="level_scatter",
    )(rows.reshape(HEADS, HEADS, piece, width))
    return mine.reshape(HEADS * piece, width)


BLOCK = 512
LOG2E = 1.4426950408889634


def dot(left_side, right_side, left_dim, right_dim):
    return lax.dot_general(
        left_side,
        right_side,
        (((left_dim,), (right_dim,)), ((), ())),
        preferred_element_type=jnp.float32,
    )


def attend_kernel(first, last, q, k, v, pos_q, start_q, pos_k, out, lse, top, total, acc):
    at = pl.program_id(0)
    rate = LOG2E * DH ** (-0.5)
    top[...] = jnp.full_like(top, -1e30)
    total[...] = jnp.zeros_like(total)
    acc[...] = jnp.zeros_like(acc)
    query = q[...]
    row_at, row_from = pos_q[...], start_q[...]

    def step(block, carry):
        rows = pl.ds(pl.multiple_of(block * BLOCK, BLOCK), BLOCK)
        scores = dot(query, k[rows, :], 1, 1)
        key_at = pos_k[block]
        scores = jnp.where((key_at >= row_from) & (key_at <= row_at), scores, -1e30)
        old = top[...]
        new = jnp.maximum(old, jnp.max(scores, axis=1, keepdims=True))
        shrink = jnp.exp2((old - new) * rate)
        weight = jnp.exp2((scores - new) * rate)
        total[...] = total[...] * shrink + jnp.sum(weight, axis=1, keepdims=True)
        acc[...] = acc[...] * shrink + dot(weight.astype(jnp.bfloat16), v[rows, :], 1, 0)
        top[...] = new
        return carry

    lax.fori_loop(first[at], last[at] + 1, step, 0)
    out[...] = acc[...] / total[...]
    lse[...] = top[...] * rate + jnp.log2(total[...])


def attend(first, last, queries, window, pos_q, start_q, pos_k):
    rows = queries.shape[0]
    span = window.shape[0]
    column = pl.BlockSpec((BLOCK, 1), lambda i, *_: (i, 0))
    grid_spec = pltpu.PrefetchScalarGridSpec(
        num_scalar_prefetch=2,
        grid=(rows // BLOCK,),
        in_specs=[
            pl.BlockSpec((BLOCK, DH), lambda i, *_: (i, 0)),
            pl.BlockSpec((span, DH), lambda i, *_: (0, 0)),
            pl.BlockSpec((span, DH), lambda i, *_: (0, 1)),
            column,
            column,
            pl.BlockSpec((span // BLOCK, 1, BLOCK), lambda i, *_: (0, 0, 0)),
        ],
        out_specs=[pl.BlockSpec((BLOCK, DH), lambda i, *_: (i, 0)), column],
        scratch_shapes=[
            pltpu.VMEM((BLOCK, 1), jnp.float32),
            pltpu.VMEM((BLOCK, 1), jnp.float32),
            pltpu.VMEM((BLOCK, DH), jnp.float32),
        ],
    )
    return pl.pallas_call(
        attend_kernel,
        grid_spec=grid_spec,
        out_shape=[
            jax.ShapeDtypeStruct((rows, DH), jnp.float32),
            jax.ShapeDtypeStruct((rows, 1), jnp.float32),
        ],
        compiler_params=pltpu.CompilerParams(vmem_limit_bytes=48 * 2**20),
        name="attend",
    )(first, last, queries, window, window, pos_q, start_q, pos_k)


def attend_back_kernel(
    first, last, q, k, v, grad, pos_q, start_q, lse, inner, pos_k, grad_q, grad_k, grad_v, acc
):
    at = pl.program_id(0)
    rate = LOG2E * DH ** (-0.5)

    @pl.when(at == 0)
    def _():
        grad_k[...] = jnp.zeros_like(grad_k)
        grad_v[...] = jnp.zeros_like(grad_v)

    acc[...] = jnp.zeros_like(acc)
    query, grad_out = q[...], grad[...]
    row_at, row_from, row_lse, row_inner = pos_q[0], start_q[0], lse[0], inner[0]

    def step(block, carry):
        rows = pl.ds(pl.multiple_of(block * BLOCK, BLOCK), BLOCK)
        key, value = k[rows, :], v[rows, :]
        scores = dot(key, query, 1, 1)
        key_at = pos_k[rows, :]
        seen = (key_at >= row_from) & (key_at <= row_at)
        soft = jnp.where(seen, jnp.exp2(scores * rate - row_lse), 0.0)
        grad_soft = dot(value, grad_out, 1, 1)
        grad_scores = (soft * (grad_soft - row_inner)).astype(jnp.bfloat16)
        grad_v[rows, :] += dot(soft.astype(jnp.bfloat16), grad_out, 1, 0)
        grad_k[rows, :] += dot(grad_scores, query, 1, 0)
        acc[...] += dot(grad_scores, key, 0, 0)
        return carry

    lax.fori_loop(first[at], last[at] + 1, step, 0)
    grad_q[...] = (acc[...] * DH ** (-0.5)).astype(jnp.bfloat16)


def attend_back(first, last, queries, window, grads, pos_q, start_q, lse, inner, pos_k):
    rows = queries.shape[0]
    span = window.shape[0]
    block = pl.BlockSpec((BLOCK, DH), lambda i, *_: (i, 0))
    line = pl.BlockSpec((1, 1, BLOCK), lambda i, *_: (i, 0, 0))
    grid_spec = pltpu.PrefetchScalarGridSpec(
        num_scalar_prefetch=2,
        grid=(rows // BLOCK,),
        in_specs=[
            block,
            pl.BlockSpec((span, DH), lambda i, *_: (0, 0)),
            pl.BlockSpec((span, DH), lambda i, *_: (0, 1)),
            block,
            line,
            line,
            line,
            line,
            pl.BlockSpec((span, 1), lambda i, *_: (0, 0)),
        ],
        out_specs=[
            block,
            pl.BlockSpec((span, DH), lambda i, *_: (0, 0)),
            pl.BlockSpec((span, DH), lambda i, *_: (0, 0)),
        ],
        scratch_shapes=[pltpu.VMEM((BLOCK, DH), jnp.float32)],
    )
    return pl.pallas_call(
        attend_back_kernel,
        grid_spec=grid_spec,
        out_shape=[
            jax.ShapeDtypeStruct((rows, DH), jnp.bfloat16),
            jax.ShapeDtypeStruct((span, DH), jnp.float32),
            jax.ShapeDtypeStruct((span, DH), jnp.float32),
        ],
        compiler_params=pltpu.CompilerParams(vmem_limit_bytes=48 * 2**20),
        name="attend_back",
    )(first, last, queries, window, window, grads, pos_q, start_q, lse, inner, pos_k)


def chosen(routes, options):
    return jnp.sum(
        (routes[..., None] == jnp.arange(options, dtype=jnp.int32)).astype(jnp.float32), axis=-2
    )


def shift(value, axis, by):
    count = lax.axis_size(axis)
    pairs = [(i, i + by) for i in range(count) if 0 <= i + by < count]
    return lax.ppermute(value, axis, pairs)


def body(
    tokens_in,
    out_grad,
    deal_order,
    seq_lengths,
    value_routes,
    output_routes,
    ffn_routes,
    norm1_gain,
    norm1_bias,
    norm2_gain,
    norm2_bias,
    query_weight,
    key_weight,
    value_weight,
    output_weight,
    value_router,
    output_router,
    ffn_router,
    ffn_in,
    ffn_out,
):
    groups = lax.axis_size("group")
    levels = lax.axis_size("level")
    level = lax.axis_index("level")
    head = lax.axis_index("head")
    count, width = tokens_in.shape
    piece = count // (levels * HEADS)
    wrows = query_weight.shape[0]
    experts = ffn_router.shape[1]
    local_experts = ffn_in.shape[1] // FH

    small = jnp.concatenate(
        [
            ffn_router,
            norm1_gain[:, None],
            norm1_bias[:, None],
            norm2_gain[:, None],
            norm2_bias[:, None],
        ],
        axis=1,
    )
    shared = small.shape[1]
    pad = -(shared + 2 * VEXP) % 128
    packed = jnp.concatenate(
        [
            query_weight.reshape(wrows, HEADS, DH),
            key_weight.reshape(wrows, HEADS, DH),
            value_weight.reshape(wrows, HEADS, VEXP * DH),
            output_weight.reshape(wrows, HEADS, VEXP * DH),
            value_router.reshape(wrows, HEADS, VEXP),
            output_router.reshape(wrows, HEADS, VEXP),
            jnp.broadcast_to(small[:, None, :], (wrows, HEADS, shared)),
            jnp.zeros((wrows, HEADS, pad), jnp.bfloat16),
        ],
        axis=2,
    )
    cols = packed.shape[2]
    mine = lax.all_to_all(
        packed.transpose(1, 0, 2), "head", split_axis=0, concat_axis=0, tiled=True
    ).reshape(HEADS * wrows, cols)
    full = lax.all_gather(mine, ("group", "level"), axis=0, tiled=True)
    base = 2 * DH + 2 * VEXP * DH
    w_query = full[:, :DH]
    w_key = full[:, DH : 2 * DH]
    w_value = full[:, 2 * DH : 2 * DH + VEXP * DH]
    w_output = full[:, 2 * DH + VEXP * DH : base]
    r_value = full[:, base : base + VEXP]
    r_output = full[:, base + VEXP : base + 2 * VEXP]
    at = base + 2 * VEXP
    r_ffn = full[:, at : at + experts]
    gain_one, bias_one, gain_two, bias_two = (
        full[:, at + experts + i].astype(jnp.float32) for i in range(4)
    )

    def gather_ffn(weight):
        whole = lax.all_gather(weight, "level", axis=0)
        return lax.all_gather(whole, "group", axis=1, tiled=True)

    w_in = gather_ffn(ffn_in)
    w_out = gather_ffn(ffn_out)

    own_tokens = to_workers(tokens_in)
    own_grads = to_workers(out_grad)
    own_routes = to_workers(ffn_routes)
    worker_in = level_gather(own_tokens, 1)

    shards = levels * HEADS
    orders = lax.all_gather(deal_order, ("level", "head"), axis=0, tiled=True)
    ramp = jnp.arange(count, dtype=jnp.int32)
    place = orders[:, None, :] == ramp[None, :, None]
    inverse = jnp.sum(place * ramp[None, None, :], axis=2)
    rows = HEADS * count
    spots = jnp.arange(shards, dtype=jnp.int32)[:, None] * count + inverse
    spots = jnp.swapaxes(spots.reshape(shards, levels, HEADS, piece), 1, 2).reshape(levels, rows)
    reach = -(-LMAX // rows)
    spots = jnp.concatenate([jnp.full((reach, rows), -1, jnp.int32), spots], axis=0)
    pos_all = lax.dynamic_slice_in_dim(spots, level, reach + 1, 0).reshape(-1)
    positions = pos_all[reach * rows :]
    tables = jnp.concatenate(
        [value_routes.reshape(count, -1), output_routes.reshape(count, -1)], axis=1
    )
    tables = lax.all_gather(tables, "head", axis=0)

    def routes_of(first):
        part = tables[:, :, first : first + 2 * HEADS].reshape(HEADS, count, HEADS, 2)
        return lax.dynamic_index_in_dim(part, head, 2, keepdims=False)

    masks = jnp.concatenate(
        [chosen(routes_of(0), VEXP), chosen(routes_of(2 * HEADS), VEXP)], axis=-1
    )
    here = lax.dynamic_slice_in_dim(place, level * HEADS, HEADS, 0)
    masks = jnp.einsum("ktr,kre->kte", low(here), low(masks), preferred_element_type=jnp.float32)
    masks = jnp.swapaxes(masks.reshape(HEADS, levels, HEADS, piece, 2 * VEXP), 1, 2)
    masks = masks.reshape(rows, 2 * VEXP)
    value_mask, out_mask = masks[:, :VEXP], masks[:, VEXP:]

    normed, scaled_one, inverse_one = layer_norm(worker_in.astype(jnp.float32), gain_one, bias_one)
    normed_one = low(normed)
    queries = low(matmul(normed_one, w_query))
    keys = low(matmul(normed_one, w_key))
    projected = matmul(worker_in, w_value).reshape(rows, VEXP, DH)
    value_sig = jax.nn.sigmoid(matmul(normed_one, r_value))
    value_gate = value_sig * value_mask
    values = low(jnp.sum(value_gate[..., None] * projected, axis=1))
    span = (reach + 1) * rows
    window = [jnp.concatenate([keys, values], axis=1)]
    for _ in range(reach):
        window.insert(0, shift(window[0], "level", 1))
    window = jnp.concatenate(window, axis=0)
    seq_ends = jnp.cumsum(seq_lengths[0])

    def starts_of(places):
        return jnp.max(jnp.where(seq_ends <= places[:, None], seq_ends, 0), axis=1)

    starts = starts_of(positions)
    blocks = rows // BLOCK
    base_block = (level - reach) * blocks
    first_block = starts_of(level * rows + jnp.arange(blocks, dtype=jnp.int32) * BLOCK) // BLOCK
    first_block = jnp.maximum(first_block - base_block, 0)
    last_block = reach * blocks + jnp.arange(blocks, dtype=jnp.int32)
    scale = DH ** (-0.5)
    attended, log_total = attend(
        first_block,
        last_block,
        queries,
        window,
        positions[:, None],
        starts[:, None],
        pos_all.reshape(span // BLOCK, 1, BLOCK),
    )

    out_sig = jax.nn.sigmoid(matmul(normed_one, r_output))
    out_gate = out_sig * out_mask
    mixed = low((out_gate[..., None] * attended[:, None, :]).reshape(rows, VEXP * DH))
    branch = low(level_scatter(low(transposed(mixed, w_output)), 2))
    middle = own_tokens.astype(jnp.float32) + branch.astype(jnp.float32)

    normed_mid, scaled_two, inverse_two = layer_norm(middle, gain_two, bias_two)
    normed_two = low(normed_mid)
    ffn_sig = jax.nn.sigmoid(matmul(normed_two, r_ffn))
    member = chosen(own_routes, experts)
    shares = (ffn_sig * member).reshape(count, levels, HEADS, local_experts)
    shares = jnp.swapaxes(shares, 1, 2).reshape(count, experts)
    spare = -experts % 128
    hidden = level_gather(jnp.pad(low(jnp.concatenate([middle, shares], axis=1)), ((0, 0), (0, spare))), 3)
    mine = levels * local_experts
    gates = lax.dynamic_slice_in_dim(hidden, width + head * mine, mine, 1)
    gates = jnp.repeat(gates.astype(jnp.float32), FH, axis=1).reshape(rows, levels, -1)
    hidden = hidden[:, :width]
    cotangent = level_gather(own_grads, 1)
    actives, grad_pres, gate_grads = [], [], []
    for i in range(levels):
        pre_act = matmul(hidden, w_in[i])
        sig = jax.nn.sigmoid(pre_act)
        act_pre = pre_act * sig
        actives.append(low(act_pre * gates[:, i]))
        grad_active = matmul(cotangent, w_out[i])
        gate_grads.append(
            jnp.sum((grad_active * act_pre).reshape(rows, local_experts, FH), axis=-1)
        )
        grad_pres.append(low(grad_active * gates[:, i] * silu_slope(pre_act, sig)))
    feed = sum(transposed(actives[i], w_out[i]) for i in range(levels))
    grad_rows = sum(transposed(grad_pres[i], w_in[i]) for i in range(levels))
    grad_in = jnp.stack([low(contract_rows(hidden, grad_pres[i])) for i in range(levels)])
    grad_out = jnp.stack([low(contract_rows(cotangent, actives[i])) for i in range(levels)])

    def scatter_ffn(grad):
        part = lax.psum_scatter(grad, "level", scatter_dimension=0)
        return lax.psum_scatter(part, "group", scatter_dimension=0, tiled=True).astype(jnp.float32)

    ffn_in_grad = scatter_ffn(grad_in)
    ffn_out_grad = scatter_ffn(grad_out)
    layer_out = to_home(low(middle + level_scatter(low(feed), 2)))
    gate_grads = jnp.concatenate(gate_grads, axis=1)
    wide = jnp.zeros((rows, experts + spare), jnp.float32)
    wide = lax.dynamic_update_slice_in_dim(wide, gate_grads, head * mine, 1)
    summed = level_scatter(low(jnp.concatenate([grad_rows, wide], axis=1)), 4)
    gate_grads = summed[:, width : width + experts].reshape(count, HEADS, levels, local_experts)
    gate_grads = jnp.swapaxes(gate_grads, 1, 2).reshape(count, experts)
    grad_logit = low(gate_grads * ffn_sig * (1.0 - ffn_sig) * member)
    grad_second = transposed(grad_logit, r_ffn)
    grad_r_ffn = contract_rows(normed_two, grad_logit)
    grad_gain_two = jnp.sum(grad_second * scaled_two, axis=0)
    grad_bias_two = jnp.sum(grad_second, axis=0)
    grad_middle = (
        own_grads.astype(jnp.float32)
        + summed[:, :width]
        + norm_back(grad_second, gain_two, scaled_two, inverse_two)
    )

    grad_branch = level_gather(low(grad_middle), 1)
    grad_mixed = matmul(grad_branch, w_output).reshape(rows, VEXP, DH)
    grad_w_output = contract_rows(grad_branch, mixed)
    grad_out_gate = jnp.sum(grad_mixed * attended[:, None, :], axis=-1)
    grad_attended = low(jnp.sum(grad_mixed * out_gate[..., None], axis=1))
    grad_out_logit = low(grad_out_gate * out_sig * (1.0 - out_sig) * out_mask)
    row_inner = jnp.sum(grad_attended.astype(jnp.float32) * attended, axis=-1)

    def lines(values):
        return values.reshape(blocks, 1, BLOCK)

    grad_queries, key_window, value_window = attend_back(
        first_block,
        last_block,
        queries,
        window,
        grad_attended,
        lines(positions),
        lines(starts),
        lines(log_total),
        lines(row_inner),
        pos_all[:, None],
    )
    grad_window = jnp.concatenate([key_window * scale, value_window], axis=1)
    grad_window = grad_window.reshape(reach + 1, rows, 2 * DH)
    grad_both = grad_window[0]
    for i in range(reach):
        grad_both = grad_window[i + 1] + shift(low(grad_both), "level", -1).astype(jnp.float32)
    grad_keys, grad_values = low(grad_both[:, :DH]), grad_both[:, DH:]
    grad_projected = low((value_gate[..., None] * grad_values[:, None, :]).reshape(rows, VEXP * DH))
    grad_value_gate = jnp.sum(grad_values[:, None, :] * projected, axis=-1)
    grad_value_logit = low(grad_value_gate * value_sig * (1.0 - value_sig) * value_mask)
    grad_first = (
        transposed(grad_queries, w_query)
        + transposed(grad_keys, w_key)
        + transposed(grad_value_logit, r_value)
        + transposed(grad_out_logit, r_output)
    )
    grad_inputs = norm_back(grad_first, gain_one, scaled_one, inverse_one) + transposed(
        grad_projected, w_value
    )
    input_grad = to_home(low(grad_middle + level_scatter(low(grad_inputs), 2))).astype(jnp.float32)

    grads = jnp.concatenate(
        [
            contract_rows(normed_one, grad_queries),
            contract_rows(normed_one, grad_keys),
            contract_rows(worker_in, grad_projected),
            grad_w_output,
            contract_rows(normed_one, grad_value_logit),
            contract_rows(normed_one, grad_out_logit),
            grad_r_ffn,
            jnp.sum(grad_first * scaled_one, axis=0)[:, None],
            jnp.sum(grad_first, axis=0)[:, None],
            grad_gain_two[:, None],
            grad_bias_two[:, None],
            jnp.zeros((width, pad), jnp.float32),
        ],
        axis=1,
    )
    part = low(grads).reshape(groups, width // groups, cols)
    part = lax.all_to_all(part, "group", split_axis=0, concat_axis=0)
    part = jnp.sum(part.astype(jnp.float32), axis=0)
    part = low(part).reshape(levels, HEADS * wrows, cols)
    part = lax.all_to_all(part, "level", split_axis=0, concat_axis=0)
    part = jnp.sum(part.astype(jnp.float32), axis=0)
    part = lax.all_to_all(
        part.reshape(HEADS, wrows, cols), "head", split_axis=0, concat_axis=0, tiled=True
    )

    def columns(first, size):
        return part[:, :, first : first + size].transpose(1, 0, 2).reshape(wrows, HEADS * size)

    common = jnp.sum(part[:, :, at:], axis=0)
    return (
        layer_out,
        input_grad,
        common[:, experts],
        common[:, experts + 1],
        common[:, experts + 2],
        common[:, experts + 3],
        columns(0, DH),
        columns(DH, DH),
        columns(2 * DH, VEXP * DH),
        columns(2 * DH + VEXP * DH, VEXP * DH),
        columns(base, VEXP),
        columns(base + VEXP, VEXP),
        common[:, :experts],
        ffn_in_grad,
        ffn_out_grad,
    )


def solution(mesh):
    groups, shards = mesh.devices.shape
    fine = Mesh(mesh.devices.reshape(groups, shards // HEADS, HEADS), TOK)
    two, one, three = P(TOK, None), P(TOK), P(TOK, None, None)
    ffn = P("group", ("level", "head"))
    return jax.shard_map(
        body,
        mesh=fine,
        in_specs=(two, two, two, P("group", None), three, three, two, one, one, one, one)
        + (two,) * 7
        + (ffn, ffn),
        out_specs=(two, two, one, one, one, one) + (two,) * 7 + (ffn, ffn),
        check_vma=False,
    )
```

time: 3010 us -> 1030 us (0.34)
  waiting for transfers between devices: 914 us -> 176 us
  starting transfers between devices: 470 us -> 50.4 us
  local copies, waits for them, and re-layouts: 494 us -> 96.1 us
  other arithmetic: 443 us -> 77.2 us
  Pallas kernels: 0 us -> 298 us
  blocking collectives: 241 us -> 63.8 us
  matrix products: 396 us -> 242 us
    reduce_scatter x9 -> x4, waiting for transfers between devices: 683 us -> 0.03 us  [the longest x2 0.02 us: scatter_ffn(): part = lax.psum_scatter(grad, 'level', scatter_dimension=0)]
    dot_general x54 -> x1, matrix products: 338 us -> 1.9 us  [body(): jnp.einsum('ktr,kre->kte', low(here), low(masks), preferred_element_type=...]
    gather x33 -> x0, local copies, waits for them, and re-layouts: 335 us -> none  [the longest x2 98.8 us: body(): gate_table = gate_pad[slot_table, expert_cols]]
    ppermute x32 -> x4, starting transfers between devices: 332 us -> 11.9 us  [shift(): return lax.ppermute(value, axis, pairs)]
    pallas_call x0 -> x10, Pallas kernels: none -> 298 us  [the longest x4 142 us: level_gather(): pl.pallas_call(gather_kernel, out_shape=jax.ShapeDtypeStruct((HEADS, HEAD...]
    scatter-add x16 -> x0, other arithmetic: 247 us -> none  [the longest x8 123 us: ffn_back(): grad_rows.at[group_rows]]
    all_gather x3 -> x2, blocking collectives: 156 us -> 52.9 us  [the longest x1 47.5 us: body(): orders = lax.all_gather(deal_order, ('level', 'head'), axis=0, tiled=True)]
    all_to_all x4 -> x8, starting transfers between devices: 136 us -> 37.8 us  [the longest x3 14.6 us: to_workers(): lax.all_to_all(rows.reshape(levels, count // levels, -1), 'level', split_...]
  transfers between devices with their start and end apart: 55 -> 21, of which waited for: 24 -> 7; matrix products, arithmetic and copies ran while one was open for 26% -> 32% of each run, Pallas kernels for 0% -> 29%
where the time goes in v1:
time: 1030 us; the launch traced here: 1020 us
  Pallas kernels  298 us (29%)
  matrix products  242 us (23%)
  waiting for transfers between devices  176 us (17%)
  local copies, waits for them, and re-layouts  96.1 us (9%)
  other arithmetic  77.2 us (7%)
  blocking collectives  63.8 us (6%)
  starting transfers between devices  50.4 us (5%)
  between operations  16.2 us (2%)
    pallas_call x4, Pallas kernels, level_gather(): pl.pallas_call(gather_kernel, out_shape=jax.ShapeDtypeStruct((HEADS, HEAD...  142 us
    pallas_call x4, Pallas kernels, level_scatter(): pl.pallas_call(scatter_kernel, out_shape=jax.ShapeDtypeStruct((HEADS, pie...  110 us
    dot_general x15, matrix products, transposed(): lax.dot_general(left_side, right_side, (((1,), (1,)), ((), ())), preferre...  109 us
    ppermute x4, waiting for transfers between devices, shift(): return lax.ppermute(value, axis, pairs)  95.8 us
    dot_general x15, matrix products, matmul(): return jnp.dot(left_side, right_side, preferred_element_type=jnp.float32)  85.4 us
    all_gather x1, blocking collectives, body(): orders = lax.all_gather(deal_order, ('level', 'head'), axis=0, tiled=True)  47.5 us
    dot_general x15, matrix products, contract_rows(): lax.dot_general(left_side, right_side, (((0,), (0,)), ((), ())), preferre...  46.6 us
    all_to_all x2, waiting for transfers between devices, to_home(): lax.all_to_all(out.reshape(levels, count // levels, -1), 'level', split_a...  42.4 us
  transfers between devices with their start and end apart: 21, of which 7 were waited for; matrix products, arithmetic and copies ran while one was open for 32% of the time, Pallas kernels for 29%

profile of v1, /device:TPU:8, one launch (start us, length us, event | category | flops | bytes accessed | tf_op | source)
XLA Modules:
  0.0 1020.1 jit_solution(7120823942931792933)
XLA Ops:
  17.6 10.9 %all_to_all.45 = bf16[4,32,1664]{2,1,0:T(8,128)(2,1)} all-to-all(bf16[4,32,1664]{2,1,0:T(8,128)(2,1)S(1)} %copy.322), channel_id=1, replica_groups=mesh['group'=2,'level'=4,'head'=4] {'head'}, dimensions={0} | all-to-all | bytes 851968 | tf_op jit(solution)/shard_map/all_to_all | solution.py:445
  40.3 47.5 %all-gather.3 = s32[16,1,512]{2,1,0:T(1,128)S(1)} all-gather(s32[1,1,512]{2,1,0:T(1,128)S(1)} %bitcast.443), channel_id=1, replica_groups=mesh['group'=2,'level'=4,'head'=4] {'level','head'}, dimensions={0}, use_global_device_ids=true | all-gather | bytes 34816 | tf_op jit(solution)/shard_map/all_gather | solution.py:475
  106.3 33.4 %level_gather.4 = bf16[4,4,128,1024]{3,2,1,0:T(8,128)(2,1)} custom-call(bf16[4,128,1024]{2,1,0:T(8,128)(2,1)} %bitcast.404), custom_call_target="tpu_custom_call" | custom-call | tf_op jit(solution)/shard_map/level_gather/pallas_call | solution.py:142
  183.2 24.4 %all-to-all-done.4 = bf16[4,128,1024]{2,1,0:T(8,128)(2,1)S(1)} async-done(((bf16[4,128,1024]{2,1,0:T(8,128)(2,1)}), bf16[4,128,1024]{2,1,0:T(8,128)(2,1)S(1)}, u32[]{:S(2)}, u32[]{:S(2)}) %all-to-all-start.4) | async-done | bytes 1048608 | tf_op jit(solution)/shard_map/all_to_all | solution.py:62
  213.2 34.8 %level_gather.6 = bf16[4,4,128,1024]{3,2,1,0:T(8,128)(2,1)} custom-call(bf16[4,128,1024]{2,1,0:T(8,128)(2,1)} %bitcast.402), custom_call_target="tpu_custom_call" | custom-call | tf_op jit(solution)/shard_map/level_gather/pallas_call | solution.py:142
  267.5 7.0 fusion.55
  275.9 9.9 maximum_maximum_fusion.k.v
  285.8 26.9 %attend.1 = (f32[2048,128]{1,0:T(8,128)S(1)}, f32[2048,1]{1,0:T(8,128)S(1)}) custom-call(s32[4]{0:T(128)S(1)} %get-tuple-element.180.first, s32[4]{0:T(128)S(1)} %get-tuple-element.179.last, bf16[2048,128]{1,0:T(8,128)(2,1)S(1)} %copy-done.4, bf16[6144,256]{1,0:T(8,128)(2,1)} %maximum_maximum_fusion.k.v, bf16[6144,256]{1,0:T(8,128)(2,1)} %maximum_maximum_fusion.k.v, ...), custom_call_target="tpu_custom_call" | custom-call | tf_op jit(solution)/shard_map/attend/pallas_call | solution.py:291
  321.0 26.4 %level_scatter.4 = f32[4,128,1024]{2,1,0:T(8,128)S(1)} custom-call(bf16[4,4,128,1024]{3,2,1,0:T(8,128)(2,1)S(1)} %bitcast.349), custom_call_target="tpu_custom_call" | custom-call | tf_op jit(solution)/shard_map/level_scatter/pallas_call | solution.py:206
  358.9 38.5 %level_gather.5 = bf16[4,4,128,1152]{3,2,1,0:T(8,128)(2,1)} custom-call(bf16[4,128,1152]{2,1,0:T(8,128)(2,1)} %bitcast.392), custom_call_target="tpu_custom_call" | custom-call | tf_op jit(solution)/shard_map/level_gather/pallas_call | solution.py:142
  431.9 7.9 broadcast_in_dim.44
  439.7 23.1 %multiply_convert_fusion.2 = (bf16[2048,512]{0,1:T(8,128)(2,1)}, bf16[2048,512]{0,1:T(8,128)(2,1)S(1)}, bf16[2048,512]{0,1:T(8,128)(2,1)}, bf16[2048,512]{0,1:T(...) fusion(f32[2048,512]{0,1:T(8,128)S(1)} %copy-done.33, ...), kind=kOutput, calls=%fused_computation.36 | convolution fusion | flops 2202009600 | bytes 72351744 | tf_op jit(solution)/shard_map/dot_general | solution.py:20
  493.3 12.1 %add_convert_fusion.1 = bf16[2048,1024]{1,0:T(8,128)(2,1)} fusion(f32[2048,1024]{1,0:T(8,128)} %fusion.50, f32[2048,1024]{1,0:T(8,128)S(1)} %fusion.42, f32[2048,1024]{1,0:T(8,128)} %fusion.46, bf16[2048,512]{0,1:T(8,128)(2,1)} %get-tuple-element.137, bf16[4,1024,512]{2,1,0:T(8,128)(2,1)} %all-gather.12.cloned.1.call-done), kind=kOutput, calls=%fused_computation.10 | convolution fusion | flops 2155872256 | bytes 32505856 | tf_op jit(solution)/shard_map/dot_general | solution.py:24
  514.6 30.4 %level_scatter.6 = f32[4,128,1152]{2,1,0:T(8,128)S(1)} custom-call(bf16[4,4,128,1152]{3,2,1,0:T(8,128)(2,1)S(1)} %pad_maximum_fusion.part), custom_call_target="tpu_custom_call" | custom-call | tf_op jit(solution)/shard_map/level_scatter/pallas_call | solution.py:206
  556.1 34.9 %level_gather.7 = bf16[4,4,128,1024]{3,2,1,0:T(8,128)(2,1)} custom-call(bf16[4,128,1024]{2,1,0:T(8,128)(2,1)} %bitcast.393), custom_call_target="tpu_custom_call" | custom-call | tf_op jit(solution)/shard_map/level_gather/pallas_call | solution.py:142
  591.1 7.0 multiply_reduce_fusion.5
  600.1 19.2 %attend_back.1 = (bf16[2048,128]{1,0:T(8,128)(2,1)S(1)}, f32[6144,128]{1,0:T(8,128)S(1)}, f32[6144,128]{1,0:T(8,128)}) custom-call(s32[4]{0:T(128)S(1)} %get-tuple-element.180.first, s32[4]{0:T(128)S(1)} %get-tuple-element.179.last, bf16[2048,128]{1,0:T(8,128)(2,1)S(1)} %copy-done.5, bf16[6144,256]{1,0:T(8,128)(2,1)} %maximum_maximum_fusion.k.v, ...), custom_call_target="tpu_custom_call" | custom-call | tf_op jit(solution)/shard_map/attend_back/pallas_call | solution.py:362
  641.1 7.0 fusion.45
  648.8 6.5 copy.357
  657.1 7.7 fusion.49
  664.8 7.1 fusion.53
  671.9 25.4 %collective-permute-done.2 = bf16[2048,256]{1,0:T(8,128)(2,1)} collective-permute-done((bf16[2048,256]{1,0:T(8,128)(2,1)S(1)}, bf16[2048,256]{1,0:T(8,128)(2,1)}, u32[]{:S(2)}, u32[]{:S(2)}) %collective-permute-start.2) | collective-permute-done | bytes 1048608 | tf_op jit(solution)/shard_map/ppermute | solution.py:384
  711.1 69.1 %collective-permute-done.3 = bf16[2048,256]{1,0:T(8,128)(2,1)S(1)} collective-permute-done((bf16[2048,256]{1,0:T(8,128)(2,1)S(1)}, bf16[2048,256]{1,0:T(8,128)(2,1)S(1)}, u32[]{:S(2)}, u32[]{:S(2)}) %collective-permute-start.3) | collective-permute-done | bytes 1048608 | tf_op jit(solution)/shard_map/ppermute | solution.py:384
  799.0 10.8 %multiply_reduce_fusion = (bf16[1024]{0:T(1024)(128)(2,1)S(1)}, f32[2048]{0:T(1024)S(1)}, f32[2048]{0:T(1024)S(1)}, bf16[1024]{0:T(1024)(128)(2,1)S(1)}, f32[2048,1024]{1,0:T(8,128)}) fusion(f32[2048]{0:T(1024)S(1)} %bitcast.439, f32[2048]{0:T(1024)S(1)} %bitcast.433, bf16[4,4,128,1024]{3,2,1,0:T(8,128)(2,1)S(1)} %copy-done.14, f32[1024]{0:T(1024)S(1)} %copy-done.64, ...), kind=kOutput, calls=%fused_computation.6 | convolution fusion | flops 564127744 | bytes 38576128 | tf_op jit(solution)/shard_map/dot_general | solution.py:24
  831.9 6.9 concatenate.74
  843.1 12.2 %add_convert_fusion.2 = bf16[2048,1024]{1,0:T(8,128)(2,1)S(1)} fusion(f32[2048,1024]{1,0:T(8,128)} %fusion.53, f32[2048,1024]{1,0:T(8,128)} %fusion.45, f32[2048,1024]{1,0:T(8,128)} %fusion.49, bf16[2048,512]{0,1:T(8,128)(2,1)} %copy-done.39, bf16[4,1024,512]{2,1,0:T(8,128)(2,1)} %all-gather.14.cloned.1.call-done), kind=kOutput, calls=%fused_computation.11 | convolution fusion | flops 2155872256 | bytes 32505856 | tf_op jit(solution)/shard_map/dot_general | solution.py:24
  855.3 26.8 %level_scatter.5 = f32[4,128,1024]{2,1,0:T(8,128)S(1)} custom-call(bf16[4,4,128,1024]{3,2,1,0:T(8,128)(2,1)S(1)} %bitcast.344), custom_call_target="tpu_custom_call" | custom-call | tf_op jit(solution)/shard_map/level_scatter/pallas_call | solution.py:206
  891.4 21.2 %all-to-all-done.3 = bf16[4,128,1024]{2,1,0:T(8,128)(2,1)} async-done(((bf16[4,128,1024]{2,1,0:T(8,128)(2,1)}), bf16[4,128,1024]{2,1,0:T(8,128)(2,1)}, u32[]{:S(2)}, u32[]{:S(2)}) %all-to-all-start.3) | async-done | bytes 1048608 | tf_op jit(solution)/shard_map/all_to_all | solution.py:73
  919.5 9.7 add_convert_fusion
  929.2 26.6 %level_scatter.7 = f32[4,128,1024]{2,1,0:T(8,128)S(1)} custom-call(bf16[4,4,128,1024]{3,2,1,0:T(8,128)(2,1)S(1)} %bitcast.348), custom_call_target="tpu_custom_call" | custom-call | tf_op jit(solution)/shard_map/level_scatter/pallas_call | solution.py:206
  964.3 21.2 %all-to-all-done.5 = bf16[4,128,1024]{2,1,0:T(8,128)(2,1)S(1)} async-done(((bf16[4,128,1024]{2,1,0:T(8,128)(2,1)}), bf16[4,128,1024]{2,1,0:T(8,128)(2,1)S(1)}, u32[]{:S(2)}, u32[]{:S(2)}) %all-to-all-start.5) | async-done | bytes 1048608 | tf_op jit(solution)/shard_map/all_to_all | solution.py:73
  990.7 10.7 %all-to-all-done.8 = f32[4,32,1664]{2,1,0:T(8,128)S(1)} async-done(((f32[4,32,1664]{2,1,0:T(8,128)}), f32[4,32,1664]{2,1,0:T(8,128)S(1)}, u32[]{:S(2)}, u32[]{:S(2)}) %all-to-all-start.8) | async-done | bytes 852000 | tf_op jit(solution)/shard_map/all_to_all | solution.py:664
  (433 shorter events, 341.0 us)
Async XLA Ops:
  7.2 91.8 %copy-start = (s32[512,16]{0,1:T(8,128)S(1)}, s32[512,16]{0,1:T(8,128)}, u32[]{:S(2)}) copy-start(s32[512,16]{0,1:T(8,128)} %param.26) | copy-start | bytes 98308
  7.2 33.1 %copy-start.75 = (s32[1,512]{1,0:T(1,128)S(1)}, s32[1,512]{1,0:T(1,128)}, u32[]{:S(2)}) copy-start(s32[1,512]{1,0:T(1,128)} %param.22) | copy-start | bytes 6148
  7.2 137.3 %all-gather.18.cloned.1.call-start = ((), (), s32[]{:S(2)}) async-start(), calls=%async_computation.21 | async-start | bytes 2621440 | tf_op jit(solution)/shard_map/all_gather | solution.py:463
  8.0 136.6 %all-gather.10.cloned.1.call-start = ((), (), s32[]{:S(2)}) async-start(), calls=%async_computation.13 | async-start | bytes 3833856 | tf_op jit(solution)/shard_map/all_gather | solution.py:448
  28.5 71.1 %all-to-all-start = ((bf16[4,128,1024]{2,1,0:T(8,128)(2,1)}), bf16[4,128,1024]{2,1,0:T(8,128)(2,1)}, u32[]{:S(2)}, u32[]{:S(2)}) async-start(bf16[4,128,1024]{2,1,0:T(8,128)(2,1)} %bitcast), calls=%async_computation | async-start | bytes 2097152 | tf_op jit(solution)/shard_map/all_to_all | solution.py:62
  33.8 214.2 %all-gather.16.cloned.1.call-start = ((), (), s32[]{:S(2)}) async-start(), calls=%async_computation.20 | async-start | bytes 2621440 | tf_op jit(solution)/shard_map/all_gather | solution.py:463
  96.9 62.0 %copy-start.43 = (f32[2048,10]{0,1:T(8,128)}, f32[2048,10]{0,1:T(8,128)S(1)}, u32[]{:S(2)}) copy-start(f32[2048,10]{0,1:T(8,128)S(1)} %reshape.476) | copy-start | bytes 245764
  98.1 41.5 %copy-start.8 = (s32[2048]{0:T(1024)}, s32[2048]{0:T(1024)S(1)}, u32[]{:S(2)}) copy-start(s32[2048]{0:T(1024)S(1)} %select_reduce_fusion.1) | copy-start | bytes 24580
  99.6 61.2 %all-to-all-start.2 = ((s32[4,128,16]{1,2,0:T(8,128)}), s32[4,128,16]{1,2,0:T(8,128)S(1)}, u32[]{:S(2)}, u32[]{:S(2)}) async-start(s32[4,128,16]{1,2,0:T(8,128)} %copy_bitcast_fusion.3), calls=%async_computation.2 | async-start | bytes 65536 | tf_op jit(solution)/shard_map/all_to_all | solution.py:62
  103.8 163.7 %all-gather.14.cloned.1.call-start = ((), (), s32[]{:S(2)}) async-start(), calls=%async_computation.15 | async-start | bytes 6291456 | tf_op jit(solution)/shard_map/all_gather | solution.py:464
  146.9 206.9 %copy-start.65 = (f32[1024]{0:T(1024)}, f32[1024]{0:T(1024)S(1)}, u32[]{:S(2)}) copy-start(f32[1024]{0:T(1024)S(1)} %get-tuple-element.123) | copy-start | bytes 12292
  146.9 206.9 %copy-start.71 = (f32[1024]{0:T(1024)}, f32[1024]{0:T(1024)S(1)}, u32[]{:S(2)}) copy-start(f32[1024]{0:T(1024)S(1)} %get-tuple-element.124) | copy-start | bytes 12292
  160.8 153.2 %copy-start.52 = (f32[2048,5]{0,1:T(8,128)}, f32[2048,5]{0,1:T(8,128)S(1)}, u32[]{:S(2)}) copy-start(f32[2048,5]{0,1:T(8,128)S(1)} %get-tuple-element.161) | copy-start | bytes 122884
  160.8 46.8 %all-to-all-start.4 = ((bf16[4,128,1024]{2,1,0:T(8,128)(2,1)}), bf16[4,128,1024]{2,1,0:T(8,128)(2,1)S(1)}, u32[]{:S(2)}, u32[]{:S(2)}) async-start(bf16[4,128,1024]{2,1,0:T(8,128)(2,1)} %bitcast.421), calls=%async_computation.4 | async-start | bytes 2097152 | tf_op jit(solution)/shard_map/all_to_all | solution.py:62
  165.9 233.0 %all-gather.12.cloned.1.call-start = ((), (), s32[]{:S(2)}) async-start(), calls=%async_computation.14 | async-start | bytes 6291456 | tf_op jit(solution)/shard_map/all_gather | solution.py:464
  176.7 71.4 %collective-permute-start = (bf16[2048,256]{1,0:T(8,128)(2,1)}, bf16[2048,256]{1,0:T(8,128)(2,1)}, u32[]{:S(2)}, u32[]{:S(2)}) collective-permute-start(bf16[2048,256]{1,0:T(8,128)(2,1)} %pad_maximum_fusion.4), channel_id=1, source_target_pairs={{0,4},{4,8},{8,12},{1,5},{5,9},{9,13},{2,6},{6,10},{10,14},{3,7},{... | collective-permute-start | bytes 3145736 | tf_op jit(solution)/shard_map/ppermute | solution.py:384
  183.2 170.7 %copy-start.49 = (f32[512,64]{0,1:T(8,128)}, f32[512,64]{0,1:T(8,128)S(1)}, u32[]{:S(2)}) copy-start(f32[512,64]{0,1:T(8,128)S(1)} %convert_reduce_fusion.2) | copy-start | bytes 393220
  248.1 670.7 %reduce-scatter.9.cloned.1.call-start = ((), (), s32[]{:S(2)}) async-start(), calls=%async_computation.18 | async-start | bytes 5242880 | tf_op jit(solution)/shard_map/reduce_scatter | solution.py:575
  248.1 27.8 %collective-permute-start.1 = (bf16[2048,256]{1,0:T(8,128)(2,1)}, bf16[2048,256]{1,0:T(8,128)(2,1)S(1)}, u32[]{:S(2)}, u32[]{:S(2)}) collective-permute-start(bf16[2048,256]{1,0:T(8,128)(2,1)} %collective-permute-done), channel_id=1, source_target_pairs={{0,4},{4,8},{8,12},{1,5},{5,9},{9,13},{2,6},{6,10},{10,14},{3,7},{... | collective-permute-start | bytes 3145736 | tf_op jit(solution)/shard_map/ppermute | solution.py:384
  477.0 485.5 %reduce-scatter.5.cloned.1.call-start = ((), (), s32[]{:S(2)}) async-start(), calls=%async_computation.16 | async-start | bytes 5242880 | tf_op jit(solution)/shard_map/reduce_scatter | solution.py:575
  556.1 34.9 %copy-start.53 = (f32[2048,5]{0,1:T(8,128)S(1)}, f32[2048,5]{0,1:T(8,128)}, u32[]{:S(2)}) copy-start(f32[2048,5]{0,1:T(8,128)} %copy-done.52) | copy-start | bytes 122884
  622.4 74.8 %collective-permute-start.2 = (bf16[2048,256]{1,0:T(8,128)(2,1)S(1)}, bf16[2048,256]{1,0:T(8,128)(2,1)}, u32[]{:S(2)}, u32[]{:S(2)}) collective-permute-start(bf16[2048,256]{1,0:T(8,128)(2,1)S(1)} %fusion.21), channel_id=1, source_target_pairs={{4,0},{8,4},{12,8},{5,1},{9,5},{13,9},{6,2},{10,6},{14,10},{7,3},{... | collective-permute-start | bytes 3145736 | tf_op jit(solution)/shard_map/ppermute | solution.py:384
  664.8 32.5 %copy-start.19 = (f32[6144,128]{1,0:T(8,128)S(1)}, f32[6144,128]{1,0:T(8,128)}, u32[]{:S(2)}) copy-start(f32[6144,128]{1,0:T(8,128)} %copy-done.18) | copy-start | bytes 9437188
  664.8 32.5 %copy-start.21 = (f32[6144,128]{1,0:T(8,128)S(1)}, f32[6144,128]{1,0:T(8,128)}, u32[]{:S(2)}) copy-start(f32[6144,128]{1,0:T(8,128)} %get-tuple-element.24) | copy-start | bytes 9437188
  698.7 81.5 %collective-permute-start.3 = (bf16[2048,256]{1,0:T(8,128)(2,1)S(1)}, bf16[2048,256]{1,0:T(8,128)(2,1)S(1)}, u32[]{:S(2)}, u32[]{:S(2)}) collective-permute-start(bf16[2048,256]{1,0:T(8,128)(2,1)S(1)} %fusion.18), channel_id=1, source_target_pairs={{4,0},{8,4},{12,8},{5,1},{9,5},{13,9},{6,2},{10,6},{14,10},{7,3},{... | collective-permute-start | bytes 3145736 | tf_op jit(solution)/shard_map/ppermute | solution.py:384
  838.8 46.1 %all-to-all-start.6 = ((bf16[2,512,1664]{2,1,0:T(8,128)(2,1)}), bf16[2,512,1664]{2,1,0:T(8,128)(2,1)S(1)}, u32[]{:S(2)}, u32[]{:S(2)}) async-start(bf16[2,512,1664]{2,1,0:T(8,128)(2,1)} %concatenate.74), calls=%async_computation.6 | async-start | bytes 6815744 | tf_op jit(solution)/shard_map/all_to_all | solution.py:659
  884.9 27.7 %all-to-all-start.3 = ((bf16[4,128,1024]{2,1,0:T(8,128)(2,1)}), bf16[4,128,1024]{2,1,0:T(8,128)(2,1)}, u32[]{:S(2)}, u32[]{:S(2)}) async-start(bf16[4,128,1024]{2,1,0:T(8,128)(2,1)} %bitcast.408), calls=%async_computation.3 | async-start | bytes 2097152 | tf_op jit(solution)/shard_map/all_to_all | solution.py:73
  912.7 44.7 %all-to-all-start.7 = ((bf16[4,128,1664]{2,1,0:T(8,128)(2,1)}), bf16[4,128,1664]{2,1,0:T(8,128)(2,1)S(1)}, u32[]{:S(2)}, u32[]{:S(2)}) async-start(bf16[4,128,1664]{2,1,0:T(8,128)(2,1)} %bitcast.377), calls=%async_computation.7 | async-start | bytes 3407872 | tf_op jit(solution)/shard_map/all_to_all | solution.py:662
  918.8 87.8 %reduce-scatter.11.cloned.1.call-start = ((), (), s32[]{:S(2)}) async-start(), calls=%async_computation.19 | async-start | bytes 1572864 | tf_op jit(solution)/shard_map/reduce_scatter | solution.py:576
  957.4 28.1 %all-to-all-start.5 = ((bf16[4,128,1024]{2,1,0:T(8,128)(2,1)}), bf16[4,128,1024]{2,1,0:T(8,128)(2,1)S(1)}, u32[]{:S(2)}, u32[]{:S(2)}) async-start(bf16[4,128,1024]{2,1,0:T(8,128)(2,1)} %bitcast.407), calls=%async_computation.5 | async-start | bytes 2097152 | tf_op jit(solution)/shard_map/all_to_all | solution.py:73
  962.5 46.3 %reduce-scatter.7.cloned.1.call-start = ((), (), s32[]{:S(2)}) async-start(), calls=%async_computation.17 | async-start | bytes 1572864 | tf_op jit(solution)/shard_map/reduce_scatter | solution.py:576
  985.5 15.8 %all-to-all-start.8 = ((f32[4,32,1664]{2,1,0:T(8,128)}), f32[4,32,1664]{2,1,0:T(8,128)S(1)}, u32[]{:S(2)}, u32[]{:S(2)}) async-start(f32[4,32,1664]{2,1,0:T(8,128)} %bitcast.409), calls=%async_computation.8 | async-start | bytes 1703936 | tf_op jit(solution)/shard_map/all_to_all | solution.py:664
  (84 other events, 719.5 us)
Sparse Core Ops, SparseCore 0:
  9.6 64.2 all-gather.17
  76.0 66.3 all-gather.9
  144.0 61.8 all-gather.15
  207.2 59.0 all-gather.13
  267.7 56.7 all-gather.11
  477.1 101.2 reduce-scatter.8
  637.4 137.6 reduce-scatter.4
  921.8 20.9 reduce-scatter.10
  965.6 20.6 reduce-scatter.6

commit v2 on v1

v2 whole, which is shorter than its diff:
```python
import functools

import jax
import jax.numpy as jnp
from jax import lax
from jax.experimental import pallas as pl
from jax.experimental.pallas import tpu as pltpu
from jax.sharding import Mesh, PartitionSpec as P

HEADS = 4
DH = 128
VEXP = 5
FH = 128
LMAX = 4096

TOK = ("group", "level", "head")


def matmul(left_side, right_side):
    return jnp.dot(left_side, right_side, preferred_element_type=jnp.float32)


def transposed(left_side, right_side):
    return lax.dot_general(
        left_side, right_side, (((1,), (1,)), ((), ())), preferred_element_type=jnp.float32
    )


def contract_rows(left_side, right_side):
    return lax.dot_general(
        left_side, right_side, (((0,), (0,)), ((), ())), preferred_element_type=jnp.float32
    )


def low(value):
    return value.astype(jnp.bfloat16)


def layer_norm(inputs, gain_vec, bias_vec):
    centred = inputs - jnp.mean(inputs, axis=-1, keepdims=True)
    inverse = lax.rsqrt(jnp.mean(centred * centred, axis=-1, keepdims=True) + 1e-05)
    scaled = centred * inverse
    return (scaled * gain_vec + bias_vec, scaled, inverse)


def norm_back(grad_normed, gain_vec, scaled, inverse):
    inner_grad = grad_normed * gain_vec
    return inverse * (
        inner_grad
        - jnp.mean(inner_grad, axis=-1, keepdims=True)
        - scaled * jnp.mean(inner_grad * scaled, axis=-1, keepdims=True)
    )


def to_workers(rows):
    levels = lax.axis_size("level")
    count = rows.shape[0]
    came = lax.all_to_all(
        rows.reshape(levels, count // levels, -1), "level", split_axis=0, concat_axis=0, tiled=True
    )
    came = came.reshape(levels, HEADS, count // levels // HEADS, -1)
    return came.transpose(1, 0, 2, 3).reshape(count, -1)


MESH = pl.DeviceIdType.MESH


def partners(head):
    near = head + 1 - 2 * lax.rem(head, 2)
    far = lax.rem(head + 2, HEADS)
    return near, far


def greet(near, far):
    barrier = pltpu.get_barrier_semaphore()
    for peer in (near, far):
        pl.semaphore_signal(barrier, inc=1, device_id={"head": peer}, device_id_type=MESH)
    pl.semaphore_wait(barrier, 2)


def remote(src, dst, send, recv, peer):
    return pltpu.make_async_remote_copy(
        src_ref=src,
        dst_ref=dst,
        send_sem=send,
        recv_sem=recv,
        device_id={"head": peer},
        device_id_type=MESH,
    )


def cost(flops, moved):
    return pl.CostEstimate(flops=int(flops), bytes_accessed=int(moved), transcendentals=0)


def gather_kernel(
    by_source, own, out, local_sem, near_send, near_recv, far_send, far_recv, pass_send, pass_recv
):
    head = lax.axis_index("head")
    near, far = partners(head)
    greet(near, far)

    def spot(i, source):
        return out.at[source, i] if by_source else out.at[i, source]

    pieces = range(HEADS)
    to_far = [remote(own.at[i], spot(i, head), far_send.at[i], far_recv.at[i], far) for i in pieces]
    to_near = [
        remote(own.at[i], spot(i, head), near_send.at[i], near_recv.at[i], near) for i in pieces
    ]
    passed = [
        remote(spot(i, far), spot(i, far), pass_send.at[i], pass_recv.at[i], near) for i in pieces
    ]
    kept = [pltpu.make_async_copy(own.at[i], spot(i, head), local_sem.at[i]) for i in pieces]
    for copy in to_far + to_near + kept:
        copy.start()
    for i in pieces:
        to_far[i].wait_recv()
        passed[i].start()
    for i in pieces:
        to_near[i].wait_recv()
        passed[i].wait_recv()
        kept[i].wait()
        to_far[i].wait_send()
        to_near[i].wait_send()
        passed[i].wait_send()


def level_gather(rows, collective_id, by_source=False):
    count, width = rows.shape
    whole = pl.pallas_call(
        functools.partial(gather_kernel, by_source),
        out_shape=jax.ShapeDtypeStruct((HEADS, HEADS, count // HEADS, width), rows.dtype),
        in_specs=[pl.BlockSpec(memory_space=pltpu.VMEM)],
        out_specs=pl.BlockSpec(memory_space=pl.ANY),
        scratch_shapes=[pltpu.SemaphoreType.DMA((HEADS,))] * 7,
        compiler_params=pltpu.CompilerParams(collective_id=collective_id, has_side_effects=True),
        cost_estimate=cost(0, 90e6),
        name="level_gather",
    )(rows.reshape(HEADS, count // HEADS, width))
    return whole.reshape(HEADS * count, width)


def scatter_kernel(
    by_source, part, out, near_buf, send_buf, far_buf, near_send, near_recv, far_send, far_recv
):
    head = lax.axis_index("head")
    near, far = partners(head)
    greet(near, far)
    across = HEADS - 1 - head
    pieces = range(HEADS)

    def spot(i, dest):
        return (dest, i) if by_source else (i, dest)

    def to_near(slot, i, dest):
        return remote(
            part.at[spot(i, dest)],
            near_buf.at[slot, i],
            near_send.at[slot, i],
            near_recv.at[slot, i],
            near,
        )

    first = [to_near(0, i, across) for i in pieces]
    second = [to_near(1, i, near) for i in pieces]
    onward = [
        remote(send_buf.at[i], far_buf.at[i], far_send.at[i], far_recv.at[i], far) for i in pieces
    ]
    for copy in first + second:
        copy.start()
    for i in pieces:
        first[i].wait_recv()
        both = part[spot(i, far)].astype(jnp.float32) + near_buf[0, i].astype(jnp.float32)
        send_buf[i] = both.astype(jnp.bfloat16)
        onward[i].start()
    for i in pieces:
        second[i].wait_recv()
        out[i] = part[spot(i, head)].astype(jnp.float32) + near_buf[1, i].astype(jnp.float32)
    for i in pieces:
        onward[i].wait_recv()
        out[i] = out[i] + far_buf[i].astype(jnp.float32)
    for i in pieces:
        first[i].wait_send()
        second[i].wait_send()
        onward[i].wait_send()


def level_scatter(rows, collective_id, by_source=False):
    total, width = rows.shape
    piece = total // (HEADS * HEADS)
    low_type = jnp.bfloat16
    mine = pl.pallas_call(
        functools.partial(scatter_kernel, by_source),
        out_shape=jax.ShapeDtypeStruct((HEADS, piece, width), jnp.float32),
        in_specs=[pl.BlockSpec(memory_space=pltpu.VMEM)],
        out_specs=pl.BlockSpec(memory_space=pltpu.VMEM),
        scratch_shapes=[
            pltpu.VMEM((2, HEADS, piece, width), low_type),
            pltpu.VMEM((HEADS, piece, width), low_type),
            pltpu.VMEM((HEADS, piece, width), low_type),
            pltpu.SemaphoreType.DMA((2, HEADS)),
            pltpu.SemaphoreType.DMA((2, HEADS)),
            pltpu.SemaphoreType.DMA((HEADS,)),
            pltpu.SemaphoreType.DMA((HEADS,)),
        ],
        compiler_params=pltpu.CompilerParams(
            collective_id=collective_id, has_side_effects=True, vmem_limit_bytes=32 * 2**20
        ),
        cost_estimate=cost(0, 80e6),
        name="level_scatter",
    )(rows.reshape(HEADS, HEADS, piece, width))
    return mine.reshape(HEADS * piece, width)


def meet(near):
    barrier = pltpu.get_barrier_semaphore()
    pl.semaphore_signal(barrier, inc=1, device_id={"head": near}, device_id_type=MESH)
    pl.semaphore_wait(barrier, 1)


def pair_scatter_kernel(by_source, part, out, out_far, near_buf, send, recv):
    head = lax.axis_index("head")
    near, far = partners(head)
    meet(near)
    across = HEADS - 1 - head
    pieces = range(HEADS)

    def spot(i, dest):
        return (dest, i) if by_source else (i, dest)

    def to_near(slot, i, dest):
        return remote(
            part.at[spot(i, dest)], near_buf.at[slot, i], send.at[slot, i], recv.at[slot, i], near
        )

    first = [to_near(0, i, across) for i in pieces]
    second = [to_near(1, i, near) for i in pieces]
    for copy in first + second:
        copy.start()
    for i in pieces:
        first[i].wait_recv()
        both = part[spot(i, far)].astype(jnp.float32) + near_buf[0, i].astype(jnp.float32)
        out_far[i] = both.astype(jnp.bfloat16)
    for i in pieces:
        second[i].wait_recv()
        out[i] = part[spot(i, head)].astype(jnp.float32) + near_buf[1, i].astype(jnp.float32)
    for i in pieces:
        first[i].wait_send()
        second[i].wait_send()


def pair_scatter(rows, collective_id, by_source=False):
    total, width = rows.shape
    piece = total // (HEADS * HEADS)
    mine, other = pl.pallas_call(
        functools.partial(pair_scatter_kernel, by_source),
        out_shape=[
            jax.ShapeDtypeStruct((HEADS, piece, width), jnp.float32),
            jax.ShapeDtypeStruct((HEADS, piece, width), jnp.bfloat16),
        ],
        in_specs=[pl.BlockSpec(memory_space=pltpu.VMEM)],
        out_specs=[pl.BlockSpec(memory_space=pltpu.VMEM)] * 2,
        scratch_shapes=[
            pltpu.VMEM((2, HEADS, piece, width), jnp.bfloat16),
            pltpu.SemaphoreType.DMA((2, HEADS)),
            pltpu.SemaphoreType.DMA((2, HEADS)),
        ],
        compiler_params=pltpu.CompilerParams(
            collective_id=collective_id, has_side_effects=True, vmem_limit_bytes=32 * 2**20
        ),
        cost_estimate=cost(0, 25e6),
        name="pair_scatter",
    )(rows.reshape(HEADS, HEADS, piece, width))
    return mine.reshape(HEADS * piece, width), other.reshape(HEADS * piece, width)


def pair_gather_kernel(by_source, own, other, out, local_sem, send, recv):
    head = lax.axis_index("head")
    near, far = partners(head)
    meet(near)
    copies, kept = [], []
    for i in range(HEADS):
        for slot, (block, source) in enumerate(((own, head), (other, far))):
            place = out.at[source, i] if by_source else out.at[i, source]
            copies.append(
                remote(block.at[i], place, send.at[slot, i], recv.at[slot, i], near)
            )
            kept.append(pltpu.make_async_copy(block.at[i], place, local_sem.at[slot, i]))
    for copy in copies + kept:
        copy.start()
    for copy in copies + kept:
        copy.wait()


def pair_gather(own, other, collective_id, by_source=False):
    count, width = own.shape
    split = (HEADS, count // HEADS, width)
    whole = pl.pallas_call(
        functools.partial(pair_gather_kernel, by_source),
        out_shape=jax.ShapeDtypeStruct((HEADS,) + split, own.dtype),
        in_specs=[pl.BlockSpec(memory_space=pltpu.VMEM)] * 2,
        out_specs=pl.BlockSpec(memory_space=pl.ANY),
        scratch_shapes=[pltpu.SemaphoreType.DMA((2, HEADS))] * 3,
        compiler_params=pltpu.CompilerParams(collective_id=collective_id, has_side_effects=True),
        cost_estimate=cost(0, 25e6),
        name="pair_gather",
    )(own.reshape(split), other.reshape(split))
    return whole.reshape(HEADS * count, width)


def to_far(rows):
    return lax.ppermute(rows, "head", [(i, (i + 2) % HEADS) for i in range(HEADS)])


def after(value, *others):
    return lax.optimization_barrier((value,) + others)[0]


def ring(axis):
    me, size = lax.axis_index(axis), lax.axis_size(axis)
    ahead = [lax.rem(me + k, size) for k in range(1, size)]
    behind = [lax.rem(me + size - k, size) for k in range(1, size)]
    return me, ahead, behind


def reach_out(src, dst, send, recv, peer):
    return pltpu.make_async_remote_copy(
        src_ref=src, dst_ref=dst, send_sem=send, recv_sem=recv, device_id=peer, device_id_type=MESH
    )


def greet_all(peers):
    barrier = pltpu.get_barrier_semaphore()
    for peer in peers:
        pl.semaphore_signal(barrier, inc=1, device_id=peer, device_id_type=MESH)
    pl.semaphore_wait(barrier, len(peers))


def start_kernel(
    tokens, weights, tables, picks, order, rows, full, routes, chosen_rows, orders, own_sem, *sems
):
    sems = iter(sems)

    def pair():
        return next(sems), next(sems)

    group, groups_ahead, _ = ring("group")
    level, levels_ahead, levels_behind = ring("level")
    head = lax.axis_index("head")
    near, far = partners(head)
    mates = [near, far, HEADS - 1 - head]
    greet_all(
        [{"head": m} for m in mates]
        + [{"level": n} for n in levels_ahead]
        + [{"group": n} for n in groups_ahead]
    )
    started = []

    def send(src, dst, send_sem, recv_sem, peer):
        copy = reach_out(src, dst, send_sem, recv_sem, peer)
        copy.start()
        started.append(copy)
        return copy

    out_s, out_r = pair()
    pick_s, pick_r = pair()
    crossing, picking = [], []
    for k, to in enumerate(levels_ahead):
        peer = {"level": to}
        crossing.append(send(tokens.at[to], rows.at[:, head, level], out_s.at[k], out_r.at[k], peer))
    mate_s, mate_r = pair()
    table_s, table_r = pair()
    order_s, order_r = pair()
    to_mates, order_mates, table_mates = [], [], []
    for k, to in enumerate(mates):
        peer = {"head": to}
        to_mates.append(
            send(weights.at[to], full.at[group, level, head], mate_s.at[k], mate_r.at[k], peer)
        )
        order_mates.append(
            send(order, orders.at[level, head], order_s.at[k], order_r.at[k], peer)
        )
    own = [
        (tokens.at[level], rows.at[:, head, level]),
        (weights.at[head], full.at[group, level, head]),
        (tables.at[head], routes.at[head]),
        (picks.at[level], chosen_rows.at[level]),
        (order, orders.at[level, head]),
    ]
    own = [pltpu.make_async_copy(src, dst, own_sem.at[i]) for i, (src, dst) in enumerate(own)]
    for copy in own:
        copy.start()
    far_s, far_r = pair()
    near_s, near_r = pair()
    pass_s, pass_r = pair()
    to_far, to_near = [], []

    def share(k, src, source):
        place = rows.at[:, head, source]
        to_far.append(send(src, place, far_s.at[k], far_r.at[k], {"head": far}))
        to_near.append(send(src, place, near_s.at[k], near_r.at[k], {"head": near}))

    share(0, tokens.at[level], level)
    block_s, block_r = pair()
    group_s, group_r = pair()
    orders_s, orders_r = pair()
    for copy in to_mates:
        copy.wait_recv()
    own[1].wait()
    blocks, grouped, ordered = [], [], []

    def to_groups(j, source):
        for k, to in enumerate(groups_ahead):
            block = full.at[group, source]
            grouped.append(
                send(block, block, group_s.at[k, j], group_r.at[k, j], {"group": to})
            )

    for k, to in enumerate(levels_ahead):
        block = full.at[group, level]
        blocks.append(send(block, block, block_s.at[k], block_r.at[k], {"level": to}))
    to_groups(0, level)
    for k, to in enumerate(mates):
        table_mates.append(
            send(tables.at[to], routes.at[head], table_s.at[k], table_r.at[k], {"head": to})
        )
    for k, to in enumerate(levels_ahead):
        picking.append(
            send(picks.at[to], chosen_rows.at[level], pick_s.at[k], pick_r.at[k], {"level": to})
        )
    for copy in order_mates:
        copy.wait_recv()
    own[4].wait()
    for k, to in enumerate(levels_ahead):
        block = orders.at[level]
        ordered.append(send(block, block, orders_s.at[k], orders_r.at[k], {"level": to}))
    for k, source in enumerate(levels_behind):
        crossing[k].wait_recv()
        share(k + 1, rows.at[:, head, source], source)
    for k, source in enumerate(levels_behind):
        blocks[k].wait_recv()
        to_groups(k + 1, source)
    passed = []
    for k, source in enumerate([level] + levels_behind):
        to_far[k].wait_recv()
        place = rows.at[:, far, source]
        passed.append(send(place, place, pass_s.at[k], pass_r.at[k], {"head": near}))
    for copy in to_near + passed + grouped + table_mates + picking + ordered:
        copy.wait_recv()
    for copy in started:
        copy.wait_send()
    for i in (0, 2, 3):
        own[i].wait()


def start(tokens, weights, tables, picks, order):
    groups, levels = lax.axis_size("group"), lax.axis_size("level")
    _, _, piece, width = tokens.shape
    shapes = [
        jax.ShapeDtypeStruct((HEADS, HEADS, levels, piece, width), tokens.dtype),
        jax.ShapeDtypeStruct((groups, levels) + weights.shape, weights.dtype),
        jax.ShapeDtypeStruct(tables.shape, tables.dtype),
        jax.ShapeDtypeStruct(picks.shape, picks.dtype),
        jax.ShapeDtypeStruct((levels, HEADS) + order.shape, order.dtype),
    ]
    dma = pltpu.SemaphoreType.DMA
    others, mates = (levels - 1,), (HEADS - 1,)
    counts = [others] * 2 + [mates] * 3 + [(levels,)] * 3 + [others, (groups - 1, levels), others]
    return pl.pallas_call(
        start_kernel,
        out_shape=shapes,
        in_specs=[pl.BlockSpec(memory_space=pltpu.VMEM)] * 5,
        out_specs=[pl.BlockSpec(memory_space=pl.ANY)] * 5,
        scratch_shapes=[dma((5,))] + [dma(c) for c in counts for _ in range(2)],
        compiler_params=pltpu.CompilerParams(collective_id=9, has_side_effects=True),
        cost_estimate=cost(0, 200e6),
        name="start",
    )(tokens, weights, tables, picks, order)


def finish_kernel(
    part,
    middle,
    done,
    grads,
    home_grad,
    home_out,
    owned,
    near_buf,
    send_buf,
    far_buf,
    total,
    back_buf,
    came_buf,
    group_buf,
    level_send,
    level_buf,
    head_send,
    own_sem,
    *sems,
):
    sems = iter(sems)

    def pair():
        return next(sems), next(sems)

    group, groups_ahead, _ = ring("group")
    level, levels_ahead, levels_behind = ring("level")
    head = lax.axis_index("head")
    near, far = partners(head)
    across = HEADS - 1 - head
    mates = [near, far, across]
    greet_all(
        [{"head": m} for m in mates]
        + [{"level": n} for n in levels_ahead]
        + [{"group": n} for n in groups_ahead]
    )
    started = []

    def send(src, dst, send_sem, recv_sem, peer):
        copy = reach_out(src, dst, send_sem, recv_sem, peer)
        copy.start()
        started.append(copy)
        return copy

    pieces = range(HEADS)
    near_s, near_r = pair()
    far_s, far_r = pair()
    group_s, group_r = pair()
    done_s, done_r = pair()
    back_s, back_r = pair()
    level_s, level_r = pair()
    mate_s, mate_r = pair()
    first, second, onward = [], [], []
    for slot, (dest, copies) in enumerate(((across, first), (near, second))):
        for i in pieces:
            copies.append(
                send(
                    part.at[i, dest],
                    near_buf.at[slot, i],
                    near_s.at[slot, i],
                    near_r.at[slot, i],
                    {"head": near},
                )
            )
    order = levels_ahead + [level]
    grouped = []
    for j, dest in enumerate(order):
        grouped.append(
            [
                send(
                    grads.at[to, dest],
                    group_buf.at[k, j],
                    group_s.at[k, j],
                    group_r.at[k, j],
                    {"group": to},
                )
                for k, to in enumerate(groups_ahead)
            ]
        )
    out_own = pltpu.make_async_copy(done.at[:, level], home_out.at[level], own_sem)
    out_own.start()
    homing = [
        send(done.at[:, to], home_out.at[level], done_s.at[k], done_r.at[k], {"level": to})
        for k, to in enumerate(levels_ahead)
    ]
    for i in pieces:
        first[i].wait_recv()
        both = part[i, far].astype(jnp.float32) + near_buf[0, i].astype(jnp.float32)
        send_buf[i] = both.astype(jnp.bfloat16)
        onward.append(send(send_buf.at[i], far_buf.at[i], far_s.at[i], far_r.at[i], {"head": far}))
    for i in pieces:
        second[i].wait_recv()
        both = part[i, head].astype(jnp.float32) + near_buf[1, i].astype(jnp.float32)
        total[i] = both + middle[i]
    leveled = []
    for j, dest in enumerate(order):
        amount = grads[group, dest].astype(jnp.float32)
        for k, copy in enumerate(grouped[j]):
            copy.wait_recv()
            amount = amount + group_buf[k, j].astype(jnp.float32)
        level_send[j] = amount.astype(jnp.bfloat16)
        if j < len(levels_ahead):
            leveled.append(
                send(level_send.at[j], level_buf.at[j], level_s.at[j], level_r.at[j], {"level": dest})
            )
    for i in pieces:
        onward[i].wait_recv()
        both = total[i] + far_buf[i].astype(jnp.float32)
        back_buf[i] = both.astype(jnp.bfloat16).reshape(back_buf.shape[1:])
    backs = [
        send(back_buf.at[:, to], came_buf.at[level], back_s.at[k], back_r.at[k], {"level": to})
        for k, to in enumerate(levels_ahead)
    ]
    amount = level_send[len(levels_ahead)].astype(jnp.float32)
    for j, copy in enumerate(leveled):
        copy.wait_recv()
        amount = amount + level_buf[j].astype(jnp.float32)
    head_send[...] = amount.astype(jnp.bfloat16)
    sharing = [
        send(head_send.at[to], owned.at[head], mate_s.at[k], mate_r.at[k], {"head": to})
        for k, to in enumerate(mates)
    ]
    owned[head] = head_send[head]
    home_grad[level] = back_buf[:, level].astype(jnp.float32)
    for k, source in enumerate(levels_behind):
        backs[k].wait_recv()
        home_grad[source] = came_buf[source].astype(jnp.float32)
    for copy in homing + sharing:
        copy.wait_recv()
    for copy in started:
        copy.wait_send()
    out_own.wait()


def finish(part, middle, done, grads):
    groups, levels = lax.axis_size("group"), lax.axis_size("level")
    _, _, piece, width = done.shape
    low_type = jnp.bfloat16
    count = levels * piece
    block = grads.shape[2:]
    dma = pltpu.SemaphoreType.DMA
    others = (levels - 1,)
    counts = [(2, HEADS), (HEADS,), (groups - 1, levels), others, others, others, (HEADS - 1,)]
    vmem = pl.BlockSpec(memory_space=pltpu.VMEM)
    return pl.pallas_call(
        finish_kernel,
        out_shape=[
            jax.ShapeDtypeStruct((levels, HEADS, piece, width), jnp.float32),
            jax.ShapeDtypeStruct((levels, HEADS, piece, width), low_type),
            jax.ShapeDtypeStruct(block, low_type),
        ],
        in_specs=[vmem] * 4,
        out_specs=[vmem] * 3,
        scratch_shapes=[
            pltpu.VMEM((2, HEADS, count, width), low_type),
            pltpu.VMEM((HEADS, count, width), low_type),
            pltpu.VMEM((HEADS, count, width), low_type),
            pltpu.VMEM((HEADS, count, width), jnp.float32),
            pltpu.VMEM((HEADS, levels, piece, width), low_type),
            pltpu.VMEM((levels, HEADS, piece, width), low_type),
            pltpu.VMEM((groups - 1, levels) + block, low_type),
            pltpu.VMEM((levels,) + block, low_type),
            pltpu.VMEM((levels - 1,) + block, low_type),
            pltpu.VMEM(block, low_type),
            dma,
        ]
        + [dma(c) for c in counts for _ in range(2)],
        compiler_params=pltpu.CompilerParams(
            collective_id=10, has_side_effects=True, vmem_limit_bytes=56 * 2**20
        ),
        cost_estimate=cost(0, 200e6),
        name="finish",
    )(part, middle, done, grads)


BLOCK = 512
LOG2E = 1.4426950408889634


def dot(left_side, right_side, left_dim, right_dim):
    return lax.dot_general(
        left_side,
        right_side,
        (((left_dim,), (right_dim,)), ((), ())),
        preferred_element_type=jnp.float32,
    )


def attend_kernel(parts, first, q, *refs):
    keys, values = refs[:parts], refs[parts : 2 * parts]
    pos_q, start_q, pos_k, out, lse, top, total, acc = refs[2 * parts :]
    at = pl.program_id(0)
    blocks = pl.num_programs(0)
    rate = LOG2E * DH ** (-0.5)
    top[...] = jnp.full_like(top, -1e30)
    total[...] = jnp.zeros_like(total)
    acc[...] = jnp.zeros_like(acc)
    query = q[...]
    row_at, row_from = pos_q[0], start_q[0]

    for part in range(parts):

        def step(block, carry, k=keys[part], v=values[part], part=part):
            rows = pl.ds(pl.multiple_of(block * BLOCK, BLOCK), BLOCK)
            spot = pl.ds(pl.multiple_of((part * blocks + block) * BLOCK, BLOCK), BLOCK)
            scores = dot(k[rows, :], query, 1, 1)
            key_at = pos_k[spot, :]
            scores = jnp.where((key_at >= row_from) & (key_at <= row_at), scores, -1e30)
            old = top[...]
            new = jnp.maximum(old, jnp.max(scores, axis=0, keepdims=True))
            shrink = jnp.exp2((old - new) * rate)
            weight = jnp.exp2((scores - new) * rate)
            total[...] = total[...] * shrink + jnp.sum(weight, axis=0, keepdims=True)
            acc[...] = acc[...] * shrink + dot(v[rows, :], weight.astype(jnp.bfloat16), 0, 0)
            top[...] = new
            return carry

        begin = jnp.maximum(first[at] - part * blocks, 0)
        end = at + 1 if part == parts - 1 else blocks
        lax.fori_loop(begin, end, step, 0)
    out[...] = (acc[...] / total[...]).T
    lse[0] = top[...] * rate + jnp.log2(total[...])


def attend(first, queries, window, pos_q, start_q, pos_k):
    rows = queries.shape[0]
    parts = len(window)
    line = pl.BlockSpec((1, 1, BLOCK), lambda i, *_: (i, 0, 0))
    grid_spec = pltpu.PrefetchScalarGridSpec(
        num_scalar_prefetch=1,
        grid=(rows // BLOCK,),
        in_specs=[pl.BlockSpec((BLOCK, DH), lambda i, *_: (i, 0))]
        + [pl.BlockSpec((rows, DH), lambda i, *_: (0, 0))] * parts
        + [pl.BlockSpec((rows, DH), lambda i, *_: (0, 1))] * parts
        + [line, line, pl.BlockSpec((parts * rows, 1), lambda i, *_: (0, 0))],
        out_specs=[pl.BlockSpec((BLOCK, DH), lambda i, *_: (i, 0)), line],
        scratch_shapes=[
            pltpu.VMEM((1, BLOCK), jnp.float32),
            pltpu.VMEM((1, BLOCK), jnp.float32),
            pltpu.VMEM((DH, BLOCK), jnp.float32),
        ],
    )
    return pl.pallas_call(
        functools.partial(attend_kernel, parts),
        grid_spec=grid_spec,
        out_shape=[
            jax.ShapeDtypeStruct((rows, DH), jnp.float32),
            jax.ShapeDtypeStruct((rows // BLOCK, 1, BLOCK), jnp.float32),
        ],
        compiler_params=pltpu.CompilerParams(vmem_limit_bytes=48 * 2**20),
        cost_estimate=cost(2e10, 1e7),
        name="attend",
    )(first, queries, *window, *window, pos_q, start_q, pos_k)


def attend_back_kernel(parts, first, q, *refs):
    keys, values = refs[:parts], refs[parts : 2 * parts]
    grad, pos_q, start_q, lse, inner, pos_k, grad_q = refs[2 * parts : 2 * parts + 7]
    grads = refs[2 * parts + 7 : 3 * parts + 7]
    sum_k, sum_v, acc = refs[3 * parts + 7 :]
    at = pl.program_id(0)
    blocks = pl.num_programs(0)
    rate = LOG2E * DH ** (-0.5)
    scale = DH ** (-0.5)

    @pl.when(at == 0)
    def _():
        sum_k[...] = jnp.zeros_like(sum_k)
        sum_v[...] = jnp.zeros_like(sum_v)

    acc[...] = jnp.zeros_like(acc)
    query, grad_out = q[...], grad[...]
    row_at, row_from, row_lse, row_inner = pos_q[0], start_q[0], lse[0], inner[0]

    for part in range(parts):

        def step(block, carry, k=keys[part], v=values[part], part=part):
            rows = pl.ds(pl.multiple_of(block * BLOCK, BLOCK), BLOCK)
            spot = pl.ds(pl.multiple_of((part * blocks + block) * BLOCK, BLOCK), BLOCK)
            key, value = k[rows, :], v[rows, :]
            scores = dot(key, query, 1, 1)
            key_at = pos_k[spot, :]
            seen = (key_at >= row_from) & (key_at <= row_at)
            soft = jnp.where(seen, jnp.exp2(scores * rate - row_lse), 0.0)
            grad_soft = dot(value, grad_out, 1, 1)
            grad_scores = (soft * (grad_soft - row_inner)).astype(jnp.bfloat16)
            sum_v[spot, :] += dot(soft.astype(jnp.bfloat16), grad_out, 1, 0)
            sum_k[spot, :] += dot(grad_scores, query, 1, 0)
            acc[...] += dot(grad_scores, key, 0, 0)
            return carry

        begin = jnp.maximum(first[at] - part * blocks, 0)
        end = at + 1 if part == parts - 1 else blocks
        lax.fori_loop(begin, end, step, 0)
    grad_q[...] = (acc[...] * scale).astype(jnp.bfloat16)

    @pl.when(at == blocks - 1)
    def _():
        size = grads[0].shape[0]
        for part in range(parts):
            spot = slice(part * size, (part + 1) * size)
            grads[part][:, :DH] = (sum_k[spot, :] * scale).astype(grads[part].dtype)
            grads[part][:, DH:] = sum_v[spot, :].astype(grads[part].dtype)


def attend_back(first, queries, window, grads, pos_q, start_q, lse, inner, pos_k):
    rows = queries.shape[0]
    parts = len(window)
    block = pl.BlockSpec((BLOCK, DH), lambda i, *_: (i, 0))
    line = pl.BlockSpec((1, 1, BLOCK), lambda i, *_: (i, 0, 0))
    grid_spec = pltpu.PrefetchScalarGridSpec(
        num_scalar_prefetch=1,
        grid=(rows // BLOCK,),
        in_specs=[block]
        + [pl.BlockSpec((rows, DH), lambda i, *_: (0, 0))] * parts
        + [pl.BlockSpec((rows, DH), lambda i, *_: (0, 1))] * parts
        + [block, line, line, line, line]
        + [pl.BlockSpec((parts * rows, 1), lambda i, *_: (0, 0))],
        out_specs=[block] + [pl.BlockSpec((rows, 2 * DH), lambda i, *_: (0, 0))] * parts,
        scratch_shapes=[
            pltpu.VMEM((parts * rows, DH), jnp.float32),
            pltpu.VMEM((parts * rows, DH), jnp.float32),
            pltpu.VMEM((BLOCK, DH), jnp.float32),
        ],
    )
    kinds = [jnp.bfloat16] * (parts - 1) + [jnp.float32]
    return pl.pallas_call(
        functools.partial(attend_back_kernel, parts),
        grid_spec=grid_spec,
        out_shape=[jax.ShapeDtypeStruct((rows, DH), jnp.bfloat16)]
        + [jax.ShapeDtypeStruct((rows, 2 * DH), kind) for kind in kinds],
        compiler_params=pltpu.CompilerParams(vmem_limit_bytes=48 * 2**20),
        cost_estimate=cost(2e10, 1e7),
        name="attend_back",
    )(first, queries, *window, *window, grads, pos_q, start_q, lse, inner, pos_k)


def front_kernel(local, head, hidden, grads, weights, gates, active, grad_pre, rows_out, acc):
    groups, levels, _, depth, width = weights.shape
    tile = hidden.shape[0]
    model = groups * depth
    acc[...] = jnp.zeros_like(acc)
    gate_grads = []
    for level in range(levels):
        pre_act = jnp.zeros((tile, width), jnp.float32)
        grad_active = jnp.zeros((tile, width), jnp.float32)
        for group in range(groups):
            part = slice(group * depth, (group + 1) * depth)
            pre_act += dot(hidden[:, part], weights[group, level, 0], 1, 0)
            grad_active += dot(grads[:, part], weights[group, level, 1], 1, 0)
        first = level * local
        gate = jnp.concatenate(
            [jnp.broadcast_to(gates[:, first + e : first + e + 1], (tile, FH)) for e in range(local)],
            axis=1,
        )
        sig = 1.0 / (1.0 + jnp.exp2(-LOG2E * pre_act))
        act_pre = pre_act * sig
        columns = slice(level * width, (level + 1) * width)
        active[:, columns] = (act_pre * gate).astype(jnp.bfloat16)
        product = grad_active * act_pre
        for e in range(local):
            gate_grads.append(
                jnp.sum(product[:, e * FH : (e + 1) * FH], axis=1, keepdims=True)
            )
        slope = sig * (1.0 + pre_act * (1.0 - sig))
        low_pre = (grad_active * gate * slope).astype(jnp.bfloat16)
        grad_pre[:, columns] = low_pre
        for group in range(groups):
            part = slice(group * depth, (group + 1) * depth)
            acc[:, part] += dot(low_pre, weights[group, level, 0], 1, 1)
    rows_out[:, :model] = acc[...].astype(jnp.bfloat16)
    spare = rows_out.shape[1] - model
    lane = lax.broadcasted_iota(jnp.int32, (tile, spare), 1) - head[0] * (levels * local)
    spread = jnp.zeros((tile, spare), jnp.float32)
    for e, column in enumerate(gate_grads):
        spread = jnp.where(lane == e, column, spread)
    rows_out[:, model:] = spread.astype(jnp.bfloat16)


def ffn_front(head, hidden, grads, weights, gates, local):
    rows, wide = hidden.shape
    groups, levels, _, depth, width = weights.shape
    tile = 512

    def by_row(columns):
        return pl.BlockSpec((tile, columns), lambda i, *_: (i, 0))

    grid_spec = pltpu.PrefetchScalarGridSpec(
        num_scalar_prefetch=1,
        grid=(rows // tile,),
        in_specs=[
            by_row(wide),
            by_row(groups * depth),
            pl.BlockSpec(
                weights.shape, lambda i, *_: (0, 0, 0, 0, 0), pipeline_mode=pl.Buffered(1)
            ),
            by_row(gates.shape[1]),
        ],
        out_specs=[by_row(levels * width), by_row(levels * width), by_row(wide)],
        scratch_shapes=[pltpu.VMEM((tile, groups * depth), jnp.float32)],
    )
    hidden_units = jax.ShapeDtypeStruct((rows, levels * width), jnp.bfloat16)
    return pl.pallas_call(
        functools.partial(front_kernel, local),
        grid_spec=grid_spec,
        out_shape=[hidden_units, hidden_units, jax.ShapeDtypeStruct((rows, wide), jnp.bfloat16)],
        compiler_params=pltpu.CompilerParams(vmem_limit_bytes=58 * 2**20),
        cost_estimate=cost(6 * rows * groups * depth * levels * width, 3e7),
        name="ffn_front",
    )(head, hidden, grads, weights, gates)


def rear_kernel(rows_in, hidden_units, weight_grads):
    groups, _, depth, _ = weight_grads.shape
    units = hidden_units[...]
    for group in range(groups):
        part = slice(group * depth, (group + 1) * depth)
        weight_grads[group, 0] = dot(rows_in[:, part], units, 0, 0).astype(jnp.bfloat16)


def feed_kernel(rows_in, low_pre, active, weights, weight_grads, feed, acc):
    groups, _, _, depth, _ = weights.shape
    level = pl.program_id(0)
    units, act = low_pre[...], active[...]
    for group in range(groups):
        part = slice(group * depth, (group + 1) * depth)
        weight_grads[group, 0] = dot(rows_in[:, part], units, 0, 0).astype(jnp.bfloat16)
        fed = dot(act, weights[group, 0, 0], 1, 1)

        @pl.when(level == 0)
        def _():
            acc[:, part] = fed

        @pl.when(level > 0)
        def _():
            acc[:, part] += fed

    @pl.when(level == pl.num_programs(0) - 1)
    def _():
        feed[...] = acc[...].astype(jnp.bfloat16)


def whole_rows(rows, columns):
    return pl.BlockSpec((rows, columns), lambda i: (0, 0), pipeline_mode=pl.Buffered(1))


def ffn_feed(hidden, grad_pre, active, weights):
    rows, wide = hidden.shape
    groups, levels, _, depth, width = weights.shape
    by_level = pl.BlockSpec((rows, width), lambda i: (0, i))
    grads_spec = pl.BlockSpec((groups, 1, depth, width), lambda i: (0, i, 0, 0))
    return pl.pallas_call(
        feed_kernel,
        grid=(levels,),
        in_specs=[
            whole_rows(rows, wide),
            by_level,
            by_level,
            pl.BlockSpec((groups, 1, 1, depth, width), lambda i: (0, i, 1, 0, 0)),
        ],
        out_specs=[grads_spec, whole_rows(rows, groups * depth)],
        out_shape=[
            jax.ShapeDtypeStruct((groups, levels, depth, width), jnp.bfloat16),
            jax.ShapeDtypeStruct((rows, groups * depth), jnp.bfloat16),
        ],
        scratch_shapes=[pltpu.VMEM((rows, groups * depth), jnp.float32)],
        compiler_params=pltpu.CompilerParams(vmem_limit_bytes=58 * 2**20),
        cost_estimate=cost(6 * rows * groups * depth * levels * width, 3e7),
        name="ffn_feed",
    )(hidden, grad_pre, active, weights)


def ffn_rear(rows_in, units, groups, levels):
    rows, wide = rows_in.shape
    width = units.shape[1] // levels
    depth = wide // groups
    return pl.pallas_call(
        rear_kernel,
        grid=(levels,),
        in_specs=[whole_rows(rows, wide), pl.BlockSpec((rows, width), lambda i: (0, i))],
        out_specs=pl.BlockSpec((groups, 1, depth, width), lambda i: (0, i, 0, 0)),
        out_shape=jax.ShapeDtypeStruct((groups, levels, depth, width), jnp.bfloat16),
        compiler_params=pltpu.CompilerParams(vmem_limit_bytes=58 * 2**20),
        cost_estimate=cost(4 * rows * groups * depth * levels * width, 3e7),
        name="ffn_rear",
    )(rows_in, units)


def chosen(routes, options):
    return jnp.sum(
        (routes[..., None] == jnp.arange(options, dtype=jnp.int32)).astype(jnp.float32), axis=-2
    )


def shift(value, axis, by):
    count = lax.axis_size(axis)
    pairs = [(i, i + by) for i in range(count) if 0 <= i + by < count]
    return lax.ppermute(value, axis, pairs)


def body(
    tokens_in,
    out_grad,
    deal_order,
    seq_lengths,
    value_routes,
    output_routes,
    ffn_routes,
    norm1_gain,
    norm1_bias,
    norm2_gain,
    norm2_bias,
    query_weight,
    key_weight,
    value_weight,
    output_weight,
    value_router,
    output_router,
    ffn_router,
    ffn_in,
    ffn_out,
):
    groups = lax.axis_size("group")
    levels = lax.axis_size("level")
    level = lax.axis_index("level")
    head = lax.axis_index("head")
    count, width = tokens_in.shape
    piece = count // (levels * HEADS)
    wrows = query_weight.shape[0]
    experts = ffn_router.shape[1]
    local_experts = ffn_in.shape[1] // FH

    small = jnp.concatenate(
        [
            ffn_router,
            norm1_gain[:, None],
            norm1_bias[:, None],
            norm2_gain[:, None],
            norm2_bias[:, None],
        ],
        axis=1,
    )
    shared = small.shape[1]
    pad = -(shared + 2 * VEXP) % 128
    packed = jnp.concatenate(
        [
            query_weight.reshape(wrows, HEADS, DH),
            key_weight.reshape(wrows, HEADS, DH),
            value_weight.reshape(wrows, HEADS, VEXP * DH),
            output_weight.reshape(wrows, HEADS, VEXP * DH),
            value_router.reshape(wrows, HEADS, VEXP),
            output_router.reshape(wrows, HEADS, VEXP),
            jnp.broadcast_to(small[:, None, :], (wrows, HEADS, shared)),
            jnp.zeros((wrows, HEADS, pad), jnp.bfloat16),
        ],
        axis=2,
    )
    cols = packed.shape[2]
    tables = jnp.concatenate(
        [value_routes.transpose(1, 2, 0), output_routes.transpose(1, 2, 0)], axis=1
    )
    picks = ffn_routes.reshape(levels, HEADS * piece, -1).transpose(0, 2, 1)
    arrived, full, tables, picks, orders = start(
        tokens_in.reshape(levels, HEADS, piece, width),
        packed.transpose(1, 0, 2),
        tables,
        picks,
        deal_order,
    )
    worker_in = arrived.reshape(HEADS * count, width)
    own_tokens = lax.dynamic_index_in_dim(arrived, head, 1, keepdims=False).reshape(count, width)
    full = full.reshape(width, cols)

    both = after(jnp.stack([ffn_in, ffn_out]), full)
    both = lax.all_gather(both, ("group", "level"), axis=0)
    both = both.reshape((groups, levels) + both.shape[1:])

    base = 2 * DH + 2 * VEXP * DH
    w_query = full[:, :DH]
    w_key = full[:, DH : 2 * DH]
    w_value = full[:, 2 * DH : 2 * DH + VEXP * DH]
    w_output = full[:, 2 * DH + VEXP * DH : base]
    r_value = full[:, base : base + VEXP]
    r_output = full[:, base + VEXP : base + 2 * VEXP]
    at = base + 2 * VEXP
    r_ffn = full[:, at : at + experts]
    gain_one, bias_one, gain_two, bias_two = (
        full[:, at + experts + i].astype(jnp.float32) for i in range(4)
    )

    own_grads = to_workers(after(out_grad, worker_in))

    ramp = jnp.arange(count, dtype=jnp.int32)
    rows = HEADS * count

    def arrival(values):
        lead, shape = values.shape[:-3], values.shape[-1:]
        four = values.reshape(lead + (HEADS, levels, HEADS, piece) + shape)
        return jnp.swapaxes(four, -4, -3).reshape(lead + (rows,) + shape)

    reach = -(-LMAX // rows)
    orders = orders.reshape(levels, HEADS, count)
    orders = jnp.concatenate([jnp.zeros((reach, HEADS, count), jnp.int32), orders], axis=0)
    orders = lax.dynamic_slice_in_dim(orders, level, reach + 1, 0)
    here = orders[:, :, None, :] == ramp[None, None, :, None]
    inverse = jnp.sum(here * ramp, axis=3)
    shard = (level - reach + jnp.arange(reach + 1, dtype=jnp.int32))[:, None] * HEADS
    shard = shard + jnp.arange(HEADS, dtype=jnp.int32)[None, :]
    pos_all = jnp.where(shard[:, :, None] < 0, -1, shard[:, :, None] * count + inverse)
    pos_all = arrival(pos_all[..., None]).reshape(-1)
    positions = pos_all[reach * rows :]
    options = jnp.arange(VEXP, dtype=jnp.int32)[None, :, None]

    def mask_of(which):
        one, two = tables[:, which, None, :], tables[:, which + 1, None, :]
        return (one == options).astype(jnp.bfloat16) + (two == options).astype(jnp.bfloat16)

    masks = jnp.concatenate([mask_of(0), mask_of(2)], axis=1)
    masks = jnp.einsum(
        "ktr,ker->kte", low(here[reach]), masks, preferred_element_type=jnp.float32
    )
    masks = arrival(masks)
    value_mask, out_mask = masks[:, :VEXP], masks[:, VEXP:]
    own_routes = picks.reshape(levels, -1, HEADS, piece).transpose(2, 0, 3, 1).reshape(count, -1)

    normed, scaled_one, inverse_one = layer_norm(worker_in.astype(jnp.float32), gain_one, bias_one)
    normed_one = low(normed)
    queries = low(matmul(normed_one, w_query))
    keys = low(matmul(normed_one, w_key))
    projected = matmul(worker_in, w_value).reshape(rows, VEXP, DH)
    value_sig = jax.nn.sigmoid(matmul(normed_one, r_value))
    value_gate = value_sig * value_mask
    values = low(jnp.sum(value_gate[..., None] * projected, axis=1))
    span = (reach + 1) * rows
    window = [jnp.concatenate([keys, values], axis=1)]
    for _ in range(reach):
        window.insert(0, shift(window[0], "level", 1))
    seq_ends = jnp.cumsum(seq_lengths[0])

    def starts_of(places):
        return jnp.max(jnp.where(seq_ends <= places[:, None], seq_ends, 0), axis=1)

    starts = starts_of(positions)
    blocks = rows // BLOCK
    base_block = (level - reach) * blocks
    first_block = starts_of(level * rows + jnp.arange(blocks, dtype=jnp.int32) * BLOCK) // BLOCK
    first_block = jnp.maximum(first_block - base_block, 0)

    def lines(values):
        return values.reshape(blocks, 1, BLOCK)

    attended, log_total = attend(
        first_block,
        queries,
        window,
        lines(positions),
        lines(starts),
        pos_all[:, None],
    )

    out_sig = jax.nn.sigmoid(matmul(normed_one, r_output))
    out_gate = out_sig * out_mask
    mixed = low((out_gate[..., None] * attended[:, None, :]).reshape(rows, VEXP * DH))
    branch = low(level_scatter(low(transposed(mixed, w_output)), 2))
    middle = own_tokens.astype(jnp.float32) + branch.astype(jnp.float32)

    normed_mid, scaled_two, inverse_two = layer_norm(middle, gain_two, bias_two)
    normed_two = low(normed_mid)
    ffn_sig = jax.nn.sigmoid(matmul(normed_two, r_ffn))
    member = chosen(own_routes, experts)
    shares = (ffn_sig * member).reshape(count, levels, HEADS, local_experts)
    shares = jnp.swapaxes(shares, 1, 2).reshape(count, experts)
    spare = -experts % 128
    extended = jnp.concatenate([middle, shares], axis=1)
    hidden = level_gather(jnp.pad(low(extended), ((0, 0), (0, spare))), 3, True)
    mine = levels * local_experts
    gates = lax.dynamic_slice_in_dim(hidden, width + head * mine, mine, 1).astype(jnp.float32)
    cotangent = level_gather(own_grads, 5, True)
    active, grad_pre, grad_rows = ffn_front(
        head[None], hidden, cotangent, both, gates, local_experts
    )
    summed, beyond = pair_scatter(grad_rows, 4, True)
    came = to_far(beyond)
    grad_in, feed = ffn_feed(after(hidden, beyond), grad_pre, active, both)
    summed = summed + after(came, feed).astype(jnp.float32)

    gate_grads = summed[:, width : width + experts].reshape(count, HEADS, levels, local_experts)
    gate_grads = jnp.swapaxes(gate_grads, 1, 2).reshape(count, experts)
    grad_logit = low(gate_grads * ffn_sig * (1.0 - ffn_sig) * member)
    grad_second = transposed(grad_logit, r_ffn)
    grad_r_ffn = contract_rows(normed_two, grad_logit)
    grad_gain_two = jnp.sum(grad_second * scaled_two, axis=0)
    grad_bias_two = jnp.sum(grad_second, axis=0)
    grad_middle = (
        own_grads.astype(jnp.float32)
        + summed[:, :width]
        + norm_back(grad_second, gain_two, scaled_two, inverse_two)
    )

    own_branch = low(grad_middle)
    came = to_far(own_branch)
    grad_out = ffn_rear(after(cotangent, own_branch), active, groups, levels)
    grad_branch = pair_gather(own_branch, after(came, grad_out), 7)
    grad_ffn = [
        lax.psum_scatter(
            g.reshape((groups * levels,) + g.shape[2:]), ("group", "level"), scatter_dimension=0
        ).astype(jnp.float32)
        for g in (grad_in, grad_out)
    ]
    grad_mixed = matmul(grad_branch, w_output).reshape(rows, VEXP, DH)
    grad_out_gate = jnp.sum(grad_mixed * attended[:, None, :], axis=-1)
    grad_attended = low(jnp.sum(grad_mixed * out_gate[..., None], axis=1))
    grad_out_logit = low(grad_out_gate * out_sig * (1.0 - out_sig) * out_mask)
    row_inner = jnp.sum(grad_attended.astype(jnp.float32) * attended, axis=-1)
    grad_queries, *grad_window = attend_back(
        first_block,
        queries,
        window,
        grad_attended,
        lines(positions),
        lines(starts),
        log_total,
        lines(row_inner),
        pos_all[:, None],
    )
    came = shift(grad_window[0], "level", -1)
    fed, beyond = pair_scatter(after(feed, grad_queries), 6, True)
    grad_w_output = contract_rows(after(grad_branch, fed), mixed)
    for i in range(1, reach + 1):
        grad_both = grad_window[i].astype(jnp.float32) + came.astype(jnp.float32)
        if i < reach:
            came = shift(low(grad_both), "level", -1)
    fed_far = to_far(after(beyond, grad_both))
    done = low(middle + fed + fed_far.astype(jnp.float32))
    grad_keys, grad_values = low(grad_both[:, :DH]), grad_both[:, DH:]
    grad_projected = low((value_gate[..., None] * grad_values[:, None, :]).reshape(rows, VEXP * DH))
    grad_value_gate = jnp.sum(grad_values[:, None, :] * projected, axis=-1)
    grad_value_logit = low(grad_value_gate * value_sig * (1.0 - value_sig) * value_mask)
    grad_first = (
        transposed(grad_queries, w_query)
        + transposed(grad_keys, w_key)
        + transposed(grad_value_logit, r_value)
        + transposed(grad_out_logit, r_output)
    )
    grad_inputs = norm_back(grad_first, gain_one, scaled_one, inverse_one) + transposed(
        grad_projected, w_value
    )
    weight_grads = jnp.concatenate(
        [
            low(grad_w_output),
            low(contract_rows(normed_one, grad_queries)),
            low(contract_rows(normed_one, grad_keys)),
            low(contract_rows(worker_in, grad_projected)),
            low(contract_rows(normed_one, grad_value_logit)),
            low(contract_rows(normed_one, grad_out_logit)),
            low(grad_r_ffn),
            low(grad_gain_two)[:, None],
            low(grad_bias_two)[:, None],
            low(jnp.sum(grad_first * scaled_one, axis=0))[:, None],
            low(jnp.sum(grad_first, axis=0))[:, None],
            jnp.zeros((width, pad), jnp.bfloat16),
        ],
        axis=1,
    )
    input_grad, layer_out, owned = finish(
        low(grad_inputs).reshape(HEADS, HEADS, levels * piece, width),
        grad_middle.reshape(HEADS, levels * piece, width),
        done.reshape(HEADS, levels, piece, width),
        weight_grads.reshape(groups, levels, HEADS, wrows, cols),
    )
    owned = owned.astype(jnp.float32)

    def columns(first, size):
        return owned[:, :, first : first + size].transpose(1, 0, 2).reshape(wrows, HEADS * size)

    at = VEXP * DH
    common = jnp.sum(owned[:, :, base + 2 * VEXP :], axis=0)
    return (
        layer_out.reshape(count, width),
        input_grad.reshape(count, width),
        common[:, experts + 2],
        common[:, experts + 3],
        common[:, experts],
        common[:, experts + 1],
        columns(at, DH),
        columns(at + DH, DH),
        columns(at + 2 * DH, VEXP * DH),
        columns(0, VEXP * DH),
        columns(base, VEXP),
        columns(base + VEXP, VEXP),
        common[:, :experts],
        grad_ffn[0],
        grad_ffn[1],
    )


def solution(mesh):
    groups, shards = mesh.devices.shape
    fine = Mesh(mesh.devices.reshape(groups, shards // HEADS, HEADS), TOK)
    two, one, three = P(TOK, None), P(TOK), P(TOK, None, None)
    ffn = P("group", ("level", "head"))
    return jax.shard_map(
        body,
        mesh=fine,
        in_specs=(two, two, two, P("group", None), three, three, two, one, one, one, one)
        + (two,) * 7
        + (ffn, ffn),
        out_specs=(two, two, one, one, one, one) + (two,) * 7 + (ffn, ffn),
        check_vma=False,
    )
```

time: 1030 us -> 853 us (0.83)
  matrix products: 242 us -> 98 us
  Pallas kernels: 298 us -> 384 us
  blocking collectives: 63.8 us -> 0 us
  other arithmetic: 77.2 us -> 53.4 us
  starting transfers between devices: 50.4 us -> 34.3 us
    pallas_call x10 -> x13, Pallas kernels: 298 us -> 384 us  [the longest x1 91.1 us: finish(): pl.pallas_call(finish_kernel, out_shape=[jax.ShapeDtypeStruct((levels, HE...]
    dot_general x15 -> x7, matrix products: 85.4 us -> 25.2 us  [matmul(): return jnp.dot(left_side, right_side, preferred_element_type=jnp.float32)]
    dot_general x15 -> x7, matrix products: 109 us -> 51.4 us  [transposed(): lax.dot_general(left_side, right_side, (((1,), (1,)), ((), ())), preferre...]
    all_to_all x5 -> x0, waiting for transfers between devices: 53.1 us -> none  [the longest x2 42.4 us: to_home(): lax.all_to_all(out.reshape(levels, count // levels, -1), 'level', split_a...]
    all_gather x2 -> x0, blocking collectives: 52.9 us -> none  [the longest x1 47.5 us: body(): orders = lax.all_gather(deal_order, ('level', 'head'), axis=0, tiled=True)]
    ppermute x4, waiting for transfers between devices: 95.8 us -> 143 us  [shift(): return lax.ppermute(value, axis, pairs)]
    dot_general x15 -> x7, matrix products: 46.6 us -> 20.6 us  [contract_rows(): lax.dot_general(left_side, right_side, (((0,), (0,)), ((), ())), preferre...]
    all_to_all x5 -> x0, starting transfers between devices: 23.2 us -> none  [the longest x2 9.31 us: to_home(): lax.all_to_all(out.reshape(levels, count // levels, -1), 'level', split_a...]
  transfers between devices with their start and end apart: 21 -> 11, of which waited for: 7 -> 6; matrix products, arithmetic and copies ran while one was open for 32% -> 24% of each run, Pallas kernels for 29% -> 31%
where the time goes in v2:
time: 853 us; the launch traced here: 844 us
  Pallas kernels  384 us (45%)
  waiting for transfers between devices  169 us (20%)
  matrix products  98 us (11%)
  local copies, waits for them, and re-layouts  90.6 us (11%)
  other arithmetic  53.4 us (6%)
  starting transfers between devices  34.3 us (4%)
  between operations  15.3 us (2%)
    ppermute x4, waiting for transfers between devices, shift(): return lax.ppermute(value, axis, pairs)  143 us
    pallas_call x1, Pallas kernels, finish(): pl.pallas_call(finish_kernel, out_shape=[jax.ShapeDtypeStruct((levels, HE...  91.1 us
    pallas_call x1, Pallas kernels, start(): pl.pallas_call(start_kernel, out_shape=shapes, in_specs=[pl.BlockSpec(mem...  77.5 us
    pallas_call x2, Pallas kernels, level_gather(): pl.pallas_call(functools.partial(gather_kernel, by_source), out_shape=jax...  59.6 us
    dot_general x7, matrix products, transposed(): lax.dot_general(left_side, right_side, (((1,), (1,)), ((), ())), preferre...  51.4 us
    pallas_call x1, Pallas kernels, ffn_front(): pl.pallas_call(functools.partial(front_kernel, local), grid_spec=grid_spe...  35.8 us
    unnamed x149, local copies, waits for them, and re-layouts  28.7 us
    pallas_call x1, Pallas kernels, ffn_feed(): pl.pallas_call(feed_kernel, grid=(levels,), in_specs=[whole_rows(rows, wi...  28.6 us
  transfers between devices with their start and end apart: 11, of which 6 were waited for; matrix products, arithmetic and copies ran while one was open for 24% of the time, Pallas kernels for 31%

profile of v2, /device:TPU:8, one launch (start us, length us, event | category | flops | bytes accessed | tf_op | source)
XLA Modules:
  0.0 844.5 jit_solution(6725360390899775605)
XLA Ops:
  20.5 77.5 %start.1 = (bf16[4,4,4,32,1024]{4,3,2,1,0:T(8,128)(2,1)}, bf16[2,4,4,32,1664]{4,3,2,1,0:T(8,128)(2,1)}, s32[4,4,512]{2,1,0:T(4,128)}, s32[4,16,128]{2,1,0:T(8,128)}, s32[4,4,1,512]{3,2,1,0:T(1,128)}) custom-call(bf16[4,4,32,1024]{3,2,1,0:T(8,128)(2,1)} %bitcast.277, bf16[4,32,1664]{2,1,0:T(8,128)(2,1)} %bitcast.267, s32[4,4,512]{2,1,0:T(4,128)} %pad_add_fusion.tables, ...), custom_call_target="tpu_custom_call" | custom-call | bytes 200000000 | tf_op jit(solution)/shard_map/start/pallas_call | solution.py:470
  128.4 5.6 multiply_reduce_fusion.6
  139.8 11.4 %collective-permute-start = (bf16[2048,256]{1,0:T(8,128)(2,1)S(1)}, bf16[2048,256]{1,0:T(8,128)(2,1)S(1)}, u32[]{:S(2)}, u32[]{:S(2)}) collective-permute-start(bf16[2048,256]{1,0:T(8,128)(2,1)S(1)} %pad_maximum_fusion.refs_2_.refs_5_), channel_id=1, source_target_pairs={{0,4},{4,8},{8,12},{1,5},{5,9},{9,13},{2,6},{6,10},{10,14},{3,7},{... | collective-permute-start | bytes 3145736 | tf_op jit(solution)/shard_map/ppermute | solution.py:980
  157.9 39.5 %collective-permute-done.refs_1_.refs_4_ = bf16[2048,256]{1,0:T(8,128)(2,1)S(1)} collective-permute-done((bf16[2048,256]{1,0:T(8,128)(2,1)S(1)}, bf16[2048,256]{1,0:T(8,128)(2,1)S(1)}, u32[]{:S(2)}, u32[]{:S(2)}) %collective-permute-start) | collective-permute-done | bytes 1048608 | tf_op jit(solution)/shard_map/ppermute | solution.py:980
  197.4 11.2 %collective-permute-start.1 = (bf16[2048,256]{1,0:T(8,128)(2,1)S(1)}, bf16[2048,256]{1,0:T(8,128)(2,1)S(1)}, u32[]{:S(2)}, u32[]{:S(2)}) collective-permute-start(bf16[2048,256]{1,0:T(8,128)(2,1)S(1)} %collective-permute-done.refs_1_.refs_4_), channel_id=1, source_target_pairs={{0,4},{4,8},{8,12},{1,5},{5,9},{9,13},{2,6},{6,10},{10,14},{3,7},{... | collective-permute-start | bytes 3145736 | tf_op jit(solution)/shard_map/ppermute | solution.py:980
  209.0 5.0 broadcast_in_dim_reshape_reshape.5.refs_8_.refs_11_
  224.3 15.4 %all-to-all-done = bf16[4,128,1024]{2,1,0:T(8,128)(2,1)} async-done(((bf16[4,128,1024]{2,1,0:T(8,128)(2,1)}), bf16[4,128,1024]{2,1,0:T(8,128)(2,1)}, u32[]{:S(2)}, u32[]{:S(2)}) %all-to-all-start) | async-done | bytes 1048608 | tf_op jit(solution)/shard_map/all_to_all | solution.py:58
  242.0 28.7 %level_gather.3 = bf16[4,4,128,1024]{3,2,1,0:T(8,128)(2,1)} custom-call(bf16[4,128,1024]{2,1,0:T(8,128)(2,1)} %bitcast.254), custom_call_target="tpu_custom_call" | custom-call | bytes 90000000 | tf_op jit(solution)/shard_map/level_gather/pallas_call | solution.py:131
  270.8 13.8 %collective-permute-done.1.refs_0_.refs_3_ = bf16[2048,256]{1,0:T(8,128)(2,1)S(1)} collective-permute-done((bf16[2048,256]{1,0:T(8,128)(2,1)S(1)}, bf16[2048,256]{1,0:T(8,128)(2,1)S(1)}, u32[]{:S(2)}, u32[]{:S(2)}) %collective-permute-start.1) | collective-permute-done | bytes 1048608 | tf_op jit(solution)/shard_map/ppermute | solution.py:980
  287.9 14.9 %attend.1 = (f32[2048,128]{1,0:T(8,128)S(1)}, f32[4,1,512]{2,1,0:T(1,128)S(1)}) custom-call(s32[4]{0:T(128)S(1)} %subtract_maximum_fusion.first, bf16[2048,128]{1,0:T(8,128)(2,1)S(1)} %copy-done.15, bf16[2048,256]{1,0:T(8,128)(2,1)S(1)} %copy-done.11, bf16[2048,256]{1,0:T(8,128)(2,1)S(1)} %collective-permute-done.refs_1_.refs_4_, ...), custom_call_target="tpu_custom_call" | custom-call | flops 20000000000 | bytes 10000000 | tf_op jit(solution)/shard_map/attend/pallas_call | solution.py:725
  303.7 6.0 convolution_convert_fusion
  309.7 27.3 %level_scatter.1 = f32[4,128,1024]{2,1,0:T(8,128)S(1)} custom-call(bf16[4,4,128,1024]{3,2,1,0:T(8,128)(2,1)S(1)} %bitcast.222), custom_call_target="tpu_custom_call" | custom-call | bytes 80000000 | tf_op jit(solution)/shard_map/level_scatter/pallas_call | solution.py:193
  349.8 30.9 %level_gather.2 = bf16[4,4,128,1152]{3,2,1,0:T(8,128)(2,1)} custom-call(bf16[4,128,1152]{2,1,0:T(8,128)(2,1)} %bitcast.251), custom_call_target="tpu_custom_call" | custom-call | bytes 90000000 | tf_op jit(solution)/shard_map/level_gather/pallas_call | solution.py:131
  383.0 35.8 %ffn_front.1 = (bf16[2048,2048]{1,0:T(8,128)(2,1)}, bf16[2048,2048]{1,0:T(8,128)(2,1)}, bf16[2048,1152]{1,0:T(8,128)(2,1)}) custom-call(s32[1]{0:T(128)} %bitcast.24.head, bf16[2048,1152]{1,0:T(8,128)(2,1)} %bitcast.249, bf16[2048,1024]{1,0:T(8,128)(2,1)} %bitcast.252, bf16[2,4,2,512,512]{4,3,2,1,0:T(8,128)(2,1)} %bitcast.315, ...), custom_call_target="tpu_custom_call" | custom-call | flops 25769803776 | bytes 30000000 | tf_op jit(solution)/shard_map/ffn_front/pallas_call | solution.py:885
  421.1 5.8 pair_scatter.2
  428.0 28.6 %ffn_feed.1 = (bf16[2,4,512,512]{3,2,1,0:T(8,128)(2,1)}, bf16[2048,1024]{1,0:T(8,128)(2,1)}) custom-call(bf16[2048,1152]{1,0:T(8,128)(2,1)} %bitcast.250, bf16[2048,2048]{1,0:T(8,128)(2,1)} %get-tuple-element.59.low_pre, bf16[2048,2048]{1,0:T(8,128)(2,1)} %get-tuple-element.60.active.hidden_units, bf16[2,4,2,512,512]{4,3,2,1,0:T(8,128)(2,1)} %bitcast.316), custom_call_target="tpu_custom_call" | custom-call | flops 25769803776 | bytes 30000000 | tf_op jit(solution)/shard_map/ffn_feed/pallas_call | solution.py:934
  474.8 13.8 %ffn_rear.1 = bf16[2,4,512,512]{3,2,1,0:T(8,128)(2,1)} custom-call(bf16[2048,1024]{1,0:T(8,128)(2,1)} %bitcast.253, bf16[2048,2048]{1,0:T(8,128)(2,1)} %get-tuple-element.60.active.hidden_units), custom_call_target="tpu_custom_call" | custom-call | flops 17179869184 | bytes 30000000 | tf_op jit(solution)/shard_map/ffn_rear/pallas_call | solution.py:959
  488.5 10.3 %collective-permute-done.3 = bf16[512,1024]{1,0:T(8,128)(2,1)S(1)} collective-permute-done((bf16[512,1024]{1,0:T(8,128)(2,1)S(1)}, bf16[512,1024]{1,0:T(8,128)(2,1)S(1)}, u32[]{:S(2)}, u32[]{:S(2)}) %collective-permute-start.3) | collective-permute-done | bytes 1048608 | tf_op jit(solution)/shard_map/ppermute | solution.py:313
  499.8 6.1 pair_gather.1
  505.9 6.6 multiply_reduce_fusion.5
  517.7 19.5 %attend_back.1 = (bf16[2048,128]{1,0:T(8,128)(2,1)S(1)}, bf16[2048,256]{1,0:T(8,128)(2,1)}, bf16[2048,256]{1,0:T(8,128)(2,1)S(1)}, f32[2048,256]{1,0:T(8,128)}) custom-call(s32[4]{0:T(128)S(1)} %subtract_maximum_fusion.first, bf16[2048,128]{1,0:T(8,128)(2,1)S(1)} %copy-done.16, bf16[2048,256]{1,0:T(8,128)(2,1)S(1)} %copy-done.12, ...), custom_call_target="tpu_custom_call" | custom-call | flops 20000000000 | bytes 10000000 | tf_op jit(solution)/shard_map/attend_back/pallas_call | solution.py:809
  550.0 58.8 %collective-permute-done.4 = bf16[2048,256]{1,0:T(8,128)(2,1)} collective-permute-done((bf16[2048,256]{1,0:T(8,128)(2,1)}, bf16[2048,256]{1,0:T(8,128)(2,1)}, u32[]{:S(2)}, u32[]{:S(2)}) %collective-permute-start.4) | collective-permute-done | bytes 1048608 | tf_op jit(solution)/shard_map/ppermute | solution.py:980
  619.4 30.7 %collective-permute-done.5 = bf16[2048,256]{1,0:T(8,128)(2,1)S(1)} collective-permute-done((bf16[2048,256]{1,0:T(8,128)(2,1)S(1)}, bf16[2048,256]{1,0:T(8,128)(2,1)S(1)}, u32[]{:S(2)}, u32[]{:S(2)}) %collective-permute-start.5) | collective-permute-done | bytes 1048608 | tf_op jit(solution)/shard_map/ppermute | solution.py:980
  656.0 5.3 multiply_convert_fusion
  666.7 5.7 fusion.23
  672.4 5.7 fusion.26
  678.1 5.6 fusion.29
  683.7 14.1 %multiply_reduce_fusion = (bf16[1024]{0:T(1024)(128)(2,1)S(1)}, f32[2048]{0:T(1024)S(1)}, f32[2048]{0:T(1024)S(1)}, bf16[1024]{0:T(1024)(128)(2,1)S(1)}, f32[2048,1024]{1,0:T(8,128)}) fusion(f32[2048]{0:T(1024)S(1)} %copy-done.59, f32[2048]{0:T(1024)S(1)} %copy-done.61, bf16[4,4,4,32,1024]{4,3,2,1,0:T(8,128)(2,1)S(1)} %copy-done.21, f32[1024]{0:T(1024)S(1)} %bitcast.296, ...), kind=kOutput, calls=%fused_computation.6 | convolution fusion | flops 564127744 | bytes 38576128 | tf_op jit(solution)/shard_map/dot_general | solution.py:24
  704.1 6.3 convolution_convert_fusion.3
  711.1 7.3 concatenate.54.grads
  718.4 11.2 %add_convert_fusion = bf16[2048,1024]{1,0:T(8,128)(2,1)} fusion(bf16[2048,1024]{1,0:T(8,128)(2,1)} %bitcast.228, f32[2048,1024]{1,0:T(8,128)} %get-tuple-element.125, f32[2048]{0:T(1024)S(1)} %broadcast_multiply_fusion.1, f32[2048]{0:T(1024)S(1)} %broadcast_multiply_fusion.2, f32[1024]{0:T(1024)S(1)} %bitcast.297, f32[2048]{0:T(1024)S(1)} %copy-done.59, ...), kind=kOutput, calls=%fused_computation.7 | convolution fusion | flops 2705326080 | bytes 20746240 | tf_op jit(solution)/shard_map/dot_general | solution.py:24
  732.3 91.1 %finish.1 = (f32[4,4,32,1024]{3,2,1,0:T(8,128)}, bf16[4,4,32,1024]{3,2,1,0:T(8,128)(2,1)}, bf16[4,32,1664]{2,1,0:T(8,128)(2,1)}) custom-call(bf16[4,4,128,1024]{3,2,1,0:T(8,128)(2,1)} %bitcast.260, f32[4,128,1024]{2,1,0:T(8,128)} %bitcast.247, bf16[4,4,32,1024]{3,2,1,0:T(8,128)(2,1)} %bitcast.261, bf16[2,4,4,32,1664]{4,3,2,1,0:T(8,128)(2,1)} %concatenate.54.grads), custom_call_target="tpu_custom_call" | custom-call | bytes 200000000 | tf_op jit(solution)/shard_map/finish/pallas_call | solution.py:627
  (301 shorter events, 173.7 us)
Async XLA Ops:
  7.2 375.8 %all-gather.3.cloned.1.call-start = ((), (), s32[]{:S(2)}) async-start(), calls=%async_computation.5 | async-start | bytes 9437184 | tf_op jit(solution)/shard_map/all_gather | solution.py:1057
  101.1 19.7 %copy-start.58 = (f32[2048]{0:T(1024)}, f32[2048]{0:T(1024)S(1)}, u32[]{:S(2)}) copy-start(f32[2048]{0:T(1024)S(1)} %div.55) | copy-start | bytes 24580
  101.1 8.1 copy-start.66
  104.2 16.6 %copy-start.60 = (f32[2048]{0:T(1024)}, f32[2048]{0:T(1024)S(1)}, u32[]{:S(2)}) copy-start(f32[2048]{0:T(1024)S(1)} %rsqrt.23) | copy-start | bytes 24580
  107.1 13.7 %copy-start.63 = (f32[1024,1]{0,1:T(1,128)}, f32[1024,1]{0,1:T(1,128)S(1)}, u32[]{:S(2)}) copy-start(f32[1024,1]{0,1:T(1,128)S(1)} %copy.268) | copy-start | bytes 12292
  139.6 17.8 %copy-start.67 = (s32[1,3]{1,0:T(1,128)S(1)}, s32[1,3]{1,0:T(1,128)}, u32[]{:S(2)}) copy-start(s32[1,3]{1,0:T(1,128)} %param.23) | copy-start | bytes 40
  139.8 145.8 %copy-start.4 = (bf16[2048,256]{1,0:T(8,128)(2,1)}, bf16[2048,256]{1,0:T(8,128)(2,1)S(1)}, u32[]{:S(2)}) copy-start(bf16[2048,256]{1,0:T(8,128)(2,1)S(1)} %pad_maximum_fusion.refs_2_.refs_5_) | copy-start | bytes 3145732
  139.8 75.4 %copy-start.65 = (s32[4,16,128]{2,1,0:T(8,128)S(1)}, s32[4,16,128]{2,1,0:T(8,128)}, u32[]{:S(2)}) copy-start(s32[4,16,128]{2,1,0:T(8,128)} %get-tuple-element.53) | copy-start | bytes 98308
  139.8 57.6 %collective-permute-start = (bf16[2048,256]{1,0:T(8,128)(2,1)S(1)}, bf16[2048,256]{1,0:T(8,128)(2,1)S(1)}, u32[]{:S(2)}, u32[]{:S(2)}) collective-permute-start(bf16[2048,256]{1,0:T(8,128)(2,1)S(1)} %pad_maximum_fusion.refs_2_.refs_5_), channel_id=1, source_target_pairs={{0,4},{4,8},{8,12},{1,5},{5,9},{9,13},{2,6},{6,10},{10,14},{3,7},{... | collective-permute-start | bytes 3145736 | tf_op jit(solution)/shard_map/ppermute | solution.py:980
  151.2 88.5 %all-to-all-start = ((bf16[4,128,1024]{2,1,0:T(8,128)(2,1)}), bf16[4,128,1024]{2,1,0:T(8,128)(2,1)}, u32[]{:S(2)}, u32[]{:S(2)}) async-start(bf16[4,128,1024]{2,1,0:T(8,128)(2,1)} %bitcast.278), calls=%async_computation | async-start | bytes 2097152 | tf_op jit(solution)/shard_map/all_to_all | solution.py:58
  155.5 674.1 %reduce-scatter.3.cloned.1.call-start = ((), (), s32[]{:S(2)}) async-start(), calls=%async_computation.3 | async-start | bytes 4718592 | tf_op jit(solution)/shard_map/reduce_scatter | solution.py:1187
  197.4 88.2 %copy-start.8 = (bf16[2048,256]{1,0:T(8,128)(2,1)}, bf16[2048,256]{1,0:T(8,128)(2,1)S(1)}, u32[]{:S(2)}) copy-start(bf16[2048,256]{1,0:T(8,128)(2,1)S(1)} %collective-permute-done.refs_1_.refs_4_) | copy-start | bytes 3145732
  197.4 87.2 %collective-permute-start.1 = (bf16[2048,256]{1,0:T(8,128)(2,1)S(1)}, bf16[2048,256]{1,0:T(8,128)(2,1)S(1)}, u32[]{:S(2)}, u32[]{:S(2)}) collective-permute-start(bf16[2048,256]{1,0:T(8,128)(2,1)S(1)} %collective-permute-done.refs_1_.refs_4_), channel_id=1, source_target_pairs={{0,4},{4,8},{8,12},{1,5},{5,9},{9,13},{2,6},{6,10},{10,14},{3,7},{... | collective-permute-start | bytes 3145736 | tf_op jit(solution)/shard_map/ppermute | solution.py:980
  217.2 128.2 %copy-start.46 = (f32[512,64]{0,1:T(8,128)}, f32[512,64]{0,1:T(8,128)S(1)}, u32[]{:S(2)}) copy-start(f32[512,64]{0,1:T(8,128)S(1)} %convert_reduce_fusion.1) | copy-start | bytes 393220
  426.9 35.4 %collective-permute-start.2 = (bf16[512,1152]{1,0:T(8,128)(2,1)}, bf16[512,1152]{1,0:T(8,128)(2,1)}, u32[]{:S(2)}, u32[]{:S(2)}) collective-permute-start(bf16[512,1152]{1,0:T(8,128)(2,1)} %bitcast.47), channel_id=1, source_target_pairs={{0,2},{1,3},{2,0},{3,1},{4,6},{5,7},{6,4},{7,5},{8,10},{9,11},{10,... | collective-permute-start | bytes 3538952 | tf_op jit(solution)/shard_map/ppermute | solution.py:313
  456.6 375.2 %reduce-scatter.5.cloned.1.call-start = ((), (), s32[]{:S(2)}) async-start(), calls=%async_computation.4 | async-start | bytes 4718592 | tf_op jit(solution)/shard_map/reduce_scatter | solution.py:1187
  473.7 14.8 %copy-start.38 = (bf16[512,1024]{1,0:T(8,128)(2,1)}, bf16[512,1024]{1,0:T(8,128)(2,1)S(1)}, u32[]{:S(2)}) copy-start(bf16[512,1024]{1,0:T(8,128)(2,1)S(1)} %get-tuple-element.93) | copy-start | bytes 3145732
  473.7 25.1 %collective-permute-start.3 = (bf16[512,1024]{1,0:T(8,128)(2,1)S(1)}, bf16[512,1024]{1,0:T(8,128)(2,1)S(1)}, u32[]{:S(2)}, u32[]{:S(2)}) collective-permute-start(bf16[512,1024]{1,0:T(8,128)(2,1)S(1)} %get-tuple-element.93), channel_id=1, source_target_pairs={{0,2},{1,3},{2,0},{3,1},{4,6},{5,7},{6,4},{7,5},{8,10},{9,11},{10,... | collective-permute-start | bytes 3145736 | tf_op jit(solution)/shard_map/ppermute | solution.py:313
  488.5 17.4 %copy-start.35 = (f32[2048,128]{0,1:T(8,128)S(1)}, f32[2048,128]{0,1:T(8,128)}, u32[]{:S(2)}) copy-start(f32[2048,128]{0,1:T(8,128)} %copy-done.34) | copy-start | bytes 3145732
  488.5 17.4 %copy-start.44 = (bf16[640,1024]{1,0:T(8,128)(2,1)S(1)}, bf16[640,1024]{1,0:T(8,128)(2,1)}, u32[]{:S(2)}) copy-start(bf16[640,1024]{1,0:T(8,128)(2,1)} %copy.232) | copy-start | bytes 3932164
  517.7 22.2 %copy-start.29 = (bf16[512,1024]{1,0:T(8,128)(2,1)S(1)}, bf16[512,1024]{1,0:T(8,128)(2,1)}, u32[]{:S(2)}) copy-start(bf16[512,1024]{1,0:T(8,128)(2,1)} %copy-done.28) | copy-start | bytes 3145732
  517.7 22.2 %copy-start.57 = (bf16[512,64]{0,1:T(8,128)(2,1)S(1)}, bf16[512,64]{0,1:T(8,128)(2,1)}, u32[]{:S(2)}) copy-start(bf16[512,64]{0,1:T(8,128)(2,1)} %copy-done.56) | copy-start | bytes 196612
  538.0 70.8 %collective-permute-start.4 = (bf16[2048,256]{1,0:T(8,128)(2,1)}, bf16[2048,256]{1,0:T(8,128)(2,1)}, u32[]{:S(2)}, u32[]{:S(2)}) collective-permute-start(bf16[2048,256]{1,0:T(8,128)(2,1)} %get-tuple-element.69), channel_id=1, source_target_pairs={{4,0},{8,4},{12,8},{5,1},{9,5},{13,9},{6,2},{10,6},{14,10},{7,3},{... | collective-permute-start | bytes 3145736 | tf_op jit(solution)/shard_map/ppermute | solution.py:980
  545.6 67.3 %copy-start.6 = (bf16[2048,128]{1,0:T(8,128)(2,1)S(1)}, bf16[2048,128]{1,0:T(8,128)(2,1)}, u32[]{:S(2)}) copy-start(bf16[2048,128]{1,0:T(8,128)(2,1)} %copy-done.5) | copy-start | bytes 1572868
  545.6 67.3 %copy-start.18 = (bf16[2048,1024]{1,0:T(8,128)(2,1)S(1)}, bf16[2048,1024]{1,0:T(8,128)(2,1)}, u32[]{:S(2)}) copy-start(bf16[2048,1024]{1,0:T(8,128)(2,1)} %copy-done.17) | copy-start | bytes 12582916
  550.0 64.9 %copy-start.13 = (bf16[4,128,1024]{2,1,0:T(8,128)(2,1)}, bf16[4,128,1024]{2,1,0:T(8,128)(2,1)S(1)}, u32[]{:S(2)}) copy-start(bf16[4,128,1024]{2,1,0:T(8,128)(2,1)S(1)} %get-tuple-element.72) | copy-start | bytes 3145732
  610.5 39.7 %collective-permute-start.5 = (bf16[2048,256]{1,0:T(8,128)(2,1)S(1)}, bf16[2048,256]{1,0:T(8,128)(2,1)S(1)}, u32[]{:S(2)}, u32[]{:S(2)}) collective-permute-start(bf16[2048,256]{1,0:T(8,128)(2,1)S(1)} %add_convert_fusion.3), channel_id=1, source_target_pairs={{4,0},{8,4},{12,8},{5,1},{9,5},{13,9},{6,2},{10,6},{14,10},{7,3},{... | collective-permute-start | bytes 3145736 | tf_op jit(solution)/shard_map/ppermute | solution.py:980
  614.9 35.3 %copy-start.41 = (f32[2048,256]{1,0:T(8,128)S(1)}, f32[2048,256]{1,0:T(8,128)}, u32[]{:S(2)}) copy-start(f32[2048,256]{1,0:T(8,128)} %get-tuple-element.67) | copy-start | bytes 6291460
  655.3 74.4 %collective-permute-start.6 = (bf16[512,1024]{1,0:T(8,128)(2,1)S(1)}, bf16[512,1024]{1,0:T(8,128)(2,1)}, u32[]{:S(2)}, u32[]{:S(2)}) collective-permute-start(bf16[512,1024]{1,0:T(8,128)(2,1)S(1)} %bitcast.227), channel_id=1, source_target_pairs={{0,2},{1,3},{2,0},{3,1},{4,6},{5,7},{6,4},{7,5},{8,10},{9,11},{10,... | collective-permute-start | bytes 3145736 | tf_op jit(solution)/shard_map/ppermute | solution.py:313
  718.4 11.3 %copy-start.25 = (f32[512,1024]{1,0:T(8,128)S(1)}, f32[512,1024]{1,0:T(8,128)}, u32[]{:S(2)}) copy-start(f32[512,1024]{1,0:T(8,128)} %copy-done.23) | copy-start | bytes 6291460
  826.5 9.6 %copy-start.42 = (f32[4,4,32,1024]{3,2,1,0:T(8,128)S(1)}, f32[4,4,32,1024]{3,2,1,0:T(8,128)}, u32[]{:S(2)}) copy-start(f32[4,4,32,1024]{3,2,1,0:T(8,128)} %get-tuple-element.76) | copy-start | bytes 6291460
  828.9 8.6 %copy-start.52 = (f32[32,118]{1,0:T(8,128)}, f32[32,118]{1,0:T(8,128)S(1)}, u32[]{:S(2)}) copy-start(f32[32,118]{1,0:T(8,128)S(1)} %slice_reduce_fusion) | copy-start | bytes 45316
  (47 other events, 179.9 us)
Sparse Core Ops, SparseCore 0:
  98.1 182.2 all-gather.2
  456.7 104.2 reduce-scatter.2
  565.1 122.2 reduce-scatter.4

commit v3 on v2

--- a/solution.py
+++ b/solution.py
@@ -60,6 +60,16 @@
     )
     came = came.reshape(levels, HEADS, count // levels // HEADS, -1)
     return came.transpose(1, 0, 2, 3).reshape(count, -1)
+
+
+def to_home(rows):
+    levels = lax.axis_size("level")
+    count = rows.shape[0]
+    out = rows.reshape(HEADS, levels, count // levels // HEADS, -1).transpose(1, 0, 2, 3)
+    back = lax.all_to_all(
+        out.reshape(levels, count // levels, -1), "level", split_axis=0, concat_axis=0, tiled=True
+    )
+    return back.reshape(count, -1)
 
 
 MESH = pl.DeviceIdType.MESH
@@ -482,10 +492,8 @@
 def finish_kernel(
     part,
     middle,
-    done,
     grads,
     home_grad,
-    home_out,
     owned,
     near_buf,
     send_buf,
@@ -497,7 +505,6 @@
     level_send,
     level_buf,
     head_send,
-    own_sem,
     *sems,
 ):
     sems = iter(sems)
@@ -528,7 +535,6 @@
     near_s, near_r = pair()
     far_s, far_r = pair()
     group_s, group_r = pair()
-    done_s, done_r = pair()
     back_s, back_r = pair()
     level_s, level_r = pair()
     mate_s, mate_r = pair()
@@ -559,12 +565,6 @@
                 for k, to in enumerate(groups_ahead)
             ]
         )
-    out_own = pltpu.make_async_copy(done.at[:, level], home_out.at[level], own_sem)
-    out_own.start()
-    homing = [
-        send(done.at[:, to], home_out.at[level], done_s.at[k], done_r.at[k], {"level": to})
-        for k, to in enumerate(levels_ahead)
-    ]
     for i in pieces:
         first[i].wait_recv()
         both = part[i, far].astype(jnp.float32) + near_buf[0, i].astype(jnp.float32)
@@ -607,32 +607,30 @@
     for k, source in enumerate(levels_behind):
         backs[k].wait_recv()
         home_grad[source] = came_buf[source].astype(jnp.float32)
-    for copy in homing + sharing:
+    for copy in sharing:
         copy.wait_recv()
     for copy in started:
         copy.wait_send()
-    out_own.wait()
-
-
-def finish(part, middle, done, grads):
+
+
+def finish(part, middle, grads):
     groups, levels = lax.axis_size("group"), lax.axis_size("level")
-    _, _, piece, width = done.shape
+    _, count, width = middle.shape
+    piece = count // levels
     low_type = jnp.bfloat16
-    count = levels * piece
     block = grads.shape[2:]
     dma = pltpu.SemaphoreType.DMA
     others = (levels - 1,)
-    counts = [(2, HEADS), (HEADS,), (groups - 1, levels), others, others, others, (HEADS - 1,)]
+    counts = [(2, HEADS), (HEADS,), (groups - 1, levels), others, others, (HEADS - 1,)]
     vmem = pl.BlockSpec(memory_space=pltpu.VMEM)
     return pl.pallas_call(
         finish_kernel,
         out_shape=[
             jax.ShapeDtypeStruct((levels, HEADS, piece, width), jnp.float32),
-            jax.ShapeDtypeStruct((levels, HEADS, piece, width), low_type),
             jax.ShapeDtypeStruct(block, low_type),
         ],
-        in_specs=[vmem] * 4,
-        out_specs=[vmem] * 3,
+        in_specs=[vmem] * 3,
+        out_specs=[vmem] * 2,
         scratch_shapes=[
             pltpu.VMEM((2, HEADS, count, width), low_type),
             pltpu.VMEM((HEADS, count, width), low_type),
@@ -644,7 +642,6 @@
             pltpu.VMEM((levels,) + block, low_type),
             pltpu.VMEM((levels - 1,) + block, low_type),
             pltpu.VMEM(block, low_type),
-            dma,
         ]
         + [dma(c) for c in counts for _ in range(2)],
         compiler_params=pltpu.CompilerParams(
@@ -652,7 +649,7 @@
         ),
         cost_estimate=cost(0, 200e6),
         name="finish",
-    )(part, middle, done, grads)
+    )(part, middle, grads)
 
 
 BLOCK = 512
@@ -817,8 +814,10 @@
     )(first, queries, *window, *window, grads, pos_q, start_q, lse, inner, pos_k)
 
 
-def front_kernel(local, head, hidden, grads, weights, gates, active, grad_pre, rows_out, acc):
-    groups, levels, _, depth, width = weights.shape
+def front_kernel(
+    local, head, hidden, grads, w_in, w_out, gates, active, grad_pre, rows_out, acc
+):
+    groups, levels, depth, width = w_in.shape
     tile = hidden.shape[0]
     model = groups * depth
     acc[...] = jnp.zeros_like(acc)
@@ -828,8 +827,8 @@
         grad_active = jnp.zeros((tile, width), jnp.float32)
         for group in range(groups):
             part = slice(group * depth, (group + 1) * depth)
-            pre_act += dot(hidden[:, part], weights[group, level, 0], 1, 0)
-            grad_active += dot(grads[:, part], weights[group, level, 1], 1, 0)
+            pre_act += dot(hidden[:, part], w_in[group, level], 1, 0)
+            grad_active += dot(grads[:, part], w_out[group, level], 1, 0)
         first = level * local
         gate = jnp.concatenate(
             [jnp.broadcast_to(gates[:, first + e : first + e + 1], (tile, FH)) for e in range(local)],
@@ -849,7 +848,7 @@
         grad_pre[:, columns] = low_pre
         for group in range(groups):
             part = slice(group * depth, (group + 1) * depth)
-            acc[:, part] += dot(low_pre, weights[group, level, 0], 1, 1)
+            acc[:, part] += dot(low_pre, w_in[group, level], 1, 1)
     rows_out[:, :model] = acc[...].astype(jnp.bfloat16)
     spare = rows_out.shape[1] - model
     lane = lax.broadcasted_iota(jnp.int32, (tile, spare), 1) - head[0] * (levels * local)
@@ -859,23 +858,23 @@
     rows_out[:, model:] = spread.astype(jnp.bfloat16)
 
 
-def ffn_front(head, hidden, grads, weights, gates, local):
+def ffn_front(head, hidden, grads, w_in, w_out, gates, local):
     rows, wide = hidden.shape
-    groups, levels, _, depth, width = weights.shape
+    groups, levels, depth, width = w_in.shape
     tile = 512
 
     def by_row(columns):
         return pl.BlockSpec((tile, columns), lambda i, *_: (i, 0))
 
+    whole = pl.BlockSpec(w_in.shape, lambda i, *_: (0, 0, 0, 0), pipeline_mode=pl.Buffered(1))
     grid_spec = pltpu.PrefetchScalarGridSpec(
         num_scalar_prefetch=1,
         grid=(rows // tile,),
         in_specs=[
             by_row(wide),
             by_row(groups * depth),
-            pl.BlockSpec(
-                weights.shape, lambda i, *_: (0, 0, 0, 0, 0), pipeline_mode=pl.Buffered(1)
-            ),
+            whole,
+            whole,
             by_row(gates.shape[1]),
         ],
         out_specs=[by_row(levels * width), by_row(levels * width), by_row(wide)],
@@ -889,7 +888,7 @@
         compiler_params=pltpu.CompilerParams(vmem_limit_bytes=58 * 2**20),
         cost_estimate=cost(6 * rows * groups * depth * levels * width, 3e7),
         name="ffn_front",
-    )(head, hidden, grads, weights, gates)
+    )(head, hidden, grads, w_in, w_out, gates)
 
 
 def rear_kernel(rows_in, hidden_units, weight_grads):
@@ -900,14 +899,171 @@
         weight_grads[group, 0] = dot(rows_in[:, part], units, 0, 0).astype(jnp.bfloat16)
 
 
-def feed_kernel(rows_in, low_pre, active, weights, weight_grads, feed, acc):
-    groups, _, _, depth, _ = weights.shape
+def normalized(rows, gain, bias):
+    values = rows.astype(jnp.float32)
+    centred = values - jnp.mean(values, axis=1, keepdims=True)
+    inverse = lax.rsqrt(jnp.mean(centred * centred, axis=1, keepdims=True) + 1e-05)
+    scaled = centred * inverse
+    return scaled, inverse, (scaled * gain + bias).astype(jnp.bfloat16)
+
+
+def project_kernel(
+    levels, rows, w_value, w_query, w_key, routers, gain, bias, order, tables,
+    query, key_value, projected, sigs, masks,
+):
+    count = rows.shape[0]
+    piece = count // (levels * HEADS)
+    _, _, normed = normalized(rows[...], gain[...], bias[...])
+    query[...] = dot(normed, w_query[...], 1, 0).astype(jnp.bfloat16)
+    key_value[:, :DH] = dot(normed, w_key[...], 1, 0).astype(jnp.bfloat16)
+    sig = 1.0 / (1.0 + jnp.exp2(-LOG2E * dot(normed, routers[...], 1, 0)))
+    sigs[...] = sig
+    product = dot(rows[...], w_value[...], 1, 0)
+    projected[...] = product
+    at = lax.broadcasted_iota(jnp.int32, (count, count), 0)
+    source = lax.rem(at // piece, levels) * HEADS + at // (piece * levels)
+    here = (source * piece + lax.rem(at, piece) == order[0]).astype(jnp.bfloat16)
+    lane = lax.broadcasted_iota(jnp.int32, (16, count), 0)
+    table = tables[0]
+    named = jnp.zeros((16, count), jnp.float32)
+    for which in range(2):
+        option = lane - which * VEXP
+        for slot in range(2):
+            pick = table[2 * which + slot : 2 * which + slot + 1, :]
+            hit = (option == pick) & (option >= 0) & (option < VEXP)
+            named = jnp.where(hit, 1.0, named)
+    mask = dot(here, named.astype(jnp.bfloat16), 1, 1)
+    masks[...] = mask
+    value = jnp.zeros((count, DH), jnp.float32)
+    for e in range(VEXP):
+        gate = sig[:, e : e + 1] * mask[:, e : e + 1]
+        value += gate * product[:, e * DH : (e + 1) * DH]
+    key_value[:, DH:] = value.astype(jnp.bfloat16)
+
+
+def project(rows, full, gain, bias, orders, tables, levels):
+    total, width = rows.shape
+    count = total // HEADS
+
+    def by_row(columns):
+        return pl.BlockSpec((count, columns), lambda i: (i, 0))
+
+    def column(size, at):
+        return pl.BlockSpec((width, size), lambda i: (0, at), pipeline_mode=pl.Buffered(1))
+
+    line = pl.BlockSpec((1, width), lambda i: (0, 0))
+    shapes = [(DH, jnp.bfloat16), (2 * DH, jnp.bfloat16), (VEXP * DH, jnp.float32)]
+    shapes += [(128, jnp.float32), (16, jnp.float32)]
+    return pl.pallas_call(
+        functools.partial(project_kernel, levels),
+        grid=(HEADS,),
+        in_specs=[by_row(width), column(VEXP * DH, 0)]
+        + [column(DH, 2 * VEXP + i) for i in range(3)]
+        + [line, line]
+        + [
+            pl.BlockSpec((1, 1, count), lambda i: (i, 0, 0)),
+            pl.BlockSpec((1,) + tables.shape[1:], lambda i: (i, 0, 0)),
+        ],
+        out_specs=[by_row(columns) for columns, _ in shapes],
+        out_shape=[jax.ShapeDtypeStruct((total, columns), kind) for columns, kind in shapes],
+        compiler_params=pltpu.CompilerParams(vmem_limit_bytes=48 * 2**20),
+        cost_estimate=cost(2 * total * width * 1024, 2e7),
+        name="project",
+    )(rows, full, full, full, full, gain, bias, orders, tables)
+
+
+def project_back_kernel(
+    rows, grads, grad_query, out_logit, projected, sigs, masks,
+    w_value, w_query, w_key, routers, gain, bias,
+    grad_rows, weight_grads, acc, sums,
+):
+    at = pl.program_id(0)
+    count = rows.shape[0]
+    values = VEXP * DH
+
+    @pl.when(at == 0)
+    def _():
+        acc[...] = jnp.zeros_like(acc)
+        sums[...] = jnp.zeros_like(sums)
+
+    scaled, inverse, normed = normalized(rows[...], gain[...], bias[...])
+    grad_key = grads[:, :DH].astype(jnp.bfloat16)
+    grad_value = grads[:, DH:]
+    sig, mask = sigs[...], masks[...]
+    lane = lax.broadcasted_iota(jnp.int32, (count, 128), 1)
+    logits = out_logit[...].astype(jnp.float32)
+    parts = []
+    for e in range(VEXP):
+        one, on = sig[:, e : e + 1], mask[:, e : e + 1]
+        parts.append((one * on * grad_value).astype(jnp.bfloat16))
+        inner = jnp.sum(grad_value * projected[:, e * DH : (e + 1) * DH], axis=1, keepdims=True)
+        logits = jnp.where(lane == e, inner * one * (1.0 - one) * on, logits)
+    grad_projected = jnp.concatenate(parts, axis=1)
+    sides = jnp.concatenate([grad_query[...], grad_key, logits.astype(jnp.bfloat16)], axis=1)
+    first = dot(sides[:, :DH], w_query[...], 1, 1)
+    first += dot(sides[:, DH : 2 * DH], w_key[...], 1, 1)
+    first += dot(sides[:, 2 * DH :], routers[...], 1, 1)
+    sums[2 * VEXP : 2 * VEXP + 1, :] += jnp.sum(first * scaled, axis=0, keepdims=True)
+    sums[2 * VEXP + 1 : 2 * VEXP + 2, :] += jnp.sum(first, axis=0, keepdims=True)
+    inner_grad = first * gain[...]
+    inner_grad = inverse * (
+        inner_grad
+        - jnp.mean(inner_grad, axis=1, keepdims=True)
+        - scaled * jnp.mean(inner_grad * scaled, axis=1, keepdims=True)
+    )
+    grad_rows[...] = (inner_grad + dot(grad_projected, w_value[...], 1, 1)).astype(jnp.bfloat16)
+    acc[:, :values] += dot(rows[...], grad_projected, 0, 0)
+    acc[:, values:] += dot(normed, sides, 0, 0)
+
+    @pl.when(at == pl.num_programs(0) - 1)
+    def _():
+        weight_grads[:, : values + 2 * DH] = acc[:, : values + 2 * DH].astype(jnp.bfloat16)
+        last = acc[:, values + 2 * DH :] + sums[...].T
+        weight_grads[:, values + 2 * DH :] = last.astype(jnp.bfloat16)
+
+
+def project_back(rows, grads, grad_query, out_logit, projected, sigs, masks, full, gain, bias):
+    total, width = rows.shape
+    count = total // HEADS
+    columns = VEXP * DH + 3 * DH
+
+    def by_row(size):
+        return pl.BlockSpec((count, size), lambda i: (i, 0))
+
+    def column(size, at):
+        return pl.BlockSpec((width, size), lambda i: (0, at), pipeline_mode=pl.Buffered(1))
+
+    line = pl.BlockSpec((1, width), lambda i: (0, 0))
+    return pl.pallas_call(
+        project_back_kernel,
+        grid=(HEADS,),
+        in_specs=[by_row(width), by_row(2 * DH), by_row(DH), by_row(128), by_row(VEXP * DH)]
+        + [by_row(128), by_row(16), column(VEXP * DH, 0)]
+        + [column(DH, 2 * VEXP + i) for i in range(3)]
+        + [line, line],
+        out_specs=[by_row(width), pl.BlockSpec((width, columns), lambda i: (0, 0))],
+        out_shape=[
+            jax.ShapeDtypeStruct((total, width), jnp.bfloat16),
+            jax.ShapeDtypeStruct((width, columns), jnp.bfloat16),
+        ],
+        scratch_shapes=[
+            pltpu.VMEM((width, columns), jnp.float32),
+            pltpu.VMEM((128, width), jnp.float32),
+        ],
+        compiler_params=pltpu.CompilerParams(vmem_limit_bytes=56 * 2**20),
+        cost_estimate=cost(4 * total * width * 1024, 4e7),
+        name="project_back",
+    )(rows, grads, grad_query, out_logit, projected, sigs, masks, full, full, full, full, gain, bias)
+
+
+def feed_kernel(rows_in, low_pre, active, w_out, weight_grads, feed, acc):
+    groups, _, depth, _ = w_out.shape
     level = pl.program_id(0)
     units, act = low_pre[...], active[...]
     for group in range(groups):
         part = slice(group * depth, (group + 1) * depth)
         weight_grads[group, 0] = dot(rows_in[:, part], units, 0, 0).astype(jnp.bfloat16)
-        fed = dot(act, weights[group, 0, 0], 1, 1)
+        fed = dot(act, w_out[group, 0], 1, 1)
 
         @pl.when(level == 0)
         def _():
@@ -926,9 +1082,9 @@
     return pl.BlockSpec((rows, columns), lambda i: (0, 0), pipeline_mode=pl.Buffered(1))
 
 
-def ffn_feed(hidden, grad_pre, active, weights):
+def ffn_feed(hidden, grad_pre, active, w_out):
     rows, wide = hidden.shape
-    groups, levels, _, depth, width = weights.shape
+    groups, levels, depth, width = w_out.shape
     by_level = pl.BlockSpec((rows, width), lambda i: (0, i))
     grads_spec = pl.BlockSpec((groups, 1, depth, width), lambda i: (0, i, 0, 0))
     return pl.pallas_call(
@@ -938,7 +1094,7 @@
             whole_rows(rows, wide),
             by_level,
             by_level,
-            pl.BlockSpec((groups, 1, 1, depth, width), lambda i: (0, i, 1, 0, 0)),
+            grads_spec,
         ],
         out_specs=[grads_spec, whole_rows(rows, groups * depth)],
         out_shape=[
@@ -949,7 +1105,7 @@
         compiler_params=pltpu.CompilerParams(vmem_limit_bytes=58 * 2**20),
         cost_estimate=cost(6 * rows * groups * depth * levels * width, 3e7),
         name="ffn_feed",
-    )(hidden, grad_pre, active, weights)
+    )(hidden, grad_pre, active, w_out)
 
 
 def ffn_rear(rows_in, units, groups, levels):
@@ -1026,10 +1182,10 @@
     pad = -(shared + 2 * VEXP) % 128
     packed = jnp.concatenate(
         [
+            value_weight.reshape(wrows, HEADS, VEXP * DH),
+            output_weight.reshape(wrows, HEADS, VEXP * DH),
             query_weight.reshape(wrows, HEADS, DH),
             key_weight.reshape(wrows, HEADS, DH),
-            value_weight.reshape(wrows, HEADS, VEXP * DH),
-            output_weight.reshape(wrows, HEADS, VEXP * DH),
             value_router.reshape(wrows, HEADS, VEXP),
             output_router.reshape(wrows, HEADS, VEXP),
             jnp.broadcast_to(small[:, None, :], (wrows, HEADS, shared)),
@@ -1053,35 +1209,43 @@
     own_tokens = lax.dynamic_index_in_dim(arrived, head, 1, keepdims=False).reshape(count, width)
     full = full.reshape(width, cols)
 
-    both = after(jnp.stack([ffn_in, ffn_out]), full)
-    both = lax.all_gather(both, ("group", "level"), axis=0)
-    both = both.reshape((groups, levels) + both.shape[1:])
-
     base = 2 * DH + 2 * VEXP * DH
-    w_query = full[:, :DH]
-    w_key = full[:, DH : 2 * DH]
-    w_value = full[:, 2 * DH : 2 * DH + VEXP * DH]
-    w_output = full[:, 2 * DH + VEXP * DH : base]
-    r_value = full[:, base : base + VEXP]
-    r_output = full[:, base + VEXP : base + 2 * VEXP]
+    w_output = full[:, VEXP * DH : 2 * VEXP * DH]
     at = base + 2 * VEXP
     r_ffn = full[:, at : at + experts]
     gain_one, bias_one, gain_two, bias_two = (
         full[:, at + experts + i].astype(jnp.float32) for i in range(4)
     )
-
-    own_grads = to_workers(after(out_grad, worker_in))
+    gain_row, bias_row = gain_one[None], bias_one[None]
+    orders = orders.reshape(levels, HEADS, count)
+    own_order = lax.dynamic_index_in_dim(orders, level, 0, keepdims=False)[:, None, :]
+    queries, key_value, projected, sigs, masks = project(
+        worker_in, full, gain_row, bias_row, own_order, tables, levels
+    )
+
+    rows = HEADS * count
+    reach = -(-LMAX // rows)
+    window = [key_value]
+    for _ in range(reach):
+        window.insert(0, shift(window[0], "level", 1))
+    own_grads = to_workers(after(out_grad, key_value))
+    cotangent = level_gather(own_grads, 5, True)
+
+    def gather_ffn(weight):
+        whole = lax.all_gather(weight, ("group", "level"), axis=0)
+        return whole.reshape((groups, levels) + weight.shape)
+
+    w_in = gather_ffn(ffn_in)
+    w_out = gather_ffn(after(ffn_out, window[0], cotangent))
 
     ramp = jnp.arange(count, dtype=jnp.int32)
-    rows = HEADS * count
 
     def arrival(values):
         lead, shape = values.shape[:-3], values.shape[-1:]
         four = values.reshape(lead + (HEADS, levels, HEADS, piece) + shape)
         return jnp.swapaxes(four, -4, -3).reshape(lead + (rows,) + shape)
 
-    reach = -(-LMAX // rows)
-    orders = orders.reshape(levels, HEADS, count)
+    orders = after(orders, key_value)
     orders = jnp.concatenate([jnp.zeros((reach, HEADS, count), jnp.int32), orders], axis=0)
     orders = lax.dynamic_slice_in_dim(orders, level, reach + 1, 0)
     here = orders[:, :, None, :] == ramp[None, None, :, None]
@@ -1091,32 +1255,8 @@
     pos_all = jnp.where(shard[:, :, None] < 0, -1, shard[:, :, None] * count + inverse)
     pos_all = arrival(pos_all[..., None]).reshape(-1)
     positions = pos_all[reach * rows :]
-    options = jnp.arange(VEXP, dtype=jnp.int32)[None, :, None]
-
-    def mask_of(which):
-        one, two = tables[:, which, None, :], tables[:, which + 1, None, :]
-        return (one == options).astype(jnp.bfloat16) + (two == options).astype(jnp.bfloat16)
-
-    masks = jnp.concatenate([mask_of(0), mask_of(2)], axis=1)
-    masks = jnp.einsum(
-        "ktr,ker->kte", low(here[reach]), masks, preferred_element_type=jnp.float32
-    )
-    masks = arrival(masks)
-    value_mask, out_mask = masks[:, :VEXP], masks[:, VEXP:]
     own_routes = picks.reshape(levels, -1, HEADS, piece).transpose(2, 0, 3, 1).reshape(count, -1)
 
-    normed, scaled_one, inverse_one = layer_norm(worker_in.astype(jnp.float32), gain_one, bias_one)
-    normed_one = low(normed)
-    queries = low(matmul(normed_one, w_query))
-    keys = low(matmul(normed_one, w_key))
-    projected = matmul(worker_in, w_value).reshape(rows, VEXP, DH)
-    value_sig = jax.nn.sigmoid(matmul(normed_one, r_value))
-    value_gate = value_sig * value_mask
-    values = low(jnp.sum(value_gate[..., None] * projected, axis=1))
-    span = (reach + 1) * rows
-    window = [jnp.concatenate([keys, values], axis=1)]
-    for _ in range(reach):
-        window.insert(0, shift(window[0], "level", 1))
     seq_ends = jnp.cumsum(seq_lengths[0])
 
     def starts_of(places):
@@ -1140,7 +1280,8 @@
         pos_all[:, None],
     )
 
-    out_sig = jax.nn.sigmoid(matmul(normed_one, r_output))
+    out_sig = sigs[:, VEXP : 2 * VEXP]
+    out_mask = masks[:, VEXP : 2 * VEXP]
     out_gate = out_sig * out_mask
     mixed = low((out_gate[..., None] * attended[:, None, :]).reshape(rows, VEXP * DH))
     branch = low(level_scatter(low(transposed(mixed, w_output)), 2))
@@ -1157,14 +1298,14 @@
     hidden = level_gather(jnp.pad(low(extended), ((0, 0), (0, spare))), 3, True)
     mine = levels * local_experts
     gates = lax.dynamic_slice_in_dim(hidden, width + head * mine, mine, 1).astype(jnp.float32)
-    cotangent = level_gather(own_grads, 5, True)
     active, grad_pre, grad_rows = ffn_front(
-        head[None], hidden, cotangent, both, gates, local_experts
+        head[None], hidden, cotangent, w_in, w_out, gates, local_experts
     )
     summed, beyond = pair_scatter(grad_rows, 4, True)
     came = to_far(beyond)
-    grad_in, feed = ffn_feed(after(hidden, beyond), grad_pre, active, both)
-    summed = summed + after(came, feed).astype(jnp.float32)
+    grad_in, feed = ffn_feed(after(hidden, beyond), grad_pre, active, w_out)
+    came, feed = lax.optimization_barrier((came, feed))
+    summed = summed + came.astype(jnp.float32)
 
     gate_grads = summed[:, width : width + experts].reshape(count, HEADS, levels, local_experts)
     gate_grads = jnp.swapaxes(gate_grads, 1, 2).reshape(count, experts)
@@ -1182,13 +1323,13 @@
     own_branch = low(grad_middle)
     came = to_far(own_branch)
     grad_out = ffn_rear(after(cotangent, own_branch), active, groups, levels)
-    grad_branch = pair_gather(own_branch, after(came, grad_out), 7)
-    grad_ffn = [
-        lax.psum_scatter(
-            g.reshape((groups * levels,) + g.shape[2:]), ("group", "level"), scatter_dimension=0
-        ).astype(jnp.float32)
-        for g in (grad_in, grad_out)
-    ]
+    came, grad_out = lax.optimization_barrier((came, grad_out))
+    grad_branch = pair_gather(own_branch, came, 7)
+
+    def sum_over_rows(grad):
+        return lax.psum_scatter(grad, ("group", "level"), scatter_dimension=0)
+
+    ffn_in_grad = sum_over_rows(grad_in.reshape((groups * levels,) + grad_in.shape[2:]))
     grad_mixed = matmul(grad_branch, w_output).reshape(rows, VEXP, DH)
     grad_out_gate = jnp.sum(grad_mixed * attended[:, None, :], axis=-1)
     grad_attended = low(jnp.sum(grad_mixed * out_gate[..., None], axis=1))
@@ -1208,71 +1349,79 @@
     came = shift(grad_window[0], "level", -1)
     fed, beyond = pair_scatter(after(feed, grad_queries), 6, True)
     grad_w_output = contract_rows(after(grad_branch, fed), mixed)
-    for i in range(1, reach + 1):
-        grad_both = grad_window[i].astype(jnp.float32) + came.astype(jnp.float32)
-        if i < reach:
-            came = shift(low(grad_both), "level", -1)
-    fed_far = to_far(after(beyond, grad_both))
-    done = low(middle + fed + fed_far.astype(jnp.float32))
-    grad_keys, grad_values = low(grad_both[:, :DH]), grad_both[:, DH:]
-    grad_projected = low((value_gate[..., None] * grad_values[:, None, :]).reshape(rows, VEXP * DH))
-    grad_value_gate = jnp.sum(grad_values[:, None, :] * projected, axis=-1)
-    grad_value_logit = low(grad_value_gate * value_sig * (1.0 - value_sig) * value_mask)
-    grad_first = (
-        transposed(grad_queries, w_query)
-        + transposed(grad_keys, w_key)
-        + transposed(grad_value_logit, r_value)
-        + transposed(grad_out_logit, r_output)
-    )
-    grad_inputs = norm_back(grad_first, gain_one, scaled_one, inverse_one) + transposed(
-        grad_projected, w_value
-    )
-    weight_grads = jnp.concatenate(
+    early = jnp.concatenate(
         [
             low(grad_w_output),
-            low(contract_rows(normed_one, grad_queries)),
-            low(contract_rows(normed_one, grad_keys)),
-            low(contract_rows(worker_in, grad_projected)),
-            low(contract_rows(normed_one, grad_value_logit)),
-            low(contract_rows(normed_one, grad_out_logit)),
             low(grad_r_ffn),
             low(grad_gain_two)[:, None],
             low(grad_bias_two)[:, None],
-            low(jnp.sum(grad_first * scaled_one, axis=0))[:, None],
-            low(jnp.sum(grad_first, axis=0))[:, None],
-            jnp.zeros((width, pad), jnp.bfloat16),
+            jnp.zeros((width, -(experts + 2) % 128), jnp.bfloat16),
         ],
         axis=1,
     )
-    input_grad, layer_out, owned = finish(
-        low(grad_inputs).reshape(HEADS, HEADS, levels * piece, width),
+    for i in range(1, reach + 1):
+        if i < reach:
+            came, fed = lax.optimization_barrier((came, fed))
+        else:
+            came, early = lax.optimization_barrier((came, early))
+        grad_both = grad_window[i].astype(jnp.float32) + came.astype(jnp.float32)
+        if i < reach:
+            grad_keys_sent = low(grad_both)
+            came = shift(grad_keys_sent, "level", -1)
+    fed_far = to_far(beyond)
+    ffn_out_grad = sum_over_rows(grad_out.reshape((groups * levels,) + grad_out.shape[2:]))
+    early = early.reshape(groups * levels, HEADS * wrows, -1)
+    early, ffn_in_grad = lax.optimization_barrier((early, ffn_in_grad))
+    early = sum_over_rows(early)
+    grad_inputs, late = project_back(
+        worker_in,
+        grad_both,
+        grad_queries,
+        jnp.pad(grad_out_logit, ((0, 0), (VEXP, 128 - 2 * VEXP))),
+        projected,
+        sigs,
+        masks,
+        full,
+        gain_row,
+        bias_row,
+    )
+
+    fed_far, grad_inputs = lax.optimization_barrier((fed_far, grad_inputs))
+    layer_out = to_home(low(middle + fed + fed_far.astype(jnp.float32)))
+
+    input_grad, owned = finish(
+        grad_inputs.reshape(HEADS, HEADS, levels * piece, width),
         grad_middle.reshape(HEADS, levels * piece, width),
-        done.reshape(HEADS, levels, piece, width),
-        weight_grads.reshape(groups, levels, HEADS, wrows, cols),
+        late.reshape(groups, levels, HEADS, wrows, -1),
     )
     owned = owned.astype(jnp.float32)
-
-    def columns(first, size):
-        return owned[:, :, first : first + size].transpose(1, 0, 2).reshape(wrows, HEADS * size)
-
-    at = VEXP * DH
-    common = jnp.sum(owned[:, :, base + 2 * VEXP :], axis=0)
+    early = lax.all_to_all(
+        early.reshape(HEADS, wrows, -1), "head", split_axis=0, concat_axis=0, tiled=True
+    ).astype(jnp.float32)
+
+    def columns(part, first, size):
+        return part[:, :, first : first + size].transpose(1, 0, 2).reshape(wrows, HEADS * size)
+
+    values = VEXP * DH
+    misc = values + 2 * DH
+    common = jnp.sum(early[:, :, values:], axis=0)
+    norms = jnp.sum(owned[:, :, misc + 2 * VEXP :], axis=0)
     return (
-        layer_out.reshape(count, width),
+        layer_out,
         input_grad.reshape(count, width),
-        common[:, experts + 2],
-        common[:, experts + 3],
+        norms[:, 0],
+        norms[:, 1],
         common[:, experts],
         common[:, experts + 1],
-        columns(at, DH),
-        columns(at + DH, DH),
-        columns(at + 2 * DH, VEXP * DH),
-        columns(0, VEXP * DH),
-        columns(base, VEXP),
-        columns(base + VEXP, VEXP),
+        columns(owned, values, DH),
+        columns(owned, values + DH, DH),
+        columns(owned, 0, values),
+        columns(early, 0, values),
+        columns(owned, misc, VEXP),
+        columns(owned, misc + VEXP, VEXP),
         common[:, :experts],
-        grad_ffn[0],
-        grad_ffn[1],
+        ffn_in_grad.astype(jnp.float32),
+        ffn_out_grad.astype(jnp.float32),
     )
 
 

time: 853 us -> 794 us (0.931)
  Pallas kernels: 384 us -> 493 us
  matrix products: 98 us -> 21.2 us
  waiting for transfers between devices: 169 us -> 120 us
  local copies, waits for them, and re-layouts: 90.6 us -> 57.8 us
  other arithmetic: 53.4 us -> 36.7 us
    ppermute x4, waiting for transfers between devices: 143 us -> 68.7 us  [shift(): return lax.ppermute(value, axis, pairs)]
    pallas_call x1, Pallas kernels: 77.5 us -> 125 us  [start(): pl.pallas_call(start_kernel, out_shape=shapes, in_specs=[pl.BlockSpec(mem...]
    dot_general x7 -> x2, matrix products: 51.4 us -> 8.25 us  [transposed(): lax.dot_general(left_side, right_side, (((1,), (1,)), ((), ())), preferre...]
    reduce_scatter x2 -> x3, waiting for transfers between devices: 0.01 us -> 39.8 us  [sum_over_rows(): return lax.psum_scatter(grad, ('group', 'level'), scatter_dimension=0)]
    pallas_call x0 -> x2, Pallas kernels: none -> 37.5 us  [the longest x1 23.2 us: project_back(): pl.pallas_call(project_back_kernel, grid=(HEADS,), in_specs=[by_row(width...]
    pallas_call x1, Pallas kernels: 91.1 us -> 109 us  [finish(): pl.pallas_call(finish_kernel, out_shape=[jax.ShapeDtypeStruct((levels, HE...]
    unnamed x149 -> x105, local copies, waits for them, and re-layouts: 28.7 us -> 11.9 us
    dot_general x7 -> x2, matrix products: 25.2 us -> 8.71 us  [matmul(): return jnp.dot(left_side, right_side, preferred_element_type=jnp.float32)]
  transfers between devices with their start and end apart: 11 -> 15, of which waited for: 6 -> 5; matrix products, arithmetic and copies ran while one was open for 24% -> 13% of each run, Pallas kernels for 31% -> 58%
where the time goes in v3:
time: 794 us; the launch traced here: 785 us
  Pallas kernels  493 us (62%)
  waiting for transfers between devices  120 us (15%)
  local copies, waits for them, and re-layouts  57.8 us (7%)
  starting transfers between devices  40.4 us (5%)
  other arithmetic  36.7 us (5%)
  matrix products  21.2 us (3%)
  between operations  15 us (2%)
    pallas_call x1, Pallas kernels, start(): pl.pallas_call(start_kernel, out_shape=shapes, in_specs=[pl.BlockSpec(mem...  125 us
    pallas_call x1, Pallas kernels, finish(): pl.pallas_call(finish_kernel, out_shape=[jax.ShapeDtypeStruct((levels, HE...  109 us
    ppermute x4, waiting for transfers between devices, shift(): return lax.ppermute(value, axis, pairs)  68.7 us
    pallas_call x2, Pallas kernels, level_gather(): pl.pallas_call(functools.partial(gather_kernel, by_source), out_shape=jax...  61.6 us
    reduce_scatter x3, waiting for transfers between devices, sum_over_rows(): return lax.psum_scatter(grad, ('group', 'level'), scatter_dimension=0)  39.8 us
    pallas_call x1, Pallas kernels, ffn_front(): pl.pallas_call(functools.partial(front_kernel, local), grid_spec=grid_spe...  35.8 us
    pallas_call x1, Pallas kernels, ffn_feed(): pl.pallas_call(feed_kernel, grid=(levels,), in_specs=[whole_rows(rows, wi...  29.1 us
    pallas_call x1, Pallas kernels, level_scatter(): pl.pallas_call(functools.partial(scatter_kernel, by_source), out_shape=ja...  27.3 us
  transfers between devices with their start and end apart: 15, of which 5 were waited for; matrix products, arithmetic and copies ran while one was open for 13% of the time, Pallas kernels for 58%

profile of v3, /device:TPU:8, one launch (start us, length us, event | category | flops | bytes accessed | tf_op | source)
XLA Modules:
  0.0 784.8 jit_solution(10262643351266189515)
XLA Ops:
  17.4 125.4 %start.1 = (bf16[4,4,4,32,1024]{4,3,2,1,0:T(8,128)(2,1)}, bf16[2,4,4,32,1664]{4,3,2,1,0:T(8,128)(2,1)}, s32[4,4,512]{2,1,0:T(4,128)}, s32[4,16,128]{2,1,0:T(8,128)}, s32[4,4,1,512]{3,2,1,0:T(1,128)}) custom-call(bf16[4,4,32,1024]{3,2,1,0:T(8,128)(2,1)} %bitcast.224, bf16[4,32,1664]{2,1,0:T(8,128)(2,1)} %bitcast.222, s32[4,4,512]{2,1,0:T(4,128)} %pad_add_fusion.tables, ...), custom_call_target="tpu_custom_call" | custom-call | bytes 200000000 | tf_op jit(solution)/shard_map/start/pallas_call | solution.py:480
  146.4 14.3 %project.1 = (bf16[2048,128]{1,0:T(8,128)(2,1)S(1)}, bf16[2048,256]{1,0:T(8,128)(2,1)S(1)}, f32[2048,640]{1,0:T(8,128)}, f32[2048,128]{1,0:T(8,128)S(1)}, f32[2048,16]{1,0:T(8,128)S(1)}) custom-call(bf16[2048,1024]{1,0:T(8,128)(2,1)} %bitcast.198, bf16[1024,1664]{1,0:T(8,128)(2,1)} %bitcast.184, bf16[1024,1664]{1,0:T(8,128)(2,1)} %bitcast.185, ...), custom_call_target="tpu_custom_call" | custom-call | flops 4294967296 | bytes 20000000 | tf_op jit(solution)/shard_map/project/pallas_call | solution.py:957
  163.6 9.8 %all-to-all-start = ((bf16[4,128,1024]{2,1,0:T(8,128)(2,1)}), bf16[4,128,1024]{2,1,0:T(8,128)(2,1)}, u32[]{:S(2)}, u32[]{:S(2)}) async-start(bf16[4,128,1024]{2,1,0:T(8,128)(2,1)} %bitcast.225), calls=%async_computation | async-start | bytes 2097152 | tf_op jit(solution)/shard_map/all_to_all | solution.py:58
  173.4 16.3 %collective-permute-done.refs_1_.refs_4_ = bf16[2048,256]{1,0:T(8,128)(2,1)} collective-permute-done((bf16[2048,256]{1,0:T(8,128)(2,1)S(1)}, bf16[2048,256]{1,0:T(8,128)(2,1)}, u32[]{:S(2)}, u32[]{:S(2)}) %collective-permute-start) | collective-permute-done | bytes 1048608 | tf_op jit(solution)/shard_map/ppermute | solution.py:1136
  189.7 12.7 %collective-permute-start.1 = (bf16[2048,256]{1,0:T(8,128)(2,1)}, bf16[2048,256]{1,0:T(8,128)(2,1)}, u32[]{:S(2)}, u32[]{:S(2)}) collective-permute-start(bf16[2048,256]{1,0:T(8,128)(2,1)} %collective-permute-done.refs_1_.refs_4_), channel_id=1, source_target_pairs={{0,4},{4,8},{8,12},{1,5},{5,9},{9,13},{2,6},{6,10},{10,14},{3,7},{... | collective-permute-start | bytes 3145736 | tf_op jit(solution)/shard_map/ppermute | solution.py:1136
  204.8 5.0 broadcast_in_dim_reshape_reshape.5.refs_8_.refs_11_
  212.2 30.6 %level_gather.3 = bf16[4,4,128,1024]{3,2,1,0:T(8,128)(2,1)} custom-call(bf16[4,128,1024]{2,1,0:T(8,128)(2,1)} %bitcast.209), custom_call_target="tpu_custom_call" | custom-call | bytes 90000000 | tf_op jit(solution)/shard_map/level_gather/pallas_call | solution.py:141
  250.0 2.9 dynamic-slice_convert_fusion
  253.0 2.9 copy.246
  255.9 16.2 %attend.1 = (f32[2048,128]{1,0:T(8,128)S(1)}, f32[4,1,512]{2,1,0:T(1,128)S(1)}) custom-call(s32[4]{0:T(128)S(1)} %subtract_maximum_fusion.first, bf16[2048,128]{1,0:T(8,128)(2,1)S(1)} %copy-done.15, bf16[2048,256]{1,0:T(8,128)(2,1)} %collective-permute-done.1.refs_0_.refs_3_, bf16[2048,256]{1,0:T(8,128)(2,1)} %collective-permute-done.refs_1_.refs_4_, ...), custom_call_target="tpu_custom_call" | custom-call | flops 20000000000 | bytes 10000000 | tf_op jit(solution)/shard_map/attend/pallas_call | solution.py:722
  273.0 6.0 convolution_convert_fusion
  279.0 27.3 %level_scatter.1 = f32[4,128,1024]{2,1,0:T(8,128)S(1)} custom-call(bf16[4,4,128,1024]{3,2,1,0:T(8,128)(2,1)S(1)} %bitcast.172), custom_call_target="tpu_custom_call" | custom-call | bytes 80000000 | tf_op jit(solution)/shard_map/level_scatter/pallas_call | solution.py:203
  309.9 3.1 fusion.17
  317.9 31.0 %level_gather.2 = bf16[4,4,128,1152]{3,2,1,0:T(8,128)(2,1)} custom-call(bf16[4,128,1152]{2,1,0:T(8,128)(2,1)} %bitcast.206), custom_call_target="tpu_custom_call" | custom-call | bytes 90000000 | tf_op jit(solution)/shard_map/level_gather/pallas_call | solution.py:141
  351.1 35.8 %ffn_front.1 = (bf16[2048,2048]{1,0:T(8,128)(2,1)}, bf16[2048,2048]{1,0:T(8,128)(2,1)}, bf16[2048,1152]{1,0:T(8,128)(2,1)}) custom-call(s32[1]{0:T(128)} %bitcast.24.head, bf16[2048,1152]{1,0:T(8,128)(2,1)} %bitcast.204, bf16[2048,1024]{1,0:T(8,128)(2,1)} %bitcast.207, bf16[2,4,512,512]{3,2,1,0:T(8,128)(2,1)} %bitcast.248, ...), custom_call_target="tpu_custom_call" | custom-call | flops 25769803776 | bytes 30000000 | tf_op jit(solution)/shard_map/ffn_front/pallas_call | solution.py:884
  389.2 5.7 pair_scatter.2
  395.9 29.1 %ffn_feed.1 = (bf16[2,4,512,512]{3,2,1,0:T(8,128)(2,1)}, bf16[2048,1024]{1,0:T(8,128)(2,1)}) custom-call(bf16[2048,1152]{1,0:T(8,128)(2,1)} %bitcast.205, bf16[2048,2048]{1,0:T(8,128)(2,1)} %get-tuple-element.80.low_pre, bf16[2048,2048]{1,0:T(8,128)(2,1)} %get-tuple-element.81.active.hidden_units, bf16[2,4,512,512]{3,2,1,0:T(8,128)(2,1)} %bitcast.250), custom_call_target="tpu_custom_call" | custom-call | flops 25769803776 | bytes 30000000 | tf_op jit(solution)/shard_map/ffn_feed/pallas_call | solution.py:1090
  436.7 13.5 %ffn_rear.1 = bf16[2,4,512,512]{3,2,1,0:T(8,128)(2,1)} custom-call(bf16[2048,1024]{1,0:T(8,128)(2,1)} %bitcast.208, bf16[2048,2048]{1,0:T(8,128)(2,1)} %get-tuple-element.81.active.hidden_units), custom_call_target="tpu_custom_call" | custom-call | flops 17179869184 | bytes 30000000 | tf_op jit(solution)/shard_map/ffn_rear/pallas_call | solution.py:1115
  450.2 10.5 %collective-permute-done.3 = bf16[512,1024]{1,0:T(8,128)(2,1)S(1)} collective-permute-done((bf16[512,1024]{1,0:T(8,128)(2,1)S(1)}, bf16[512,1024]{1,0:T(8,128)(2,1)S(1)}, u32[]{:S(2)}, u32[]{:S(2)}) %collective-permute-start.3) | collective-permute-done | bytes 1048608 | tf_op jit(solution)/shard_map/ppermute | solution.py:323
  461.7 6.2 pair_gather.1
  468.0 6.6 multiply_reduce_fusion
  476.3 21.7 %attend_back.1 = (bf16[2048,128]{1,0:T(8,128)(2,1)S(1)}, bf16[2048,256]{1,0:T(8,128)(2,1)S(1)}, bf16[2048,256]{1,0:T(8,128)(2,1)S(1)}, f32[2048,256]{1,0:T(8,128)}) custom-call(s32[4]{0:T(128)S(1)} %subtract_maximum_fusion.first, bf16[2048,128]{1,0:T(8,128)(2,1)S(1)} %copy-done.16, bf16[2048,256]{1,0:T(8,128)(2,1)} %collective-permute-done.1.refs_0_.refs_3_, ...), custom_call_target="tpu_custom_call" | custom-call | flops 20000000000 | bytes 10000000 | tf_op jit(solution)/shard_map/attend_back/pallas_call | solution.py:806
  500.0 4.4 pair_scatter.3
  504.4 37.3 %collective-permute-done.4 = bf16[2048,256]{1,0:T(8,128)(2,1)S(1)} collective-permute-done((bf16[2048,256]{1,0:T(8,128)(2,1)S(1)}, bf16[2048,256]{1,0:T(8,128)(2,1)S(1)}, u32[]{:S(2)}, u32[]{:S(2)}) %collective-permute-start.4) | collective-permute-done | bytes 1048608 | tf_op jit(solution)/shard_map/ppermute | solution.py:1136
  545.8 4.0 convolution_convert_fusion.1
  549.8 5.2 concatenate.24
  555.0 15.1 %collective-permute-done.6 = bf16[2048,256]{1,0:T(8,128)(2,1)} collective-permute-done((bf16[2048,256]{1,0:T(8,128)(2,1)}, bf16[2048,256]{1,0:T(8,128)(2,1)}, u32[]{:S(2)}, u32[]{:S(2)}) %collective-permute-start.6) | collective-permute-done | bytes 1048608 | tf_op jit(solution)/shard_map/ppermute | solution.py:1136
  584.3 23.2 %project_back.1 = (bf16[2048,1024]{1,0:T(8,128)(2,1)}, bf16[1024,1024]{1,0:T(8,128)(2,1)}) custom-call(bf16[2048,1024]{1,0:T(8,128)(2,1)} %bitcast.199, f32[2048,256]{1,0:T(8,128)} %convert_add_fusion.grads, bf16[2048,128]{1,0:T(8,128)(2,1)} %copy-done.17, bf16[2048,128]{1,0:T(8,128)(2,1)} %pad.10.out_logit, f32[2048,640]{1,0:T(8,128)} %get-tuple-element.99.projected, ...), custom_call_target="tpu_custom_call" | custom-call | flops 8589934592 | bytes 40000000 | tf_op jit(solution)/shard_map/project_back/pallas_call | solution.py:1037
  609.2 4.2 all-to-all-start.1
  613.4 108.9 %finish.1 = (f32[4,4,32,1024]{3,2,1,0:T(8,128)}, bf16[4,32,1024]{2,1,0:T(8,128)(2,1)}) custom-call(bf16[4,4,128,1024]{3,2,1,0:T(8,128)(2,1)} %bitcast.214, f32[4,128,1024]{2,1,0:T(8,128)} %bitcast.200, bf16[2,4,4,32,1024]{4,3,2,1,0:T(8,128)(2,1)} %bitcast.221), custom_call_target="tpu_custom_call" | custom-call | bytes 200000000 | tf_op jit(solution)/shard_map/finish/pallas_call | solution.py:626
  728.9 3.4 all-to-all-start.2
  732.2 39.8 %reduce-scatter.8.cloned.1.call-done = bf16[1,512,512]{2,1,0:T(8,128)(2,1)} async-done(((bf16[8,512,512]{2,1,0:T(8,128)(2,1)}), bf16[1,512,512]{2,1,0:T(8,128)(2,1)}) %reduce-scatter.8.cloned.1.call-update) | async-done | bytes 524304 | tf_op jit(solution)/shard_map/reduce_scatter | solution.py:1330
  (234 shorter events, 91.6 us)
Async XLA Ops:
  7.2 9.6 %copy-start.45 = (s32[512,16]{0,1:T(8,128)S(1)}, s32[512,16]{0,1:T(8,128)}, u32[]{:S(2)}) copy-start(s32[512,16]{0,1:T(8,128)} %param.26) | copy-start | bytes 98308
  7.2 343.9 %all-gather.5.cloned.1.call-start = ((), (), s32[]{:S(2)}) async-start(), calls=%async_computation.9 | async-start | bytes 4718592 | tf_op jit(solution)/shard_map/all_gather | solution.py:1235
  145.6 15.1 %copy-start.11 = (f32[1024]{0:T(1024)}, f32[1024]{0:T(1024)S(1)}, u32[]{:S(2)}) copy-start(f32[1024]{0:T(1024)S(1)} %get-tuple-element.117) | copy-start | bytes 12292
  145.6 15.0 %copy-start.12 = (f32[1024]{0:T(1024)}, f32[1024]{0:T(1024)S(1)}, u32[]{:S(2)}) copy-start(f32[1024]{0:T(1024)S(1)} %get-tuple-element.118) | copy-start | bytes 12292
  161.5 81.6 %copy-start.3 = (f32[2048,128]{1,0:T(8,128)}, f32[2048,128]{1,0:T(8,128)S(1)}, u32[]{:S(2)}) copy-start(f32[2048,128]{1,0:T(8,128)S(1)} %get-tuple-element.67.sigs) | copy-start | bytes 3145732
  161.5 81.6 %copy-start.5 = (f32[2048,16]{1,0:T(8,128)}, f32[2048,16]{1,0:T(8,128)S(1)}, u32[]{:S(2)}) copy-start(f32[2048,16]{1,0:T(8,128)S(1)} %get-tuple-element.68.masks) | copy-start | bytes 393220
  161.5 94.4 %copy-start.13 = (bf16[2048,256]{1,0:T(8,128)(2,1)}, bf16[2048,256]{1,0:T(8,128)(2,1)S(1)}, u32[]{:S(2)}) copy-start(bf16[2048,256]{1,0:T(8,128)(2,1)S(1)} %get-tuple-element.70.refs_2_.refs_5_) | copy-start | bytes 3145732
  161.5 11.9 %copy-start.43 = (s32[4,4,1,512]{3,2,1,0:T(1,128)S(1)}, s32[4,4,1,512]{3,2,1,0:T(1,128)}, u32[]{:S(2)}) copy-start(s32[4,4,1,512]{3,2,1,0:T(1,128)} %get-tuple-element.65) | copy-start | bytes 98308
  161.5 43.2 %copy-start.48 = (s32[1,3]{1,0:T(1,128)S(1)}, s32[1,3]{1,0:T(1,128)}, u32[]{:S(2)}) copy-start(s32[1,3]{1,0:T(1,128)} %param.23) | copy-start | bytes 40
  161.5 28.2 %collective-permute-start = (bf16[2048,256]{1,0:T(8,128)(2,1)S(1)}, bf16[2048,256]{1,0:T(8,128)(2,1)}, u32[]{:S(2)}, u32[]{:S(2)}) collective-permute-start(bf16[2048,256]{1,0:T(8,128)(2,1)S(1)} %get-tuple-element.70.refs_2_.refs_5_), channel_id=1, source_target_pairs={{0,4},{4,8},{8,12},{1,5},{5,9},{9,13},{2,6},{6,10},{10,14},{3,7},{... | collective-permute-start | bytes 3145736 | tf_op jit(solution)/shard_map/ppermute | solution.py:1136
  163.6 46.3 %all-to-all-start = ((bf16[4,128,1024]{2,1,0:T(8,128)(2,1)}), bf16[4,128,1024]{2,1,0:T(8,128)(2,1)}, u32[]{:S(2)}, u32[]{:S(2)}) async-start(bf16[4,128,1024]{2,1,0:T(8,128)(2,1)} %bitcast.225), calls=%async_computation | async-start | bytes 2097152 | tf_op jit(solution)/shard_map/all_to_all | solution.py:58
  173.4 177.8 %all-gather.7.cloned.1.call-start = ((), (), s32[]{:S(2)}) async-start(), calls=%async_computation.10 | async-start | bytes 4718592 | tf_op jit(solution)/shard_map/all_gather | solution.py:1235
  189.7 53.1 %collective-permute-start.1 = (bf16[2048,256]{1,0:T(8,128)(2,1)}, bf16[2048,256]{1,0:T(8,128)(2,1)}, u32[]{:S(2)}, u32[]{:S(2)}) collective-permute-start(bf16[2048,256]{1,0:T(8,128)(2,1)} %collective-permute-done.refs_1_.refs_4_), channel_id=1, source_target_pairs={{0,4},{4,8},{8,12},{1,5},{5,9},{9,13},{2,6},{6,10},{10,14},{3,7},{... | collective-permute-start | bytes 3145736 | tf_op jit(solution)/shard_map/ppermute | solution.py:1136
  242.8 328.9 %reduce-scatter.4.cloned.1.call-start = ((), (), s32[]{:S(2)}) async-start(), calls=%async_computation.6 | async-start | bytes 4718592 | tf_op jit(solution)/shard_map/reduce_scatter | solution.py:1330
  250.0 63.3 %copy-start.36 = (f32[512,64]{0,1:T(8,128)}, f32[512,64]{0,1:T(8,128)S(1)}, u32[]{:S(2)}) copy-start(f32[512,64]{0,1:T(8,128)S(1)} %convert_reduce_fusion) | copy-start | bytes 393220
  395.0 30.1 %collective-permute-start.2 = (bf16[512,1152]{1,0:T(8,128)(2,1)}, bf16[512,1152]{1,0:T(8,128)(2,1)}, u32[]{:S(2)}, u32[]{:S(2)}) collective-permute-start(bf16[512,1152]{1,0:T(8,128)(2,1)} %bitcast.38), channel_id=1, source_target_pairs={{0,2},{1,3},{2,0},{3,1},{4,6},{5,7},{6,4},{7,5},{8,10},{9,11},{10,... | collective-permute-start | bytes 3538952 | tf_op jit(solution)/shard_map/ppermute | solution.py:323
  425.0 303.9 %reduce-scatter.6.cloned.1.call-start = ((), (), s32[]{:S(2)}) async-start(), calls=%async_computation.7 | async-start | bytes 1769472 | tf_op jit(solution)/shard_map/reduce_scatter | solution.py:1330
  435.5 14.7 %copy-start.30 = (bf16[512,1024]{1,0:T(8,128)(2,1)}, bf16[512,1024]{1,0:T(8,128)(2,1)S(1)}, u32[]{:S(2)}) copy-start(bf16[512,1024]{1,0:T(8,128)(2,1)S(1)} %get-tuple-element.125) | copy-start | bytes 3145732
  435.5 25.2 %collective-permute-start.3 = (bf16[512,1024]{1,0:T(8,128)(2,1)S(1)}, bf16[512,1024]{1,0:T(8,128)(2,1)S(1)}, u32[]{:S(2)}, u32[]{:S(2)}) collective-permute-start(bf16[512,1024]{1,0:T(8,128)(2,1)S(1)} %get-tuple-element.125), channel_id=1, source_target_pairs={{0,2},{1,3},{2,0},{3,1},{4,6},{5,7},{6,4},{7,5},{8,10},{9,11},{10,... | collective-permute-start | bytes 3145736 | tf_op jit(solution)/shard_map/ppermute | solution.py:323
  476.3 23.6 %copy-start.7 = (bf16[2048,1024]{1,0:T(8,128)(2,1)S(1)}, bf16[2048,1024]{1,0:T(8,128)(2,1)}, u32[]{:S(2)}) copy-start(bf16[2048,1024]{1,0:T(8,128)(2,1)} %get-tuple-element.90) | copy-start | bytes 12582916
  498.0 43.7 %collective-permute-start.4 = (bf16[2048,256]{1,0:T(8,128)(2,1)S(1)}, bf16[2048,256]{1,0:T(8,128)(2,1)S(1)}, u32[]{:S(2)}, u32[]{:S(2)}) collective-permute-start(bf16[2048,256]{1,0:T(8,128)(2,1)S(1)} %get-tuple-element.87), channel_id=1, source_target_pairs={{4,0},{8,4},{12,8},{5,1},{9,5},{13,9},{6,2},{10,6},{14,10},{7,3},{... | collective-permute-start | bytes 3145736 | tf_op jit(solution)/shard_map/ppermute | solution.py:1136
  500.0 45.8 %copy-start.29 = (bf16[4,4,128,1024]{3,2,1,0:T(8,128)(2,1)S(1)}, bf16[4,4,128,1024]{3,2,1,0:T(8,128)(2,1)}, u32[]{:S(2)}) copy-start(bf16[4,4,128,1024]{3,2,1,0:T(8,128)(2,1)} %pair_gather.1) | copy-start | bytes 12582916
  504.4 41.3 %copy-start.8 = (f32[4,128,1024]{2,1,0:T(8,128)}, f32[4,128,1024]{2,1,0:T(8,128)S(1)}, u32[]{:S(2)}) copy-start(f32[4,128,1024]{2,1,0:T(8,128)S(1)} %get-tuple-element.91) | copy-start | bytes 6291460
  504.4 41.0 %copy-start.22 = (bf16[512,1024]{1,0:T(8,128)(2,1)S(1)}, bf16[512,1024]{1,0:T(8,128)(2,1)}, u32[]{:S(2)}) copy-start(bf16[512,1024]{1,0:T(8,128)(2,1)} %copy-done.21) | copy-start | bytes 3145732
  504.4 41.0 %copy-start.40 = (bf16[512,64]{0,1:T(8,128)(2,1)S(1)}, bf16[512,64]{0,1:T(8,128)(2,1)}, u32[]{:S(2)}) copy-start(bf16[512,64]{0,1:T(8,128)(2,1)} %copy-done.39) | copy-start | bytes 196612
  542.9 27.2 %collective-permute-start.6 = (bf16[2048,256]{1,0:T(8,128)(2,1)}, bf16[2048,256]{1,0:T(8,128)(2,1)}, u32[]{:S(2)}, u32[]{:S(2)}) collective-permute-start(bf16[2048,256]{1,0:T(8,128)(2,1)} %add_convert_fusion.1), channel_id=1, source_target_pairs={{4,0},{8,4},{12,8},{5,1},{9,5},{13,9},{6,2},{10,6},{14,10},{7,3},{... | collective-permute-start | bytes 3145736 | tf_op jit(solution)/shard_map/ppermute | solution.py:1136
  574.6 197.4 %reduce-scatter.8.cloned.1.call-start = ((), (), s32[]{:S(2)}) async-start(), calls=%async_computation.8 | async-start | bytes 4718592 | tf_op jit(solution)/shard_map/reduce_scatter | solution.py:1330
  579.9 27.6 %collective-permute-start.5 = (bf16[512,1024]{1,0:T(8,128)(2,1)S(1)}, bf16[512,1024]{1,0:T(8,128)(2,1)S(1)}, u32[]{:S(2)}, u32[]{:S(2)}) collective-permute-start(bf16[512,1024]{1,0:T(8,128)(2,1)S(1)} %bitcast.182), channel_id=1, source_target_pairs={{0,2},{1,3},{2,0},{3,1},{4,6},{5,7},{6,4},{7,5},{8,10},{9,11},{10,... | collective-permute-start | bytes 3145736 | tf_op jit(solution)/shard_map/ppermute | solution.py:323
  584.3 23.3 %copy-start.9 = (f32[4,128,1024]{2,1,0:T(8,128)S(1)}, f32[4,128,1024]{2,1,0:T(8,128)}, u32[]{:S(2)}) copy-start(f32[4,128,1024]{2,1,0:T(8,128)} %copy-done.8) | copy-start | bytes 6291460
  584.3 23.3 %copy-start.20 = (f32[512,1024]{1,0:T(8,128)S(1)}, f32[512,1024]{1,0:T(8,128)}, u32[]{:S(2)}) copy-start(f32[512,1024]{1,0:T(8,128)} %copy-done.18) | copy-start | bytes 6291460
  609.2 118.6 %all-to-all-start.1 = ((bf16[4,128,1024]{2,1,0:T(8,128)(2,1)}), bf16[4,128,1024]{2,1,0:T(8,128)(2,1)S(1)}, u32[]{:S(2)}, u32[]{:S(2)}) async-start(bf16[4,128,1024]{2,1,0:T(8,128)(2,1)} %bitcast.52), calls=%async_computation.1 | async-start | bytes 2097152 | tf_op jit(solution)/shard_map/all_to_all | solution.py:69
  728.9 45.3 %all-to-all-start.2 = ((bf16[4,32,768]{2,1,0:T(8,128)(2,1)}), bf16[4,32,768]{2,1,0:T(8,128)(2,1)S(1)}, u32[]{:S(2)}, u32[]{:S(2)}) async-start(bf16[4,32,768]{2,1,0:T(8,128)(2,1)} %bitcast.233), calls=%async_computation.4 | async-start | bytes 393216 | tf_op jit(solution)/shard_map/all_to_all | solution.py:1398
  (32 other events, 115.7 us)
Sparse Core Ops, SparseCore 0:
  10.2 125.5 all-gather.4
  242.9 72.9 all-gather.6
  425.1 101.7 reduce-scatter.3
  574.8 82.7 reduce-scatter.5
  661.1 110.9 reduce-scatter.7

commit v4 on v3

--- a/solution.py
+++ b/solution.py
@@ -50,16 +50,6 @@
         - jnp.mean(inner_grad, axis=-1, keepdims=True)
         - scaled * jnp.mean(inner_grad * scaled, axis=-1, keepdims=True)
     )
-
-
-def to_workers(rows):
-    levels = lax.axis_size("level")
-    count = rows.shape[0]
-    came = lax.all_to_all(
-        rows.reshape(levels, count // levels, -1), "level", split_axis=0, concat_axis=0, tiled=True
-    )
-    came = came.reshape(levels, HEADS, count // levels // HEADS, -1)
-    return came.transpose(1, 0, 2, 3).reshape(count, -1)
 
 
 def to_home(rows):
@@ -348,7 +338,8 @@
 
 
 def start_kernel(
-    tokens, weights, tables, picks, order, rows, full, routes, chosen_rows, orders, own_sem, *sems
+    tokens, cotangents, weights, tables, picks, order,
+    rows, grads, full, routes, chosen_rows, orders, own_sem, *sems
 ):
     sems = iter(sems)
 
@@ -397,6 +388,7 @@
         (tables.at[head], routes.at[head]),
         (picks.at[level], chosen_rows.at[level]),
         (order, orders.at[level, head]),
+        (cotangents.at[level], grads.at[:, level]),
     ]
     own = [pltpu.make_async_copy(src, dst, own_sem.at[i]) for i, (src, dst) in enumerate(own)]
     for copy in own:
@@ -412,13 +404,15 @@
         to_near.append(send(src, place, near_s.at[k], near_r.at[k], {"head": near}))
 
     share(0, tokens.at[level], level)
-    block_s, block_r = pair()
+    up_s, up_r = pair()
+    down_s, down_r = pair()
     group_s, group_r = pair()
     orders_s, orders_r = pair()
     for copy in to_mates:
         copy.wait_recv()
     own[1].wait()
-    blocks, grouped, ordered = [], [], []
+    last = len(levels_ahead)
+    grouped, ordered = [], []
 
     def to_groups(j, source):
         for k, to in enumerate(groups_ahead):
@@ -427,9 +421,30 @@
                 send(block, block, group_s.at[k, j], group_r.at[k, j], {"group": to})
             )
 
-    for k, to in enumerate(levels_ahead):
-        block = full.at[group, level]
-        blocks.append(send(block, block, block_s.at[k], block_r.at[k], {"level": to}))
+    def hop(k, step):
+        send_sem, recv_sem = (up_s, up_r) if step > 0 else (down_s, down_r)
+        block = full.at[group, lax.rem(level - step * k + last + 1, last + 1)]
+        to = lax.rem(level + step + last + 1, last + 1)
+        return reach_out(block, block, send_sem.at[k], recv_sem.at[k], {"level": to})
+
+    def sends(k, step):
+        return (level >= k) & (level < last) if step > 0 else (level <= last - k) & (level > 0)
+
+    def receives(k, step):
+        return level >= k + 1 if step > 0 else level <= last - k - 1
+
+    def start_hop(k, step):
+        @pl.when(sends(k, step))
+        def _():
+            hop(k, step).start()
+
+    def wait_hop(k, step):
+        @pl.when(receives(k, step))
+        def _():
+            hop(k, step).wait_recv()
+
+    for step in (1, -1):
+        start_hop(0, step)
     to_groups(0, level)
     for k, to in enumerate(mates):
         table_mates.append(
@@ -438,6 +453,12 @@
     for k, to in enumerate(levels_ahead):
         picking.append(
             send(picks.at[to], chosen_rows.at[level], pick_s.at[k], pick_r.at[k], {"level": to})
+        )
+    grad_s, grad_r = pair()
+    crossed = []
+    for k, to in enumerate(levels_ahead):
+        crossed.append(
+            send(cotangents.at[to], grads.at[:, level], grad_s.at[k], grad_r.at[k], {"level": to})
         )
     for copy in order_mates:
         copy.wait_recv()
@@ -448,27 +469,39 @@
     for k, source in enumerate(levels_behind):
         crossing[k].wait_recv()
         share(k + 1, rows.at[:, head, source], source)
+    for k in range(last):
+        for step in (1, -1):
+            wait_hop(k, step)
+            if k + 1 < last:
+                start_hop(k + 1, step)
     for k, source in enumerate(levels_behind):
-        blocks[k].wait_recv()
         to_groups(k + 1, source)
     passed = []
     for k, source in enumerate([level] + levels_behind):
         to_far[k].wait_recv()
         place = rows.at[:, far, source]
         passed.append(send(place, place, pass_s.at[k], pass_r.at[k], {"head": near}))
-    for copy in to_near + passed + grouped + table_mates + picking + ordered:
+    for copy in to_near + passed + grouped + table_mates + picking + ordered + crossed:
         copy.wait_recv()
     for copy in started:
         copy.wait_send()
-    for i in (0, 2, 3):
+    for k in range(last):
+        for step in (1, -1):
+
+            @pl.when(sends(k, step))
+            def _(k=k, step=step):
+                hop(k, step).wait_send()
+
+    for i in (0, 2, 3, 5):
         own[i].wait()
 
 
-def start(tokens, weights, tables, picks, order):
+def start(tokens, cotangents, weights, tables, picks, order):
     groups, levels = lax.axis_size("group"), lax.axis_size("level")
     _, _, piece, width = tokens.shape
     shapes = [
         jax.ShapeDtypeStruct((HEADS, HEADS, levels, piece, width), tokens.dtype),
+        jax.ShapeDtypeStruct((HEADS, levels, piece, width), tokens.dtype),
         jax.ShapeDtypeStruct((groups, levels) + weights.shape, weights.dtype),
         jax.ShapeDtypeStruct(tables.shape, tables.dtype),
         jax.ShapeDtypeStruct(picks.shape, picks.dtype),
@@ -476,41 +509,35 @@
     ]
     dma = pltpu.SemaphoreType.DMA
     others, mates = (levels - 1,), (HEADS - 1,)
-    counts = [others] * 2 + [mates] * 3 + [(levels,)] * 3 + [others, (groups - 1, levels), others]
+    counts = [others] * 2 + [mates] * 3 + [(levels,)] * 3
+    counts += [others, others, (groups - 1, levels), others, others]
     return pl.pallas_call(
         start_kernel,
         out_shape=shapes,
-        in_specs=[pl.BlockSpec(memory_space=pltpu.VMEM)] * 5,
-        out_specs=[pl.BlockSpec(memory_space=pl.ANY)] * 5,
-        scratch_shapes=[dma((5,))] + [dma(c) for c in counts for _ in range(2)],
+        in_specs=[pl.BlockSpec(memory_space=pltpu.VMEM)] * 6,
+        out_specs=[pl.BlockSpec(memory_space=pl.ANY)] * 6,
+        scratch_shapes=[dma((6,))] + [dma(c) for c in counts for _ in range(2)],
         compiler_params=pltpu.CompilerParams(collective_id=9, has_side_effects=True),
         cost_estimate=cost(0, 200e6),
         name="start",
-    )(tokens, weights, tables, picks, order)
-
-
-def finish_kernel(
-    part,
-    middle,
-    grads,
-    home_grad,
-    owned,
-    near_buf,
-    send_buf,
-    far_buf,
-    total,
-    back_buf,
-    came_buf,
-    group_buf,
-    level_send,
-    level_buf,
-    head_send,
-    *sems,
-):
-    sems = iter(sems)
+    )(tokens, cotangents, weights, tables, picks, order)
+
+
+def finish_kernel(count, *refs):
+    refs = iter(refs)
+
+    def take(n):
+        return [next(refs) for _ in range(n)]
+
+    part, middle = take(2)
+    grads = take(count)
+    (home_grad,) = take(1)
+    owned = take(count)
+    near_buf, send_buf, far_buf, total, back_buf, came_buf = take(6)
+    group_buf, level_send, level_buf, head_send = (take(count) for _ in range(4))
 
     def pair():
-        return next(sems), next(sems)
+        return next(refs), next(refs)
 
     group, groups_ahead, _ = ring("group")
     level, levels_ahead, levels_behind = ring("level")
@@ -532,10 +559,11 @@
         return copy
 
     pieces = range(HEADS)
+    sets = range(count)
     near_s, near_r = pair()
     far_s, far_r = pair()
+    back_s, back_r = pair()
     group_s, group_r = pair()
-    back_s, back_r = pair()
     level_s, level_r = pair()
     mate_s, mate_r = pair()
     first, second, onward = [], [], []
@@ -551,20 +579,19 @@
                 )
             )
     order = levels_ahead + [level]
-    grouped = []
+    grouped = {}
     for j, dest in enumerate(order):
-        grouped.append(
-            [
+        for p in sets:
+            grouped[j, p] = [
                 send(
-                    grads.at[to, dest],
-                    group_buf.at[k, j],
-                    group_s.at[k, j],
-                    group_r.at[k, j],
+                    grads[p].at[to, dest],
+                    group_buf[p].at[k, j],
+                    group_s.at[p, k, j],
+                    group_r.at[p, k, j],
                     {"group": to},
                 )
                 for k, to in enumerate(groups_ahead)
             ]
-        )
     for i in pieces:
         first[i].wait_recv()
         both = part[i, far].astype(jnp.float32) + near_buf[0, i].astype(jnp.float32)
@@ -574,17 +601,22 @@
         second[i].wait_recv()
         both = part[i, head].astype(jnp.float32) + near_buf[1, i].astype(jnp.float32)
         total[i] = both + middle[i]
-    leveled = []
+    leveled = {}
     for j, dest in enumerate(order):
-        amount = grads[group, dest].astype(jnp.float32)
-        for k, copy in enumerate(grouped[j]):
-            copy.wait_recv()
-            amount = amount + group_buf[k, j].astype(jnp.float32)
-        level_send[j] = amount.astype(jnp.bfloat16)
-        if j < len(levels_ahead):
-            leveled.append(
-                send(level_send.at[j], level_buf.at[j], level_s.at[j], level_r.at[j], {"level": dest})
-            )
+        for p in sets:
+            amount = grads[p][group, dest].astype(jnp.float32)
+            for k, copy in enumerate(grouped[j, p]):
+                copy.wait_recv()
+                amount = amount + group_buf[p][k, j].astype(jnp.float32)
+            level_send[p][j] = amount.astype(jnp.bfloat16)
+            if j < len(levels_ahead):
+                leveled[j, p] = send(
+                    level_send[p].at[j],
+                    level_buf[p].at[j],
+                    level_s.at[p, j],
+                    level_r.at[p, j],
+                    {"level": dest},
+                )
     for i in pieces:
         onward[i].wait_recv()
         both = total[i] + far_buf[i].astype(jnp.float32)
@@ -593,16 +625,24 @@
         send(back_buf.at[:, to], came_buf.at[level], back_s.at[k], back_r.at[k], {"level": to})
         for k, to in enumerate(levels_ahead)
     ]
-    amount = level_send[len(levels_ahead)].astype(jnp.float32)
-    for j, copy in enumerate(leveled):
-        copy.wait_recv()
-        amount = amount + level_buf[j].astype(jnp.float32)
-    head_send[...] = amount.astype(jnp.bfloat16)
-    sharing = [
-        send(head_send.at[to], owned.at[head], mate_s.at[k], mate_r.at[k], {"head": to})
-        for k, to in enumerate(mates)
-    ]
-    owned[head] = head_send[head]
+    sharing = []
+    for p in sets:
+        amount = level_send[p][len(levels_ahead)].astype(jnp.float32)
+        for j in range(len(levels_ahead)):
+            leveled[j, p].wait_recv()
+            amount = amount + level_buf[p][j].astype(jnp.float32)
+        head_send[p][...] = amount.astype(jnp.bfloat16)
+        sharing += [
+            send(
+                head_send[p].at[to],
+                owned[p].at[head],
+                mate_s.at[p, k],
+                mate_r.at[p, k],
+                {"head": to},
+            )
+            for k, to in enumerate(mates)
+        ]
+        owned[p][head] = head_send[p][head]
     home_grad[level] = back_buf[:, level].astype(jnp.float32)
     for k, source in enumerate(levels_behind):
         backs[k].wait_recv()
@@ -613,24 +653,23 @@
         copy.wait_send()
 
 
-def finish(part, middle, grads):
+def finish(part, middle, *grads):
     groups, levels = lax.axis_size("group"), lax.axis_size("level")
     _, count, width = middle.shape
     piece = count // levels
     low_type = jnp.bfloat16
-    block = grads.shape[2:]
+    blocks = [grad.shape[2:] for grad in grads]
+    sets = len(grads)
     dma = pltpu.SemaphoreType.DMA
-    others = (levels - 1,)
-    counts = [(2, HEADS), (HEADS,), (groups - 1, levels), others, others, (HEADS - 1,)]
+    counts = [(2, HEADS), (HEADS,), (levels - 1,)]
+    counts += [(sets, groups - 1, levels), (sets, levels - 1), (sets, HEADS - 1)]
     vmem = pl.BlockSpec(memory_space=pltpu.VMEM)
     return pl.pallas_call(
-        finish_kernel,
-        out_shape=[
-            jax.ShapeDtypeStruct((levels, HEADS, piece, width), jnp.float32),
-            jax.ShapeDtypeStruct(block, low_type),
-        ],
-        in_specs=[vmem] * 3,
-        out_specs=[vmem] * 2,
+        functools.partial(finish_kernel, sets),
+        out_shape=[jax.ShapeDtypeStruct((levels, HEADS, piece, width), jnp.float32)]
+        + [jax.ShapeDtypeStruct(block, low_type) for block in blocks],
+        in_specs=[vmem] * (2 + sets),
+        out_specs=[vmem] * (1 + sets),
         scratch_shapes=[
             pltpu.VMEM((2, HEADS, count, width), low_type),
             pltpu.VMEM((HEADS, count, width), low_type),
@@ -638,18 +677,18 @@
             pltpu.VMEM((HEADS, count, width), jnp.float32),
             pltpu.VMEM((HEADS, levels, piece, width), low_type),
             pltpu.VMEM((levels, HEADS, piece, width), low_type),
-            pltpu.VMEM((groups - 1, levels) + block, low_type),
-            pltpu.VMEM((levels,) + block, low_type),
-            pltpu.VMEM((levels - 1,) + block, low_type),
-            pltpu.VMEM(block, low_type),
         ]
+        + [pltpu.VMEM((groups - 1, levels) + block, low_type) for block in blocks]
+        + [pltpu.VMEM((levels,) + block, low_type) for block in blocks]
+        + [pltpu.VMEM((levels - 1,) + block, low_type) for block in blocks]
+        + [pltpu.VMEM(block, low_type) for block in blocks]
         + [dma(c) for c in counts for _ in range(2)],
         compiler_params=pltpu.CompilerParams(
             collective_id=10, has_side_effects=True, vmem_limit_bytes=56 * 2**20
         ),
         cost_estimate=cost(0, 200e6),
         name="finish",
-    )(part, middle, grads)
+    )(part, middle, *grads)
 
 
 BLOCK = 512
@@ -1198,8 +1237,9 @@
         [value_routes.transpose(1, 2, 0), output_routes.transpose(1, 2, 0)], axis=1
     )
     picks = ffn_routes.reshape(levels, HEADS * piece, -1).transpose(0, 2, 1)
-    arrived, full, tables, picks, orders = start(
+    arrived, own_grads, full, tables, picks, orders = start(
         tokens_in.reshape(levels, HEADS, piece, width),
+        out_grad.reshape(levels, HEADS, piece, width),
         packed.transpose(1, 0, 2),
         tables,
         picks,
@@ -1226,17 +1266,20 @@
     rows = HEADS * count
     reach = -(-LMAX // rows)
     window = [key_value]
-    for _ in range(reach):
-        window.insert(0, shift(window[0], "level", 1))
-    own_grads = to_workers(after(out_grad, key_value))
+    own_grads = own_grads.reshape(count, width)
     cotangent = level_gather(own_grads, 5, True)
+    for i in range(reach):
+        came = shift(window[0], "level", 1)
+        if i == 0:
+            came, cotangent = lax.optimization_barrier((came, cotangent))
+        window.insert(0, came)
 
     def gather_ffn(weight):
         whole = lax.all_gather(weight, ("group", "level"), axis=0)
         return whole.reshape((groups, levels) + weight.shape)
 
     w_in = gather_ffn(ffn_in)
-    w_out = gather_ffn(after(ffn_out, window[0], cotangent))
+    w_out = gather_ffn(ffn_out)
 
     ramp = jnp.arange(count, dtype=jnp.int32)
 
@@ -1304,7 +1347,7 @@
     summed, beyond = pair_scatter(grad_rows, 4, True)
     came = to_far(beyond)
     grad_in, feed = ffn_feed(after(hidden, beyond), grad_pre, active, w_out)
-    came, feed = lax.optimization_barrier((came, feed))
+    came, feed, grad_in = lax.optimization_barrier((came, feed, grad_in))
     summed = summed + came.astype(jnp.float32)
 
     gate_grads = summed[:, width : width + experts].reshape(count, HEADS, levels, local_experts)
@@ -1370,9 +1413,6 @@
             came = shift(grad_keys_sent, "level", -1)
     fed_far = to_far(beyond)
     ffn_out_grad = sum_over_rows(grad_out.reshape((groups * levels,) + grad_out.shape[2:]))
-    early = early.reshape(groups * levels, HEADS * wrows, -1)
-    early, ffn_in_grad = lax.optimization_barrier((early, ffn_in_grad))
-    early = sum_over_rows(early)
     grad_inputs, late = project_back(
         worker_in,
         grad_both,
@@ -1389,15 +1429,13 @@
     fed_far, grad_inputs = lax.optimization_barrier((fed_far, grad_inputs))
     layer_out = to_home(low(middle + fed + fed_far.astype(jnp.float32)))
 
-    input_grad, owned = finish(
+    input_grad, owned, early = finish(
         grad_inputs.reshape(HEADS, HEADS, levels * piece, width),
         grad_middle.reshape(HEADS, levels * piece, width),
         late.reshape(groups, levels, HEADS, wrows, -1),
-    )
-    owned = owned.astype(jnp.float32)
-    early = lax.all_to_all(
-        early.reshape(HEADS, wrows, -1), "head", split_axis=0, concat_axis=0, tiled=True
-    ).astype(jnp.float32)
+        early.reshape(groups, levels, HEADS, wrows, -1),
+    )
+    owned, early = owned.astype(jnp.float32), early.astype(jnp.float32)
 
     def columns(part, first, size):
         return part[:, :, first : first + size].transpose(1, 0, 2).reshape(wrows, HEADS * size)

time: 794 us -> 802 us (1.010)
  waiting for transfers between devices: 120 us -> 147 us
  starting transfers between devices: 40.4 us -> 17.1 us
    ppermute x4, waiting for transfers between devices: 68.7 us -> 136 us  [shift(): return lax.ppermute(value, axis, pairs)]
    reduce_scatter x3 -> x2, waiting for transfers between devices: 39.8 us -> 0.01 us  [sum_over_rows(): return lax.psum_scatter(grad, ('group', 'level'), scatter_dimension=0)]
    pallas_call x1, Pallas kernels: 125 us -> 152 us  [start(): pl.pallas_call(start_kernel, out_shape=shapes, in_specs=[pl.BlockSpec(mem...]
    pallas_call x1, Pallas kernels: 109 us -> 93.1 us  [finish(): pl.pallas_call(functools.partial(finish_kernel, sets), out_shape=[jax.Sha...]
    all_to_all x2 -> x0, starting transfers between devices: 13.2 us -> none  [the longest x1 9.83 us: to_workers(): lax.all_to_all(rows.reshape(levels, count // levels, -1), 'level', split_...]
    ppermute x4, starting transfers between devices: 19.1 us -> 8.96 us  [shift(): return lax.ppermute(value, axis, pairs)]
    unnamed x105 -> x110, local copies, waits for them, and re-layouts: 11.9 us -> 17.6 us
  transfers between devices with their start and end apart: 15 -> 12, of which waited for: 5 -> 5; matrix products, arithmetic and copies ran while one was open for 13% -> 12% of each run, Pallas kernels for 58% -> 58%
where the time goes in v4:
time: 802 us; the launch traced here: 791 us
  Pallas kernels  501 us (62%)
  waiting for transfers between devices  147 us (18%)
  local copies, waits for them, and re-layouts  52.4 us (7%)
  other arithmetic  38.5 us (5%)
  matrix products  20.2 us (3%)
  starting transfers between devices  17.1 us (2%)
  between operations  14.9 us (2%)
    pallas_call x1, Pallas kernels, start(): pl.pallas_call(start_kernel, out_shape=shapes, in_specs=[pl.BlockSpec(mem...  152 us
    ppermute x4, waiting for transfers between devices, shift(): return lax.ppermute(value, axis, pairs)  136 us
    pallas_call x1, Pallas kernels, finish(): pl.pallas_call(functools.partial(finish_kernel, sets), out_shape=[jax.Sha...  93.1 us
    pallas_call x2, Pallas kernels, level_gather(): pl.pallas_call(functools.partial(gather_kernel, by_source), out_shape=jax...  59.4 us
    pallas_call x1, Pallas kernels, ffn_front(): pl.pallas_call(functools.partial(front_kernel, local), grid_spec=grid_spe...  35.7 us
    pallas_call x1, Pallas kernels, ffn_feed(): pl.pallas_call(feed_kernel, grid=(levels,), in_specs=[whole_rows(rows, wi...  28.7 us
    pallas_call x1, Pallas kernels, level_scatter(): pl.pallas_call(functools.partial(scatter_kernel, by_source), out_shape=ja...  27.3 us
    pallas_call x1, Pallas kernels, project_back(): pl.pallas_call(project_back_kernel, grid=(HEADS,), in_specs=[by_row(width...  23.3 us
  transfers between devices with their start and end apart: 12, of which 5 were waited for; matrix products, arithmetic and copies ran while one was open for 12% of the time, Pallas kernels for 58%

profile of v4, /device:TPU:8, one launch (start us, length us, event | category | flops | bytes accessed | tf_op | source)
XLA Modules:
  0.0 790.7 jit_solution(15373164440708436527)
XLA Ops:
  17.5 151.6 %start.1 = (bf16[4,4,4,32,1024]{4,3,2,1,0:T(8,128)(2,1)}, bf16[4,4,32,1024]{3,2,1,0:T(8,128)(2,1)}, bf16[2,4,4,32,1664]{4,3,2,1,0:T(8,128)(2,1)}, s32[4,4,512]{2...) custom-call(bf16[4,4,32,1024]{3,2,1,0:T(8,128)(2,1)} %bitcast.220, bf16[4,4,32,1024]{3,2,1,0:T(8,128)(2,1)} %bitcast.221, ...), custom_call_target="tpu_custom_call" | custom-call | bytes 200000000 | tf_op jit(solution)/shard_map/start/pallas_call | solution.py:514
  172.7 14.3 %project.1 = (bf16[2048,128]{1,0:T(8,128)(2,1)S(1)}, bf16[2048,256]{1,0:T(8,128)(2,1)S(1)}, f32[2048,640]{1,0:T(8,128)}, f32[2048,128]{1,0:T(8,128)S(1)}, f32[2048,16]{1,0:T(8,128)S(1)}) custom-call(bf16[2048,1024]{1,0:T(8,128)(2,1)} %bitcast.194, bf16[1024,1664]{1,0:T(8,128)(2,1)} %bitcast.180, bf16[1024,1664]{1,0:T(8,128)(2,1)} %bitcast.181, ...), custom_call_target="tpu_custom_call" | custom-call | flops 4294967296 | bytes 20000000 | tf_op jit(solution)/shard_map/project/pallas_call | solution.py:996
  191.5 28.4 %level_gather.2 = bf16[4,4,128,1024]{3,2,1,0:T(8,128)(2,1)} custom-call(bf16[4,128,1024]{2,1,0:T(8,128)(2,1)} %bitcast.212), custom_call_target="tpu_custom_call" | custom-call | bytes 90000000 | tf_op jit(solution)/shard_map/level_gather/pallas_call | solution.py:131
  221.7 17.6 %collective-permute-done.refs_1_.refs_4_ = bf16[2048,256]{1,0:T(8,128)(2,1)} collective-permute-done((bf16[2048,256]{1,0:T(8,128)(2,1)S(1)}, bf16[2048,256]{1,0:T(8,128)(2,1)}, u32[]{:S(2)}, u32[]{:S(2)}) %collective-permute-start) | collective-permute-done | bytes 1048608 | tf_op jit(solution)/shard_map/ppermute | solution.py:1175
  239.3 2.6 collective-permute-start.1
  242.4 5.0 broadcast_in_dim_reshape_reshape.5.refs_8_.refs_11_
  248.6 2.8 dynamic-slice_convert_fusion
  251.5 44.1 %collective-permute-done.1.refs_0_.refs_3_ = bf16[2048,256]{1,0:T(8,128)(2,1)S(1)} collective-permute-done((bf16[2048,256]{1,0:T(8,128)(2,1)}, bf16[2048,256]{1,0:T(8,128)(2,1)S(1)}, u32[]{:S(2)}, u32[]{:S(2)}) %collective-permute-start.1) | collective-permute-done | bytes 1048608 | tf_op jit(solution)/shard_map/ppermute | solution.py:1175
  297.0 16.0 %attend.1 = (f32[2048,128]{1,0:T(8,128)S(1)}, f32[4,1,512]{2,1,0:T(1,128)S(1)}) custom-call(s32[4]{0:T(128)S(1)} %subtract_maximum_fusion.first, bf16[2048,128]{1,0:T(8,128)(2,1)S(1)} %copy-done.17, bf16[2048,256]{1,0:T(8,128)(2,1)S(1)} %collective-permute-done.1.refs_0_.refs_3_, bf16[2048,256]{1,0:T(8,128)(2,1)} %collective-permute-done.refs_1_.refs_4_, ...), custom_call_target="tpu_custom_call" | custom-call | flops 20000000000 | bytes 10000000 | tf_op jit(solution)/shard_map/attend/pallas_call | solution.py:761
  313.9 6.0 convolution_convert_fusion
  320.0 27.3 %level_scatter.1 = f32[4,128,1024]{2,1,0:T(8,128)S(1)} custom-call(bf16[4,4,128,1024]{3,2,1,0:T(8,128)(2,1)S(1)} %bitcast.168), custom_call_target="tpu_custom_call" | custom-call | bytes 80000000 | tf_op jit(solution)/shard_map/level_scatter/pallas_call | solution.py:193
  350.8 3.1 fusion.17
  358.8 31.0 %level_gather.3 = bf16[4,4,128,1152]{3,2,1,0:T(8,128)(2,1)} custom-call(bf16[4,128,1152]{2,1,0:T(8,128)(2,1)} %bitcast.201), custom_call_target="tpu_custom_call" | custom-call | bytes 90000000 | tf_op jit(solution)/shard_map/level_gather/pallas_call | solution.py:131
  392.0 35.7 %ffn_front.1 = (bf16[2048,2048]{1,0:T(8,128)(2,1)}, bf16[2048,2048]{1,0:T(8,128)(2,1)}, bf16[2048,1152]{1,0:T(8,128)(2,1)}) custom-call(s32[1]{0:T(128)} %bitcast.24.head, bf16[2048,1152]{1,0:T(8,128)(2,1)} %bitcast.199, bf16[2048,1024]{1,0:T(8,128)(2,1)} %bitcast.202, bf16[2,4,512,512]{3,2,1,0:T(8,128)(2,1)} %bitcast.244, ...), custom_call_target="tpu_custom_call" | custom-call | flops 25769803776 | bytes 30000000 | tf_op jit(solution)/shard_map/ffn_front/pallas_call | solution.py:923
  427.8 2.3 copy-done.2
  430.1 4.7 pair_scatter.2
  435.7 28.7 %ffn_feed.1 = (bf16[2,4,512,512]{3,2,1,0:T(8,128)(2,1)}, bf16[2048,1024]{1,0:T(8,128)(2,1)}) custom-call(bf16[2048,1152]{1,0:T(8,128)(2,1)} %bitcast.200, bf16[2048,2048]{1,0:T(8,128)(2,1)} %get-tuple-element.82.low_pre, bf16[2048,2048]{1,0:T(8,128)(2,1)} %get-tuple-element.83.active.hidden_units, bf16[2,4,512,512]{3,2,1,0:T(8,128)(2,1)} %bitcast.243), custom_call_target="tpu_custom_call" | custom-call | flops 25769803776 | bytes 30000000 | tf_op jit(solution)/shard_map/ffn_feed/pallas_call | solution.py:1129
  465.6 2.6 slice_bitcast_fusion
  468.1 2.6 copy.243
  482.6 13.4 %ffn_rear.1 = bf16[2,4,512,512]{3,2,1,0:T(8,128)(2,1)} custom-call(bf16[2048,1024]{1,0:T(8,128)(2,1)} %bitcast.203, bf16[2048,2048]{1,0:T(8,128)(2,1)} %get-tuple-element.83.active.hidden_units), custom_call_target="tpu_custom_call" | custom-call | flops 17179869184 | bytes 30000000 | tf_op jit(solution)/shard_map/ffn_rear/pallas_call | solution.py:1154
  496.0 10.5 %collective-permute-done.3 = bf16[512,1024]{1,0:T(8,128)(2,1)S(1)} collective-permute-done((bf16[512,1024]{1,0:T(8,128)(2,1)S(1)}, bf16[512,1024]{1,0:T(8,128)(2,1)S(1)}, u32[]{:S(2)}, u32[]{:S(2)}) %collective-permute-start.3) | collective-permute-done | bytes 1048608 | tf_op jit(solution)/shard_map/ppermute | solution.py:313
  507.5 6.2 pair_gather.1
  513.8 6.6 multiply_reduce_fusion
  524.4 21.4 %attend_back.1 = (bf16[2048,128]{1,0:T(8,128)(2,1)S(1)}, bf16[2048,256]{1,0:T(8,128)(2,1)}, bf16[2048,256]{1,0:T(8,128)(2,1)S(1)}, f32[2048,256]{1,0:T(8,128)}) custom-call(s32[4]{0:T(128)S(1)} %subtract_maximum_fusion.first, bf16[2048,128]{1,0:T(8,128)(2,1)S(1)} %copy-done.18, bf16[2048,256]{1,0:T(8,128)(2,1)S(1)} %copy-done.15, ...), custom_call_target="tpu_custom_call" | custom-call | flops 20000000000 | bytes 10000000 | tf_op jit(solution)/shard_map/attend_back/pallas_call | solution.py:845
  551.9 5.4 pair_scatter.3
  557.3 35.5 %collective-permute-done.4 = bf16[2048,256]{1,0:T(8,128)(2,1)S(1)} collective-permute-done((bf16[2048,256]{1,0:T(8,128)(2,1)}, bf16[2048,256]{1,0:T(8,128)(2,1)S(1)}, u32[]{:S(2)}, u32[]{:S(2)}) %collective-permute-start.4) | collective-permute-done | bytes 1048608 | tf_op jit(solution)/shard_map/ppermute | solution.py:1175
  599.1 2.9 convolution_convert_fusion.1
  602.7 38.6 %collective-permute-done.6 = bf16[2048,256]{1,0:T(8,128)(2,1)} collective-permute-done((bf16[2048,256]{1,0:T(8,128)(2,1)}, bf16[2048,256]{1,0:T(8,128)(2,1)}, u32[]{:S(2)}, u32[]{:S(2)}) %collective-permute-start.6) | collective-permute-done | bytes 1048608 | tf_op jit(solution)/shard_map/ppermute | solution.py:1175
  641.2 3.5 convert_add_fusion.grads
  644.7 23.3 %project_back.1 = (bf16[2048,1024]{1,0:T(8,128)(2,1)}, bf16[1024,1024]{1,0:T(8,128)(2,1)}) custom-call(bf16[2048,1024]{1,0:T(8,128)(2,1)} %bitcast.195, f32[2048,256]{1,0:T(8,128)} %convert_add_fusion.grads, bf16[2048,128]{1,0:T(8,128)(2,1)} %copy-done.19, bf16[2048,128]{1,0:T(8,128)(2,1)} %pad.10.out_logit, f32[2048,640]{1,0:T(8,128)} %get-tuple-element.102.projected, ...), custom_call_target="tpu_custom_call" | custom-call | flops 8589934592 | bytes 40000000 | tf_op jit(solution)/shard_map/project_back/pallas_call | solution.py:1076
  671.0 4.7 all-to-all-start
  677.3 93.1 %finish.1 = (f32[4,4,32,1024]{3,2,1,0:T(8,128)}, bf16[4,32,1024]{2,1,0:T(8,128)(2,1)}, bf16[4,32,768]{2,1,0:T(8,128)(2,1)}) custom-call(bf16[4,4,128,1024]{3,2,1,0:T(8,128)(2,1)} %bitcast.208, f32[4,128,1024]{2,1,0:T(8,128)} %bitcast.196, bf16[2,4,4,32,1024]{4,3,2,1,0:T(8,128)(2,1)} %bitcast.216, bf16[2,4,4,32,768]{4,3,2,1,0:T(8,128)(2,1)} %bitcast.197), custom_call_target="tpu_custom_call" | custom-call | bytes 200000000 | tf_op jit(solution)/shard_map/finish/pallas_call | solution.py:667
  (230 shorter events, 84.2 us)
Async XLA Ops:
  7.2 384.8 %all-gather.7.cloned.1.call-start = ((), (), s32[]{:S(2)}) async-start(), calls=%async_computation.6 | async-start | bytes 4718592 | tf_op jit(solution)/shard_map/all_gather | solution.py:1278
  8.0 384.1 %all-gather.5.cloned.1.call-start = ((), (), s32[]{:S(2)}) async-start(), calls=%async_computation.5 | async-start | bytes 4718592 | tf_op jit(solution)/shard_map/all_gather | solution.py:1278
  171.9 15.1 %copy-start.11 = (f32[1024]{0:T(1024)}, f32[1024]{0:T(1024)S(1)}, u32[]{:S(2)}) copy-start(f32[1024]{0:T(1024)S(1)} %get-tuple-element.119) | copy-start | bytes 12292
  171.9 15.1 %copy-start.12 = (f32[1024]{0:T(1024)}, f32[1024]{0:T(1024)S(1)}, u32[]{:S(2)}) copy-start(f32[1024]{0:T(1024)S(1)} %get-tuple-element.120) | copy-start | bytes 12292
  172.7 17.1 %copy-start.46 = (s32[4,4,1,512]{3,2,1,0:T(1,128)S(1)}, s32[4,4,1,512]{3,2,1,0:T(1,128)}, u32[]{:S(2)}) copy-start(s32[4,4,1,512]{3,2,1,0:T(1,128)} %get-tuple-element.66) | copy-start | bytes 98308
  187.8 32.3 %copy-start.3 = (f32[2048,128]{1,0:T(8,128)}, f32[2048,128]{1,0:T(8,128)S(1)}, u32[]{:S(2)}) copy-start(f32[2048,128]{1,0:T(8,128)S(1)} %get-tuple-element.68.sigs) | copy-start | bytes 3145732
  187.8 32.3 %copy-start.5 = (f32[2048,16]{1,0:T(8,128)}, f32[2048,16]{1,0:T(8,128)S(1)}, u32[]{:S(2)}) copy-start(f32[2048,16]{1,0:T(8,128)S(1)} %get-tuple-element.69.masks) | copy-start | bytes 393220
  187.8 107.8 %copy-start.13 = (bf16[2048,256]{1,0:T(8,128)(2,1)}, bf16[2048,256]{1,0:T(8,128)(2,1)S(1)}, u32[]{:S(2)}) copy-start(bf16[2048,256]{1,0:T(8,128)(2,1)S(1)} %get-tuple-element.71.refs_2_.refs_5_) | copy-start | bytes 3145732
  187.8 51.5 %collective-permute-start = (bf16[2048,256]{1,0:T(8,128)(2,1)S(1)}, bf16[2048,256]{1,0:T(8,128)(2,1)}, u32[]{:S(2)}, u32[]{:S(2)}) collective-permute-start(bf16[2048,256]{1,0:T(8,128)(2,1)S(1)} %get-tuple-element.71.refs_2_.refs_5_), channel_id=1, source_target_pairs={{0,4},{4,8},{8,12},{1,5},{5,9},{9,13},{2,6},{6,10},{10,14},{3,7},{... | collective-permute-start | bytes 3145736 | tf_op jit(solution)/shard_map/ppermute | solution.py:1175
  189.7 587.5 %reduce-scatter.3.cloned.1.call-start = ((), (), s32[]{:S(2)}) async-start(), calls=%async_computation.3 | async-start | bytes 4718592 | tf_op jit(solution)/shard_map/reduce_scatter | solution.py:1373
  219.9 22.2 %copy-start.51 = (s32[1,3]{1,0:T(1,128)S(1)}, s32[1,3]{1,0:T(1,128)}, u32[]{:S(2)}) copy-start(s32[1,3]{1,0:T(1,128)} %param.23) | copy-start | bytes 40
  221.7 25.7 %copy-start.29 = (f32[2048,5]{1,0:T(8,128)S(1)}, f32[2048,5]{1,0:T(8,128)}, u32[]{:S(2)}) copy-start(f32[2048,5]{1,0:T(8,128)} %slice_multiply_fusion) | copy-start | bytes 122884
  239.3 56.4 %collective-permute-start.1 = (bf16[2048,256]{1,0:T(8,128)(2,1)}, bf16[2048,256]{1,0:T(8,128)(2,1)S(1)}, u32[]{:S(2)}, u32[]{:S(2)}) collective-permute-start(bf16[2048,256]{1,0:T(8,128)(2,1)} %collective-permute-done.refs_1_.refs_4_), channel_id=1, source_target_pairs={{0,4},{4,8},{8,12},{1,5},{5,9},{9,13},{2,6},{6,10},{10,14},{3,7},{... | collective-permute-start | bytes 3145736 | tf_op jit(solution)/shard_map/ppermute | solution.py:1175
  248.6 105.7 %copy-start.38 = (f32[512,64]{0,1:T(8,128)}, f32[512,64]{0,1:T(8,128)S(1)}, u32[]{:S(2)}) copy-start(f32[512,64]{0,1:T(8,128)S(1)} %convert_reduce_fusion) | copy-start | bytes 393220
  295.6 17.4 %copy-start.14 = (bf16[2048,256]{1,0:T(8,128)(2,1)}, bf16[2048,256]{1,0:T(8,128)(2,1)S(1)}, u32[]{:S(2)}) copy-start(bf16[2048,256]{1,0:T(8,128)(2,1)S(1)} %collective-permute-done.1.refs_0_.refs_3_) | copy-start | bytes 3145732
  434.9 29.6 %collective-permute-start.2 = (bf16[512,1152]{1,0:T(8,128)(2,1)S(1)}, bf16[512,1152]{1,0:T(8,128)(2,1)S(1)}, u32[]{:S(2)}, u32[]{:S(2)}) collective-permute-start(bf16[512,1152]{1,0:T(8,128)(2,1)S(1)} %bitcast.178), channel_id=1, source_target_pairs={{0,2},{1,3},{2,0},{3,1},{4,6},{5,7},{6,4},{7,5},{8,10},{9,11},{10,... | collective-permute-start | bytes 3538952 | tf_op jit(solution)/shard_map/ppermute | solution.py:313
  465.5 313.9 %reduce-scatter.5.cloned.1.call-start = ((), (), s32[]{:S(2)}) async-start(), calls=%async_computation.4 | async-start | bytes 4718592 | tf_op jit(solution)/shard_map/reduce_scatter | solution.py:1373
  481.4 14.7 %copy-start.33 = (bf16[512,1024]{1,0:T(8,128)(2,1)}, bf16[512,1024]{1,0:T(8,128)(2,1)S(1)}, u32[]{:S(2)}) copy-start(bf16[512,1024]{1,0:T(8,128)(2,1)S(1)} %get-tuple-element.127) | copy-start | bytes 3145732
  481.4 25.2 %collective-permute-start.3 = (bf16[512,1024]{1,0:T(8,128)(2,1)S(1)}, bf16[512,1024]{1,0:T(8,128)(2,1)S(1)}, u32[]{:S(2)}, u32[]{:S(2)}) collective-permute-start(bf16[512,1024]{1,0:T(8,128)(2,1)S(1)} %get-tuple-element.127), channel_id=1, source_target_pairs={{0,2},{1,3},{2,0},{3,1},{4,6},{5,7},{6,4},{7,5},{8,10},{9,11},{10,... | collective-permute-start | bytes 3145736 | tf_op jit(solution)/shard_map/ppermute | solution.py:313
  524.4 24.6 %copy-start.24 = (bf16[512,1024]{1,0:T(8,128)(2,1)S(1)}, bf16[512,1024]{1,0:T(8,128)(2,1)}, u32[]{:S(2)}) copy-start(bf16[512,1024]{1,0:T(8,128)(2,1)} %copy-done.23) | copy-start | bytes 3145732
  524.4 24.6 %copy-start.42 = (bf16[512,64]{0,1:T(8,128)(2,1)S(1)}, bf16[512,64]{0,1:T(8,128)(2,1)}, u32[]{:S(2)}) copy-start(bf16[512,64]{0,1:T(8,128)(2,1)} %copy-done.41) | copy-start | bytes 196612
  524.4 24.9 %copy-start.45 = (f32[2048,5]{0,1:T(8,128)S(1)}, f32[2048,5]{0,1:T(8,128)}, u32[]{:S(2)}) copy-start(f32[2048,5]{0,1:T(8,128)} %get-tuple-element.113) | copy-start | bytes 122884
  546.6 46.2 %collective-permute-start.4 = (bf16[2048,256]{1,0:T(8,128)(2,1)}, bf16[2048,256]{1,0:T(8,128)(2,1)S(1)}, u32[]{:S(2)}, u32[]{:S(2)}) collective-permute-start(bf16[2048,256]{1,0:T(8,128)(2,1)} %get-tuple-element.90), channel_id=1, source_target_pairs={{4,0},{8,4},{12,8},{5,1},{9,5},{13,9},{6,2},{10,6},{14,10},{7,3},{... | collective-permute-start | bytes 3145736 | tf_op jit(solution)/shard_map/ppermute | solution.py:1175
  551.9 47.2 %copy-start.35 = (bf16[2048,5,128]{0,2,1:T(8,128)(2,1)S(1)}, bf16[2048,5,128]{0,2,1:T(8,128)(2,1)}, u32[]{:S(2)}) copy-start(bf16[2048,5,128]{0,2,1:T(8,128)(2,1)} %copy-done.34) | copy-start | bytes 7864324
  557.3 39.6 %copy-start.8 = (f32[4,128,1024]{2,1,0:T(8,128)}, f32[4,128,1024]{2,1,0:T(8,128)S(1)}, u32[]{:S(2)}) copy-start(f32[4,128,1024]{2,1,0:T(8,128)S(1)} %get-tuple-element.94) | copy-start | bytes 6291460
  557.3 39.0 %copy-start.4 = (f32[2048,128]{1,0:T(8,128)S(1)}, f32[2048,128]{1,0:T(8,128)}, u32[]{:S(2)}) copy-start(f32[2048,128]{1,0:T(8,128)} %copy-done.3) | copy-start | bytes 3145732
  557.3 39.0 %copy-start.6 = (f32[2048,16]{1,0:T(8,128)S(1)}, f32[2048,16]{1,0:T(8,128)}, u32[]{:S(2)}) copy-start(f32[2048,16]{1,0:T(8,128)} %copy-done.5) | copy-start | bytes 393220
  594.0 47.2 %collective-permute-start.6 = (bf16[2048,256]{1,0:T(8,128)(2,1)}, bf16[2048,256]{1,0:T(8,128)(2,1)}, u32[]{:S(2)}, u32[]{:S(2)}) collective-permute-start(bf16[2048,256]{1,0:T(8,128)(2,1)} %add_convert_fusion.1), channel_id=1, source_target_pairs={{4,0},{8,4},{12,8},{5,1},{9,5},{13,9},{6,2},{10,6},{14,10},{7,3},{... | collective-permute-start | bytes 3145736 | tf_op jit(solution)/shard_map/ppermute | solution.py:1175
  597.9 70.2 %collective-permute-start.5 = (bf16[512,1024]{1,0:T(8,128)(2,1)}, bf16[512,1024]{1,0:T(8,128)(2,1)}, u32[]{:S(2)}, u32[]{:S(2)}) collective-permute-start(bf16[512,1024]{1,0:T(8,128)(2,1)} %bitcast.46), channel_id=1, source_target_pairs={{0,2},{1,3},{2,0},{3,1},{4,6},{5,7},{6,4},{7,5},{8,10},{9,11},{10,... | collective-permute-start | bytes 3145736 | tf_op jit(solution)/shard_map/ppermute | solution.py:313
  644.7 23.4 %copy-start.9 = (f32[4,128,1024]{2,1,0:T(8,128)S(1)}, f32[4,128,1024]{2,1,0:T(8,128)}, u32[]{:S(2)}) copy-start(f32[4,128,1024]{2,1,0:T(8,128)} %copy-done.8) | copy-start | bytes 6291460
  644.7 23.4 %copy-start.22 = (f32[512,1024]{1,0:T(8,128)S(1)}, f32[512,1024]{1,0:T(8,128)}, u32[]{:S(2)}) copy-start(f32[512,1024]{1,0:T(8,128)} %copy-done.20) | copy-start | bytes 6291460
  671.0 106.3 %all-to-all-start = ((bf16[4,128,1024]{2,1,0:T(8,128)(2,1)}), bf16[4,128,1024]{2,1,0:T(8,128)(2,1)S(1)}, u32[]{:S(2)}, u32[]{:S(2)}) async-start(bf16[4,128,1024]{2,1,0:T(8,128)(2,1)} %bitcast.210), calls=%async_computation | async-start | bytes 2097152 | tf_op jit(solution)/shard_map/all_to_all | solution.py:59
  (32 other events, 115.0 us)
Sparse Core Ops, SparseCore 0:
  10.2 116.5 all-gather.6
  189.9 106.9 all-gather.4
  465.6 95.7 reduce-scatter.2
  565.3 125.7 reduce-scatter.4

commit v5 on v4

--- a/solution.py
+++ b/solution.py
@@ -404,15 +404,13 @@
         to_near.append(send(src, place, near_s.at[k], near_r.at[k], {"head": near}))
 
     share(0, tokens.at[level], level)
-    up_s, up_r = pair()
-    down_s, down_r = pair()
+    block_s, block_r = pair()
     group_s, group_r = pair()
     orders_s, orders_r = pair()
     for copy in to_mates:
         copy.wait_recv()
     own[1].wait()
-    last = len(levels_ahead)
-    grouped, ordered = [], []
+    blocks, grouped, ordered = [], [], []
 
     def to_groups(j, source):
         for k, to in enumerate(groups_ahead):
@@ -421,30 +419,9 @@
                 send(block, block, group_s.at[k, j], group_r.at[k, j], {"group": to})
             )
 
-    def hop(k, step):
-        send_sem, recv_sem = (up_s, up_r) if step > 0 else (down_s, down_r)
-        block = full.at[group, lax.rem(level - step * k + last + 1, last + 1)]
-        to = lax.rem(level + step + last + 1, last + 1)
-        return reach_out(block, block, send_sem.at[k], recv_sem.at[k], {"level": to})
-
-    def sends(k, step):
-        return (level >= k) & (level < last) if step > 0 else (level <= last - k) & (level > 0)
-
-    def receives(k, step):
-        return level >= k + 1 if step > 0 else level <= last - k - 1
-
-    def start_hop(k, step):
-        @pl.when(sends(k, step))
-        def _():
-            hop(k, step).start()
-
-    def wait_hop(k, step):
-        @pl.when(receives(k, step))
-        def _():
-            hop(k, step).wait_recv()
-
-    for step in (1, -1):
-        start_hop(0, step)
+    for k, to in enumerate(levels_ahead):
+        block = full.at[group, level]
+        blocks.append(send(block, block, block_s.at[k], block_r.at[k], {"level": to}))
     to_groups(0, level)
     for k, to in enumerate(mates):
         table_mates.append(
@@ -453,12 +430,6 @@
     for k, to in enumerate(levels_ahead):
         picking.append(
             send(picks.at[to], chosen_rows.at[level], pick_s.at[k], pick_r.at[k], {"level": to})
-        )
-    grad_s, grad_r = pair()
-    crossed = []
-    for k, to in enumerate(levels_ahead):
-        crossed.append(
-            send(cotangents.at[to], grads.at[:, level], grad_s.at[k], grad_r.at[k], {"level": to})
         )
     for copy in order_mates:
         copy.wait_recv()
@@ -469,12 +440,14 @@
     for k, source in enumerate(levels_behind):
         crossing[k].wait_recv()
         share(k + 1, rows.at[:, head, source], source)
-    for k in range(last):
-        for step in (1, -1):
-            wait_hop(k, step)
-            if k + 1 < last:
-                start_hop(k + 1, step)
+    grad_s, grad_r = pair()
+    crossed = []
+    for k, to in enumerate(levels_ahead):
+        crossed.append(
+            send(cotangents.at[to], grads.at[:, level], grad_s.at[k], grad_r.at[k], {"level": to})
+        )
     for k, source in enumerate(levels_behind):
+        blocks[k].wait_recv()
         to_groups(k + 1, source)
     passed = []
     for k, source in enumerate([level] + levels_behind):
@@ -485,13 +458,6 @@
         copy.wait_recv()
     for copy in started:
         copy.wait_send()
-    for k in range(last):
-        for step in (1, -1):
-
-            @pl.when(sends(k, step))
-            def _(k=k, step=step):
-                hop(k, step).wait_send()
-
     for i in (0, 2, 3, 5):
         own[i].wait()
 
@@ -510,7 +476,7 @@
     dma = pltpu.SemaphoreType.DMA
     others, mates = (levels - 1,), (HEADS - 1,)
     counts = [others] * 2 + [mates] * 3 + [(levels,)] * 3
-    counts += [others, others, (groups - 1, levels), others, others]
+    counts += [others, (groups - 1, levels), others, others]
     return pl.pallas_call(
         start_kernel,
         out_shape=shapes,
@@ -853,21 +819,28 @@
     )(first, queries, *window, *window, grads, pos_q, start_q, lse, inner, pos_k)
 
 
-def front_kernel(
-    local, head, hidden, grads, w_in, w_out, gates, active, grad_pre, rows_out, acc
-):
-    groups, levels, depth, width = w_in.shape
+def columns_of(ref, group, groups, step, depth):
+    at = lax.rem(group + step + groups, groups) * depth
+    return ref.at[:, pl.ds(pl.multiple_of(at, 128), depth)]
+
+
+def front_kernel(groups, local, place, hidden, grads, *refs):
+    w_in, w_out = refs[:groups], refs[groups : 2 * groups]
+    gates, active, grad_pre, rows_out, turned, acc = refs[2 * groups :]
+    levels, depth, width = w_in[0].shape
     tile = hidden.shape[0]
     model = groups * depth
-    acc[...] = jnp.zeros_like(acc)
+    parts = [slice(step * depth, (step + 1) * depth) for step in range(groups)]
+    for step in range(groups):
+        turned[0, :, parts[step]] = columns_of(hidden, place[1], groups, -step, depth)[...]
+        turned[1, :, parts[step]] = columns_of(grads, place[1], groups, -step, depth)[...]
     gate_grads = []
     for level in range(levels):
         pre_act = jnp.zeros((tile, width), jnp.float32)
         grad_active = jnp.zeros((tile, width), jnp.float32)
-        for group in range(groups):
-            part = slice(group * depth, (group + 1) * depth)
-            pre_act += dot(hidden[:, part], w_in[group, level], 1, 0)
-            grad_active += dot(grads[:, part], w_out[group, level], 1, 0)
+        for step in range(groups):
+            pre_act += dot(turned[0, :, parts[step]], w_in[step][level], 1, 0)
+            grad_active += dot(turned[1, :, parts[step]], w_out[step][level], 1, 0)
         first = level * local
         gate = jnp.concatenate(
             [jnp.broadcast_to(gates[:, first + e : first + e + 1], (tile, FH)) for e in range(local)],
@@ -885,57 +858,139 @@
         slope = sig * (1.0 + pre_act * (1.0 - sig))
         low_pre = (grad_active * gate * slope).astype(jnp.bfloat16)
         grad_pre[:, columns] = low_pre
-        for group in range(groups):
-            part = slice(group * depth, (group + 1) * depth)
-            acc[:, part] += dot(low_pre, w_in[group, level], 1, 1)
-    rows_out[:, :model] = acc[...].astype(jnp.bfloat16)
+        for step in range(groups):
+            back = dot(low_pre, w_in[step][level], 1, 1)
+            acc[:, parts[step]] = back if level == 0 else acc[:, parts[step]] + back
+    for step in range(groups):
+        columns_of(rows_out, place[1], groups, -step, depth)[...] = acc[:, parts[step]].astype(
+            jnp.bfloat16
+        )
     spare = rows_out.shape[1] - model
-    lane = lax.broadcasted_iota(jnp.int32, (tile, spare), 1) - head[0] * (levels * local)
+    lane = lax.broadcasted_iota(jnp.int32, (tile, spare), 1) - place[0] * (levels * local)
     spread = jnp.zeros((tile, spare), jnp.float32)
     for e, column in enumerate(gate_grads):
         spread = jnp.where(lane == e, column, spread)
     rows_out[:, model:] = spread.astype(jnp.bfloat16)
 
 
-def ffn_front(head, hidden, grads, w_in, w_out, gates, local):
+def ffn_front(place, hidden, grads, w_in, w_out, gates, local):
     rows, wide = hidden.shape
-    groups, levels, depth, width = w_in.shape
+    groups = len(w_in)
+    levels, depth, width = w_in[0].shape
     tile = 512
 
     def by_row(columns):
         return pl.BlockSpec((tile, columns), lambda i, *_: (i, 0))
 
-    whole = pl.BlockSpec(w_in.shape, lambda i, *_: (0, 0, 0, 0), pipeline_mode=pl.Buffered(1))
+    whole = pl.BlockSpec(w_in[0].shape, lambda i, *_: (0, 0, 0), pipeline_mode=pl.Buffered(1))
     grid_spec = pltpu.PrefetchScalarGridSpec(
         num_scalar_prefetch=1,
         grid=(rows // tile,),
-        in_specs=[
-            by_row(wide),
-            by_row(groups * depth),
-            whole,
-            whole,
-            by_row(gates.shape[1]),
+        in_specs=[by_row(wide), by_row(groups * depth)]
+        + [whole] * (2 * groups)
+        + [by_row(gates.shape[1])],
+        out_specs=[by_row(levels * width), by_row(levels * width), by_row(wide)],
+        scratch_shapes=[
+            pltpu.VMEM((2, tile, groups * depth), jnp.bfloat16),
+            pltpu.VMEM((tile, groups * depth), jnp.float32),
         ],
-        out_specs=[by_row(levels * width), by_row(levels * width), by_row(wide)],
-        scratch_shapes=[pltpu.VMEM((tile, groups * depth), jnp.float32)],
     )
     hidden_units = jax.ShapeDtypeStruct((rows, levels * width), jnp.bfloat16)
     return pl.pallas_call(
-        functools.partial(front_kernel, local),
+        functools.partial(front_kernel, groups, local),
         grid_spec=grid_spec,
         out_shape=[hidden_units, hidden_units, jax.ShapeDtypeStruct((rows, wide), jnp.bfloat16)],
         compiler_params=pltpu.CompilerParams(vmem_limit_bytes=58 * 2**20),
         cost_estimate=cost(6 * rows * groups * depth * levels * width, 3e7),
         name="ffn_front",
-    )(head, hidden, grads, w_in, w_out, gates)
-
-
-def rear_kernel(rows_in, hidden_units, weight_grads):
-    groups, _, depth, _ = weight_grads.shape
+    )(place, hidden, grads, *w_in, *w_out, gates)
+
+
+def rear_kernel(groups, place, rows_in, hidden_units, *weight_grads):
+    _, depth, _ = weight_grads[0].shape
     units = hidden_units[...]
-    for group in range(groups):
-        part = slice(group * depth, (group + 1) * depth)
-        weight_grads[group, 0] = dot(rows_in[:, part], units, 0, 0).astype(jnp.bfloat16)
+    for step in range(groups):
+        part = columns_of(rows_in, place[1], groups, step, depth)
+        weight_grads[step][0] = dot(part[...], units, 0, 0).astype(jnp.bfloat16)
+
+
+def feed_kernel(groups, place, active, *refs):
+    weights = refs[:groups]
+    feed, acc = refs[groups:]
+    _, depth, _ = weights[0].shape
+    level = pl.program_id(0)
+    act = active[...]
+    for step in range(groups):
+        fed = dot(act, weights[step][0], 1, 1)
+        part = slice(step * depth, (step + 1) * depth)
+
+        @pl.when(level == 0)
+        def _():
+            acc[:, part] = fed
+
+        @pl.when(level > 0)
+        def _():
+            acc[:, part] += fed
+
+    @pl.when(level == pl.num_programs(0) - 1)
+    def _():
+        for step in range(groups):
+            part = slice(step * depth, (step + 1) * depth)
+            columns_of(feed, place[1], groups, -step, depth)[...] = acc[:, part].astype(
+                jnp.bfloat16
+            )
+
+
+def whole_rows(rows, columns):
+    return pl.BlockSpec((rows, columns), lambda i, *_: (0, 0), pipeline_mode=pl.Buffered(1))
+
+
+def ffn_feed(place, active, weights):
+    rows = active.shape[0]
+    groups = len(weights)
+    levels, depth, width = weights[0].shape
+    return pl.pallas_call(
+        functools.partial(feed_kernel, groups),
+        grid_spec=pltpu.PrefetchScalarGridSpec(
+            num_scalar_prefetch=1,
+            grid=(levels,),
+            in_specs=[pl.BlockSpec((rows, width), lambda i, *_: (0, i))]
+            + [pl.BlockSpec((1, depth, width), lambda i, *_: (i, 0, 0))] * groups,
+            out_specs=whole_rows(rows, groups * depth),
+            scratch_shapes=[pltpu.VMEM((rows, groups * depth), jnp.float32)],
+        ),
+        out_shape=jax.ShapeDtypeStruct((rows, groups * depth), jnp.bfloat16),
+        compiler_params=pltpu.CompilerParams(vmem_limit_bytes=58 * 2**20),
+        cost_estimate=cost(2 * rows * groups * depth * levels * width, 3e7),
+        name="ffn_feed",
+    )(place, active, *weights)
+
+
+def ffn_rear(place, rows_in, units, model, groups, levels):
+    rows, wide = rows_in.shape
+    width = units.shape[1] // levels
+    depth = model // groups
+    return pl.pallas_call(
+        functools.partial(rear_kernel, groups),
+        grid_spec=pltpu.PrefetchScalarGridSpec(
+            num_scalar_prefetch=1,
+            grid=(levels,),
+            in_specs=[
+                whole_rows(rows, wide),
+                pl.BlockSpec((rows, width), lambda i, *_: (0, i)),
+            ],
+            out_specs=[pl.BlockSpec((1, depth, width), lambda i, *_: (i, 0, 0))] * groups,
+        ),
+        out_shape=[jax.ShapeDtypeStruct((levels, depth, width), jnp.bfloat16)] * groups,
+        compiler_params=pltpu.CompilerParams(vmem_limit_bytes=58 * 2**20),
+        cost_estimate=cost(2 * rows * groups * depth * levels * width, 3e7),
+        name="ffn_rear",
+    )(place, rows_in, units)
+
+
+def turn(value, axis, by):
+    size = lax.axis_size(axis)
+    return lax.ppermute(value, axis, [(i, (i + by) % size) for i in range(size)])
 
 
 def normalized(rows, gain, bias):
@@ -1095,74 +1150,6 @@
     )(rows, grads, grad_query, out_logit, projected, sigs, masks, full, full, full, full, gain, bias)
 
 
-def feed_kernel(rows_in, low_pre, active, w_out, weight_grads, feed, acc):
-    groups, _, depth, _ = w_out.shape
-    level = pl.program_id(0)
-    units, act = low_pre[...], active[...]
-    for group in range(groups):
-        part = slice(group * depth, (group + 1) * depth)
-        weight_grads[group, 0] = dot(rows_in[:, part], units, 0, 0).astype(jnp.bfloat16)
-        fed = dot(act, w_out[group, 0], 1, 1)
-
-        @pl.when(level == 0)
-        def _():
-            acc[:, part] = fed
-
-        @pl.when(level > 0)
-        def _():
-            acc[:, part] += fed
-
-    @pl.when(level == pl.num_programs(0) - 1)
-    def _():
-        feed[...] = acc[...].astype(jnp.bfloat16)
-
-
-def whole_rows(rows, columns):
-    return pl.BlockSpec((rows, columns), lambda i: (0, 0), pipeline_mode=pl.Buffered(1))
-
-
-def ffn_feed(hidden, grad_pre, active, w_out):
-    rows, wide = hidden.shape
-    groups, levels, depth, width = w_out.shape
-    by_level = pl.BlockSpec((rows, width), lambda i: (0, i))
-    grads_spec = pl.BlockSpec((groups, 1, depth, width), lambda i: (0, i, 0, 0))
-    return pl.pallas_call(
-        feed_kernel,
-        grid=(levels,),
-        in_specs=[
-            whole_rows(rows, wide),
-            by_level,
-            by_level,
-            grads_spec,
-        ],
-        out_specs=[grads_spec, whole_rows(rows, groups * depth)],
-        out_shape=[
-            jax.ShapeDtypeStruct((groups, levels, depth, width), jnp.bfloat16),
-            jax.ShapeDtypeStruct((rows, groups * depth), jnp.bfloat16),
-        ],
-        scratch_shapes=[pltpu.VMEM((rows, groups * depth), jnp.float32)],
-        compiler_params=pltpu.CompilerParams(vmem_limit_bytes=58 * 2**20),
-        cost_estimate=cost(6 * rows * groups * depth * levels * width, 3e7),
-        name="ffn_feed",
-    )(hidden, grad_pre, active, w_out)
-
-
-def ffn_rear(rows_in, units, groups, levels):
-    rows, wide = rows_in.shape
-    width = units.shape[1] // levels
-    depth = wide // groups
-    return pl.pallas_call(
-        rear_kernel,
-        grid=(levels,),
-        in_specs=[whole_rows(rows, wide), pl.BlockSpec((rows, width), lambda i: (0, i))],
-        out_specs=pl.BlockSpec((groups, 1, depth, width), lambda i: (0, i, 0, 0)),
-        out_shape=jax.ShapeDtypeStruct((groups, levels, depth, width), jnp.bfloat16),
-        compiler_params=pltpu.CompilerParams(vmem_limit_bytes=58 * 2**20),
-        cost_estimate=cost(4 * rows * groups * depth * levels * width, 3e7),
-        name="ffn_rear",
-    )(rows_in, units)
-
-
 def chosen(routes, options):
     return jnp.sum(
         (routes[..., None] == jnp.arange(options, dtype=jnp.int32)).astype(jnp.float32), axis=-2
@@ -1247,7 +1234,8 @@
     )
     worker_in = arrived.reshape(HEADS * count, width)
     own_tokens = lax.dynamic_index_in_dim(arrived, head, 1, keepdims=False).reshape(count, width)
-    full = full.reshape(width, cols)
+    in_rows = [turn(ffn_in, "group", k) for k in range(1, groups)]
+    full, in_rows = lax.optimization_barrier((full.reshape(width, cols), in_rows))
 
     base = 2 * DH + 2 * VEXP * DH
     w_output = full[:, VEXP * DH : 2 * VEXP * DH]
@@ -1265,21 +1253,6 @@
 
     rows = HEADS * count
     reach = -(-LMAX // rows)
-    window = [key_value]
-    own_grads = own_grads.reshape(count, width)
-    cotangent = level_gather(own_grads, 5, True)
-    for i in range(reach):
-        came = shift(window[0], "level", 1)
-        if i == 0:
-            came, cotangent = lax.optimization_barrier((came, cotangent))
-        window.insert(0, came)
-
-    def gather_ffn(weight):
-        whole = lax.all_gather(weight, ("group", "level"), axis=0)
-        return whole.reshape((groups, levels) + weight.shape)
-
-    w_in = gather_ffn(ffn_in)
-    w_out = gather_ffn(ffn_out)
 
     ramp = jnp.arange(count, dtype=jnp.int32)
 
@@ -1288,7 +1261,6 @@
         four = values.reshape(lead + (HEADS, levels, HEADS, piece) + shape)
         return jnp.swapaxes(four, -4, -3).reshape(lead + (rows,) + shape)
 
-    orders = after(orders, key_value)
     orders = jnp.concatenate([jnp.zeros((reach, HEADS, count), jnp.int32), orders], axis=0)
     orders = lax.dynamic_slice_in_dim(orders, level, reach + 1, 0)
     here = orders[:, :, None, :] == ramp[None, None, :, None]
@@ -1298,8 +1270,6 @@
     pos_all = jnp.where(shard[:, :, None] < 0, -1, shard[:, :, None] * count + inverse)
     pos_all = arrival(pos_all[..., None]).reshape(-1)
     positions = pos_all[reach * rows :]
-    own_routes = picks.reshape(levels, -1, HEADS, piece).transpose(2, 0, 3, 1).reshape(count, -1)
-
     seq_ends = jnp.cumsum(seq_lengths[0])
 
     def starts_of(places):
@@ -1310,6 +1280,25 @@
     base_block = (level - reach) * blocks
     first_block = starts_of(level * rows + jnp.arange(blocks, dtype=jnp.int32) * BLOCK) // BLOCK
     first_block = jnp.maximum(first_block - base_block, 0)
+
+    window = [key_value]
+    own_grads = own_grads.reshape(count, width)
+    for i in range(reach):
+        came = shift(window[0], "level", 1)
+        if i == 0:
+            came, own_grads, pos_all, starts, ffn_out, in_rows = lax.optimization_barrier(
+                (came, own_grads, pos_all, starts, ffn_out, [ffn_in] + in_rows)
+            )
+            cotangent = level_gather(own_grads, 5, True)
+        if i == reach - 1:
+            came, cotangent = lax.optimization_barrier((came, cotangent))
+        window.insert(0, came)
+    place = jnp.stack([head, lax.axis_index("group")])
+    out_here = lax.all_gather(ffn_out, "level", axis=0)
+    w_in = [lax.all_gather(part, "level", axis=0) for part in in_rows]
+
+    own_routes = picks.reshape(levels, -1, HEADS, piece).transpose(2, 0, 3, 1).reshape(count, -1)
+
 
     def lines(values):
         return values.reshape(blocks, 1, BLOCK)
@@ -1328,6 +1317,8 @@
     out_gate = out_sig * out_mask
     mixed = low((out_gate[..., None] * attended[:, None, :]).reshape(rows, VEXP * DH))
     branch = low(level_scatter(low(transposed(mixed, w_output)), 2))
+    branch, out_here = lax.optimization_barrier((branch, out_here))
+    w_out = [out_here] + [turn(out_here, "group", k) for k in range(1, groups)]
     middle = own_tokens.astype(jnp.float32) + branch.astype(jnp.float32)
 
     normed_mid, scaled_two, inverse_two = layer_norm(middle, gain_two, bias_two)
@@ -1342,12 +1333,15 @@
     mine = levels * local_experts
     gates = lax.dynamic_slice_in_dim(hidden, width + head * mine, mine, 1).astype(jnp.float32)
     active, grad_pre, grad_rows = ffn_front(
-        head[None], hidden, cotangent, w_in, w_out, gates, local_experts
+        place, hidden, cotangent, w_in, w_out, gates, local_experts
     )
     summed, beyond = pair_scatter(grad_rows, 4, True)
     came = to_far(beyond)
-    grad_in, feed = ffn_feed(after(hidden, beyond), grad_pre, active, w_out)
-    came, feed, grad_in = lax.optimization_barrier((came, feed, grad_in))
+    grad_in = ffn_rear(place, hidden, grad_pre, width, groups, levels)
+    in_came = [turn(grad_in[k], "group", k) for k in range(1, groups)]
+    grad_out = ffn_rear(place, cotangent, active, width, groups, levels)
+    out_came = [turn(grad_out[k], "group", k) for k in range(1, groups)]
+    came, grad_in, grad_out = lax.optimization_barrier((came, grad_in, grad_out))
     summed = summed + came.astype(jnp.float32)
 
     gate_grads = summed[:, width : width + experts].reshape(count, HEADS, levels, local_experts)
@@ -1365,14 +1359,18 @@
 
     own_branch = low(grad_middle)
     came = to_far(own_branch)
-    grad_out = ffn_rear(after(cotangent, own_branch), active, groups, levels)
-    came, grad_out = lax.optimization_barrier((came, grad_out))
+    feed = ffn_feed(place, active, w_out)
+    came, feed = lax.optimization_barrier((came, feed))
     grad_branch = pair_gather(own_branch, came, 7)
 
-    def sum_over_rows(grad):
-        return lax.psum_scatter(grad, ("group", "level"), scatter_dimension=0)
-
-    ffn_in_grad = sum_over_rows(grad_in.reshape((groups * levels,) + grad_in.shape[2:]))
+    def sum_over_rows(own, others):
+        total = own[0].astype(jnp.float32)
+        for other in others:
+            total = total + other.astype(jnp.float32)
+        return lax.psum_scatter(low(total), "level", scatter_dimension=0)
+
+    grad_branch, in_came = lax.optimization_barrier((grad_branch, in_came))
+    ffn_in_grad = sum_over_rows(grad_in, in_came)
     grad_mixed = matmul(grad_branch, w_output).reshape(rows, VEXP, DH)
     grad_out_gate = jnp.sum(grad_mixed * attended[:, None, :], axis=-1)
     grad_attended = low(jnp.sum(grad_mixed * out_gate[..., None], axis=1))
@@ -1390,8 +1388,10 @@
         pos_all[:, None],
     )
     came = shift(grad_window[0], "level", -1)
-    fed, beyond = pair_scatter(after(feed, grad_queries), 6, True)
-    grad_w_output = contract_rows(after(grad_branch, fed), mixed)
+    grad_queries, out_came = lax.optimization_barrier((grad_queries, out_came))
+    ffn_out_grad = sum_over_rows(grad_out, out_came)
+    fed, beyond = pair_scatter(feed, 6, True)
+    grad_w_output = contract_rows(grad_branch, mixed)
     early = jnp.concatenate(
         [
             low(grad_w_output),
@@ -1412,7 +1412,6 @@
             grad_keys_sent = low(grad_both)
             came = shift(grad_keys_sent, "level", -1)
     fed_far = to_far(beyond)
-    ffn_out_grad = sum_over_rows(grad_out.reshape((groups * levels,) + grad_out.shape[2:]))
     grad_inputs, late = project_back(
         worker_in,
         grad_both,

time: 802 us -> 733 us (0.914)
  Pallas kernels: 501 us -> 429 us
  waiting for transfers between devices: 147 us -> 108 us
  other arithmetic: 38.5 us -> 54.9 us
  local copies, waits for them, and re-layouts: 52.4 us -> 62.6 us
  starting transfers between devices: 17.1 us -> 25.3 us
    pallas_call x1, Pallas kernels: 152 us -> 89.7 us  [start(): pl.pallas_call(start_kernel, out_shape=shapes, in_specs=[pl.BlockSpec(mem...]
    ppermute x4, waiting for transfers between devices: 136 us -> 101 us  [shift(): return lax.ppermute(value, axis, pairs)]
    convert_element_type x7 -> x9, other arithmetic: 7.87 us -> 20.6 us  [low(): return value.astype(jnp.bfloat16)]
    pallas_call x1, Pallas kernels: 93.1 us -> 80.7 us  [finish(): pl.pallas_call(functools.partial(finish_kernel, sets), out_shape=[jax.Sha...]
    pallas_call x3 -> x4, Pallas kernels: 77.9 us -> 83.5 us  [the longest x1 37.1 us: ffn_front(): pl.pallas_call(functools.partial(front_kernel, groups, local), grid_spec=...]
    unnamed x110 -> x90, local copies, waits for them, and re-layouts: 17.6 us -> 21.2 us
  transfers between devices with their start and end apart: 12 -> 17, of which waited for: 5 -> 6; matrix products, arithmetic and copies ran while one was open for 12% -> 16% of each run, Pallas kernels for 58% -> 52%
where the time goes in v5:
time: 733 us; the launch traced here: 720 us
  Pallas kernels  429 us (59%)
  waiting for transfers between devices  108 us (15%)
  local copies, waits for them, and re-layouts  62.6 us (9%)
  other arithmetic  54.9 us (7%)
  matrix products  25.4 us (3%)
  starting transfers between devices  25.3 us (3%)
  between operations  15 us (2%)
    ppermute x4, waiting for transfers between devices, shift(): return lax.ppermute(value, axis, pairs)  101 us
    pallas_call x1, Pallas kernels, start(): pl.pallas_call(start_kernel, out_shape=shapes, in_specs=[pl.BlockSpec(mem...  89.7 us
    pallas_call x1, Pallas kernels, finish(): pl.pallas_call(functools.partial(finish_kernel, sets), out_shape=[jax.Sha...  80.7 us
    pallas_call x2, Pallas kernels, level_gather(): pl.pallas_call(functools.partial(gather_kernel, by_source), out_shape=jax...  59.2 us
    pallas_call x1, Pallas kernels, ffn_front(): pl.pallas_call(functools.partial(front_kernel, groups, local), grid_spec=...  37.1 us
    pallas_call x2, Pallas kernels, ffn_rear(): pl.pallas_call(functools.partial(rear_kernel, groups), grid_spec=pltpu.Pr...  28 us
    pallas_call x1, Pallas kernels, level_scatter(): pl.pallas_call(functools.partial(scatter_kernel, by_source), out_shape=ja...  26.5 us
    pallas_call x1, Pallas kernels, project_back(): pl.pallas_call(project_back_kernel, grid=(HEADS,), in_specs=[by_row(width...  23.3 us
  transfers between devices with their start and end apart: 17, of which 6 were waited for; matrix products, arithmetic and copies ran while one was open for 16% of the time, Pallas kernels for 52%

profile of v5, /device:TPU:8, one launch (start us, length us, event | category | flops | bytes accessed | tf_op | source)
XLA Modules:
  0.0 720.4 jit_solution(3971120935365842940)
XLA Ops:
  19.0 89.7 %start.1 = (bf16[4,4,4,32,1024]{4,3,2,1,0:T(8,128)(2,1)}, bf16[4,4,32,1024]{3,2,1,0:T(8,128)(2,1)}, bf16[2,4,4,32,1664]{4,3,2,1,0:T(8,128)(2,1)}, s32[4,4,512]{2...) custom-call(bf16[4,4,32,1024]{3,2,1,0:T(8,128)(2,1)} %bitcast.210, bf16[4,4,32,1024]{3,2,1,0:T(8,128)(2,1)} %bitcast.211, ...), custom_call_target="tpu_custom_call" | custom-call | bytes 200000000 | tf_op jit(solution)/shard_map/start/pallas_call | solution.py:480
  113.2 14.3 %project.1 = (bf16[2048,128]{1,0:T(8,128)(2,1)S(1)}, bf16[2048,256]{1,0:T(8,128)(2,1)S(1)}, f32[2048,640]{1,0:T(8,128)}, f32[2048,128]{1,0:T(8,128)S(1)}, f32[2048,16]{1,0:T(8,128)S(1)}) custom-call(bf16[2048,1024]{1,0:T(8,128)(2,1)} %bitcast.186, bf16[1024,1664]{1,0:T(8,128)(2,1)} %bitcast.169, bf16[1024,1664]{1,0:T(8,128)(2,1)} %bitcast.170, ...), custom_call_target="tpu_custom_call" | custom-call | flops 4294967296 | bytes 20000000 | tf_op jit(solution)/shard_map/project/pallas_call | solution.py:1051
  133.7 21.2 %collective-permute-done.1.refs_1_.refs_4_ = bf16[2048,256]{1,0:T(8,128)(2,1)} collective-permute-done((bf16[2048,256]{1,0:T(8,128)(2,1)S(1)}, bf16[2048,256]{1,0:T(8,128)(2,1)}, u32[]{:S(2)}, u32[]{:S(2)}) %collective-permute-start.1) | collective-permute-done | bytes 1048608 | tf_op jit(solution)/shard_map/ppermute | solution.py:1162
  156.0 5.0 collective-permute-start.2
  167.8 28.4 %level_gather.2 = bf16[4,4,128,1024]{3,2,1,0:T(8,128)(2,1)} custom-call(bf16[4,128,1024]{2,1,0:T(8,128)(2,1)} %bitcast.194), custom_call_target="tpu_custom_call" | custom-call | bytes 90000000 | tf_op jit(solution)/shard_map/level_gather/pallas_call | solution.py:131
  198.7 15.1 %collective-permute-done.2.refs_0_.refs_3_ = bf16[2048,256]{1,0:T(8,128)(2,1)S(1)} collective-permute-done((bf16[2048,256]{1,0:T(8,128)(2,1)}, bf16[2048,256]{1,0:T(8,128)(2,1)S(1)}, u32[]{:S(2)}, u32[]{:S(2)}) %collective-permute-start.2) | collective-permute-done | bytes 1048608 | tf_op jit(solution)/shard_map/ppermute | solution.py:1162
  218.2 14.5 %attend.1 = (f32[2048,128]{1,0:T(8,128)S(1)}, f32[4,1,512]{2,1,0:T(1,128)S(1)}) custom-call(s32[4]{0:T(128)S(1)} %subtract_maximum_fusion.first, bf16[2048,128]{1,0:T(8,128)(2,1)S(1)} %copy-done.18, bf16[2048,256]{1,0:T(8,128)(2,1)S(1)} %copy-done.15, bf16[2048,256]{1,0:T(8,128)(2,1)} %collective-permute-done.1.refs_1_.refs_4_, ...), custom_call_target="tpu_custom_call" | custom-call | flops 20000000000 | bytes 10000000 | tf_op jit(solution)/shard_map/attend/pallas_call | solution.py:727
  235.8 6.0 convolution_convert_fusion
  241.8 26.5 %level_scatter.1 = f32[4,128,1024]{2,1,0:T(8,128)S(1)} custom-call(bf16[4,4,128,1024]{3,2,1,0:T(8,128)(2,1)S(1)} %bitcast.158), custom_call_target="tpu_custom_call" | custom-call | bytes 80000000 | tf_op jit(solution)/shard_map/level_scatter/pallas_call | solution.py:193
  283.8 30.8 %level_gather.3 = bf16[4,4,128,1152]{3,2,1,0:T(8,128)(2,1)} custom-call(bf16[4,128,1152]{2,1,0:T(8,128)(2,1)} %bitcast.193), custom_call_target="tpu_custom_call" | custom-call | bytes 90000000 | tf_op jit(solution)/shard_map/level_gather/pallas_call | solution.py:131
  318.7 37.1 %ffn_front.1 = (bf16[2048,2048]{1,0:T(8,128)(2,1)}, bf16[2048,2048]{1,0:T(8,128)(2,1)}, bf16[2048,1152]{1,0:T(8,128)(2,1)}) custom-call(s32[2]{0:T(128)} %pad_add_fusion.1.place, bf16[2048,1152]{1,0:T(8,128)(2,1)} %bitcast.190, bf16[2048,1024]{1,0:T(8,128)(2,1)} %bitcast.196, bf16[4,512,512]{2,1,0:T(8,128)(2,1)} %bitcast.236, ...), custom_call_target="tpu_custom_call" | custom-call | flops 25769803776 | bytes 30000000 | tf_op jit(solution)/shard_map/ffn_front/pallas_call | solution.py:899
  358.1 5.7 pair_scatter.2
  364.6 14.0 %ffn_rear.2 = (bf16[4,512,512]{2,1,0:T(8,128)(2,1)}, bf16[4,512,512]{2,1,0:T(8,128)(2,1)}) custom-call(s32[2]{0:T(128)} %pad_add_fusion.1.place, bf16[2048,1152]{1,0:T(8,128)(2,1)} %bitcast.191, bf16[2048,2048]{1,0:T(8,128)(2,1)} %get-tuple-element.103.hidden_units), custom_call_target="tpu_custom_call" | custom-call | flops 8589934592 | bytes 30000000 | tf_op jit(solution)/shard_map/ffn_rear/pallas_call | solution.py:973
  380.5 14.0 %ffn_rear.3 = (bf16[4,512,512]{2,1,0:T(8,128)(2,1)}, bf16[4,512,512]{2,1,0:T(8,128)(2,1)}) custom-call(s32[2]{0:T(128)} %pad_add_fusion.1.place, bf16[2048,1024]{1,0:T(8,128)(2,1)} %bitcast.197, bf16[2048,2048]{1,0:T(8,128)(2,1)} %get-tuple-element.106.hidden_units.active), custom_call_target="tpu_custom_call" | custom-call | flops 8589934592 | bytes 30000000 | tf_op jit(solution)/shard_map/ffn_rear/pallas_call | solution.py:973
  405.8 3.3 fusion.17
  410.6 18.3 %ffn_feed.1 = bf16[2048,1024]{1,0:T(8,128)(2,1)} custom-call(s32[2]{0:T(128)} %pad_add_fusion.1.place, bf16[2048,2048]{1,0:T(8,128)(2,1)} %get-tuple-element.106.hidden_units.active, bf16[4,512,512]{2,1,0:T(8,128)(2,1)} %bitcast.235, bf16[4,512,512]{2,1,0:T(8,128)(2,1)} %collective-permute-done.3.refs_3_.refs_1_), custom_call_target="tpu_custom_call" | custom-call | flops 8589934592 | bytes 30000000 | tf_op jit(solution)/shard_map/ffn_feed/pallas_call | solution.py:952
  428.9 4.8 collective-permute-done.5
  434.7 6.1 pair_gather.1
  440.8 8.0 %fusion.6 = f32[2048,640]{0,1:T(8,128)} fusion(bf16[2048,1024]{1,0:T(8,128)(2,1)} %bitcast.198, bf16[1024,1664]{1,0:T(8,128)(2,1)} %bitcast.176), kind=kOutput, calls=%fused_computation.30 | convolution fusion | flops 2684354560 | bytes 10747904 | tf_op jit(solution)/shard_map/dot_general | solution.py:20
  448.8 3.5 add_convert_fusion.1
  452.4 4.6 multiply_reduce_fusion
  463.8 20.1 %attend_back.1 = (bf16[2048,128]{1,0:T(8,128)(2,1)S(1)}, bf16[2048,256]{1,0:T(8,128)(2,1)}, bf16[2048,256]{1,0:T(8,128)(2,1)S(1)}, f32[2048,256]{1,0:T(8,128)}) custom-call(s32[4]{0:T(128)S(1)} %subtract_maximum_fusion.first, bf16[2048,128]{1,0:T(8,128)(2,1)S(1)} %copy-done.19, bf16[2048,256]{1,0:T(8,128)(2,1)S(1)} %copy-done.16, ...), custom_call_target="tpu_custom_call" | custom-call | flops 20000000000 | bytes 10000000 | tf_op jit(solution)/shard_map/attend_back/pallas_call | solution.py:811
  486.1 5.4 pair_scatter.3
  498.4 27.8 %collective-permute-done.7 = bf16[2048,256]{1,0:T(8,128)(2,1)} collective-permute-done((bf16[2048,256]{1,0:T(8,128)(2,1)}, bf16[2048,256]{1,0:T(8,128)(2,1)}, u32[]{:S(2)}, u32[]{:S(2)}) %collective-permute-start.7) | collective-permute-done | bytes 1048608 | tf_op jit(solution)/shard_map/ppermute | solution.py:1162
  531.2 3.6 add_convert_fusion
  534.8 6.2 convolution_convert_fusion.1
  541.0 5.3 concatenate.24
  546.3 36.9 %collective-permute-done.9 = bf16[2048,256]{1,0:T(8,128)(2,1)} collective-permute-done((bf16[2048,256]{1,0:T(8,128)(2,1)}, bf16[2048,256]{1,0:T(8,128)(2,1)}, u32[]{:S(2)}, u32[]{:S(2)}) %collective-permute-start.9) | collective-permute-done | bytes 1048608 | tf_op jit(solution)/shard_map/ppermute | solution.py:1162
  583.2 3.5 convert_add_fusion.1.grads
  586.7 23.3 %project_back.1 = (bf16[2048,1024]{1,0:T(8,128)(2,1)}, bf16[1024,1024]{1,0:T(8,128)(2,1)}) custom-call(bf16[2048,1024]{1,0:T(8,128)(2,1)} %bitcast.187, f32[2048,256]{1,0:T(8,128)} %convert_add_fusion.1.grads, bf16[2048,128]{1,0:T(8,128)(2,1)} %copy-done.20, bf16[2048,128]{1,0:T(8,128)(2,1)} %pad.10.out_logit, f32[2048,640]{1,0:T(8,128)} %get-tuple-element.124.projected, ...), custom_call_target="tpu_custom_call" | custom-call | flops 8589934592 | bytes 40000000 | tf_op jit(solution)/shard_map/project_back/pallas_call | solution.py:1131
  613.1 3.5 all-to-all-start
  618.2 80.7 %finish.1 = (f32[4,4,32,1024]{3,2,1,0:T(8,128)}, bf16[4,32,1024]{2,1,0:T(8,128)(2,1)}, bf16[4,32,768]{2,1,0:T(8,128)(2,1)}) custom-call(bf16[4,4,128,1024]{3,2,1,0:T(8,128)(2,1)} %bitcast.200, f32[4,128,1024]{2,1,0:T(8,128)} %bitcast.185, bf16[2,4,4,32,1024]{4,3,2,1,0:T(8,128)(2,1)} %bitcast.207, bf16[2,4,4,32,768]{4,3,2,1,0:T(8,128)(2,1)} %bitcast.188), custom_call_target="tpu_custom_call" | custom-call | bytes 200000000 | tf_op jit(solution)/shard_map/finish/pallas_call | solution.py:633
  (222 shorter events, 118.2 us)
Async XLA Ops:
  7.2 11.2 %copy-start.40 = (s32[512,16]{0,1:T(8,128)S(1)}, s32[512,16]{0,1:T(8,128)}, u32[]{:S(2)}) copy-start(s32[512,16]{0,1:T(8,128)} %param.26) | copy-start | bytes 98308
  7.2 262.3 %all-gather.7.cloned.1.call-start = ((), (), s32[]{:S(2)}) async-start(), calls=%async_computation.5 | async-start | bytes 2621440 | tf_op jit(solution)/shard_map/all_gather | solution.py:1297
  7.3 102.9 %collective-permute-start = (bf16[512,512]{1,0:T(8,128)(2,1)}, bf16[512,512]{1,0:T(8,128)(2,1)S(1)}, u32[]{:S(2)}, u32[]{:S(2)}) collective-permute-start(bf16[512,512]{1,0:T(8,128)(2,1)} %param.38), channel_id=1, source_target_pairs={{0,16},{16,0},{1,17},{17,1},{2,18},{18,2},{3,19},{19,3},{4,20},{20... | collective-permute-start | bytes 1572872 | tf_op jit(solution)/shard_map/ppermute | solution.py:993
  112.4 15.1 %copy-start.10 = (f32[1024]{0:T(1024)}, f32[1024]{0:T(1024)S(1)}, u32[]{:S(2)}) copy-start(f32[1024]{0:T(1024)S(1)} %get-tuple-element.143) | copy-start | bytes 12292
  112.4 15.1 %copy-start.11 = (f32[1024]{0:T(1024)}, f32[1024]{0:T(1024)S(1)}, u32[]{:S(2)}) copy-start(f32[1024]{0:T(1024)S(1)} %get-tuple-element.144) | copy-start | bytes 12292
  113.2 20.0 %copy-start.41 = (s32[1,3]{1,0:T(1,128)S(1)}, s32[1,3]{1,0:T(1,128)}, u32[]{:S(2)}) copy-start(s32[1,3]{1,0:T(1,128)} %param.23) | copy-start | bytes 40
  113.2 48.5 %copy-start.39 = (s32[4,16,128]{2,1,0:T(8,128)S(1)}, s32[4,16,128]{2,1,0:T(8,128)}, u32[]{:S(2)}) copy-start(s32[4,16,128]{2,1,0:T(8,128)} %get-tuple-element.95) | copy-start | bytes 98308
  128.3 367.3 %copy-start.3 = (f32[2048,128]{1,0:T(8,128)}, f32[2048,128]{1,0:T(8,128)S(1)}, u32[]{:S(2)}) copy-start(f32[2048,128]{1,0:T(8,128)S(1)} %get-tuple-element.81.sigs) | copy-start | bytes 3145732
  128.3 367.3 %copy-start.4 = (f32[2048,16]{1,0:T(8,128)}, f32[2048,16]{1,0:T(8,128)S(1)}, u32[]{:S(2)}) copy-start(f32[2048,16]{1,0:T(8,128)S(1)} %get-tuple-element.82.masks) | copy-start | bytes 393220
  128.3 26.6 %collective-permute-start.1 = (bf16[2048,256]{1,0:T(8,128)(2,1)S(1)}, bf16[2048,256]{1,0:T(8,128)(2,1)}, u32[]{:S(2)}, u32[]{:S(2)}) collective-permute-start(bf16[2048,256]{1,0:T(8,128)(2,1)S(1)} %get-tuple-element.84.refs_2_.refs_5_), channel_id=1, source_target_pairs={{0,4},{4,8},{8,12},{1,5},{5,9},{9,13},{2,6},{6,10},{10,14},{3,7},{... | collective-permute-start | bytes 3145736 | tf_op jit(solution)/shard_map/ppermute | solution.py:1162
  155.0 161.9 %all-gather.9.cloned.1.call-start = ((), (), s32[]{:S(2)}) async-start(), calls=%async_computation.6 | async-start | bytes 2621440 | tf_op jit(solution)/shard_map/all_gather | solution.py:1298
  155.7 161.2 %all-gather.11.cloned.1.call-start = ((), (), s32[]{:S(2)}) async-start(), calls=%async_computation.7 | async-start | bytes 2621440 | tf_op jit(solution)/shard_map/all_gather | solution.py:1298
  156.0 57.8 %collective-permute-start.2 = (bf16[2048,256]{1,0:T(8,128)(2,1)}, bf16[2048,256]{1,0:T(8,128)(2,1)S(1)}, u32[]{:S(2)}, u32[]{:S(2)}) collective-permute-start(bf16[2048,256]{1,0:T(8,128)(2,1)} %collective-permute-done.1.refs_1_.refs_4_), channel_id=1, source_target_pairs={{0,4},{4,8},{8,12},{1,5},{5,9},{9,13},{2,6},{6,10},{10,14},{3,7},{... | collective-permute-start | bytes 3145736 | tf_op jit(solution)/shard_map/ppermute | solution.py:1162
  198.4 508.2 %reduce-scatter.3.cloned.1.call-start = ((), (), s32[]{:S(2)}) async-start(), calls=%async_computation.3 | async-start | bytes 2621440 | tf_op jit(solution)/shard_map/reduce_scatter | solution.py:1370
  269.5 49.1 %collective-permute-start.3 = (bf16[4,512,512]{2,1,0:T(8,128)(2,1)}, bf16[4,512,512]{2,1,0:T(8,128)(2,1)}, u32[]{:S(2)}, u32[]{:S(2)}) collective-permute-start(bf16[4,512,512]{2,1,0:T(8,128)(2,1)} %bitcast.233), channel_id=1, source_target_pairs={{0,16},{16,0},{1,17},{17,1},{2,18},{18,2},{3,19},{19,3},{4,20},{20... | collective-permute-start | bytes 6291464 | tf_op jit(solution)/shard_map/ppermute | solution.py:993
  363.9 30.6 %collective-permute-start.4 = (bf16[512,1152]{1,0:T(8,128)(2,1)}, bf16[512,1152]{1,0:T(8,128)(2,1)}, u32[]{:S(2)}, u32[]{:S(2)}) collective-permute-start(bf16[512,1152]{1,0:T(8,128)(2,1)} %bitcast.36), channel_id=1, source_target_pairs={{0,2},{1,3},{2,0},{3,1},{4,6},{5,7},{6,4},{7,5},{8,10},{9,11},{10,... | collective-permute-start | bytes 3538952 | tf_op jit(solution)/shard_map/ppermute | solution.py:313
  378.6 62.2 %collective-permute-start.6 = (bf16[4,512,512]{2,1,0:T(8,128)(2,1)}, bf16[4,512,512]{2,1,0:T(8,128)(2,1)}, u32[]{:S(2)}, u32[]{:S(2)}) collective-permute-start(bf16[4,512,512]{2,1,0:T(8,128)(2,1)} %get-tuple-element.105), channel_id=1, source_target_pairs={{0,16},{16,0},{1,17},{17,1},{2,18},{18,2},{3,19},{19,3},{4,20},{20... | collective-permute-start | bytes 6291464 | tf_op jit(solution)/shard_map/ppermute | solution.py:993
  409.1 19.8 %copy-start.30 = (bf16[512,1024]{1,0:T(8,128)(2,1)}, bf16[512,1024]{1,0:T(8,128)(2,1)S(1)}, u32[]{:S(2)}) copy-start(bf16[512,1024]{1,0:T(8,128)(2,1)S(1)} %get-tuple-element.151) | copy-start | bytes 3145732
  409.1 24.6 %collective-permute-start.5 = (bf16[512,1024]{1,0:T(8,128)(2,1)S(1)}, bf16[512,1024]{1,0:T(8,128)(2,1)S(1)}, u32[]{:S(2)}, u32[]{:S(2)}) collective-permute-start(bf16[512,1024]{1,0:T(8,128)(2,1)S(1)} %get-tuple-element.151), channel_id=1, source_target_pairs={{0,2},{1,3},{2,0},{3,1},{4,6},{5,7},{6,4},{7,5},{8,10},{9,11},{10,... | collective-permute-start | bytes 3145736 | tf_op jit(solution)/shard_map/ppermute | solution.py:313
  410.5 83.7 %collective-permute-start.10 = (bf16[4,512,512]{2,1,0:T(8,128)(2,1)}, bf16[4,512,512]{2,1,0:T(8,128)(2,1)}, u32[]{:S(2)}, u32[]{:S(2)}) collective-permute-start(bf16[4,512,512]{2,1,0:T(8,128)(2,1)} %get-tuple-element.108), channel_id=1, source_target_pairs={{0,16},{16,0},{1,17},{17,1},{2,18},{18,2},{3,19},{19,3},{4,20},{20... | collective-permute-start | bytes 6291464 | tf_op jit(solution)/shard_map/ppermute | solution.py:993
  440.8 8.0 %copy-start.34 = (bf16[4,512,512]{2,1,0:T(8,128)(2,1)S(1)}, bf16[4,512,512]{2,1,0:T(8,128)(2,1)}, u32[]{:S(2)}) copy-start(bf16[4,512,512]{2,1,0:T(8,128)(2,1)} %get-tuple-element.133) | copy-start | bytes 6291460
  452.3 256.5 %reduce-scatter.5.cloned.1.call-start = ((), (), s32[]{:S(2)}) async-start(), calls=%async_computation.4 | async-start | bytes 2621440 | tf_op jit(solution)/shard_map/reduce_scatter | solution.py:1370
  463.8 22.0 %copy-start.23 = (f32[512,1024]{1,0:T(8,128)S(1)}, f32[512,1024]{1,0:T(8,128)}, u32[]{:S(2)}) copy-start(f32[512,1024]{1,0:T(8,128)} %copy-done.21) | copy-start | bytes 6291460
  463.8 22.4 %copy-start.5 = (bf16[2048,1024]{1,0:T(8,128)(2,1)S(1)}, bf16[2048,1024]{1,0:T(8,128)(2,1)}, u32[]{:S(2)}) copy-start(bf16[2048,1024]{1,0:T(8,128)(2,1)} %ffn_feed.1) | copy-start | bytes 12582916
  483.8 42.5 %collective-permute-start.7 = (bf16[2048,256]{1,0:T(8,128)(2,1)}, bf16[2048,256]{1,0:T(8,128)(2,1)}, u32[]{:S(2)}, u32[]{:S(2)}) collective-permute-start(bf16[2048,256]{1,0:T(8,128)(2,1)} %get-tuple-element.113), channel_id=1, source_target_pairs={{4,0},{8,4},{12,8},{5,1},{9,5},{13,9},{6,2},{10,6},{14,10},{7,3},{... | collective-permute-start | bytes 3145736 | tf_op jit(solution)/shard_map/ppermute | solution.py:1162
  492.8 117.2 %collective-permute-start.8 = (bf16[512,1024]{1,0:T(8,128)(2,1)}, bf16[512,1024]{1,0:T(8,128)(2,1)}, u32[]{:S(2)}, u32[]{:S(2)}) collective-permute-start(bf16[512,1024]{1,0:T(8,128)(2,1)} %bitcast.45), channel_id=1, source_target_pairs={{0,2},{1,3},{2,0},{3,1},{4,6},{5,7},{6,4},{7,5},{8,10},{9,11},{10,... | collective-permute-start | bytes 3145736 | tf_op jit(solution)/shard_map/ppermute | solution.py:313
  497.4 33.8 %copy-start.33 = (bf16[4,512,512]{2,1,0:T(8,128)(2,1)S(1)}, bf16[4,512,512]{2,1,0:T(8,128)(2,1)}, u32[]{:S(2)}) copy-start(bf16[4,512,512]{2,1,0:T(8,128)(2,1)} %get-tuple-element.135) | copy-start | bytes 6291460
  528.7 54.4 %collective-permute-start.9 = (bf16[2048,256]{1,0:T(8,128)(2,1)}, bf16[2048,256]{1,0:T(8,128)(2,1)}, u32[]{:S(2)}, u32[]{:S(2)}) collective-permute-start(bf16[2048,256]{1,0:T(8,128)(2,1)} %add_convert_fusion.3), channel_id=1, source_target_pairs={{4,0},{8,4},{12,8},{5,1},{9,5},{13,9},{6,2},{10,6},{14,10},{7,3},{... | collective-permute-start | bytes 3145736 | tf_op jit(solution)/shard_map/ppermute | solution.py:1162
  586.7 23.3 %copy-start.7 = (f32[4,128,1024]{2,1,0:T(8,128)S(1)}, f32[4,128,1024]{2,1,0:T(8,128)}, u32[]{:S(2)}) copy-start(f32[4,128,1024]{2,1,0:T(8,128)} %copy-done.6) | copy-start | bytes 6291460
  586.7 23.3 %copy-start.25 = (bf16[4,1,4,32,1024]{4,3,2,1,0:T(8,128)(2,1)S(1)}, bf16[4,1,4,32,1024]{4,3,2,1,0:T(8,128)(2,1)}, u32[]{:S(2)}) copy-start(bf16[4,1,4,32,1024]{4,3,2,1,0:T(8,128)(2,1)} %constant_dynamic-slice_fusion) | copy-start | bytes 3145732
  586.7 23.3 %copy-start.27 = (bf16[4,128,1024]{2,1,0:T(8,128)(2,1)S(1)}, bf16[4,128,1024]{2,1,0:T(8,128)(2,1)}, u32[]{:S(2)}) copy-start(bf16[4,128,1024]{2,1,0:T(8,128)(2,1)} %convert_element_type.201) | copy-start | bytes 3145732
  613.1 93.6 %all-to-all-start = ((bf16[4,128,1024]{2,1,0:T(8,128)(2,1)}), bf16[4,128,1024]{2,1,0:T(8,128)(2,1)S(1)}, u32[]{:S(2)}, u32[]{:S(2)}) async-start(bf16[4,128,1024]{2,1,0:T(8,128)(2,1)} %bitcast.202), calls=%async_computation | async-start | bytes 2097152 | tf_op jit(solution)/shard_map/all_to_all | solution.py:59
  (27 other events, 74.1 us)
Sparse Core Ops, SparseCore 0:
  155.1 61.0 all-gather.6
  217.7 43.8 all-gather.8
  263.2 44.6 all-gather.10
  452.4 58.2 reduce-scatter.2
  534.9 57.8 reduce-scatter.4

commit v6 on v5

--- a/solution.py
+++ b/solution.py
@@ -16,40 +16,14 @@
 TOK = ("group", "level", "head")
 
 
-def matmul(left_side, right_side):
-    return jnp.dot(left_side, right_side, preferred_element_type=jnp.float32)
-
-
 def transposed(left_side, right_side):
     return lax.dot_general(
         left_side, right_side, (((1,), (1,)), ((), ())), preferred_element_type=jnp.float32
     )
 
 
-def contract_rows(left_side, right_side):
-    return lax.dot_general(
-        left_side, right_side, (((0,), (0,)), ((), ())), preferred_element_type=jnp.float32
-    )
-
-
 def low(value):
     return value.astype(jnp.bfloat16)
-
-
-def layer_norm(inputs, gain_vec, bias_vec):
-    centred = inputs - jnp.mean(inputs, axis=-1, keepdims=True)
-    inverse = lax.rsqrt(jnp.mean(centred * centred, axis=-1, keepdims=True) + 1e-05)
-    scaled = centred * inverse
-    return (scaled * gain_vec + bias_vec, scaled, inverse)
-
-
-def norm_back(grad_normed, gain_vec, scaled, inverse):
-    inner_grad = grad_normed * gain_vec
-    return inverse * (
-        inner_grad
-        - jnp.mean(inner_grad, axis=-1, keepdims=True)
-        - scaled * jnp.mean(inner_grad * scaled, axis=-1, keepdims=True)
-    )
 
 
 def to_home(rows):
@@ -313,10 +287,6 @@
     return lax.ppermute(rows, "head", [(i, (i + 2) % HEADS) for i in range(HEADS)])
 
 
-def after(value, *others):
-    return lax.optimization_barrier((value,) + others)[0]
-
-
 def ring(axis):
     me, size = lax.axis_index(axis), lax.axis_size(axis)
     ahead = [lax.rem(me + k, size) for k in range(1, size)]
@@ -338,8 +308,8 @@
 
 
 def start_kernel(
-    tokens, cotangents, weights, tables, picks, order,
-    rows, grads, full, routes, chosen_rows, orders, own_sem, *sems
+    tokens, cotangents, value, output, query, key, extra, tables, picks, order,
+    rows, grads, full, routes, chosen_rows, orders, weights, own_sem, *sems
 ):
     sems = iter(sems)
 
@@ -351,6 +321,13 @@
     head = lax.axis_index("head")
     near, far = partners(head)
     mates = [near, far, HEADS - 1 - head]
+    for to in range(HEADS):
+        at = 0
+        for part in (value, output, query, key):
+            size = part.shape[1] // HEADS
+            weights[to, :, at : at + size] = part[:, to * size : (to + 1) * size]
+            at += size
+        weights[to, :, at:] = extra[to]
     greet_all(
         [{"head": m} for m in mates]
         + [{"level": n} for n in levels_ahead]
@@ -462,13 +439,15 @@
         own[i].wait()
 
 
-def start(tokens, cotangents, weights, tables, picks, order):
+def start(tokens, cotangents, weights, extra, tables, picks, order):
     groups, levels = lax.axis_size("group"), lax.axis_size("level")
     _, _, piece, width = tokens.shape
+    columns = sum(part.shape[1] for part in weights) // HEADS + extra.shape[2]
+    block = extra.shape[:2] + (columns,)
     shapes = [
         jax.ShapeDtypeStruct((HEADS, HEADS, levels, piece, width), tokens.dtype),
         jax.ShapeDtypeStruct((HEADS, levels, piece, width), tokens.dtype),
-        jax.ShapeDtypeStruct((groups, levels) + weights.shape, weights.dtype),
+        jax.ShapeDtypeStruct((groups, levels) + block, extra.dtype),
         jax.ShapeDtypeStruct(tables.shape, tables.dtype),
         jax.ShapeDtypeStruct(picks.shape, picks.dtype),
         jax.ShapeDtypeStruct((levels, HEADS) + order.shape, order.dtype),
@@ -480,17 +459,18 @@
     return pl.pallas_call(
         start_kernel,
         out_shape=shapes,
-        in_specs=[pl.BlockSpec(memory_space=pltpu.VMEM)] * 6,
+        in_specs=[pl.BlockSpec(memory_space=pltpu.VMEM)] * 10,
         out_specs=[pl.BlockSpec(memory_space=pl.ANY)] * 6,
-        scratch_shapes=[dma((6,))] + [dma(c) for c in counts for _ in range(2)],
+        scratch_shapes=[pltpu.VMEM(block, extra.dtype), dma((6,))] + [dma(c) for c in counts for _ in range(2)],
         compiler_params=pltpu.CompilerParams(collective_id=9, has_side_effects=True),
         cost_estimate=cost(0, 200e6),
         name="start",
-    )(tokens, cotangents, weights, tables, picks, order)
-
-
-def finish_kernel(count, *refs):
+    )(tokens, cotangents, *weights, extra, tables, picks, order)
+
+
+def finish_kernel(layout, *refs):
     refs = iter(refs)
+    count = len(layout)
 
     def take(n):
         return [next(refs) for _ in range(n)]
@@ -498,9 +478,9 @@
     part, middle = take(2)
     grads = take(count)
     (home_grad,) = take(1)
-    owned = take(count)
+    results = [take(len(pieces)) for pieces in layout]
     near_buf, send_buf, far_buf, total, back_buf, came_buf = take(6)
-    group_buf, level_send, level_buf, head_send = (take(count) for _ in range(4))
+    group_buf, level_send, level_buf, head_send, owned = (take(count) for _ in range(5))
 
     def pair():
         return next(refs), next(refs)
@@ -615,11 +595,19 @@
         home_grad[source] = came_buf[source].astype(jnp.float32)
     for copy in sharing:
         copy.wait_recv()
+    for p in sets:
+        for out, (first_column, size, joined) in zip(results[p], layout[p]):
+            for h in range(HEADS):
+                value = owned[p][h, :, first_column : first_column + size].astype(jnp.float32)
+                if joined:
+                    out[:, h * size : (h + 1) * size] = value
+                else:
+                    out[h] = value
     for copy in started:
         copy.wait_send()
 
 
-def finish(part, middle, *grads):
+def finish(layout, part, middle, *grads):
     groups, levels = lax.axis_size("group"), lax.axis_size("level")
     _, count, width = middle.shape
     piece = count // levels
@@ -630,12 +618,16 @@
     counts = [(2, HEADS), (HEADS,), (levels - 1,)]
     counts += [(sets, groups - 1, levels), (sets, levels - 1), (sets, HEADS - 1)]
     vmem = pl.BlockSpec(memory_space=pltpu.VMEM)
+    shapes = []
+    for pieces in layout:
+        for _, size, joined in pieces:
+            shape = (blocks[0][1], HEADS * size) if joined else (HEADS, blocks[0][1], size)
+            shapes.append(jax.ShapeDtypeStruct(shape, jnp.float32))
     return pl.pallas_call(
-        functools.partial(finish_kernel, sets),
-        out_shape=[jax.ShapeDtypeStruct((levels, HEADS, piece, width), jnp.float32)]
-        + [jax.ShapeDtypeStruct(block, low_type) for block in blocks],
+        functools.partial(finish_kernel, layout),
+        out_shape=[jax.ShapeDtypeStruct((levels, HEADS, piece, width), jnp.float32)] + shapes,
         in_specs=[vmem] * (2 + sets),
-        out_specs=[vmem] * (1 + sets),
+        out_specs=[vmem] * (1 + len(shapes)),
         scratch_shapes=[
             pltpu.VMEM((2, HEADS, count, width), low_type),
             pltpu.VMEM((HEADS, count, width), low_type),
@@ -647,7 +639,7 @@
         + [pltpu.VMEM((groups - 1, levels) + block, low_type) for block in blocks]
         + [pltpu.VMEM((levels,) + block, low_type) for block in blocks]
         + [pltpu.VMEM((levels - 1,) + block, low_type) for block in blocks]
-        + [pltpu.VMEM(block, low_type) for block in blocks]
+        + [pltpu.VMEM(block, low_type) for block in blocks] * 2
         + [dma(c) for c in counts for _ in range(2)],
         compiler_params=pltpu.CompilerParams(
             collective_id=10, has_side_effects=True, vmem_limit_bytes=56 * 2**20
@@ -988,6 +980,172 @@
     )(place, rows_in, units)
 
 
+def named_by(routes, count):
+    lane = lax.broadcasted_iota(jnp.int32, (routes.shape[0], count), 1)
+    member = jnp.zeros(lane.shape, jnp.float32)
+    for slot in range(routes.shape[1]):
+        member = jnp.where(lane == routes[:, slot : slot + 1], 1.0, member)
+    return member
+
+
+def middle_kernel(rows, branch, routes, router, gain, bias, middle, extended, sig_out):
+    experts = router.shape[1]
+    width = rows.shape[1]
+    rounded = branch[...].astype(jnp.bfloat16).astype(jnp.float32)
+    value = rows[...].astype(jnp.float32) + rounded
+    middle[...] = value
+    _, _, normed = normalized(value, gain[...], bias[...])
+    sig = 1.0 / (1.0 + jnp.exp2(-LOG2E * dot(normed, router[...], 1, 0)))
+    sig_out[...] = sig
+    extended[:, :width] = value.astype(jnp.bfloat16)
+    gates = (sig * named_by(routes[...], experts)).astype(jnp.bfloat16)
+    spare = extended.shape[1] - width - experts
+    if spare:
+        gates = jnp.concatenate([gates, jnp.zeros((gates.shape[0], spare), gates.dtype)], axis=1)
+    extended[:, width:] = gates
+
+
+def enter_ffn(rows, branch, routes, router, gain, bias):
+    count, width = rows.shape
+    experts = router.shape[1]
+    wide = width + experts + -experts % 128
+    return pl.pallas_call(
+        middle_kernel,
+        out_shape=[
+            jax.ShapeDtypeStruct((count, width), jnp.float32),
+            jax.ShapeDtypeStruct((count, wide), jnp.bfloat16),
+            jax.ShapeDtypeStruct((count, experts), jnp.float32),
+        ],
+        compiler_params=pltpu.CompilerParams(vmem_limit_bytes=40 * 2**20),
+        cost_estimate=cost(1e9, 1e7),
+        name="middle",
+    )(rows, branch, routes, router, gain, bias)
+
+
+def leave_kernel(
+    middle, own, came, cotangent, sigs, routes, router, gain, bias, grad_out, low_out, weight_grads
+):
+    experts = router.shape[1]
+    count, width = middle.shape
+    scaled, inverse, normed = normalized(middle[...], gain[...], bias[...])
+    total = own[...] + came[...].astype(jnp.float32)
+    sig = sigs[...]
+    member = named_by(routes[...], experts)
+    gate_grads = total[:, width : width + experts]
+    logit = (gate_grads * sig * (1.0 - sig) * member).astype(jnp.bfloat16)
+    second = dot(logit, router[...], 1, 1)
+    inner_grad = second * gain[...]
+    inner_grad = inverse * (
+        inner_grad
+        - jnp.mean(inner_grad, axis=1, keepdims=True)
+        - scaled * jnp.mean(inner_grad * scaled, axis=1, keepdims=True)
+    )
+    grad = cotangent[...].astype(jnp.float32) + total[:, :width] + inner_grad
+    grad_out[...] = grad
+    low_out[...] = grad.astype(jnp.bfloat16)
+    spare = weight_grads.shape[1] - experts
+    sums = [
+        jnp.sum(second * scaled, axis=0, keepdims=True),
+        jnp.sum(second, axis=0, keepdims=True),
+        jnp.zeros((126, width), jnp.float32),
+    ]
+    side = jnp.concatenate(sums, axis=0).T[:, :spare]
+    both = jnp.concatenate([dot(normed, logit, 0, 0), side], axis=1)
+    weight_grads[...] = both.astype(jnp.bfloat16)
+
+
+def leave_ffn(middle, own, came, cotangent, sigs, routes, router, gain, bias):
+    count, width = middle.shape
+    experts = router.shape[1]
+    columns = experts + 2 + -(experts + 2) % 128
+    return pl.pallas_call(
+        leave_kernel,
+        out_shape=[
+            jax.ShapeDtypeStruct((count, width), jnp.float32),
+            jax.ShapeDtypeStruct((count, width), jnp.bfloat16),
+            jax.ShapeDtypeStruct((width, columns), jnp.bfloat16),
+        ],
+        compiler_params=pltpu.CompilerParams(vmem_limit_bytes=48 * 2**20),
+        cost_estimate=cost(1e9, 1e7),
+        name="leave_ffn",
+    )(middle, own, came, cotangent, sigs, routes, router, gain, bias)
+
+
+def branch_back_kernel(
+    grads, w_output, attended, sigs, masks, grad_attended, inner, out_logit, weight_grads, acc
+):
+    at = pl.program_id(0)
+    count = grads.shape[0]
+    sig, mask, values = sigs[...], masks[...], attended[...]
+    mixed_grad = dot(grads[...], w_output[...], 1, 0)
+    lane = lax.broadcasted_iota(jnp.int32, (count, 128), 1)
+    logits = jnp.zeros((count, 128), jnp.float32)
+    total = jnp.zeros((count, DH), jnp.float32)
+    parts = []
+    for e in range(VEXP):
+        k = VEXP + e
+        one, on = sig[:, k : k + 1], mask[:, k : k + 1]
+        part = mixed_grad[:, e * DH : (e + 1) * DH]
+        total += part * (one * on)
+        gate_grad = jnp.sum(part * values, axis=1, keepdims=True)
+        logits = jnp.where(lane == k, gate_grad * one * (1.0 - one) * on, logits)
+        parts.append((one * on * values).astype(jnp.bfloat16))
+    out_logit[...] = logits.astype(jnp.bfloat16)
+    rounded = total.astype(jnp.bfloat16)
+    grad_attended[...] = rounded
+    product = rounded.astype(jnp.float32) * values
+    inner[0] = jnp.sum(product.T, axis=0, keepdims=True)
+    amount = dot(grads[...], jnp.concatenate(parts, axis=1), 0, 0)
+
+    @pl.when(at == 0)
+    def _():
+        acc[...] = amount
+
+    @pl.when(at > 0)
+    def _():
+        acc[...] += amount
+
+    @pl.when(at == pl.num_programs(0) - 1)
+    def _():
+        weight_grads[...] = acc[...].astype(jnp.bfloat16)
+
+
+def branch_back(grads, full, attended, sigs, masks):
+    rows, width = grads.shape
+    values = VEXP * DH
+
+    def by_row(size):
+        return pl.BlockSpec((BLOCK, size), lambda i: (i, 0))
+
+    return pl.pallas_call(
+        branch_back_kernel,
+        grid=(rows // BLOCK,),
+        in_specs=[
+            by_row(width),
+            pl.BlockSpec((width, values), lambda i: (0, 1), pipeline_mode=pl.Buffered(1)),
+            by_row(DH),
+            by_row(128),
+            by_row(16),
+        ],
+        out_specs=[
+            by_row(DH),
+            pl.BlockSpec((1, 1, BLOCK), lambda i: (i, 0, 0)),
+            by_row(128),
+            pl.BlockSpec((width, values), lambda i: (0, 0)),
+        ],
+        out_shape=[
+            jax.ShapeDtypeStruct((rows, DH), jnp.bfloat16),
+            jax.ShapeDtypeStruct((rows // BLOCK, 1, BLOCK), jnp.float32),
+            jax.ShapeDtypeStruct((rows, 128), jnp.bfloat16),
+            jax.ShapeDtypeStruct((width, values), jnp.bfloat16),
+        ],
+        scratch_shapes=[pltpu.VMEM((width, values), jnp.float32)],
+        compiler_params=pltpu.CompilerParams(vmem_limit_bytes=48 * 2**20),
+        cost_estimate=cost(4 * rows * width * values, 2e7),
+        name="branch_back",
+    )(grads, full, attended, sigs, masks)
+
+
 def turn(value, axis, by):
     size = lax.axis_size(axis)
     return lax.ppermute(value, axis, [(i, (i + by) % size) for i in range(size)])
@@ -1150,12 +1308,6 @@
     )(rows, grads, grad_query, out_logit, projected, sigs, masks, full, full, full, full, gain, bias)
 
 
-def chosen(routes, options):
-    return jnp.sum(
-        (routes[..., None] == jnp.arange(options, dtype=jnp.int32)).astype(jnp.float32), axis=-2
-    )
-
-
 def shift(value, axis, by):
     count = lax.axis_size(axis)
     pairs = [(i, i + by) for i in range(count) if 0 <= i + by < count]
@@ -1206,12 +1358,8 @@
     )
     shared = small.shape[1]
     pad = -(shared + 2 * VEXP) % 128
-    packed = jnp.concatenate(
+    extra = jnp.concatenate(
         [
-            value_weight.reshape(wrows, HEADS, VEXP * DH),
-            output_weight.reshape(wrows, HEADS, VEXP * DH),
-            query_weight.reshape(wrows, HEADS, DH),
-            key_weight.reshape(wrows, HEADS, DH),
             value_router.reshape(wrows, HEADS, VEXP),
             output_router.reshape(wrows, HEADS, VEXP),
             jnp.broadcast_to(small[:, None, :], (wrows, HEADS, shared)),
@@ -1219,7 +1367,7 @@
         ],
         axis=2,
     )
-    cols = packed.shape[2]
+    cols = 2 * DH + 2 * VEXP * DH + extra.shape[2]
     tables = jnp.concatenate(
         [value_routes.transpose(1, 2, 0), output_routes.transpose(1, 2, 0)], axis=1
     )
@@ -1227,7 +1375,8 @@
     arrived, own_grads, full, tables, picks, orders = start(
         tokens_in.reshape(levels, HEADS, piece, width),
         out_grad.reshape(levels, HEADS, piece, width),
-        packed.transpose(1, 0, 2),
+        [value_weight, output_weight, query_weight, key_weight],
+        extra.transpose(1, 0, 2),
         tables,
         picks,
         deal_order,
@@ -1235,12 +1384,22 @@
     worker_in = arrived.reshape(HEADS * count, width)
     own_tokens = lax.dynamic_index_in_dim(arrived, head, 1, keepdims=False).reshape(count, width)
     in_rows = [turn(ffn_in, "group", k) for k in range(1, groups)]
-    full, in_rows = lax.optimization_barrier((full.reshape(width, cols), in_rows))
+    full, in_rows, ffn_out = lax.optimization_barrier(
+        (full.reshape(width, cols), in_rows, ffn_out)
+    )
 
     base = 2 * DH + 2 * VEXP * DH
     w_output = full[:, VEXP * DH : 2 * VEXP * DH]
     at = base + 2 * VEXP
-    r_ffn = full[:, at : at + experts]
+    def relabelled(expert):
+        share = expert // local_experts
+        return (share % HEADS * levels + share // HEADS) * local_experts + expert % local_experts
+
+    labels = jnp.arange(experts, dtype=jnp.int32)
+    moved = low(relabelled(labels)[:, None] == labels[None, :])
+    r_ffn = low(
+        jnp.dot(full[:, at : at + experts], moved, preferred_element_type=jnp.float32)
+    )
     gain_one, bias_one, gain_two, bias_two = (
         full[:, at + experts + i].astype(jnp.float32) for i in range(4)
     )
@@ -1281,23 +1440,25 @@
     first_block = starts_of(level * rows + jnp.arange(blocks, dtype=jnp.int32) * BLOCK) // BLOCK
     first_block = jnp.maximum(first_block - base_block, 0)
 
+    own_routes = picks.reshape(levels, -1, HEADS, piece).transpose(2, 0, 3, 1).reshape(count, -1)
+    own_routes = relabelled(own_routes)
+    ffn_side = (own_routes, r_ffn, gain_two[None], bias_two[None], own_tokens)
+
     window = [key_value]
     own_grads = own_grads.reshape(count, width)
     for i in range(reach):
         came = shift(window[0], "level", 1)
         if i == 0:
-            came, own_grads, pos_all, starts, ffn_out, in_rows = lax.optimization_barrier(
-                (came, own_grads, pos_all, starts, ffn_out, [ffn_in] + in_rows)
+            came, own_grads, pos_all, starts, in_rows = lax.optimization_barrier(
+                (came, own_grads, pos_all, starts, [ffn_in] + in_rows)
             )
             cotangent = level_gather(own_grads, 5, True)
         if i == reach - 1:
-            came, cotangent = lax.optimization_barrier((came, cotangent))
+            came, cotangent, ffn_side = lax.optimization_barrier((came, cotangent, ffn_side))
         window.insert(0, came)
     place = jnp.stack([head, lax.axis_index("group")])
     out_here = lax.all_gather(ffn_out, "level", axis=0)
     w_in = [lax.all_gather(part, "level", axis=0) for part in in_rows]
-
-    own_routes = picks.reshape(levels, -1, HEADS, piece).transpose(2, 0, 3, 1).reshape(count, -1)
 
 
     def lines(values):
@@ -1316,20 +1477,13 @@
     out_mask = masks[:, VEXP : 2 * VEXP]
     out_gate = out_sig * out_mask
     mixed = low((out_gate[..., None] * attended[:, None, :]).reshape(rows, VEXP * DH))
-    branch = low(level_scatter(low(transposed(mixed, w_output)), 2))
+    branch = level_scatter(low(transposed(mixed, w_output)), 2)
     branch, out_here = lax.optimization_barrier((branch, out_here))
     w_out = [out_here] + [turn(out_here, "group", k) for k in range(1, groups)]
-    middle = own_tokens.astype(jnp.float32) + branch.astype(jnp.float32)
-
-    normed_mid, scaled_two, inverse_two = layer_norm(middle, gain_two, bias_two)
-    normed_two = low(normed_mid)
-    ffn_sig = jax.nn.sigmoid(matmul(normed_two, r_ffn))
-    member = chosen(own_routes, experts)
-    shares = (ffn_sig * member).reshape(count, levels, HEADS, local_experts)
-    shares = jnp.swapaxes(shares, 1, 2).reshape(count, experts)
-    spare = -experts % 128
-    extended = jnp.concatenate([middle, shares], axis=1)
-    hidden = level_gather(jnp.pad(low(extended), ((0, 0), (0, spare))), 3, True)
+
+    own_routes, r_ffn, gain_two, bias_two, own_tokens = ffn_side
+    middle, extended, ffn_sig = enter_ffn(own_tokens, branch, own_routes, r_ffn, gain_two, bias_two)
+    hidden = level_gather(extended, 3, True)
     mine = levels * local_experts
     gates = lax.dynamic_slice_in_dim(hidden, width + head * mine, mine, 1).astype(jnp.float32)
     active, grad_pre, grad_rows = ffn_front(
@@ -1342,22 +1496,9 @@
     grad_out = ffn_rear(place, cotangent, active, width, groups, levels)
     out_came = [turn(grad_out[k], "group", k) for k in range(1, groups)]
     came, grad_in, grad_out = lax.optimization_barrier((came, grad_in, grad_out))
-    summed = summed + came.astype(jnp.float32)
-
-    gate_grads = summed[:, width : width + experts].reshape(count, HEADS, levels, local_experts)
-    gate_grads = jnp.swapaxes(gate_grads, 1, 2).reshape(count, experts)
-    grad_logit = low(gate_grads * ffn_sig * (1.0 - ffn_sig) * member)
-    grad_second = transposed(grad_logit, r_ffn)
-    grad_r_ffn = contract_rows(normed_two, grad_logit)
-    grad_gain_two = jnp.sum(grad_second * scaled_two, axis=0)
-    grad_bias_two = jnp.sum(grad_second, axis=0)
-    grad_middle = (
-        own_grads.astype(jnp.float32)
-        + summed[:, :width]
-        + norm_back(grad_second, gain_two, scaled_two, inverse_two)
-    )
-
-    own_branch = low(grad_middle)
+    grad_middle, own_branch, early = leave_ffn(
+        middle, summed, came, own_grads, ffn_sig, own_routes, r_ffn, gain_two, bias_two
+    )
     came = to_far(own_branch)
     feed = ffn_feed(place, active, w_out)
     came, feed = lax.optimization_barrier((came, feed))
@@ -1371,11 +1512,9 @@
 
     grad_branch, in_came = lax.optimization_barrier((grad_branch, in_came))
     ffn_in_grad = sum_over_rows(grad_in, in_came)
-    grad_mixed = matmul(grad_branch, w_output).reshape(rows, VEXP, DH)
-    grad_out_gate = jnp.sum(grad_mixed * attended[:, None, :], axis=-1)
-    grad_attended = low(jnp.sum(grad_mixed * out_gate[..., None], axis=1))
-    grad_out_logit = low(grad_out_gate * out_sig * (1.0 - out_sig) * out_mask)
-    row_inner = jnp.sum(grad_attended.astype(jnp.float32) * attended, axis=-1)
+    grad_attended, row_inner, grad_out_logit, grad_w_output = branch_back(
+        grad_branch, full, attended, sigs, masks
+    )
     grad_queries, *grad_window = attend_back(
         first_block,
         queries,
@@ -1384,29 +1523,16 @@
         lines(positions),
         lines(starts),
         log_total,
-        lines(row_inner),
+        row_inner,
         pos_all[:, None],
     )
     came = shift(grad_window[0], "level", -1)
     grad_queries, out_came = lax.optimization_barrier((grad_queries, out_came))
     ffn_out_grad = sum_over_rows(grad_out, out_came)
     fed, beyond = pair_scatter(feed, 6, True)
-    grad_w_output = contract_rows(grad_branch, mixed)
-    early = jnp.concatenate(
-        [
-            low(grad_w_output),
-            low(grad_r_ffn),
-            low(grad_gain_two)[:, None],
-            low(grad_bias_two)[:, None],
-            jnp.zeros((width, -(experts + 2) % 128), jnp.bfloat16),
-        ],
-        axis=1,
-    )
     for i in range(1, reach + 1):
         if i < reach:
             came, fed = lax.optimization_barrier((came, fed))
-        else:
-            came, early = lax.optimization_barrier((came, early))
         grad_both = grad_window[i].astype(jnp.float32) + came.astype(jnp.float32)
         if i < reach:
             grad_keys_sent = low(grad_both)
@@ -1416,7 +1542,7 @@
         worker_in,
         grad_both,
         grad_queries,
-        jnp.pad(grad_out_logit, ((0, 0), (VEXP, 128 - 2 * VEXP))),
+        grad_out_logit,
         projected,
         sigs,
         masks,
@@ -1428,21 +1554,31 @@
     fed_far, grad_inputs = lax.optimization_barrier((fed_far, grad_inputs))
     layer_out = to_home(low(middle + fed + fed_far.astype(jnp.float32)))
 
-    input_grad, owned, early = finish(
+    values = VEXP * DH
+    layout = (
+        ((0, values, True), (values, DH, True), (values + DH, DH, True), (values + 2 * DH, DH, False)),
+        ((0, values, True),),
+        ((0, early.shape[1], False),),
+    )
+
+    def by_owner(grads):
+        return grads.reshape(groups, levels, HEADS, wrows, -1)
+
+    input_grad, grad_value, grad_query, grad_key, sides, grad_output, common = finish(
+        layout,
         grad_inputs.reshape(HEADS, HEADS, levels * piece, width),
         grad_middle.reshape(HEADS, levels * piece, width),
-        late.reshape(groups, levels, HEADS, wrows, -1),
-        early.reshape(groups, levels, HEADS, wrows, -1),
-    )
-    owned, early = owned.astype(jnp.float32), early.astype(jnp.float32)
-
-    def columns(part, first, size):
-        return part[:, :, first : first + size].transpose(1, 0, 2).reshape(wrows, HEADS * size)
-
-    values = VEXP * DH
-    misc = values + 2 * DH
-    common = jnp.sum(early[:, :, values:], axis=0)
-    norms = jnp.sum(owned[:, :, misc + 2 * VEXP :], axis=0)
+        by_owner(late),
+        by_owner(grad_w_output),
+        by_owner(early),
+    )
+    norms = jnp.sum(sides[:, :, 2 * VEXP : 2 * VEXP + 2], axis=0)
+    common = jnp.sum(common[:, :, : experts + 2], axis=0)
+    router_grad = common[:, :experts].reshape(wrows, HEADS, levels, local_experts)
+
+    def side(first):
+        return sides[:, :, first : first + VEXP].transpose(1, 0, 2).reshape(wrows, HEADS * VEXP)
+
     return (
         layer_out,
         input_grad.reshape(count, width),
@@ -1450,13 +1586,13 @@
         norms[:, 1],
         common[:, experts],
         common[:, experts + 1],
-        columns(owned, values, DH),
-        columns(owned, values + DH, DH),
-        columns(owned, 0, values),
-        columns(early, 0, values),
-        columns(owned, misc, VEXP),
-        columns(owned, misc + VEXP, VEXP),
-        common[:, :experts],
+        grad_query,
+        grad_key,
+        grad_value,
+        grad_output,
+        side(0),
+        side(VEXP),
+        jnp.swapaxes(router_grad, 1, 2).reshape(wrows, experts),
         ffn_in_grad.astype(jnp.float32),
         ffn_out_grad.astype(jnp.float32),
     )

time: 733 us -> 735 us (level)
  waiting for transfers between devices: 108 us -> 153 us
  Pallas kernels: 429 us -> 454 us
  other arithmetic: 54.9 us -> 31.2 us
  local copies, waits for them, and re-layouts: 62.6 us -> 42.4 us
  matrix products: 25.4 us -> 6.3 us
    ppermute x4, waiting for transfers between devices: 101 us -> 142 us  [shift(): return lax.ppermute(value, axis, pairs)]
    pallas_call x1 -> x4, Pallas kernels: 80.7 us -> 104 us  [the longest x1 81.6 us: finish(): pl.pallas_call(functools.partial(finish_kernel, layout), out_shape=[jax.S...]
    dot_general x4 -> x1, matrix products: 16.6 us -> 1.24 us  [body(): jnp.dot(full[:, at:at + experts], moved, preferred_element_type=jnp.float32)]
    convert_element_type x9 -> x5, other arithmetic: 20.6 us -> 9.41 us  [low(): return value.astype(jnp.bfloat16)]
    reshape x14 -> x2, local copies, waits for them, and re-layouts: 8.83 us -> 1.22 us  [side(): sides[:, :, first:first + VEXP].transpose(1, 0, 2)]
    unnamed x90 -> x92, local copies, waits for them, and re-layouts: 21.2 us -> 22.6 us
  transfers between devices with their start and end apart: 17 -> 17, of which waited for: 6 -> 6; matrix products, arithmetic and copies ran while one was open for 16% -> 8% of each run, Pallas kernels for 52% -> 57%
where the time goes in v6:
time: 735 us; the launch traced here: 724 us
  Pallas kernels  454 us (62%)
  waiting for transfers between devices  153 us (21%)
  local copies, waits for them, and re-layouts  42.4 us (6%)
  other arithmetic  31.2 us (4%)
  starting transfers between devices  22.5 us (3%)
  between operations  14.6 us (2%)
    ppermute x4, waiting for transfers between devices, shift(): return lax.ppermute(value, axis, pairs)  142 us
    pallas_call x1, Pallas kernels, start(): pl.pallas_call(start_kernel, out_shape=shapes, in_specs=[pl.BlockSpec(mem...  89.7 us
    pallas_call x1, Pallas kernels, finish(): pl.pallas_call(functools.partial(finish_kernel, layout), out_shape=[jax.S...  81.6 us
    pallas_call x2, Pallas kernels, level_gather(): pl.pallas_call(functools.partial(gather_kernel, by_source), out_shape=jax...  59.5 us
    pallas_call x1, Pallas kernels, ffn_front(): pl.pallas_call(functools.partial(front_kernel, groups, local), grid_spec=...  36.9 us
    pallas_call x2, Pallas kernels, ffn_rear(): pl.pallas_call(functools.partial(rear_kernel, groups), grid_spec=pltpu.Pr...  28.2 us
    pallas_call x1, Pallas kernels, level_scatter(): pl.pallas_call(functools.partial(scatter_kernel, by_source), out_shape=ja...  27.3 us
    pallas_call x1, Pallas kernels, project_back(): pl.pallas_call(project_back_kernel, grid=(HEADS,), in_specs=[by_row(width...  23.4 us
  transfers between devices with their start and end apart: 17, of which 6 were waited for; matrix products, arithmetic and copies ran while one was open for 8% of the time, Pallas kernels for 57%

profile of v6, /device:TPU:8, one launch (start us, length us, event | category | flops | bytes accessed | tf_op | source)
XLA Modules:
  0.0 724.2 jit_solution(6609516588886097763)
XLA Ops:
  17.0 89.7 %start.1 = (bf16[4,4,4,32,1024]{4,3,2,1,0:T(8,128)(2,1)}, bf16[4,4,32,1024]{3,2,1,0:T(8,128)(2,1)}, bf16[2,4,4,32,1664]{4,3,2,1,0:T(8,128)(2,1)}, s32[4,4,512]{2...) custom-call(bf16[4,4,32,1024]{3,2,1,0:T(8,128)(2,1)} %bitcast.168, bf16[4,4,32,1024]{3,2,1,0:T(8,128)(2,1)} %bitcast.169, ...), custom_call_target="tpu_custom_call" | custom-call | bytes 200000000 | tf_op jit(solution)/shard_map/start/pallas_call | solution.py:459
  111.4 14.3 %project.1 = (bf16[2048,128]{1,0:T(8,128)(2,1)S(1)}, bf16[2048,256]{1,0:T(8,128)(2,1)S(1)}, f32[2048,640]{1,0:T(8,128)}, f32[2048,128]{1,0:T(8,128)S(1)}, f32[2048,16]{1,0:T(8,128)S(1)}) custom-call(bf16[2048,1024]{1,0:T(8,128)(2,1)} %bitcast.153, bf16[1024,1664]{1,0:T(8,128)(2,1)} %bitcast.142, bf16[1024,1664]{1,0:T(8,128)(2,1)} %bitcast.143, ...), custom_call_target="tpu_custom_call" | custom-call | flops 4294967296 | bytes 20000000 | tf_op jit(solution)/shard_map/project/pallas_call | solution.py:1209
  131.1 47.0 %collective-permute-done.1.refs_1_.refs_4_ = bf16[2048,256]{1,0:T(8,128)(2,1)} collective-permute-done((bf16[2048,256]{1,0:T(8,128)(2,1)S(1)}, bf16[2048,256]{1,0:T(8,128)(2,1)}, u32[]{:S(2)}, u32[]{:S(2)}) %collective-permute-start.1) | collective-permute-done | bytes 1048608 | tf_op jit(solution)/shard_map/ppermute | solution.py:1314
  178.5 2.3 constant_dynamic-slice_fusion
  180.8 4.5 collective-permute-start.2
  195.0 28.6 %level_gather.2 = bf16[4,4,128,1024]{3,2,1,0:T(8,128)(2,1)} custom-call(bf16[4,128,1024]{2,1,0:T(8,128)(2,1)} %bitcast.119), custom_call_target="tpu_custom_call" | custom-call | bytes 90000000 | tf_op jit(solution)/shard_map/level_gather/pallas_call | solution.py:105
  224.1 17.6 %collective-permute-done.2.refs_0_.refs_3_ = bf16[2048,256]{1,0:T(8,128)(2,1)} collective-permute-done((bf16[2048,256]{1,0:T(8,128)(2,1)}, bf16[2048,256]{1,0:T(8,128)(2,1)}, u32[]{:S(2)}, u32[]{:S(2)}) %collective-permute-start.2) | collective-permute-done | bytes 1048608 | tf_op jit(solution)/shard_map/ppermute | solution.py:1314
  242.8 16.2 %attend.1 = (f32[2048,128]{1,0:T(8,128)S(1)}, f32[4,1,512]{2,1,0:T(1,128)S(1)}) custom-call(s32[4]{0:T(128)S(1)} %subtract_maximum_fusion.first, bf16[2048,128]{1,0:T(8,128)(2,1)S(1)} %copy-done.27, bf16[2048,256]{1,0:T(8,128)(2,1)} %collective-permute-done.2.refs_0_.refs_3_, bf16[2048,256]{1,0:T(8,128)(2,1)} %collective-permute-done.1.refs_1_.refs_4_, ...), custom_call_target="tpu_custom_call" | custom-call | flops 20000000000 | bytes 10000000 | tf_op jit(solution)/shard_map/attend/pallas_call | solution.py:719
  260.0 5.1 convolution_convert_fusion
  265.1 27.3 %level_scatter.1 = f32[4,128,1024]{2,1,0:T(8,128)S(1)} custom-call(bf16[4,4,128,1024]{3,2,1,0:T(8,128)(2,1)S(1)} %bitcast.117), custom_call_target="tpu_custom_call" | custom-call | bytes 80000000 | tf_op jit(solution)/shard_map/level_scatter/pallas_call | solution.py:167
  301.3 30.9 %level_gather.3 = bf16[4,4,128,1152]{3,2,1,0:T(8,128)(2,1)} custom-call(bf16[4,128,1152]{2,1,0:T(8,128)(2,1)} %bitcast.125), custom_call_target="tpu_custom_call" | custom-call | bytes 90000000 | tf_op jit(solution)/shard_map/level_gather/pallas_call | solution.py:105
  334.5 5.6 collective-permute-done.3.refs_3_.refs_1_
  340.1 36.9 %ffn_front.1 = (bf16[2048,2048]{1,0:T(8,128)(2,1)}, bf16[2048,2048]{1,0:T(8,128)(2,1)}, bf16[2048,1152]{1,0:T(8,128)(2,1)}) custom-call(s32[2]{0:T(128)} %pad_add_fusion.1.place, bf16[2048,1152]{1,0:T(8,128)(2,1)} %bitcast.156, bf16[2048,1024]{1,0:T(8,128)(2,1)} %bitcast.158, bf16[4,512,512]{2,1,0:T(8,128)(2,1)} %bitcast.187, ...), custom_call_target="tpu_custom_call" | custom-call | flops 25769803776 | bytes 30000000 | tf_op jit(solution)/shard_map/ffn_front/pallas_call | solution.py:891
  377.1 2.3 copy-done.4
  379.4 4.7 pair_scatter.2
  386.4 14.0 %ffn_rear.2 = (bf16[4,512,512]{2,1,0:T(8,128)(2,1)}, bf16[4,512,512]{2,1,0:T(8,128)(2,1)}) custom-call(s32[2]{0:T(128)} %pad_add_fusion.1.place, bf16[2048,1152]{1,0:T(8,128)(2,1)} %bitcast.157, bf16[2048,2048]{1,0:T(8,128)(2,1)} %get-tuple-element.127.hidden_units), custom_call_target="tpu_custom_call" | custom-call | flops 8589934592 | bytes 30000000 | tf_op jit(solution)/shard_map/ffn_rear/pallas_call | solution.py:965
  402.2 14.2 %ffn_rear.3 = (bf16[4,512,512]{2,1,0:T(8,128)(2,1)}, bf16[4,512,512]{2,1,0:T(8,128)(2,1)}) custom-call(s32[2]{0:T(128)} %pad_add_fusion.1.place, bf16[2048,1024]{1,0:T(8,128)(2,1)} %bitcast.159, bf16[2048,2048]{1,0:T(8,128)(2,1)} %get-tuple-element.130.hidden_units.active), custom_call_target="tpu_custom_call" | custom-call | flops 8589934592 | bytes 30000000 | tf_op jit(solution)/shard_map/ffn_rear/pallas_call | solution.py:965
  416.5 7.0 leave_ffn.1
  424.9 18.2 %ffn_feed.1 = bf16[2048,1024]{1,0:T(8,128)(2,1)} custom-call(s32[2]{0:T(128)} %pad_add_fusion.1.place, bf16[2048,2048]{1,0:T(8,128)(2,1)} %get-tuple-element.130.hidden_units.active, bf16[4,512,512]{2,1,0:T(8,128)(2,1)} %bitcast.186, bf16[4,512,512]{2,1,0:T(8,128)(2,1)} %collective-permute-done.3.refs_3_.refs_1_), custom_call_target="tpu_custom_call" | custom-call | flops 8589934592 | bytes 30000000 | tf_op jit(solution)/shard_map/ffn_feed/pallas_call | solution.py:944
  443.1 5.0 collective-permute-done.5
  449.0 6.2 pair_gather.1
  455.3 3.5 add_convert_fusion.1
  460.3 13.0 %branch_back.1 = (bf16[2048,128]{1,0:T(8,128)(2,1)S(1)}, f32[4,1,512]{2,1,0:T(1,128)S(1)}, bf16[2048,128]{1,0:T(8,128)(2,1)S(1)}, bf16[1024,640]{1,0:T(8,128)(2,1)S(1)}) custom-call(bf16[2048,1024]{1,0:T(8,128)(2,1)} %bitcast.160, bf16[1024,1664]{1,0:T(8,128)(2,1)} %bitcast.148, f32[2048,128]{1,0:T(8,128)S(1)} %copy-done.17, ...), custom_call_target="tpu_custom_call" | custom-call | flops 5368709120 | bytes 20000000 | tf_op jit(solution)/shard_map/branch_back/pallas_call | solution.py:1120
  475.2 21.6 %attend_back.1 = (bf16[2048,128]{1,0:T(8,128)(2,1)S(1)}, bf16[2048,256]{1,0:T(8,128)(2,1)S(1)}, bf16[2048,256]{1,0:T(8,128)(2,1)S(1)}, f32[2048,256]{1,0:T(8,128)}) custom-call(s32[4]{0:T(128)S(1)} %subtract_maximum_fusion.first, bf16[2048,128]{1,0:T(8,128)(2,1)S(1)} %copy-done.28, bf16[2048,256]{1,0:T(8,128)(2,1)} %collective-permute-done.2.refs_0_.refs_3_, ...), custom_call_target="tpu_custom_call" | custom-call | flops 20000000000 | bytes 10000000 | tf_op jit(solution)/shard_map/attend_back/pallas_call | solution.py:803
  498.7 4.4 pair_scatter.3
  503.2 31.7 %collective-permute-done.7 = bf16[2048,256]{1,0:T(8,128)(2,1)S(1)} collective-permute-done((bf16[2048,256]{1,0:T(8,128)(2,1)S(1)}, bf16[2048,256]{1,0:T(8,128)(2,1)S(1)}, u32[]{:S(2)}, u32[]{:S(2)}) %collective-permute-start.7) | collective-permute-done | bytes 1048608 | tf_op jit(solution)/shard_map/ppermute | solution.py:1314
  538.0 3.5 add_convert_fusion
  542.7 46.0 %collective-permute-done.9 = bf16[2048,256]{1,0:T(8,128)(2,1)} collective-permute-done((bf16[2048,256]{1,0:T(8,128)(2,1)}, bf16[2048,256]{1,0:T(8,128)(2,1)}, u32[]{:S(2)}, u32[]{:S(2)}) %collective-permute-start.9) | collective-permute-done | bytes 1048608 | tf_op jit(solution)/shard_map/ppermute | solution.py:1314
  588.7 3.4 convert_add_fusion.grads
  592.1 23.4 %project_back.1 = (bf16[2048,1024]{1,0:T(8,128)(2,1)}, bf16[1024,1024]{1,0:T(8,128)(2,1)}) custom-call(bf16[2048,1024]{1,0:T(8,128)(2,1)} %bitcast.154, f32[2048,256]{1,0:T(8,128)} %convert_add_fusion.grads, bf16[2048,128]{1,0:T(8,128)(2,1)} %copy-done.30, bf16[2048,128]{1,0:T(8,128)(2,1)} %copy-done.29, f32[2048,640]{1,0:T(8,128)} %get-tuple-element.152.projected, ...), custom_call_target="tpu_custom_call" | custom-call | flops 8589934592 | bytes 40000000 | tf_op jit(solution)/shard_map/project_back/pallas_call | solution.py:1289
  617.2 3.5 all-to-all-start
  620.7 81.6 %finish.1 = (f32[4,4,32,1024]{3,2,1,0:T(8,128)}, f32[32,2560]{1,0:T(8,128)}, f32[32,512]{1,0:T(8,128)}, f32[32,512]{1,0:T(8,128)}, f32[4,32,128]{2,1,0:T(8,128)}...) custom-call(bf16[4,4,128,1024]{3,2,1,0:T(8,128)(2,1)} %bitcast.161, f32[4,128,1024]{2,1,0:T(8,128)} %bitcast.165, ...), custom_call_target="tpu_custom_call" | custom-call | bytes 200000000 | tf_op jit(solution)/shard_map/finish/pallas_call | solution.py:626
  (185 shorter events, 76.3 us)
Async XLA Ops:
  7.2 285.2 %all-gather.7.cloned.1.call-start = ((), (), s32[]{:S(2)}) async-start(), calls=%async_computation.5 | async-start | bytes 2621440 | tf_op jit(solution)/shard_map/all_gather | solution.py:1460
  7.2 99.5 %collective-permute-start = (bf16[512,512]{1,0:T(8,128)(2,1)}, bf16[512,512]{1,0:T(8,128)(2,1)S(1)}, u32[]{:S(2)}, u32[]{:S(2)}) collective-permute-start(bf16[512,512]{1,0:T(8,128)(2,1)} %param.38), channel_id=1, source_target_pairs={{0,16},{16,0},{1,17},{17,1},{2,18},{18,2},{3,19},{19,3},{4,20},{20... | collective-permute-start | bytes 1572872 | tf_op jit(solution)/shard_map/ppermute | solution.py:1151
  106.8 227.7 %all-gather.9.cloned.1.call-start = ((), (), s32[]{:S(2)}) async-start(), calls=%async_computation.6 | async-start | bytes 2621440 | tf_op jit(solution)/shard_map/all_gather | solution.py:1461
  110.6 15.1 %copy-start.23 = (f32[1024]{0:T(1024)}, f32[1024]{0:T(1024)S(1)}, u32[]{:S(2)}) copy-start(f32[1024]{0:T(1024)S(1)} %get-tuple-element.248) | copy-start | bytes 12292
  110.7 15.1 %copy-start.24 = (f32[1024]{0:T(1024)}, f32[1024]{0:T(1024)S(1)}, u32[]{:S(2)}) copy-start(f32[1024]{0:T(1024)S(1)} %get-tuple-element.249) | copy-start | bytes 12292
  111.4 19.2 %copy-start.41 = (s32[1,3]{1,0:T(1,128)S(1)}, s32[1,3]{1,0:T(1,128)}, u32[]{:S(2)}) copy-start(s32[1,3]{1,0:T(1,128)} %param.23) | copy-start | bytes 40
  126.6 61.8 %copy-start.11 = (f32[2048,16]{1,0:T(8,128)}, f32[2048,16]{1,0:T(8,128)S(1)}, u32[]{:S(2)}) copy-start(f32[2048,16]{1,0:T(8,128)S(1)} %get-tuple-element.106.masks) | copy-start | bytes 393220
  126.6 115.2 %copy-start.25 = (bf16[2048,256]{1,0:T(8,128)(2,1)}, bf16[2048,256]{1,0:T(8,128)(2,1)S(1)}, u32[]{:S(2)}) copy-start(bf16[2048,256]{1,0:T(8,128)(2,1)S(1)} %get-tuple-element.98.refs_2_.refs_5_) | copy-start | bytes 3145732
  126.6 332.3 %copy-start.10 = (f32[2048,128]{1,0:T(8,128)}, f32[2048,128]{1,0:T(8,128)S(1)}, u32[]{:S(2)}) copy-start(f32[2048,128]{1,0:T(8,128)S(1)} %get-tuple-element.105.sigs) | copy-start | bytes 3145732
  126.6 58.8 %copy-start.40 = (s32[4,16,128]{2,1,0:T(8,128)S(1)}, s32[4,16,128]{2,1,0:T(8,128)}, u32[]{:S(2)}) copy-start(s32[4,16,128]{2,1,0:T(8,128)} %get-tuple-element.103) | copy-start | bytes 98308
  126.6 51.6 %collective-permute-start.1 = (bf16[2048,256]{1,0:T(8,128)(2,1)S(1)}, bf16[2048,256]{1,0:T(8,128)(2,1)}, u32[]{:S(2)}, u32[]{:S(2)}) collective-permute-start(bf16[2048,256]{1,0:T(8,128)(2,1)S(1)} %get-tuple-element.98.refs_2_.refs_5_), channel_id=1, source_target_pairs={{0,4},{4,8},{8,12},{1,5},{5,9},{9,13},{2,6},{6,10},{10,14},{3,7},{... | collective-permute-start | bytes 3145736 | tf_op jit(solution)/shard_map/ppermute | solution.py:1314
  178.2 156.3 %all-gather.11.cloned.1.call-start = ((), (), s32[]{:S(2)}) async-start(), calls=%async_computation.7 | async-start | bytes 2621440 | tf_op jit(solution)/shard_map/all_gather | solution.py:1461
  180.8 61.0 %collective-permute-start.2 = (bf16[2048,256]{1,0:T(8,128)(2,1)}, bf16[2048,256]{1,0:T(8,128)(2,1)}, u32[]{:S(2)}, u32[]{:S(2)}) collective-permute-start(bf16[2048,256]{1,0:T(8,128)(2,1)} %collective-permute-done.1.refs_1_.refs_4_), channel_id=1, source_target_pairs={{0,4},{4,8},{8,12},{1,5},{5,9},{9,13},{2,6},{6,10},{10,14},{3,7},{... | collective-permute-start | bytes 3145736 | tf_op jit(solution)/shard_map/ppermute | solution.py:1314
  223.6 484.4 %reduce-scatter.3.cloned.1.call-start = ((), (), s32[]{:S(2)}) async-start(), calls=%async_computation.3 | async-start | bytes 2621440 | tf_op jit(solution)/shard_map/reduce_scatter | solution.py:1511
  292.4 47.7 %collective-permute-start.3 = (bf16[4,512,512]{2,1,0:T(8,128)(2,1)}, bf16[4,512,512]{2,1,0:T(8,128)(2,1)}, u32[]{:S(2)}, u32[]{:S(2)}) collective-permute-start(bf16[4,512,512]{2,1,0:T(8,128)(2,1)} %bitcast.184), channel_id=1, source_target_pairs={{0,16},{16,0},{1,17},{17,1},{2,18},{18,2},{3,19},{19,3},{4,20},{20... | collective-permute-start | bytes 6291464 | tf_op jit(solution)/shard_map/ppermute | solution.py:1151
  385.6 30.9 %collective-permute-start.4 = (bf16[512,1152]{1,0:T(8,128)(2,1)S(1)}, bf16[512,1152]{1,0:T(8,128)(2,1)S(1)}, u32[]{:S(2)}, u32[]{:S(2)}) collective-permute-start(bf16[512,1152]{1,0:T(8,128)(2,1)S(1)} %bitcast.139), channel_id=1, source_target_pairs={{0,2},{1,3},{2,0},{3,1},{4,6},{5,7},{6,4},{7,5},{8,10},{9,11},{10,... | collective-permute-start | bytes 3538952 | tf_op jit(solution)/shard_map/ppermute | solution.py:287
  400.4 54.9 %collective-permute-start.6 = (bf16[4,512,512]{2,1,0:T(8,128)(2,1)}, bf16[4,512,512]{2,1,0:T(8,128)(2,1)}, u32[]{:S(2)}, u32[]{:S(2)}) collective-permute-start(bf16[4,512,512]{2,1,0:T(8,128)(2,1)} %get-tuple-element.129), channel_id=1, source_target_pairs={{0,16},{16,0},{1,17},{17,1},{2,18},{18,2},{3,19},{19,3},{4,20},{20... | collective-permute-start | bytes 6291464 | tf_op jit(solution)/shard_map/ppermute | solution.py:1151
  402.2 14.2 %copy-start.15 = (s32[512,16]{1,0:T(8,128)S(1)}, s32[512,16]{1,0:T(8,128)}, u32[]{:S(2)}) copy-start(s32[512,16]{1,0:T(8,128)} %fusion.4.routes) | copy-start | bytes 98308
  402.2 14.2 %copy-start.21 = (f32[512,64]{1,0:T(8,128)S(1)}, f32[512,64]{1,0:T(8,128)}, u32[]{:S(2)}) copy-start(f32[512,64]{1,0:T(8,128)} %copy-done.20) | copy-start | bytes 393220
  423.5 19.6 %copy-start.18 = (bf16[512,1024]{1,0:T(8,128)(2,1)}, bf16[512,1024]{1,0:T(8,128)(2,1)S(1)}, u32[]{:S(2)}) copy-start(bf16[512,1024]{1,0:T(8,128)(2,1)S(1)} %get-tuple-element.135) | copy-start | bytes 3145732
  423.5 19.6 %copy-start.19 = (bf16[1024,128]{1,0:T(8,128)(2,1)}, bf16[1024,128]{1,0:T(8,128)(2,1)S(1)}, u32[]{:S(2)}) copy-start(bf16[1024,128]{1,0:T(8,128)(2,1)S(1)} %get-tuple-element.159) | copy-start | bytes 786436
  423.5 24.6 %collective-permute-start.5 = (bf16[512,1024]{1,0:T(8,128)(2,1)S(1)}, bf16[512,1024]{1,0:T(8,128)(2,1)S(1)}, u32[]{:S(2)}, u32[]{:S(2)}) collective-permute-start(bf16[512,1024]{1,0:T(8,128)(2,1)S(1)} %get-tuple-element.135), channel_id=1, source_target_pairs={{0,2},{1,3},{2,0},{3,1},{4,6},{5,7},{6,4},{7,5},{8,10},{9,11},{10,... | collective-permute-start | bytes 3145736 | tf_op jit(solution)/shard_map/ppermute | solution.py:287
  424.5 113.5 %collective-permute-start.10 = (bf16[4,512,512]{2,1,0:T(8,128)(2,1)}, bf16[4,512,512]{2,1,0:T(8,128)(2,1)}, u32[]{:S(2)}, u32[]{:S(2)}) collective-permute-start(bf16[4,512,512]{2,1,0:T(8,128)(2,1)} %get-tuple-element.132), channel_id=1, source_target_pairs={{0,16},{16,0},{1,17},{17,1},{2,18},{18,2},{3,19},{19,3},{4,20},{20... | collective-permute-start | bytes 6291464 | tf_op jit(solution)/shard_map/ppermute | solution.py:1151
  458.8 251.4 %reduce-scatter.5.cloned.1.call-start = ((), (), s32[]{:S(2)}) async-start(), calls=%async_computation.4 | async-start | bytes 2621440 | tf_op jit(solution)/shard_map/reduce_scatter | solution.py:1511
  460.3 14.9 %copy-start.28 = (bf16[2048,128]{1,0:T(8,128)(2,1)S(1)}, bf16[2048,128]{1,0:T(8,128)(2,1)}, u32[]{:S(2)}) copy-start(bf16[2048,128]{1,0:T(8,128)(2,1)} %copy-done.26) | copy-start | bytes 1572868
  475.2 23.5 %copy-start.5 = (bf16[2048,1024]{1,0:T(8,128)(2,1)S(1)}, bf16[2048,1024]{1,0:T(8,128)(2,1)}, u32[]{:S(2)}) copy-start(bf16[2048,1024]{1,0:T(8,128)(2,1)} %ffn_feed.1) | copy-start | bytes 12582916
  496.8 38.0 %collective-permute-start.7 = (bf16[2048,256]{1,0:T(8,128)(2,1)S(1)}, bf16[2048,256]{1,0:T(8,128)(2,1)S(1)}, u32[]{:S(2)}, u32[]{:S(2)}) collective-permute-start(bf16[2048,256]{1,0:T(8,128)(2,1)S(1)} %get-tuple-element.141), channel_id=1, source_target_pairs={{4,0},{8,4},{12,8},{5,1},{9,5},{13,9},{6,2},{10,6},{14,10},{7,3},{... | collective-permute-start | bytes 3145736 | tf_op jit(solution)/shard_map/ppermute | solution.py:1314
  503.2 34.8 %copy-start.31 = (bf16[4,512,512]{2,1,0:T(8,128)(2,1)S(1)}, bf16[4,512,512]{2,1,0:T(8,128)(2,1)}, u32[]{:S(2)}) copy-start(bf16[4,512,512]{2,1,0:T(8,128)(2,1)} %get-tuple-element.169) | copy-start | bytes 6291460
  536.1 52.6 %collective-permute-start.9 = (bf16[2048,256]{1,0:T(8,128)(2,1)}, bf16[2048,256]{1,0:T(8,128)(2,1)}, u32[]{:S(2)}, u32[]{:S(2)}) collective-permute-start(bf16[2048,256]{1,0:T(8,128)(2,1)} %add_convert_fusion.3), channel_id=1, source_target_pairs={{4,0},{8,4},{12,8},{5,1},{9,5},{13,9},{6,2},{10,6},{14,10},{7,3},{... | collective-permute-start | bytes 3145736 | tf_op jit(solution)/shard_map/ppermute | solution.py:1314
  541.6 73.9 %collective-permute-start.8 = (bf16[512,1024]{1,0:T(8,128)(2,1)S(1)}, bf16[512,1024]{1,0:T(8,128)(2,1)S(1)}, u32[]{:S(2)}, u32[]{:S(2)}) collective-permute-start(bf16[512,1024]{1,0:T(8,128)(2,1)S(1)} %bitcast.140), channel_id=1, source_target_pairs={{0,2},{1,3},{2,0},{3,1},{4,6},{5,7},{6,4},{7,5},{8,10},{9,11},{10,... | collective-permute-start | bytes 3145736 | tf_op jit(solution)/shard_map/ppermute | solution.py:287
  592.1 23.4 %copy-start.3 = (f32[512,1024]{1,0:T(8,128)S(1)}, f32[512,1024]{1,0:T(8,128)}, u32[]{:S(2)}) copy-start(f32[512,1024]{1,0:T(8,128)} %copy-done.2) | copy-start | bytes 6291460
  617.2 90.9 %all-to-all-start = ((bf16[4,128,1024]{2,1,0:T(8,128)(2,1)}), bf16[4,128,1024]{2,1,0:T(8,128)(2,1)S(1)}, u32[]{:S(2)}, u32[]{:S(2)}) async-start(bf16[4,128,1024]{2,1,0:T(8,128)(2,1)} %bitcast.46), calls=%async_computation | async-start | bytes 2097152 | tf_op jit(solution)/shard_map/all_to_all | solution.py:33
  (27 other events, 75.7 us)
Sparse Core Ops, SparseCore 0:
  106.9 72.5 all-gather.6
  181.1 60.9 all-gather.8
  243.7 44.5 all-gather.10
  458.9 46.3 reduce-scatter.2
  541.7 55.9 reduce-scatter.4

commit v7 on v6

--- a/solution.py
+++ b/solution.py
@@ -1384,9 +1384,7 @@
     worker_in = arrived.reshape(HEADS * count, width)
     own_tokens = lax.dynamic_index_in_dim(arrived, head, 1, keepdims=False).reshape(count, width)
     in_rows = [turn(ffn_in, "group", k) for k in range(1, groups)]
-    full, in_rows, ffn_out = lax.optimization_barrier(
-        (full.reshape(width, cols), in_rows, ffn_out)
-    )
+    full, in_rows = lax.optimization_barrier((full.reshape(width, cols), in_rows))
 
     base = 2 * DH + 2 * VEXP * DH
     w_output = full[:, VEXP * DH : 2 * VEXP * DH]
@@ -1449,8 +1447,8 @@
     for i in range(reach):
         came = shift(window[0], "level", 1)
         if i == 0:
-            came, own_grads, pos_all, starts, in_rows = lax.optimization_barrier(
-                (came, own_grads, pos_all, starts, [ffn_in] + in_rows)
+            came, own_grads, pos_all, starts, ffn_out, in_rows = lax.optimization_barrier(
+                (came, own_grads, pos_all, starts, ffn_out, [ffn_in] + in_rows)
             )
             cotangent = level_gather(own_grads, 5, True)
         if i == reach - 1:
@@ -1504,14 +1502,17 @@
     came, feed = lax.optimization_barrier((came, feed))
     grad_branch = pair_gather(own_branch, came, 7)
 
-    def sum_over_rows(own, others):
+    def sum_of(own, others):
         total = own[0].astype(jnp.float32)
         for other in others:
             total = total + other.astype(jnp.float32)
-        return lax.psum_scatter(low(total), "level", scatter_dimension=0)
-
-    grad_branch, in_came = lax.optimization_barrier((grad_branch, in_came))
-    ffn_in_grad = sum_over_rows(grad_in, in_came)
+        return low(total)
+
+    def over_levels(total):
+        return lax.psum_scatter(total, "level", scatter_dimension=0)
+
+    grad_branch, in_total = lax.optimization_barrier((grad_branch, sum_of(grad_in, in_came)))
+    ffn_in_grad = over_levels(in_total)
     grad_attended, row_inner, grad_out_logit, grad_w_output = branch_back(
         grad_branch, full, attended, sigs, masks
     )
@@ -1527,8 +1528,6 @@
         pos_all[:, None],
     )
     came = shift(grad_window[0], "level", -1)
-    grad_queries, out_came = lax.optimization_barrier((grad_queries, out_came))
-    ffn_out_grad = sum_over_rows(grad_out, out_came)
     fed, beyond = pair_scatter(feed, 6, True)
     for i in range(1, reach + 1):
         if i < reach:
@@ -1537,6 +1536,8 @@
         if i < reach:
             grad_keys_sent = low(grad_both)
             came = shift(grad_keys_sent, "level", -1)
+    grad_both, out_came = lax.optimization_barrier((grad_both, out_came))
+    ffn_out_grad = over_levels(sum_of(grad_out, out_came))
     fed_far = to_far(beyond)
     grad_inputs, late = project_back(
         worker_in,

time: 735 us -> 718 us (0.977)
  waiting for transfers between devices: 153 us -> 108 us
  Pallas kernels: 454 us -> 474 us
  starting transfers between devices: 22.5 us -> 38 us
    ppermute x4, waiting for transfers between devices: 142 us -> 86.1 us  [shift(): return lax.ppermute(value, axis, pairs)]
    pallas_call x1, Pallas kernels: 81.6 us -> 97.7 us  [finish(): pl.pallas_call(functools.partial(finish_kernel, layout), out_shape=[jax.S...]
    ppermute x4, starting transfers between devices: 4.97 us -> 18.8 us  [turn(): lax.ppermute(value, axis, [(i, (i + by) % size) for i in range(size)])]
    ppermute x3, waiting for transfers between devices: 5 us -> 15.4 us  [to_far(): lax.ppermute(rows, 'head', [(i, (i + 2) % HEADS) for i in range(HEADS)])]
    unnamed x92 -> x100, local copies, waits for them, and re-layouts: 22.6 us -> 21.6 us
  transfers between devices with their start and end apart: 17 -> 17, of which waited for: 6 -> 7; matrix products, arithmetic and copies ran while one was open for 8% -> 7% of each run, Pallas kernels for 57% -> 55%
where the time goes in v7:
time: 718 us; the launch traced here: 709 us
  Pallas kernels  474 us (66%)
  waiting for transfers between devices  108 us (15%)
  local copies, waits for them, and re-layouts  41.5 us (6%)
  starting transfers between devices  38 us (5%)
  other arithmetic  26.8 us (4%)
  between operations  14.8 us (2%)
    pallas_call x1, Pallas kernels, finish(): pl.pallas_call(functools.partial(finish_kernel, layout), out_shape=[jax.S...  97.7 us
    pallas_call x1, Pallas kernels, start(): pl.pallas_call(start_kernel, out_shape=shapes, in_specs=[pl.BlockSpec(mem...  89.7 us
    ppermute x4, waiting for transfers between devices, shift(): return lax.ppermute(value, axis, pairs)  86.1 us
    pallas_call x2, Pallas kernels, level_gather(): pl.pallas_call(functools.partial(gather_kernel, by_source), out_shape=jax...  59.1 us
    pallas_call x1, Pallas kernels, ffn_front(): pl.pallas_call(functools.partial(front_kernel, groups, local), grid_spec=...  37.2 us
    pallas_call x2, Pallas kernels, ffn_rear(): pl.pallas_call(functools.partial(rear_kernel, groups), grid_spec=pltpu.Pr...  28.6 us
    pallas_call x1, Pallas kernels, level_scatter(): pl.pallas_call(functools.partial(scatter_kernel, by_source), out_shape=ja...  27 us
    pallas_call x1, Pallas kernels, project_back(): pl.pallas_call(project_back_kernel, grid=(HEADS,), in_specs=[by_row(width...  23.5 us
  transfers between devices with their start and end apart: 17, of which 7 were waited for; matrix products, arithmetic and copies ran while one was open for 7% of the time, Pallas kernels for 55%

profile of v7, /device:TPU:8, one launch (start us, length us, event | category | flops | bytes accessed | tf_op | source)
XLA Modules:
  0.0 709.4 jit_solution(13345368471397065466)
XLA Ops:
  17.0 89.7 %start.1 = (bf16[4,4,4,32,1024]{4,3,2,1,0:T(8,128)(2,1)}, bf16[4,4,32,1024]{3,2,1,0:T(8,128)(2,1)}, bf16[2,4,4,32,1664]{4,3,2,1,0:T(8,128)(2,1)}, s32[4,4,512]{2...) custom-call(bf16[4,4,32,1024]{3,2,1,0:T(8,128)(2,1)} %bitcast.169, bf16[4,4,32,1024]{3,2,1,0:T(8,128)(2,1)} %bitcast.170, ...), custom_call_target="tpu_custom_call" | custom-call | bytes 200000000 | tf_op jit(solution)/shard_map/start/pallas_call | solution.py:459
  111.3 14.4 %project.1 = (bf16[2048,128]{1,0:T(8,128)(2,1)S(1)}, bf16[2048,256]{1,0:T(8,128)(2,1)}, f32[2048,640]{1,0:T(8,128)}, f32[2048,128]{1,0:T(8,128)S(1)}, f32[2048,16]{1,0:T(8,128)S(1)}) custom-call(bf16[2048,1024]{1,0:T(8,128)(2,1)} %bitcast.154, bf16[1024,1664]{1,0:T(8,128)(2,1)} %bitcast.143, bf16[1024,1664]{1,0:T(8,128)(2,1)} %bitcast.144, ...), custom_call_target="tpu_custom_call" | custom-call | flops 4294967296 | bytes 20000000 | tf_op jit(solution)/shard_map/project/pallas_call | solution.py:1209
  131.0 22.3 %collective-permute-done.1.refs_1_.refs_4_ = bf16[2048,256]{1,0:T(8,128)(2,1)S(1)} collective-permute-done((bf16[2048,256]{1,0:T(8,128)(2,1)}, bf16[2048,256]{1,0:T(8,128)(2,1)S(1)}, u32[]{:S(2)}, u32[]{:S(2)}) %collective-permute-start.1) | collective-permute-done | bytes 1048608 | tf_op jit(solution)/shard_map/ppermute | solution.py:1314
  154.3 2.3 constant_dynamic-slice_fusion
  156.6 5.3 collective-permute-start.2
  171.6 28.4 %level_gather.2 = bf16[4,4,128,1024]{3,2,1,0:T(8,128)(2,1)} custom-call(bf16[4,128,1024]{2,1,0:T(8,128)(2,1)} %bitcast.121), custom_call_target="tpu_custom_call" | custom-call | bytes 90000000 | tf_op jit(solution)/shard_map/level_gather/pallas_call | solution.py:105
  200.3 13.7 %collective-permute-done.2.refs_0_.refs_3_ = bf16[2048,256]{1,0:T(8,128)(2,1)} collective-permute-done((bf16[2048,256]{1,0:T(8,128)(2,1)S(1)}, bf16[2048,256]{1,0:T(8,128)(2,1)}, u32[]{:S(2)}, u32[]{:S(2)}) %collective-permute-start.2) | collective-permute-done | bytes 1048608 | tf_op jit(solution)/shard_map/ppermute | solution.py:1314
  215.1 17.7 %attend.1 = (f32[2048,128]{1,0:T(8,128)S(1)}, f32[4,1,512]{2,1,0:T(1,128)S(1)}) custom-call(s32[4]{0:T(128)S(1)} %subtract_maximum_fusion.first, bf16[2048,128]{1,0:T(8,128)(2,1)S(1)} %copy-done.27, bf16[2048,256]{1,0:T(8,128)(2,1)} %collective-permute-done.2.refs_0_.refs_3_, bf16[2048,256]{1,0:T(8,128)(2,1)S(1)} %collective-permute-done.1.refs_1_.refs_4_, ...), custom_call_target="tpu_custom_call" | custom-call | flops 20000000000 | bytes 10000000 | tf_op jit(solution)/shard_map/attend/pallas_call | solution.py:719
  233.7 5.1 convolution_convert_fusion
  238.8 27.0 %level_scatter.1 = f32[4,128,1024]{2,1,0:T(8,128)S(1)} custom-call(bf16[4,4,128,1024]{3,2,1,0:T(8,128)(2,1)S(1)} %bitcast.119), custom_call_target="tpu_custom_call" | custom-call | bytes 80000000 | tf_op jit(solution)/shard_map/level_scatter/pallas_call | solution.py:167
  265.9 7.6 %collective-permute-start.3 = (bf16[4,512,512]{2,1,0:T(8,128)(2,1)}, bf16[4,512,512]{2,1,0:T(8,128)(2,1)}, u32[]{:S(2)}, u32[]{:S(2)}) collective-permute-start(bf16[4,512,512]{2,1,0:T(8,128)(2,1)} %bitcast.184), channel_id=1, source_target_pairs={{0,16},{16,0},{1,17},{17,1},{2,18},{18,2},{3,19},{19,3},{4,20},{20... | collective-permute-start | bytes 6291464 | tf_op jit(solution)/shard_map/ppermute | solution.py:1151
  281.1 30.7 %level_gather.3 = bf16[4,4,128,1152]{3,2,1,0:T(8,128)(2,1)} custom-call(bf16[4,128,1152]{2,1,0:T(8,128)(2,1)} %bitcast.127), custom_call_target="tpu_custom_call" | custom-call | bytes 90000000 | tf_op jit(solution)/shard_map/level_gather/pallas_call | solution.py:105
  314.1 5.4 collective-permute-done.3.refs_3_.refs_1_
  319.5 37.2 %ffn_front.1 = (bf16[2048,2048]{1,0:T(8,128)(2,1)}, bf16[2048,2048]{1,0:T(8,128)(2,1)}, bf16[2048,1152]{1,0:T(8,128)(2,1)}) custom-call(s32[2]{0:T(128)} %pad_add_fusion.1.place, bf16[2048,1152]{1,0:T(8,128)(2,1)} %bitcast.157, bf16[2048,1024]{1,0:T(8,128)(2,1)} %bitcast.159, bf16[4,512,512]{2,1,0:T(8,128)(2,1)} %bitcast.187, ...), custom_call_target="tpu_custom_call" | custom-call | flops 25769803776 | bytes 30000000 | tf_op jit(solution)/shard_map/ffn_front/pallas_call | solution.py:891
  356.7 14.5 %ffn_rear.2 = (bf16[4,512,512]{2,1,0:T(8,128)(2,1)}, bf16[4,512,512]{2,1,0:T(8,128)(2,1)}) custom-call(s32[2]{0:T(128)} %pad_add_fusion.1.place, bf16[2048,1152]{1,0:T(8,128)(2,1)} %bitcast.158, bf16[2048,2048]{1,0:T(8,128)(2,1)} %get-tuple-element.127.hidden_units), custom_call_target="tpu_custom_call" | custom-call | flops 8589934592 | bytes 30000000 | tf_op jit(solution)/shard_map/ffn_rear/pallas_call | solution.py:965
  373.1 5.8 pair_scatter.2
  380.9 14.1 %ffn_rear.3 = (bf16[4,512,512]{2,1,0:T(8,128)(2,1)}, bf16[4,512,512]{2,1,0:T(8,128)(2,1)}) custom-call(s32[2]{0:T(128)} %pad_add_fusion.1.place, bf16[2048,1024]{1,0:T(8,128)(2,1)} %bitcast.160, bf16[2048,2048]{1,0:T(8,128)(2,1)} %get-tuple-element.130.hidden_units.active), custom_call_target="tpu_custom_call" | custom-call | flops 8589934592 | bytes 30000000 | tf_op jit(solution)/shard_map/ffn_rear/pallas_call | solution.py:965
  395.1 13.4 %collective-permute-done.4.came = bf16[512,1152]{1,0:T(8,128)(2,1)S(1)} collective-permute-done((bf16[512,1152]{1,0:T(8,128)(2,1)}, bf16[512,1152]{1,0:T(8,128)(2,1)S(1)}, u32[]{:S(2)}, u32[]{:S(2)}) %collective-permute-start.4) | collective-permute-done | bytes 1179680 | tf_op jit(solution)/shard_map/ppermute | solution.py:287
  408.5 7.0 leave_ffn.1
  416.1 18.4 %ffn_feed.1 = bf16[2048,1024]{1,0:T(8,128)(2,1)} custom-call(s32[2]{0:T(128)} %pad_add_fusion.1.place, bf16[2048,2048]{1,0:T(8,128)(2,1)} %get-tuple-element.130.hidden_units.active, bf16[4,512,512]{2,1,0:T(8,128)(2,1)} %bitcast.186, bf16[4,512,512]{2,1,0:T(8,128)(2,1)} %collective-permute-done.3.refs_3_.refs_1_), custom_call_target="tpu_custom_call" | custom-call | flops 8589934592 | bytes 30000000 | tf_op jit(solution)/shard_map/ffn_feed/pallas_call | solution.py:944
  434.5 3.5 add_convert_fusion.1
  440.0 6.2 pair_gather.1
  446.3 12.4 %branch_back.1 = (bf16[2048,128]{1,0:T(8,128)(2,1)S(1)}, f32[4,1,512]{2,1,0:T(1,128)S(1)}, bf16[2048,128]{1,0:T(8,128)(2,1)S(1)}, bf16[1024,640]{1,0:T(8,128)(2,1)S(1)}) custom-call(bf16[2048,1024]{1,0:T(8,128)(2,1)} %bitcast.161, bf16[1024,1664]{1,0:T(8,128)(2,1)} %bitcast.149, f32[2048,128]{1,0:T(8,128)S(1)} %copy-done.16, ...), custom_call_target="tpu_custom_call" | custom-call | flops 5368709120 | bytes 20000000 | tf_op jit(solution)/shard_map/branch_back/pallas_call | solution.py:1120
  463.7 23.4 %attend_back.1 = (bf16[2048,128]{1,0:T(8,128)(2,1)S(1)}, bf16[2048,256]{1,0:T(8,128)(2,1)S(1)}, bf16[2048,256]{1,0:T(8,128)(2,1)S(1)}, f32[2048,256]{1,0:T(8,128)}) custom-call(s32[4]{0:T(128)S(1)} %subtract_maximum_fusion.first, bf16[2048,128]{1,0:T(8,128)(2,1)S(1)} %copy-done.28, bf16[2048,256]{1,0:T(8,128)(2,1)} %collective-permute-done.2.refs_0_.refs_3_, ...), custom_call_target="tpu_custom_call" | custom-call | flops 20000000000 | bytes 10000000 | tf_op jit(solution)/shard_map/attend_back/pallas_call | solution.py:803
  489.0 7.7 %collective-permute-start.10 = (bf16[4,512,512]{2,1,0:T(8,128)(2,1)}, bf16[4,512,512]{2,1,0:T(8,128)(2,1)S(1)}, u32[]{:S(2)}, u32[]{:S(2)}) collective-permute-start(bf16[4,512,512]{2,1,0:T(8,128)(2,1)} %get-tuple-element.132), channel_id=1, source_target_pairs={{0,16},{16,0},{1,17},{17,1},{2,18},{18,2},{3,19},{19,3},{4,20},{20... | collective-permute-start | bytes 6291464 | tf_op jit(solution)/shard_map/ppermute | solution.py:1151
  496.7 4.4 pair_scatter.3
  501.1 25.5 %collective-permute-done.7 = bf16[2048,256]{1,0:T(8,128)(2,1)S(1)} collective-permute-done((bf16[2048,256]{1,0:T(8,128)(2,1)S(1)}, bf16[2048,256]{1,0:T(8,128)(2,1)S(1)}, u32[]{:S(2)}, u32[]{:S(2)}) %collective-permute-start.7) | collective-permute-done | bytes 1048608 | tf_op jit(solution)/shard_map/ppermute | solution.py:1314
  526.9 2.5 collective-permute-start.9
  529.4 24.6 %collective-permute-done.9 = bf16[2048,256]{1,0:T(8,128)(2,1)S(1)} collective-permute-done((bf16[2048,256]{1,0:T(8,128)(2,1)S(1)}, bf16[2048,256]{1,0:T(8,128)(2,1)S(1)}, u32[]{:S(2)}, u32[]{:S(2)}) %collective-permute-start.9) | collective-permute-done | bytes 1048608 | tf_op jit(solution)/shard_map/ppermute | solution.py:1314
  559.9 23.5 %project_back.1 = (bf16[2048,1024]{1,0:T(8,128)(2,1)}, bf16[1024,1024]{1,0:T(8,128)(2,1)}) custom-call(bf16[2048,1024]{1,0:T(8,128)(2,1)} %bitcast.155, f32[2048,256]{1,0:T(8,128)} %convert_add_fusion.grads, bf16[2048,128]{1,0:T(8,128)(2,1)} %copy-done.30, bf16[2048,128]{1,0:T(8,128)(2,1)} %copy-done.29, f32[2048,640]{1,0:T(8,128)} %get-tuple-element.153.projected, ...), custom_call_target="tpu_custom_call" | custom-call | flops 8589934592 | bytes 40000000 | tf_op jit(solution)/shard_map/project_back/pallas_call | solution.py:1289
  585.1 4.5 all-to-all-start
  589.5 97.7 %finish.1 = (f32[4,4,32,1024]{3,2,1,0:T(8,128)}, f32[32,2560]{1,0:T(8,128)}, f32[32,512]{1,0:T(8,128)}, f32[32,512]{1,0:T(8,128)}, f32[4,32,128]{2,1,0:T(8,128)}...) custom-call(bf16[4,4,128,1024]{3,2,1,0:T(8,128)(2,1)} %bitcast.162, f32[4,128,1024]{2,1,0:T(8,128)} %bitcast.166, ...), custom_call_target="tpu_custom_call" | custom-call | bytes 200000000 | tf_op jit(solution)/shard_map/finish/pallas_call | solution.py:626
  (194 shorter events, 78.9 us)
Async XLA Ops:
  7.2 258.7 %all-gather.7.cloned.1.call-start = ((), (), s32[]{:S(2)}) async-start(), calls=%async_computation.5 | async-start | bytes 2621440 | tf_op jit(solution)/shard_map/all_gather | solution.py:1458
  7.2 101.0 %collective-permute-start = (bf16[512,512]{1,0:T(8,128)(2,1)}, bf16[512,512]{1,0:T(8,128)(2,1)S(1)}, u32[]{:S(2)}, u32[]{:S(2)}) collective-permute-start(bf16[512,512]{1,0:T(8,128)(2,1)} %param.38), channel_id=1, source_target_pairs={{0,16},{16,0},{1,17},{17,1},{2,18},{18,2},{3,19},{19,3},{4,20},{20... | collective-permute-start | bytes 1572872 | tf_op jit(solution)/shard_map/ppermute | solution.py:1151
  111.2 19.2 %copy-start.43 = (s32[1,3]{1,0:T(1,128)S(1)}, s32[1,3]{1,0:T(1,128)}, u32[]{:S(2)}) copy-start(s32[1,3]{1,0:T(1,128)} %param.23) | copy-start | bytes 40
  126.4 38.6 %copy-start.10 = (f32[2048,16]{1,0:T(8,128)}, f32[2048,16]{1,0:T(8,128)S(1)}, u32[]{:S(2)}) copy-start(f32[2048,16]{1,0:T(8,128)S(1)} %get-tuple-element.106.masks) | copy-start | bytes 393220
  126.4 319.8 %copy-start.9 = (f32[2048,128]{1,0:T(8,128)}, f32[2048,128]{1,0:T(8,128)S(1)}, u32[]{:S(2)}) copy-start(f32[2048,128]{1,0:T(8,128)S(1)} %get-tuple-element.105.sigs) | copy-start | bytes 3145732
  126.4 35.5 %copy-start.42 = (s32[4,16,128]{2,1,0:T(8,128)S(1)}, s32[4,16,128]{2,1,0:T(8,128)}, u32[]{:S(2)}) copy-start(s32[4,16,128]{2,1,0:T(8,128)} %get-tuple-element.103) | copy-start | bytes 98308
  126.4 26.8 %collective-permute-start.1 = (bf16[2048,256]{1,0:T(8,128)(2,1)}, bf16[2048,256]{1,0:T(8,128)(2,1)S(1)}, u32[]{:S(2)}, u32[]{:S(2)}) collective-permute-start(bf16[2048,256]{1,0:T(8,128)(2,1)} %get-tuple-element.98.refs_2_.refs_5_), channel_id=1, source_target_pairs={{0,4},{4,8},{8,12},{1,5},{5,9},{9,13},{2,6},{6,10},{10,14},{3,7},{... | collective-permute-start | bytes 3145736 | tf_op jit(solution)/shard_map/ppermute | solution.py:1314
  153.3 60.8 %copy-start.24 = (bf16[2048,256]{1,0:T(8,128)(2,1)}, bf16[2048,256]{1,0:T(8,128)(2,1)S(1)}, u32[]{:S(2)}) copy-start(bf16[2048,256]{1,0:T(8,128)(2,1)S(1)} %collective-permute-done.1.refs_1_.refs_4_) | copy-start | bytes 3145732
  153.3 160.8 %all-gather.9.cloned.1.call-start = ((), (), s32[]{:S(2)}) async-start(), calls=%async_computation.6 | async-start | bytes 2621440 | tf_op jit(solution)/shard_map/all_gather | solution.py:1459
  154.0 160.1 %all-gather.11.cloned.1.call-start = ((), (), s32[]{:S(2)}) async-start(), calls=%async_computation.7 | async-start | bytes 2621440 | tf_op jit(solution)/shard_map/all_gather | solution.py:1459
  156.6 57.5 %collective-permute-start.2 = (bf16[2048,256]{1,0:T(8,128)(2,1)S(1)}, bf16[2048,256]{1,0:T(8,128)(2,1)}, u32[]{:S(2)}, u32[]{:S(2)}) collective-permute-start(bf16[2048,256]{1,0:T(8,128)(2,1)S(1)} %collective-permute-done.1.refs_1_.refs_4_), channel_id=1, source_target_pairs={{0,4},{4,8},{8,12},{1,5},{5,9},{9,13},{2,6},{6,10},{10,14},{3,7},{... | collective-permute-start | bytes 3145736 | tf_op jit(solution)/shard_map/ppermute | solution.py:1314
  200.1 492.8 %reduce-scatter.3.cloned.1.call-start = ((), (), s32[]{:S(2)}) async-start(), calls=%async_computation.3 | async-start | bytes 2621440 | tf_op jit(solution)/shard_map/reduce_scatter | solution.py:1512
  265.9 53.6 %collective-permute-start.3 = (bf16[4,512,512]{2,1,0:T(8,128)(2,1)}, bf16[4,512,512]{2,1,0:T(8,128)(2,1)}, u32[]{:S(2)}, u32[]{:S(2)}) collective-permute-start(bf16[4,512,512]{2,1,0:T(8,128)(2,1)} %bitcast.184), channel_id=1, source_target_pairs={{0,16},{16,0},{1,17},{17,1},{2,18},{18,2},{3,19},{19,3},{4,20},{20... | collective-permute-start | bytes 6291464 | tf_op jit(solution)/shard_map/ppermute | solution.py:1151
  356.7 16.5 %slice-start.1 = ((s8[4718592]{0:T(1024)(128)(4,1)}), s8[524288]{0:T(1024)(128)(4,1)S(1)}, s32[]{:S(2)}) async-start(s8[4718592]{0:T(1024)(128)(4,1)} %bitcast.116), calls=%async_computation.9 | async-start | bytes 1048576
  371.2 63.3 %collective-permute-start.6 = (bf16[4,512,512]{2,1,0:T(8,128)(2,1)}, bf16[4,512,512]{2,1,0:T(8,128)(2,1)}, u32[]{:S(2)}, u32[]{:S(2)}) collective-permute-start(bf16[4,512,512]{2,1,0:T(8,128)(2,1)} %get-tuple-element.129), channel_id=1, source_target_pairs={{0,16},{16,0},{1,17},{17,1},{2,18},{18,2},{3,19},{19,3},{4,20},{20... | collective-permute-start | bytes 6291464 | tf_op jit(solution)/shard_map/ppermute | solution.py:1151
  380.4 28.1 %collective-permute-start.4 = (bf16[512,1152]{1,0:T(8,128)(2,1)}, bf16[512,1152]{1,0:T(8,128)(2,1)S(1)}, u32[]{:S(2)}, u32[]{:S(2)}) collective-permute-start(bf16[512,1152]{1,0:T(8,128)(2,1)} %bitcast.37), channel_id=1, source_target_pairs={{0,2},{1,3},{2,0},{3,1},{4,6},{5,7},{6,4},{7,5},{8,10},{9,11},{10,... | collective-permute-start | bytes 3538952 | tf_op jit(solution)/shard_map/ppermute | solution.py:287
  380.9 27.6 %copy-start.5 = (bf16[4,4,32,1024]{3,2,1,0:T(8,128)(2,1)S(1)}, bf16[4,4,32,1024]{3,2,1,0:T(8,128)(2,1)}, u32[]{:S(2)}) copy-start(bf16[4,4,32,1024]{3,2,1,0:T(8,128)(2,1)} %get-tuple-element.99) | copy-start | bytes 3145732
  380.9 27.6 %copy-start.14 = (s32[512,16]{1,0:T(8,128)S(1)}, s32[512,16]{1,0:T(8,128)}, u32[]{:S(2)}) copy-start(s32[512,16]{1,0:T(8,128)} %fusion.4.routes) | copy-start | bytes 98308
  380.9 27.6 %copy-start.20 = (f32[512,64]{1,0:T(8,128)S(1)}, f32[512,64]{1,0:T(8,128)}, u32[]{:S(2)}) copy-start(f32[512,64]{1,0:T(8,128)} %copy-done.19) | copy-start | bytes 393220
  415.5 18.9 %copy-start.17 = (bf16[512,1024]{1,0:T(8,128)(2,1)}, bf16[512,1024]{1,0:T(8,128)(2,1)S(1)}, u32[]{:S(2)}) copy-start(bf16[512,1024]{1,0:T(8,128)(2,1)S(1)} %get-tuple-element.135) | copy-start | bytes 3145732
  415.5 18.9 %copy-start.18 = (bf16[1024,128]{1,0:T(8,128)(2,1)}, bf16[1024,128]{1,0:T(8,128)(2,1)S(1)}, u32[]{:S(2)}) copy-start(bf16[1024,128]{1,0:T(8,128)(2,1)S(1)} %get-tuple-element.160) | copy-start | bytes 786436
  415.5 19.0 %copy-start.34 = (bf16[4,512,512]{2,1,0:T(8,128)(2,1)S(1)}, bf16[4,512,512]{2,1,0:T(8,128)(2,1)}, u32[]{:S(2)}) copy-start(bf16[4,512,512]{2,1,0:T(8,128)(2,1)} %get-tuple-element.137) | copy-start | bytes 6291460
  415.5 24.5 %collective-permute-start.5 = (bf16[512,1024]{1,0:T(8,128)(2,1)S(1)}, bf16[512,1024]{1,0:T(8,128)(2,1)}, u32[]{:S(2)}, u32[]{:S(2)}) collective-permute-start(bf16[512,1024]{1,0:T(8,128)(2,1)S(1)} %get-tuple-element.135), channel_id=1, source_target_pairs={{0,2},{1,3},{2,0},{3,1},{4,6},{5,7},{6,4},{7,5},{8,10},{9,11},{10,... | collective-permute-start | bytes 3145736 | tf_op jit(solution)/shard_map/ppermute | solution.py:287
  461.3 233.7 %reduce-scatter.5.cloned.1.call-start = ((), (), s32[]{:S(2)}) async-start(), calls=%async_computation.4 | async-start | bytes 2621440 | tf_op jit(solution)/shard_map/reduce_scatter | solution.py:1512
  463.7 33.0 %copy-start.4 = (bf16[2048,1024]{1,0:T(8,128)(2,1)S(1)}, bf16[2048,1024]{1,0:T(8,128)(2,1)}, u32[]{:S(2)}) copy-start(bf16[2048,1024]{1,0:T(8,128)(2,1)} %ffn_feed.1) | copy-start | bytes 12582916
  487.1 39.5 %collective-permute-start.7 = (bf16[2048,256]{1,0:T(8,128)(2,1)S(1)}, bf16[2048,256]{1,0:T(8,128)(2,1)S(1)}, u32[]{:S(2)}, u32[]{:S(2)}) collective-permute-start(bf16[2048,256]{1,0:T(8,128)(2,1)S(1)} %get-tuple-element.142), channel_id=1, source_target_pairs={{4,0},{8,4},{12,8},{5,1},{9,5},{13,9},{6,2},{10,6},{14,10},{7,3},{... | collective-permute-start | bytes 3145736 | tf_op jit(solution)/shard_map/ppermute | solution.py:1314
  489.0 66.5 %collective-permute-start.10 = (bf16[4,512,512]{2,1,0:T(8,128)(2,1)}, bf16[4,512,512]{2,1,0:T(8,128)(2,1)S(1)}, u32[]{:S(2)}, u32[]{:S(2)}) collective-permute-start(bf16[4,512,512]{2,1,0:T(8,128)(2,1)} %get-tuple-element.132), channel_id=1, source_target_pairs={{0,16},{16,0},{1,17},{17,1},{2,18},{18,2},{3,19},{19,3},{4,20},{20... | collective-permute-start | bytes 6291464 | tf_op jit(solution)/shard_map/ppermute | solution.py:1151
  501.1 52.9 %copy-start.36 = (f32[2048,256]{1,0:T(8,128)S(1)}, f32[2048,256]{1,0:T(8,128)}, u32[]{:S(2)}) copy-start(f32[2048,256]{1,0:T(8,128)} %get-tuple-element.147) | copy-start | bytes 6291460
  526.9 27.1 %collective-permute-start.9 = (bf16[2048,256]{1,0:T(8,128)(2,1)S(1)}, bf16[2048,256]{1,0:T(8,128)(2,1)S(1)}, u32[]{:S(2)}, u32[]{:S(2)}) collective-permute-start(bf16[2048,256]{1,0:T(8,128)(2,1)S(1)} %add_convert_fusion.3), channel_id=1, source_target_pairs={{4,0},{8,4},{12,8},{5,1},{9,5},{13,9},{6,2},{10,6},{14,10},{7,3},{... | collective-permute-start | bytes 3145736 | tf_op jit(solution)/shard_map/ppermute | solution.py:1314
  558.3 25.0 %collective-permute-start.8 = (bf16[512,1024]{1,0:T(8,128)(2,1)S(1)}, bf16[512,1024]{1,0:T(8,128)(2,1)S(1)}, u32[]{:S(2)}, u32[]{:S(2)}) collective-permute-start(bf16[512,1024]{1,0:T(8,128)(2,1)S(1)} %bitcast.141), channel_id=1, source_target_pairs={{0,2},{1,3},{2,0},{3,1},{4,6},{5,7},{6,4},{7,5},{8,10},{9,11},{10,... | collective-permute-start | bytes 3145736 | tf_op jit(solution)/shard_map/ppermute | solution.py:287
  559.9 23.5 %copy-start.3 = (f32[512,1024]{1,0:T(8,128)S(1)}, f32[512,1024]{1,0:T(8,128)}, u32[]{:S(2)}) copy-start(f32[512,1024]{1,0:T(8,128)} %copy-done.2) | copy-start | bytes 6291460
  585.1 107.9 %all-to-all-start = ((bf16[4,128,1024]{2,1,0:T(8,128)(2,1)}), bf16[4,128,1024]{2,1,0:T(8,128)(2,1)S(1)}, u32[]{:S(2)}, u32[]{:S(2)}) async-start(bf16[4,128,1024]{2,1,0:T(8,128)(2,1)} %bitcast.46), calls=%async_computation | async-start | bytes 2097152 | tf_op jit(solution)/shard_map/all_to_all | solution.py:33
  (31 other events, 121.1 us)
Sparse Core Ops, SparseCore 0:
  153.4 63.0 all-gather.6
  218.1 42.9 all-gather.8
  262.6 44.6 all-gather.10
  461.5 49.4 reduce-scatter.2
  558.4 52.8 reduce-scatter.4

commit v8 on v7

--- a/solution.py
+++ b/solution.py
@@ -817,9 +817,9 @@
 
 
 def front_kernel(groups, local, place, hidden, grads, *refs):
-    w_in, w_out = refs[:groups], refs[groups : 2 * groups]
-    gates, active, grad_pre, rows_out, turned, acc = refs[2 * groups :]
-    levels, depth, width = w_in[0].shape
+    w_in, w_out = refs[0], refs[1 : groups + 1]
+    gates, active, grad_pre, rows_out, turned, acc = refs[groups + 1 :]
+    levels, _, depth, width = w_in.shape
     tile = hidden.shape[0]
     model = groups * depth
     parts = [slice(step * depth, (step + 1) * depth) for step in range(groups)]
@@ -831,7 +831,7 @@
         pre_act = jnp.zeros((tile, width), jnp.float32)
         grad_active = jnp.zeros((tile, width), jnp.float32)
         for step in range(groups):
-            pre_act += dot(turned[0, :, parts[step]], w_in[step][level], 1, 0)
+            pre_act += dot(turned[0, :, parts[step]], w_in[level, step], 1, 0)
             grad_active += dot(turned[1, :, parts[step]], w_out[step][level], 1, 0)
         first = level * local
         gate = jnp.concatenate(
@@ -851,7 +851,7 @@
         low_pre = (grad_active * gate * slope).astype(jnp.bfloat16)
         grad_pre[:, columns] = low_pre
         for step in range(groups):
-            back = dot(low_pre, w_in[step][level], 1, 1)
+            back = dot(low_pre, w_in[level, step], 1, 1)
             acc[:, parts[step]] = back if level == 0 else acc[:, parts[step]] + back
     for step in range(groups):
         columns_of(rows_out, place[1], groups, -step, depth)[...] = acc[:, parts[step]].astype(
@@ -867,19 +867,21 @@
 
 def ffn_front(place, hidden, grads, w_in, w_out, gates, local):
     rows, wide = hidden.shape
-    groups = len(w_in)
-    levels, depth, width = w_in[0].shape
+    levels, groups, depth, width = w_in.shape
     tile = 512
 
     def by_row(columns):
         return pl.BlockSpec((tile, columns), lambda i, *_: (i, 0))
 
-    whole = pl.BlockSpec(w_in[0].shape, lambda i, *_: (0, 0, 0), pipeline_mode=pl.Buffered(1))
+    once = pl.Buffered(1)
+    whole = pl.BlockSpec(w_out[0].shape, lambda i, *_: (0, 0, 0), pipeline_mode=once)
+    stacked = pl.BlockSpec(w_in.shape, lambda i, *_: (0, 0, 0, 0), pipeline_mode=once)
     grid_spec = pltpu.PrefetchScalarGridSpec(
         num_scalar_prefetch=1,
         grid=(rows // tile,),
         in_specs=[by_row(wide), by_row(groups * depth)]
-        + [whole] * (2 * groups)
+        + [stacked]
+        + [whole] * groups
         + [by_row(gates.shape[1])],
         out_specs=[by_row(levels * width), by_row(levels * width), by_row(wide)],
         scratch_shapes=[
@@ -895,7 +897,7 @@
         compiler_params=pltpu.CompilerParams(vmem_limit_bytes=58 * 2**20),
         cost_estimate=cost(6 * rows * groups * depth * levels * width, 3e7),
         name="ffn_front",
-    )(place, hidden, grads, *w_in, *w_out, gates)
+    )(place, hidden, grads, w_in, *w_out, gates)
 
 
 def rear_kernel(groups, place, rows_in, hidden_units, *weight_grads):
@@ -1456,7 +1458,7 @@
         window.insert(0, came)
     place = jnp.stack([head, lax.axis_index("group")])
     out_here = lax.all_gather(ffn_out, "level", axis=0)
-    w_in = [lax.all_gather(part, "level", axis=0) for part in in_rows]
+    w_in = lax.all_gather(jnp.stack(in_rows), "level", axis=0)
 
 
     def lines(values):
@@ -1474,10 +1476,10 @@
     out_sig = sigs[:, VEXP : 2 * VEXP]
     out_mask = masks[:, VEXP : 2 * VEXP]
     out_gate = out_sig * out_mask
+    attended, out_here = lax.optimization_barrier((attended, out_here))
+    w_out = [out_here] + [turn(out_here, "group", k) for k in range(1, groups)]
     mixed = low((out_gate[..., None] * attended[:, None, :]).reshape(rows, VEXP * DH))
     branch = level_scatter(low(transposed(mixed, w_output)), 2)
-    branch, out_here = lax.optimization_barrier((branch, out_here))
-    w_out = [out_here] + [turn(out_here, "group", k) for k in range(1, groups)]
 
     own_routes, r_ffn, gain_two, bias_two, own_tokens = ffn_side
     middle, extended, ffn_sig = enter_ffn(own_tokens, branch, own_routes, r_ffn, gain_two, bias_two)
@@ -1488,6 +1490,7 @@
         place, hidden, cotangent, w_in, w_out, gates, local_experts
     )
     summed, beyond = pair_scatter(grad_rows, 4, True)
+    beyond, hidden = lax.optimization_barrier((beyond, hidden))
     came = to_far(beyond)
     grad_in = ffn_rear(place, hidden, grad_pre, width, groups, levels)
     in_came = [turn(grad_in[k], "group", k) for k in range(1, groups)]
@@ -1511,8 +1514,8 @@
     def over_levels(total):
         return lax.psum_scatter(total, "level", scatter_dimension=0)
 
-    grad_branch, in_total = lax.optimization_barrier((grad_branch, sum_of(grad_in, in_came)))
-    ffn_in_grad = over_levels(in_total)
+    grad_branch, in_came = lax.optimization_barrier((grad_branch, in_came))
+    ffn_in_grad = over_levels(sum_of(grad_in, in_came))
     grad_attended, row_inner, grad_out_logit, grad_w_output = branch_back(
         grad_branch, full, attended, sigs, masks
     )

time: 718 us -> 710 us (0.989)
  waiting for transfers between devices: 108 us -> 97.3 us
    ppermute x3, waiting for transfers between devices: 15.4 us -> 5.88 us  [to_far(): lax.ppermute(rows, 'head', [(i, (i + 2) % HEADS) for i in range(HEADS)])]
    unnamed x100 -> x86, local copies, waits for them, and re-layouts: 21.6 us -> 22.3 us
  transfers between devices with their start and end apart: 17 -> 16, of which waited for: 7 -> 5; matrix products, arithmetic and copies ran while one was open for 7% -> 7% of each run, Pallas kernels for 55% -> 57%
where the time goes in v8:
time: 710 us; the launch traced here: 703 us
  Pallas kernels  469 us (66%)
  waiting for transfers between devices  97.3 us (14%)
  starting transfers between devices  45 us (6%)
  local copies, waits for them, and re-layouts  42.8 us (6%)
  other arithmetic  28.4 us (4%)
  between operations  14.6 us (2%)
    pallas_call x1, Pallas kernels, finish(): pl.pallas_call(functools.partial(finish_kernel, layout), out_shape=[jax.S...  98.2 us
    ppermute x4, waiting for transfers between devices, shift(): return lax.ppermute(value, axis, pairs)  91.3 us
    pallas_call x1, Pallas kernels, start(): pl.pallas_call(start_kernel, out_shape=shapes, in_specs=[pl.BlockSpec(mem...  89.7 us
    pallas_call x2, Pallas kernels, level_gather(): pl.pallas_call(functools.partial(gather_kernel, by_source), out_shape=jax...  59.5 us
    pallas_call x1, Pallas kernels, ffn_front(): pl.pallas_call(functools.partial(front_kernel, groups, local), grid_spec=...  36.9 us
    pallas_call x2, Pallas kernels, ffn_rear(): pl.pallas_call(functools.partial(rear_kernel, groups), grid_spec=pltpu.Pr...  28.2 us
    pallas_call x1, Pallas kernels, level_scatter(): pl.pallas_call(functools.partial(scatter_kernel, by_source), out_shape=ja...  27.3 us
    ppermute x4, starting transfers between devices, turn(): lax.ppermute(value, axis, [(i, (i + by) % size) for i in range(size)])  25.1 us
  transfers between devices with their start and end apart: 16, of which 5 were waited for; matrix products, arithmetic and copies ran while one was open for 7% of the time, Pallas kernels for 57%

profile of v8, /device:TPU:8, one launch (start us, length us, event | category | flops | bytes accessed | tf_op | source)
XLA Modules:
  0.0 703.4 jit_solution(2865601450275673024)
XLA Ops:
  17.0 89.7 %start.1 = (bf16[4,4,4,32,1024]{4,3,2,1,0:T(8,128)(2,1)}, bf16[4,4,32,1024]{3,2,1,0:T(8,128)(2,1)}, bf16[2,4,4,32,1664]{4,3,2,1,0:T(8,128)(2,1)}, s32[4,4,512]{2...) custom-call(bf16[4,4,32,1024]{3,2,1,0:T(8,128)(2,1)} %bitcast.167, bf16[4,4,32,1024]{3,2,1,0:T(8,128)(2,1)} %bitcast.168, ...), custom_call_target="tpu_custom_call" | custom-call | bytes 200000000 | tf_op jit(solution)/shard_map/start/pallas_call | solution.py:459
  111.3 14.4 %project.1 = (bf16[2048,128]{1,0:T(8,128)(2,1)S(1)}, bf16[2048,256]{1,0:T(8,128)(2,1)}, f32[2048,640]{1,0:T(8,128)}, f32[2048,128]{1,0:T(8,128)S(1)}, f32[2048,16]{1,0:T(8,128)S(1)}) custom-call(bf16[2048,1024]{1,0:T(8,128)(2,1)} %bitcast.152, bf16[1024,1664]{1,0:T(8,128)(2,1)} %bitcast.141, bf16[1024,1664]{1,0:T(8,128)(2,1)} %bitcast.142, ...), custom_call_target="tpu_custom_call" | custom-call | flops 4294967296 | bytes 20000000 | tf_op jit(solution)/shard_map/project/pallas_call | solution.py:1211
  131.1 22.4 %collective-permute-done.1.refs_1_.refs_4_ = bf16[2048,256]{1,0:T(8,128)(2,1)} collective-permute-done((bf16[2048,256]{1,0:T(8,128)(2,1)}, bf16[2048,256]{1,0:T(8,128)(2,1)}, u32[]{:S(2)}, u32[]{:S(2)}) %collective-permute-start.1) | collective-permute-done | bytes 1048608 | tf_op jit(solution)/shard_map/ppermute | solution.py:1316
  155.1 5.7 collective-permute-start.2
  167.3 28.4 %level_gather.2 = bf16[4,4,128,1024]{3,2,1,0:T(8,128)(2,1)} custom-call(bf16[4,128,1024]{2,1,0:T(8,128)(2,1)} %bitcast.120), custom_call_target="tpu_custom_call" | custom-call | bytes 90000000 | tf_op jit(solution)/shard_map/level_gather/pallas_call | solution.py:105
  195.7 17.1 %collective-permute-done.2.refs_0_.refs_3_ = bf16[2048,256]{1,0:T(8,128)(2,1)} collective-permute-done((bf16[2048,256]{1,0:T(8,128)(2,1)}, bf16[2048,256]{1,0:T(8,128)(2,1)}, u32[]{:S(2)}, u32[]{:S(2)}) %collective-permute-start.2) | collective-permute-done | bytes 1048608 | tf_op jit(solution)/shard_map/ppermute | solution.py:1316
  213.9 14.9 %attend.1 = (f32[2048,128]{1,0:T(8,128)S(1)}, f32[4,1,512]{2,1,0:T(1,128)S(1)}) custom-call(s32[4]{0:T(128)S(1)} %subtract_maximum_fusion.first, bf16[2048,128]{1,0:T(8,128)(2,1)S(1)} %copy-done.20, bf16[2048,256]{1,0:T(8,128)(2,1)} %collective-permute-done.2.refs_0_.refs_3_, bf16[2048,256]{1,0:T(8,128)(2,1)} %collective-permute-done.1.refs_1_.refs_4_, ...), custom_call_target="tpu_custom_call" | custom-call | flops 20000000000 | bytes 10000000 | tf_op jit(solution)/shard_map/attend/pallas_call | solution.py:719
  229.8 10.2 %collective-permute-start.3 = (bf16[4,512,512]{2,1,0:T(8,128)(2,1)}, bf16[4,512,512]{2,1,0:T(8,128)(2,1)}, u32[]{:S(2)}, u32[]{:S(2)}) collective-permute-start(bf16[4,512,512]{2,1,0:T(8,128)(2,1)} %bitcast.186), channel_id=1, source_target_pairs={{0,16},{16,0},{1,17},{17,1},{2,18},{18,2},{3,19},{19,3},{4,20},{20... | collective-permute-start | bytes 6291464 | tf_op jit(solution)/shard_map/ppermute | solution.py:1153
  243.7 2.6 copy.139
  248.0 5.1 convolution_convert_fusion
  253.1 27.3 %level_scatter.1 = f32[4,128,1024]{2,1,0:T(8,128)S(1)} custom-call(bf16[4,4,128,1024]{3,2,1,0:T(8,128)(2,1)S(1)} %bitcast.118), custom_call_target="tpu_custom_call" | custom-call | bytes 80000000 | tf_op jit(solution)/shard_map/level_scatter/pallas_call | solution.py:167
  284.7 31.1 %level_gather.3 = bf16[4,4,128,1152]{3,2,1,0:T(8,128)(2,1)} custom-call(bf16[4,128,1152]{2,1,0:T(8,128)(2,1)} %bitcast.126), custom_call_target="tpu_custom_call" | custom-call | bytes 90000000 | tf_op jit(solution)/shard_map/level_gather/pallas_call | solution.py:105
  318.0 36.9 %ffn_front.1 = (bf16[2048,2048]{1,0:T(8,128)(2,1)}, bf16[2048,2048]{1,0:T(8,128)(2,1)}, bf16[2048,1152]{1,0:T(8,128)(2,1)}) custom-call(s32[2]{0:T(128)} %pad_add_fusion.1.place, bf16[2048,1152]{1,0:T(8,128)(2,1)} %bitcast.155, bf16[2048,1024]{1,0:T(8,128)(2,1)} %bitcast.157, bf16[4,2,512,512]{3,2,1,0:T(8,128)(2,1)} %bitcast.185, ...), custom_call_target="tpu_custom_call" | custom-call | flops 25769803776 | bytes 30000000 | tf_op jit(solution)/shard_map/ffn_front/pallas_call | solution.py:893
  354.9 2.3 copy-done.4
  357.3 5.8 pair_scatter.2
  365.3 14.0 %ffn_rear.2 = (bf16[4,512,512]{2,1,0:T(8,128)(2,1)}, bf16[4,512,512]{2,1,0:T(8,128)(2,1)}) custom-call(s32[2]{0:T(128)} %pad_add_fusion.1.place, bf16[2048,1152]{1,0:T(8,128)(2,1)} %bitcast.156, bf16[2048,2048]{1,0:T(8,128)(2,1)} %get-tuple-element.131.hidden_units), custom_call_target="tpu_custom_call" | custom-call | flops 8589934592 | bytes 30000000 | tf_op jit(solution)/shard_map/ffn_rear/pallas_call | solution.py:967
  379.4 14.2 %ffn_rear.3 = (bf16[4,512,512]{2,1,0:T(8,128)(2,1)}, bf16[4,512,512]{2,1,0:T(8,128)(2,1)}) custom-call(s32[2]{0:T(128)} %pad_add_fusion.1.place, bf16[2048,1024]{1,0:T(8,128)(2,1)} %bitcast.158, bf16[2048,2048]{1,0:T(8,128)(2,1)} %get-tuple-element.134.hidden_units.active), custom_call_target="tpu_custom_call" | custom-call | flops 8589934592 | bytes 30000000 | tf_op jit(solution)/shard_map/ffn_rear/pallas_call | solution.py:967
  393.6 7.4 %leave_ffn.1 = (f32[512,1024]{1,0:T(8,128)}, bf16[512,1024]{1,0:T(8,128)(2,1)}, bf16[1024,128]{1,0:T(8,128)(2,1)S(1)}) custom-call(f32[512,1024]{1,0:T(8,128)} %copy-done.2, f32[512,1152]{1,0:T(8,128)} %bitcast.122, bf16[512,1152]{1,0:T(8,128)(2,1)S(1)} %collective-permute-done.4.came, bf16[512,1024]{1,0:T(8,128)(2,1)S(1)} %bitcast.121, ...), custom_call_target="tpu_custom_call" | custom-call | flops 1000000000 | bytes 10000000 | tf_op jit(solution)/shard_map/leave_ffn/pallas_call | solution.py:1063
  402.9 18.2 %ffn_feed.1 = bf16[2048,1024]{1,0:T(8,128)(2,1)} custom-call(s32[2]{0:T(128)} %pad_add_fusion.1.place, bf16[2048,2048]{1,0:T(8,128)(2,1)} %get-tuple-element.134.hidden_units.active, bf16[4,512,512]{2,1,0:T(8,128)(2,1)} %bitcast.188, bf16[4,512,512]{2,1,0:T(8,128)(2,1)} %collective-permute-done.3.refs_2_.refs_1_), custom_call_target="tpu_custom_call" | custom-call | flops 8589934592 | bytes 30000000 | tf_op jit(solution)/shard_map/ffn_feed/pallas_call | solution.py:946
  421.1 5.9 collective-permute-done.5
  427.9 6.1 pair_gather.1
  434.2 12.6 %branch_back.1 = (bf16[2048,128]{1,0:T(8,128)(2,1)S(1)}, f32[4,1,512]{2,1,0:T(1,128)S(1)}, bf16[2048,128]{1,0:T(8,128)(2,1)S(1)}, bf16[1024,640]{1,0:T(8,128)(2,1)S(1)}) custom-call(bf16[2048,1024]{1,0:T(8,128)(2,1)} %bitcast.159, bf16[1024,1664]{1,0:T(8,128)(2,1)} %bitcast.147, f32[2048,128]{1,0:T(8,128)S(1)} %copy-done.14, ...), custom_call_target="tpu_custom_call" | custom-call | flops 5368709120 | bytes 20000000 | tf_op jit(solution)/shard_map/branch_back/pallas_call | solution.py:1122
  449.4 3.6 add_convert_fusion.1
  454.1 20.2 %attend_back.1 = (bf16[2048,128]{1,0:T(8,128)(2,1)S(1)}, bf16[2048,256]{1,0:T(8,128)(2,1)S(1)}, bf16[2048,256]{1,0:T(8,128)(2,1)S(1)}, f32[2048,256]{1,0:T(8,128)}) custom-call(s32[4]{0:T(128)S(1)} %subtract_maximum_fusion.first, bf16[2048,128]{1,0:T(8,128)(2,1)S(1)} %copy-done.21, bf16[2048,256]{1,0:T(8,128)(2,1)} %collective-permute-done.2.refs_0_.refs_3_, ...), custom_call_target="tpu_custom_call" | custom-call | flops 20000000000 | bytes 10000000 | tf_op jit(solution)/shard_map/attend_back/pallas_call | solution.py:803
  476.3 13.2 %collective-permute-start.10 = (bf16[4,512,512]{2,1,0:T(8,128)(2,1)S(1)}, bf16[4,512,512]{2,1,0:T(8,128)(2,1)S(1)}, u32[]{:S(2)}, u32[]{:S(2)}) collective-permute-start(bf16[4,512,512]{2,1,0:T(8,128)(2,1)S(1)} %copy-done.37), channel_id=1, source_target_pairs={{0,16},{16,0},{1,17},{17,1},{2,18},{18,2},{3,19},{19,3},{4,20},{20... | collective-permute-start | bytes 6291464 | tf_op jit(solution)/shard_map/ppermute | solution.py:1153
  489.4 4.4 pair_scatter.3
  493.8 27.4 %collective-permute-done.7 = bf16[2048,256]{1,0:T(8,128)(2,1)S(1)} collective-permute-done((bf16[2048,256]{1,0:T(8,128)(2,1)S(1)}, bf16[2048,256]{1,0:T(8,128)(2,1)S(1)}, u32[]{:S(2)}, u32[]{:S(2)}) %collective-permute-start.7) | collective-permute-done | bytes 1048608 | tf_op jit(solution)/shard_map/ppermute | solution.py:1316
  523.7 24.4 %collective-permute-done.9 = bf16[2048,256]{1,0:T(8,128)(2,1)S(1)} collective-permute-done((bf16[2048,256]{1,0:T(8,128)(2,1)S(1)}, bf16[2048,256]{1,0:T(8,128)(2,1)S(1)}, u32[]{:S(2)}, u32[]{:S(2)}) %collective-permute-start.9) | collective-permute-done | bytes 1048608 | tf_op jit(solution)/shard_map/ppermute | solution.py:1316
  553.8 23.2 %project_back.1 = (bf16[2048,1024]{1,0:T(8,128)(2,1)}, bf16[1024,1024]{1,0:T(8,128)(2,1)}) custom-call(bf16[2048,1024]{1,0:T(8,128)(2,1)} %bitcast.153, f32[2048,256]{1,0:T(8,128)} %convert_add_fusion.grads, bf16[2048,128]{1,0:T(8,128)(2,1)} %copy-done.23, bf16[2048,128]{1,0:T(8,128)(2,1)} %copy-done.22, f32[2048,640]{1,0:T(8,128)} %get-tuple-element.156.projected, ...), custom_call_target="tpu_custom_call" | custom-call | flops 8589934592 | bytes 40000000 | tf_op jit(solution)/shard_map/project_back/pallas_call | solution.py:1291
  578.7 4.6 all-to-all-start
  583.3 98.2 %finish.1 = (f32[4,4,32,1024]{3,2,1,0:T(8,128)}, f32[32,2560]{1,0:T(8,128)}, f32[32,512]{1,0:T(8,128)}, f32[32,512]{1,0:T(8,128)}, f32[4,32,128]{2,1,0:T(8,128)}...) custom-call(bf16[4,4,128,1024]{3,2,1,0:T(8,128)(2,1)} %bitcast.160, f32[4,128,1024]{2,1,0:T(8,128)} %bitcast.164, ...), custom_call_target="tpu_custom_call" | custom-call | bytes 200000000 | tf_op jit(solution)/shard_map/finish/pallas_call | solution.py:626
  687.2 2.3 bitcast_convert_fusion.1
  (177 shorter events, 75.0 us)
Async XLA Ops:
  7.2 9.2 %copy-start = (s32[512,16]{0,1:T(8,128)S(1)}, s32[512,16]{0,1:T(8,128)}, u32[]{:S(2)}) copy-start(s32[512,16]{0,1:T(8,128)} %param.26) | copy-start | bytes 98308
  7.2 222.6 %all-gather.5.cloned.1.call-start = ((), (), s32[]{:S(2)}) async-start(), calls=%async_computation.5 | async-start | bytes 2621440 | tf_op jit(solution)/shard_map/all_gather | solution.py:1460
  7.2 101.0 %collective-permute-start = (bf16[512,512]{1,0:T(8,128)(2,1)}, bf16[512,512]{1,0:T(8,128)(2,1)S(1)}, u32[]{:S(2)}, u32[]{:S(2)}) collective-permute-start(bf16[512,512]{1,0:T(8,128)(2,1)} %param.38), channel_id=1, source_target_pairs={{0,16},{16,0},{1,17},{17,1},{2,18},{18,2},{3,19},{19,3},{4,20},{20... | collective-permute-start | bytes 1572872 | tf_op jit(solution)/shard_map/ppermute | solution.py:1153
  110.5 15.2 %copy-start.17 = (f32[1024]{0:T(1024)}, f32[1024]{0:T(1024)S(1)}, u32[]{:S(2)}) copy-start(f32[1024]{0:T(1024)S(1)} %get-tuple-element.252) | copy-start | bytes 12292
  110.5 15.2 %copy-start.18 = (f32[1024]{0:T(1024)}, f32[1024]{0:T(1024)S(1)}, u32[]{:S(2)}) copy-start(f32[1024]{0:T(1024)S(1)} %get-tuple-element.253) | copy-start | bytes 12292
  111.3 19.3 %copy-start.38 = (s32[1,3]{1,0:T(1,128)S(1)}, s32[1,3]{1,0:T(1,128)}, u32[]{:S(2)}) copy-start(s32[1,3]{1,0:T(1,128)} %param.23) | copy-start | bytes 40
  111.3 42.2 %copy-start.31 = (bf16[512,512]{1,0:T(8,128)(2,1)S(1)}, bf16[512,512]{1,0:T(8,128)(2,1)}, u32[]{:S(2)}) copy-start(bf16[512,512]{1,0:T(8,128)(2,1)} %param.38) | copy-start | bytes 1572868
  126.5 307.6 %copy-start.10 = (f32[2048,128]{1,0:T(8,128)}, f32[2048,128]{1,0:T(8,128)S(1)}, u32[]{:S(2)}) copy-start(f32[2048,128]{1,0:T(8,128)S(1)} %get-tuple-element.107.sigs) | copy-start | bytes 3145732
  126.5 307.6 %copy-start.11 = (f32[2048,16]{1,0:T(8,128)}, f32[2048,16]{1,0:T(8,128)S(1)}, u32[]{:S(2)}) copy-start(f32[2048,16]{1,0:T(8,128)S(1)} %get-tuple-element.108.masks) | copy-start | bytes 393220
  126.5 28.3 %copy-start.36 = (s32[4,16,128]{2,1,0:T(8,128)S(1)}, s32[4,16,128]{2,1,0:T(8,128)}, u32[]{:S(2)}) copy-start(s32[4,16,128]{2,1,0:T(8,128)} %get-tuple-element.105) | copy-start | bytes 98308
  126.5 26.9 %collective-permute-start.1 = (bf16[2048,256]{1,0:T(8,128)(2,1)}, bf16[2048,256]{1,0:T(8,128)(2,1)}, u32[]{:S(2)}, u32[]{:S(2)}) collective-permute-start(bf16[2048,256]{1,0:T(8,128)(2,1)} %get-tuple-element.100.refs_2_.refs_5_), channel_id=1, source_target_pairs={{0,4},{4,8},{8,12},{1,5},{5,9},{9,13},{2,6},{6,10},{10,14},{3,7},{... | collective-permute-start | bytes 3145736 | tf_op jit(solution)/shard_map/ppermute | solution.py:1316
  153.5 164.5 %all-gather.7.cloned.1.call-start = ((), (), s32[]{:S(2)}) async-start(), calls=%async_computation.6 | async-start | bytes 5242880 | tf_op jit(solution)/shard_map/all_gather | solution.py:1461
  154.6 532.6 %reduce-scatter.3.cloned.1.call-start = ((), (), s32[]{:S(2)}) async-start(), calls=%async_computation.3 | async-start | bytes 2621440 | tf_op jit(solution)/shard_map/reduce_scatter | solution.py:1515
  155.1 57.8 %collective-permute-start.2 = (bf16[2048,256]{1,0:T(8,128)(2,1)}, bf16[2048,256]{1,0:T(8,128)(2,1)}, u32[]{:S(2)}, u32[]{:S(2)}) collective-permute-start(bf16[2048,256]{1,0:T(8,128)(2,1)} %collective-permute-done.1.refs_1_.refs_4_), channel_id=1, source_target_pairs={{0,4},{4,8},{8,12},{1,5},{5,9},{9,13},{2,6},{6,10},{10,14},{3,7},{... | collective-permute-start | bytes 3145736 | tf_op jit(solution)/shard_map/ppermute | solution.py:1316
  229.8 88.2 %collective-permute-start.3 = (bf16[4,512,512]{2,1,0:T(8,128)(2,1)}, bf16[4,512,512]{2,1,0:T(8,128)(2,1)}, u32[]{:S(2)}, u32[]{:S(2)}) collective-permute-start(bf16[4,512,512]{2,1,0:T(8,128)(2,1)} %bitcast.186), channel_id=1, source_target_pairs={{0,16},{16,0},{1,17},{17,1},{2,18},{18,2},{3,19},{19,3},{4,20},{20... | collective-permute-start | bytes 6291464 | tf_op jit(solution)/shard_map/ppermute | solution.py:1153
  253.1 27.3 %copy-start.12 = (bf16[4,1,4,32,1024]{4,3,2,1,0:T(8,128)(2,1)S(1)}, bf16[4,1,4,32,1024]{4,3,2,1,0:T(8,128)(2,1)}, u32[]{:S(2)}) copy-start(bf16[4,1,4,32,1024]{4,3,2,1,0:T(8,128)(2,1)} %constant_dynamic-slice_fusion) | copy-start | bytes 3145732
  364.5 29.1 %collective-permute-start.4 = (bf16[512,1152]{1,0:T(8,128)(2,1)}, bf16[512,1152]{1,0:T(8,128)(2,1)S(1)}, u32[]{:S(2)}, u32[]{:S(2)}) collective-permute-start(bf16[512,1152]{1,0:T(8,128)(2,1)} %bitcast.38), channel_id=1, source_target_pairs={{0,2},{1,3},{2,0},{3,1},{4,6},{5,7},{6,4},{7,5},{8,10},{9,11},{10,... | collective-permute-start | bytes 3538952 | tf_op jit(solution)/shard_map/ppermute | solution.py:287
  379.3 54.8 %collective-permute-start.6 = (bf16[4,512,512]{2,1,0:T(8,128)(2,1)}, bf16[4,512,512]{2,1,0:T(8,128)(2,1)}, u32[]{:S(2)}, u32[]{:S(2)}) collective-permute-start(bf16[4,512,512]{2,1,0:T(8,128)(2,1)} %get-tuple-element.133), channel_id=1, source_target_pairs={{0,16},{16,0},{1,17},{17,1},{2,18},{18,2},{3,19},{19,3},{4,20},{20... | collective-permute-start | bytes 6291464 | tf_op jit(solution)/shard_map/ppermute | solution.py:1153
  379.4 14.2 %copy-start.6 = (bf16[4,4,32,1024]{3,2,1,0:T(8,128)(2,1)S(1)}, bf16[4,4,32,1024]{3,2,1,0:T(8,128)(2,1)}, u32[]{:S(2)}) copy-start(bf16[4,4,32,1024]{3,2,1,0:T(8,128)(2,1)} %get-tuple-element.101) | copy-start | bytes 3145732
  401.7 25.2 %collective-permute-start.5 = (bf16[512,1024]{1,0:T(8,128)(2,1)}, bf16[512,1024]{1,0:T(8,128)(2,1)S(1)}, u32[]{:S(2)}, u32[]{:S(2)}) collective-permute-start(bf16[512,1024]{1,0:T(8,128)(2,1)} %get-tuple-element.139), channel_id=1, source_target_pairs={{0,2},{1,3},{2,0},{3,1},{4,6},{5,7},{6,4},{7,5},{8,10},{9,11},{10,... | collective-permute-start | bytes 3145736 | tf_op jit(solution)/shard_map/ppermute | solution.py:287
  434.1 15.3 %copy-start.27 = (bf16[4,512,512]{2,1,0:T(8,128)(2,1)S(1)}, bf16[4,512,512]{2,1,0:T(8,128)(2,1)}, u32[]{:S(2)}) copy-start(bf16[4,512,512]{2,1,0:T(8,128)(2,1)} %get-tuple-element.171) | copy-start | bytes 6291460
  453.0 236.5 %reduce-scatter.5.cloned.1.call-start = ((), (), s32[]{:S(2)}) async-start(), calls=%async_computation.4 | async-start | bytes 2621440 | tf_op jit(solution)/shard_map/reduce_scatter | solution.py:1515
  454.1 22.1 %copy-start.37 = (bf16[4,512,512]{2,1,0:T(8,128)(2,1)S(1)}, bf16[4,512,512]{2,1,0:T(8,128)(2,1)}, u32[]{:S(2)}) copy-start(bf16[4,512,512]{2,1,0:T(8,128)(2,1)} %get-tuple-element.136) | copy-start | bytes 6291460
  454.1 35.3 %copy-start.5 = (bf16[2048,1024]{1,0:T(8,128)(2,1)S(1)}, bf16[2048,1024]{1,0:T(8,128)(2,1)}, u32[]{:S(2)}) copy-start(bf16[2048,1024]{1,0:T(8,128)(2,1)} %ffn_feed.1) | copy-start | bytes 12582916
  474.3 47.2 %copy-start.23 = (bf16[2048,128]{1,0:T(8,128)(2,1)}, bf16[2048,128]{1,0:T(8,128)(2,1)S(1)}, u32[]{:S(2)}) copy-start(bf16[2048,128]{1,0:T(8,128)(2,1)S(1)} %get-tuple-element.154.grad_query) | copy-start | bytes 1572868
  474.3 46.9 %collective-permute-start.7 = (bf16[2048,256]{1,0:T(8,128)(2,1)S(1)}, bf16[2048,256]{1,0:T(8,128)(2,1)S(1)}, u32[]{:S(2)}, u32[]{:S(2)}) collective-permute-start(bf16[2048,256]{1,0:T(8,128)(2,1)S(1)} %get-tuple-element.145), channel_id=1, source_target_pairs={{4,0},{8,4},{12,8},{5,1},{9,5},{13,9},{6,2},{10,6},{14,10},{7,3},{... | collective-permute-start | bytes 3145736 | tf_op jit(solution)/shard_map/ppermute | solution.py:1316
  476.3 73.4 %collective-permute-start.10 = (bf16[4,512,512]{2,1,0:T(8,128)(2,1)S(1)}, bf16[4,512,512]{2,1,0:T(8,128)(2,1)S(1)}, u32[]{:S(2)}, u32[]{:S(2)}) collective-permute-start(bf16[4,512,512]{2,1,0:T(8,128)(2,1)S(1)} %copy-done.37), channel_id=1, source_target_pairs={{0,16},{16,0},{1,17},{17,1},{2,18},{18,2},{3,19},{19,3},{4,20},{20... | collective-permute-start | bytes 6291464 | tf_op jit(solution)/shard_map/ppermute | solution.py:1153
  493.8 54.3 %copy-start.29 = (f32[2048,256]{1,0:T(8,128)S(1)}, f32[2048,256]{1,0:T(8,128)}, u32[]{:S(2)}) copy-start(f32[2048,256]{1,0:T(8,128)} %get-tuple-element.150) | copy-start | bytes 6291460
  521.5 26.6 %collective-permute-start.9 = (bf16[2048,256]{1,0:T(8,128)(2,1)S(1)}, bf16[2048,256]{1,0:T(8,128)(2,1)S(1)}, u32[]{:S(2)}, u32[]{:S(2)}) collective-permute-start(bf16[2048,256]{1,0:T(8,128)(2,1)S(1)} %add_convert_fusion.3), channel_id=1, source_target_pairs={{4,0},{8,4},{12,8},{5,1},{9,5},{13,9},{6,2},{10,6},{14,10},{7,3},{... | collective-permute-start | bytes 3145736 | tf_op jit(solution)/shard_map/ppermute | solution.py:1316
  552.4 24.7 %collective-permute-start.8 = (bf16[512,1024]{1,0:T(8,128)(2,1)S(1)}, bf16[512,1024]{1,0:T(8,128)(2,1)S(1)}, u32[]{:S(2)}, u32[]{:S(2)}) collective-permute-start(bf16[512,1024]{1,0:T(8,128)(2,1)S(1)} %bitcast.139), channel_id=1, source_target_pairs={{0,2},{1,3},{2,0},{3,1},{4,6},{5,7},{6,4},{7,5},{8,10},{9,11},{10,... | collective-permute-start | bytes 3145736 | tf_op jit(solution)/shard_map/ppermute | solution.py:287
  553.8 23.2 %copy-start.3 = (f32[512,1024]{1,0:T(8,128)S(1)}, f32[512,1024]{1,0:T(8,128)}, u32[]{:S(2)}) copy-start(f32[512,1024]{1,0:T(8,128)} %copy-done.2) | copy-start | bytes 6291460
  578.7 108.5 %all-to-all-start = ((bf16[4,128,1024]{2,1,0:T(8,128)(2,1)}), bf16[4,128,1024]{2,1,0:T(8,128)(2,1)S(1)}, u32[]{:S(2)}, u32[]{:S(2)}) async-start(bf16[4,128,1024]{2,1,0:T(8,128)(2,1)} %bitcast.47), calls=%async_computation | async-start | bytes 2097152 | tf_op jit(solution)/shard_map/all_to_all | solution.py:33
  (23 other events, 46.9 us)
Sparse Core Ops, SparseCore 0:
  153.6 61.5 all-gather.4
  216.8 77.4 all-gather.6
  453.1 53.6 reduce-scatter.2
  552.5 53.2 reduce-scatter.4

commit v9 on v8

--- a/solution.py
+++ b/solution.py
@@ -806,7 +806,7 @@
         out_shape=[jax.ShapeDtypeStruct((rows, DH), jnp.bfloat16)]
         + [jax.ShapeDtypeStruct((rows, 2 * DH), kind) for kind in kinds],
         compiler_params=pltpu.CompilerParams(vmem_limit_bytes=48 * 2**20),
-        cost_estimate=cost(2e10, 1e7),
+        cost_estimate=cost(2e9, 1e6),
         name="attend_back",
     )(first, queries, *window, *window, grads, pos_q, start_q, lse, inner, pos_k)
 
@@ -955,7 +955,7 @@
         ),
         out_shape=jax.ShapeDtypeStruct((rows, groups * depth), jnp.bfloat16),
         compiler_params=pltpu.CompilerParams(vmem_limit_bytes=58 * 2**20),
-        cost_estimate=cost(2 * rows * groups * depth * levels * width, 3e7),
+        cost_estimate=cost(1e3, 1e3),
         name="ffn_feed",
     )(place, active, *weights)
 
@@ -977,7 +977,7 @@
         ),
         out_shape=[jax.ShapeDtypeStruct((levels, depth, width), jnp.bfloat16)] * groups,
         compiler_params=pltpu.CompilerParams(vmem_limit_bytes=58 * 2**20),
-        cost_estimate=cost(2 * rows * groups * depth * levels * width, 3e7),
+        cost_estimate=cost(1e3, 1e3),
         name="ffn_rear",
     )(place, rows_in, units)
 
@@ -1143,7 +1143,7 @@
         ],
         scratch_shapes=[pltpu.VMEM((width, values), jnp.float32)],
         compiler_params=pltpu.CompilerParams(vmem_limit_bytes=48 * 2**20),
-        cost_estimate=cost(4 * rows * width * values, 2e7),
+        cost_estimate=cost(1e8, 1e6),
         name="branch_back",
     )(grads, full, attended, sigs, masks)
 
@@ -1305,7 +1305,7 @@
             pltpu.VMEM((128, width), jnp.float32),
         ],
         compiler_params=pltpu.CompilerParams(vmem_limit_bytes=56 * 2**20),
-        cost_estimate=cost(4 * total * width * 1024, 4e7),
+        cost_estimate=cost(total * width * 512, 4e6),
         name="project_back",
     )(rows, grads, grad_query, out_logit, projected, sigs, masks, full, full, full, full, gain, bias)
 

time: 710 us -> 702 us (0.989)
  starting transfers between devices: 45 us -> 23 us
    ppermute x4, starting transfers between devices: 25.1 us -> 3.82 us  [turn(): lax.ppermute(value, axis, [(i, (i + by) % size) for i in range(size)])]
  transfers between devices with their start and end apart: 16 -> 16, of which waited for: 5 -> 5; matrix products, arithmetic and copies ran while one was open for 7% -> 7% of each run, Pallas kernels for 57% -> 60%
where the time goes in v9:
time: 702 us; the launch traced here: 696 us
  Pallas kernels  476 us (68%)
  waiting for transfers between devices  103 us (15%)
  local copies, waits for them, and re-layouts  42.3 us (6%)
  other arithmetic  31.1 us (4%)
  starting transfers between devices  23 us (3%)
  between operations  14.6 us (2%)
    pallas_call x1, Pallas kernels, finish(): pl.pallas_call(functools.partial(finish_kernel, layout), out_shape=[jax.S...  102 us
    ppermute x4, waiting for transfers between devices, shift(): return lax.ppermute(value, axis, pairs)  97.1 us
    pallas_call x1, Pallas kernels, start(): pl.pallas_call(start_kernel, out_shape=shapes, in_specs=[pl.BlockSpec(mem...  89.7 us
    pallas_call x2, Pallas kernels, level_gather(): pl.pallas_call(functools.partial(gather_kernel, by_source), out_shape=jax...  59.9 us
    pallas_call x1, Pallas kernels, ffn_front(): pl.pallas_call(functools.partial(front_kernel, groups, local), grid_spec=...  36.9 us
    pallas_call x2, Pallas kernels, ffn_rear(): pl.pallas_call(functools.partial(rear_kernel, groups), grid_spec=pltpu.Pr...  28.2 us
    pallas_call x1, Pallas kernels, level_scatter(): pl.pallas_call(functools.partial(scatter_kernel, by_source), out_shape=ja...  26.7 us
    pallas_call x1, Pallas kernels, project_back(): pl.pallas_call(project_back_kernel, grid=(HEADS,), in_specs=[by_row(width...  23.4 us
  transfers between devices with their start and end apart: 16, of which 5 were waited for; matrix products, arithmetic and copies ran while one was open for 7% of the time, Pallas kernels for 60%

profile of v9, /device:TPU:8, one launch (start us, length us, event | category | flops | bytes accessed | tf_op | source)
XLA Modules:
  0.0 696.4 jit_solution(13777088709596150725)
XLA Ops:
  17.0 89.7 %start.1 = (bf16[4,4,4,32,1024]{4,3,2,1,0:T(8,128)(2,1)}, bf16[4,4,32,1024]{3,2,1,0:T(8,128)(2,1)}, bf16[2,4,4,32,1664]{4,3,2,1,0:T(8,128)(2,1)}, s32[4,4,512]{2...) custom-call(bf16[4,4,32,1024]{3,2,1,0:T(8,128)(2,1)} %bitcast.170, bf16[4,4,32,1024]{3,2,1,0:T(8,128)(2,1)} %bitcast.171, ...), custom_call_target="tpu_custom_call" | custom-call | bytes 200000000 | tf_op jit(solution)/shard_map/start/pallas_call | solution.py:459
  111.3 14.3 %project.1 = (bf16[2048,128]{1,0:T(8,128)(2,1)S(1)}, bf16[2048,256]{1,0:T(8,128)(2,1)S(1)}, f32[2048,640]{1,0:T(8,128)}, f32[2048,128]{1,0:T(8,128)S(1)}, f32[2048,16]{1,0:T(8,128)S(1)}) custom-call(bf16[2048,1024]{1,0:T(8,128)(2,1)} %bitcast.152, bf16[1024,1664]{1,0:T(8,128)(2,1)} %bitcast.141, bf16[1024,1664]{1,0:T(8,128)(2,1)} %bitcast.142, ...), custom_call_target="tpu_custom_call" | custom-call | flops 4294967296 | bytes 20000000 | tf_op jit(solution)/shard_map/project/pallas_call | solution.py:1211
  131.0 22.2 %collective-permute-done.1.refs_1_.refs_4_ = bf16[2048,256]{1,0:T(8,128)(2,1)} collective-permute-done((bf16[2048,256]{1,0:T(8,128)(2,1)S(1)}, bf16[2048,256]{1,0:T(8,128)(2,1)}, u32[]{:S(2)}, u32[]{:S(2)}) %collective-permute-start.1) | collective-permute-done | bytes 1048608 | tf_op jit(solution)/shard_map/ppermute | solution.py:1316
  153.3 2.3 pad_maximum_fusion
  157.6 5.6 collective-permute-start.2
  163.4 2.4 constant_dynamic-slice_fusion
  168.2 2.3 copy.138.refs_8_.refs_11_
  170.4 28.4 %level_gather.2 = bf16[4,4,128,1024]{3,2,1,0:T(8,128)(2,1)} custom-call(bf16[4,128,1024]{2,1,0:T(8,128)(2,1)} %bitcast.120), custom_call_target="tpu_custom_call" | custom-call | bytes 90000000 | tf_op jit(solution)/shard_map/level_gather/pallas_call | solution.py:105
  198.9 16.5 %collective-permute-done.2.refs_0_.refs_3_ = bf16[2048,256]{1,0:T(8,128)(2,1)} collective-permute-done((bf16[2048,256]{1,0:T(8,128)(2,1)}, bf16[2048,256]{1,0:T(8,128)(2,1)}, u32[]{:S(2)}, u32[]{:S(2)}) %collective-permute-start.2) | collective-permute-done | bytes 1048608 | tf_op jit(solution)/shard_map/ppermute | solution.py:1316
  217.6 16.2 %attend.1 = (f32[2048,128]{1,0:T(8,128)S(1)}, f32[4,1,512]{2,1,0:T(1,128)S(1)}) custom-call(s32[4]{0:T(128)S(1)} %subtract_maximum_fusion.first, bf16[2048,128]{1,0:T(8,128)(2,1)S(1)} %copy-done.18, bf16[2048,256]{1,0:T(8,128)(2,1)} %collective-permute-done.2.refs_0_.refs_3_, bf16[2048,256]{1,0:T(8,128)(2,1)} %collective-permute-done.1.refs_1_.refs_4_, ...), custom_call_target="tpu_custom_call" | custom-call | flops 20000000000 | bytes 10000000 | tf_op jit(solution)/shard_map/attend/pallas_call | solution.py:719
  240.8 5.1 convolution_convert_fusion
  245.9 26.7 %level_scatter.1 = f32[4,128,1024]{2,1,0:T(8,128)S(1)} custom-call(bf16[4,4,128,1024]{3,2,1,0:T(8,128)(2,1)S(1)} %bitcast.119), custom_call_target="tpu_custom_call" | custom-call | bytes 80000000 | tf_op jit(solution)/shard_map/level_scatter/pallas_call | solution.py:167
  277.5 31.5 %level_gather.3 = bf16[4,4,128,1152]{3,2,1,0:T(8,128)(2,1)} custom-call(bf16[4,128,1152]{2,1,0:T(8,128)(2,1)} %bitcast.126), custom_call_target="tpu_custom_call" | custom-call | bytes 90000000 | tf_op jit(solution)/shard_map/level_gather/pallas_call | solution.py:105
  311.2 36.9 %ffn_front.1 = (bf16[2048,2048]{1,0:T(8,128)(2,1)}, bf16[2048,2048]{1,0:T(8,128)(2,1)}, bf16[2048,1152]{1,0:T(8,128)(2,1)}) custom-call(s32[2]{0:T(128)} %pad_add_fusion.1.place, bf16[2048,1152]{1,0:T(8,128)(2,1)} %bitcast.155, bf16[2048,1024]{1,0:T(8,128)(2,1)} %bitcast.157, bf16[4,2,512,512]{3,2,1,0:T(8,128)(2,1)} %bitcast.187, ...), custom_call_target="tpu_custom_call" | custom-call | flops 25769803776 | bytes 30000000 | tf_op jit(solution)/shard_map/ffn_front/pallas_call | solution.py:893
  348.1 2.3 copy-done.7
  350.5 5.8 pair_scatter.2
  358.8 14.0 %ffn_rear.2 = (bf16[4,512,512]{2,1,0:T(8,128)(2,1)}, bf16[4,512,512]{2,1,0:T(8,128)(2,1)}) custom-call(s32[2]{0:T(128)} %pad_add_fusion.1.place, bf16[2048,1152]{1,0:T(8,128)(2,1)} %bitcast.156, bf16[2048,2048]{1,0:T(8,128)(2,1)} %get-tuple-element.131.hidden_units), custom_call_target="tpu_custom_call" | custom-call | flops 1000 | bytes 1000 | tf_op jit(solution)/shard_map/ffn_rear/pallas_call | solution.py:967
  374.9 14.2 %ffn_rear.3 = (bf16[4,512,512]{2,1,0:T(8,128)(2,1)}, bf16[4,512,512]{2,1,0:T(8,128)(2,1)}) custom-call(s32[2]{0:T(128)} %pad_add_fusion.1.place, bf16[2048,1024]{1,0:T(8,128)(2,1)} %bitcast.158, bf16[2048,2048]{1,0:T(8,128)(2,1)} %get-tuple-element.134.hidden_units.active), custom_call_target="tpu_custom_call" | custom-call | flops 1000 | bytes 1000 | tf_op jit(solution)/shard_map/ffn_rear/pallas_call | solution.py:967
  390.1 7.3 %leave_ffn.1 = (f32[512,1024]{1,0:T(8,128)}, bf16[512,1024]{1,0:T(8,128)(2,1)}, bf16[1024,128]{1,0:T(8,128)(2,1)S(1)}) custom-call(f32[512,1024]{1,0:T(8,128)} %copy-done.5, f32[512,1152]{1,0:T(8,128)} %bitcast.122, bf16[512,1152]{1,0:T(8,128)(2,1)S(1)} %collective-permute-done.4.came, bf16[512,1024]{1,0:T(8,128)(2,1)S(1)} %bitcast.121, ...), custom_call_target="tpu_custom_call" | custom-call | flops 1000000000 | bytes 10000000 | tf_op jit(solution)/shard_map/leave_ffn/pallas_call | solution.py:1063
  398.9 18.2 %ffn_feed.1 = bf16[2048,1024]{1,0:T(8,128)(2,1)} custom-call(s32[2]{0:T(128)} %pad_add_fusion.1.place, bf16[2048,2048]{1,0:T(8,128)(2,1)} %get-tuple-element.134.hidden_units.active, bf16[4,512,512]{2,1,0:T(8,128)(2,1)} %bitcast.166, bf16[4,512,512]{2,1,0:T(8,128)(2,1)} %collective-permute-done.3.refs_2_.refs_1_), custom_call_target="tpu_custom_call" | custom-call | flops 1000 | bytes 1000 | tf_op jit(solution)/shard_map/ffn_feed/pallas_call | solution.py:946
  417.1 6.1 collective-permute-done.5
  423.3 6.1 pair_gather.1
  429.3 4.2 add_convert_fusion.1
  433.6 12.9 %branch_back.1 = (bf16[2048,128]{1,0:T(8,128)(2,1)S(1)}, f32[4,1,512]{2,1,0:T(1,128)S(1)}, bf16[2048,128]{1,0:T(8,128)(2,1)S(1)}, bf16[1024,640]{1,0:T(8,128)(2,1)S(1)}) custom-call(bf16[2048,1024]{1,0:T(8,128)(2,1)} %bitcast.159, bf16[1024,1664]{1,0:T(8,128)(2,1)} %bitcast.147, f32[2048,128]{1,0:T(8,128)S(1)} %get-tuple-element.115.attended, ...), custom_call_target="tpu_custom_call" | custom-call | flops 100000000 | bytes 1000000 | tf_op jit(solution)/shard_map/branch_back/pallas_call | solution.py:1122
  448.4 22.0 %attend_back.1 = (bf16[2048,128]{1,0:T(8,128)(2,1)S(1)}, bf16[2048,256]{1,0:T(8,128)(2,1)S(1)}, bf16[2048,256]{1,0:T(8,128)(2,1)S(1)}, f32[2048,256]{1,0:T(8,128)}) custom-call(s32[4]{0:T(128)S(1)} %subtract_maximum_fusion.first, bf16[2048,128]{1,0:T(8,128)(2,1)S(1)} %copy-done.19, bf16[2048,256]{1,0:T(8,128)(2,1)} %collective-permute-done.2.refs_0_.refs_3_, ...), custom_call_target="tpu_custom_call" | custom-call | flops 2000000000 | bytes 1000000 | tf_op jit(solution)/shard_map/attend_back/pallas_call | solution.py:803
  472.4 4.4 pair_scatter.3
  476.8 31.2 %collective-permute-done.7 = bf16[2048,256]{1,0:T(8,128)(2,1)S(1)} collective-permute-done((bf16[2048,256]{1,0:T(8,128)(2,1)S(1)}, bf16[2048,256]{1,0:T(8,128)(2,1)S(1)}, u32[]{:S(2)}, u32[]{:S(2)}) %collective-permute-start.7) | collective-permute-done | bytes 1048608 | tf_op jit(solution)/shard_map/ppermute | solution.py:1316
  510.3 27.1 %collective-permute-done.9 = bf16[2048,256]{1,0:T(8,128)(2,1)S(1)} collective-permute-done((bf16[2048,256]{1,0:T(8,128)(2,1)S(1)}, bf16[2048,256]{1,0:T(8,128)(2,1)S(1)}, u32[]{:S(2)}, u32[]{:S(2)}) %collective-permute-start.9) | collective-permute-done | bytes 1048608 | tf_op jit(solution)/shard_map/ppermute | solution.py:1316
  543.0 23.4 %project_back.1 = (bf16[2048,1024]{1,0:T(8,128)(2,1)}, bf16[1024,1024]{1,0:T(8,128)(2,1)}) custom-call(bf16[2048,1024]{1,0:T(8,128)(2,1)} %bitcast.153, f32[2048,256]{1,0:T(8,128)} %convert_add_fusion.grads, bf16[2048,128]{1,0:T(8,128)(2,1)} %copy-done.21, bf16[2048,128]{1,0:T(8,128)(2,1)} %copy-done.20, f32[2048,640]{1,0:T(8,128)} %get-tuple-element.156.projected, ...), custom_call_target="tpu_custom_call" | custom-call | flops 1073741824 | bytes 4000000 | tf_op jit(solution)/shard_map/project_back/pallas_call | solution.py:1291
  568.0 4.5 all-to-all-start
  572.5 102.0 %finish.1 = (f32[4,4,32,1024]{3,2,1,0:T(8,128)}, f32[32,2560]{1,0:T(8,128)}, f32[32,512]{1,0:T(8,128)}, f32[32,512]{1,0:T(8,128)}, f32[4,32,128]{2,1,0:T(8,128)}...) custom-call(bf16[4,4,128,1024]{3,2,1,0:T(8,128)(2,1)} %bitcast.160, f32[4,128,1024]{2,1,0:T(8,128)} %bitcast.167, ...), custom_call_target="tpu_custom_call" | custom-call | bytes 200000000 | tf_op jit(solution)/shard_map/finish/pallas_call | solution.py:626
  680.2 2.3 bitcast_convert_fusion.1
  (177 shorter events, 73.9 us)
Async XLA Ops:
  7.2 226.7 %all-gather.5.cloned.1.call-start = ((), (), s32[]{:S(2)}) async-start(), calls=%async_computation.5 | async-start | bytes 2621440 | tf_op jit(solution)/shard_map/all_gather | solution.py:1460
  7.2 101.0 %collective-permute-start = (bf16[512,512]{1,0:T(8,128)(2,1)}, bf16[512,512]{1,0:T(8,128)(2,1)S(1)}, u32[]{:S(2)}, u32[]{:S(2)}) collective-permute-start(bf16[512,512]{1,0:T(8,128)(2,1)} %param.38), channel_id=1, source_target_pairs={{0,16},{16,0},{1,17},{17,1},{2,18},{18,2},{3,19},{19,3},{4,20},{20... | collective-permute-start | bytes 1572872 | tf_op jit(solution)/shard_map/ppermute | solution.py:1153
  110.5 15.1 %copy-start.25 = (f32[1024]{0:T(1024)}, f32[1024]{0:T(1024)S(1)}, u32[]{:S(2)}) copy-start(f32[1024]{0:T(1024)S(1)} %get-tuple-element.252) | copy-start | bytes 12292
  110.5 15.1 %copy-start.26 = (f32[1024]{0:T(1024)}, f32[1024]{0:T(1024)S(1)}, u32[]{:S(2)}) copy-start(f32[1024]{0:T(1024)S(1)} %get-tuple-element.253) | copy-start | bytes 12292
  111.3 19.2 %copy-start.38 = (s32[1,3]{1,0:T(1,128)S(1)}, s32[1,3]{1,0:T(1,128)}, u32[]{:S(2)}) copy-start(s32[1,3]{1,0:T(1,128)} %param.23) | copy-start | bytes 40
  126.4 39.3 %copy-start.9 = (bf16[2048,256]{1,0:T(8,128)(2,1)}, bf16[2048,256]{1,0:T(8,128)(2,1)S(1)}, u32[]{:S(2)}) copy-start(bf16[2048,256]{1,0:T(8,128)(2,1)S(1)} %get-tuple-element.100.refs_2_.refs_5_) | copy-start | bytes 3145732
  126.4 307.1 %copy-start.3 = (f32[2048,128]{1,0:T(8,128)}, f32[2048,128]{1,0:T(8,128)S(1)}, u32[]{:S(2)}) copy-start(f32[2048,128]{1,0:T(8,128)S(1)} %get-tuple-element.107.sigs) | copy-start | bytes 3145732
  126.4 307.1 %copy-start.4 = (f32[2048,16]{1,0:T(8,128)}, f32[2048,16]{1,0:T(8,128)S(1)}, u32[]{:S(2)}) copy-start(f32[2048,16]{1,0:T(8,128)S(1)} %get-tuple-element.108.masks) | copy-start | bytes 393220
  126.4 29.3 %copy-start.36 = (s32[4,16,128]{2,1,0:T(8,128)S(1)}, s32[4,16,128]{2,1,0:T(8,128)}, u32[]{:S(2)}) copy-start(s32[4,16,128]{2,1,0:T(8,128)} %get-tuple-element.105) | copy-start | bytes 98308
  126.4 26.7 %collective-permute-start.1 = (bf16[2048,256]{1,0:T(8,128)(2,1)S(1)}, bf16[2048,256]{1,0:T(8,128)(2,1)}, u32[]{:S(2)}, u32[]{:S(2)}) collective-permute-start(bf16[2048,256]{1,0:T(8,128)(2,1)S(1)} %get-tuple-element.100.refs_2_.refs_5_), channel_id=1, source_target_pairs={{0,4},{4,8},{8,12},{1,5},{5,9},{9,13},{2,6},{6,10},{10,14},{3,7},{... | collective-permute-start | bytes 3145736 | tf_op jit(solution)/shard_map/ppermute | solution.py:1316
  153.2 158.0 %all-gather.7.cloned.1.call-start = ((), (), s32[]{:S(2)}) async-start(), calls=%async_computation.6 | async-start | bytes 5242880 | tf_op jit(solution)/shard_map/all_gather | solution.py:1461
  155.6 524.6 %reduce-scatter.3.cloned.1.call-start = ((), (), s32[]{:S(2)}) async-start(), calls=%async_computation.3 | async-start | bytes 2621440 | tf_op jit(solution)/shard_map/reduce_scatter | solution.py:1515
  157.6 57.8 %collective-permute-start.2 = (bf16[2048,256]{1,0:T(8,128)(2,1)}, bf16[2048,256]{1,0:T(8,128)(2,1)}, u32[]{:S(2)}, u32[]{:S(2)}) collective-permute-start(bf16[2048,256]{1,0:T(8,128)(2,1)} %collective-permute-done.1.refs_1_.refs_4_), channel_id=1, source_target_pairs={{0,4},{4,8},{8,12},{1,5},{5,9},{9,13},{2,6},{6,10},{10,14},{3,7},{... | collective-permute-start | bytes 3145736 | tf_op jit(solution)/shard_map/ppermute | solution.py:1316
  233.9 77.4 %collective-permute-start.3 = (bf16[4,512,512]{2,1,0:T(8,128)(2,1)}, bf16[4,512,512]{2,1,0:T(8,128)(2,1)}, u32[]{:S(2)}, u32[]{:S(2)}) collective-permute-start(bf16[4,512,512]{2,1,0:T(8,128)(2,1)} %bitcast.164), channel_id=1, source_target_pairs={{0,16},{16,0},{1,17},{17,1},{2,18},{18,2},{3,19},{19,3},{4,20},{20... | collective-permute-start | bytes 6291464 | tf_op jit(solution)/shard_map/ppermute | solution.py:1153
  245.8 26.7 %copy-start.14 = (bf16[4,1,4,32,1024]{4,3,2,1,0:T(8,128)(2,1)S(1)}, bf16[4,1,4,32,1024]{4,3,2,1,0:T(8,128)(2,1)}, u32[]{:S(2)}) copy-start(bf16[4,1,4,32,1024]{4,3,2,1,0:T(8,128)(2,1)} %constant_dynamic-slice_fusion) | copy-start | bytes 3145732
  245.9 26.7 %copy-start.15 = (s32[512,16]{1,0:T(8,128)S(1)}, s32[512,16]{1,0:T(8,128)}, u32[]{:S(2)}) copy-start(s32[512,16]{1,0:T(8,128)} %fusion.4.routes) | copy-start | bytes 98308
  357.7 31.4 %collective-permute-start.4 = (bf16[512,1152]{1,0:T(8,128)(2,1)}, bf16[512,1152]{1,0:T(8,128)(2,1)S(1)}, u32[]{:S(2)}, u32[]{:S(2)}) collective-permute-start(bf16[512,1152]{1,0:T(8,128)(2,1)} %bitcast.38), channel_id=1, source_target_pairs={{0,2},{1,3},{2,0},{3,1},{4,6},{5,7},{6,4},{7,5},{8,10},{9,11},{10,... | collective-permute-start | bytes 3538952 | tf_op jit(solution)/shard_map/ppermute | solution.py:287
  372.8 56.6 %collective-permute-start.6 = (bf16[4,512,512]{2,1,0:T(8,128)(2,1)}, bf16[4,512,512]{2,1,0:T(8,128)(2,1)}, u32[]{:S(2)}, u32[]{:S(2)}) collective-permute-start(bf16[4,512,512]{2,1,0:T(8,128)(2,1)} %get-tuple-element.133), channel_id=1, source_target_pairs={{0,16},{16,0},{1,17},{17,1},{2,18},{18,2},{3,19},{19,3},{4,20},{20... | collective-permute-start | bytes 6291464 | tf_op jit(solution)/shard_map/ppermute | solution.py:1153
  374.9 14.2 %copy-start.16 = (s32[512,16]{1,0:T(8,128)S(1)}, s32[512,16]{1,0:T(8,128)}, u32[]{:S(2)}) copy-start(s32[512,16]{1,0:T(8,128)} %fusion.4.routes) | copy-start | bytes 98308
  398.1 25.2 %collective-permute-start.5 = (bf16[512,1024]{1,0:T(8,128)(2,1)}, bf16[512,1024]{1,0:T(8,128)(2,1)}, u32[]{:S(2)}, u32[]{:S(2)}) collective-permute-start(bf16[512,1024]{1,0:T(8,128)(2,1)} %get-tuple-element.139), channel_id=1, source_target_pairs={{0,2},{1,3},{2,0},{3,1},{4,6},{5,7},{6,4},{7,5},{8,10},{9,11},{10,... | collective-permute-start | bytes 3145736 | tf_op jit(solution)/shard_map/ppermute | solution.py:287
  433.5 249.0 %reduce-scatter.5.cloned.1.call-start = ((), (), s32[]{:S(2)}) async-start(), calls=%async_computation.4 | async-start | bytes 2621440 | tf_op jit(solution)/shard_map/reduce_scatter | solution.py:1515
  433.6 14.8 %copy-start.19 = (bf16[2048,128]{1,0:T(8,128)(2,1)S(1)}, bf16[2048,128]{1,0:T(8,128)(2,1)}, u32[]{:S(2)}) copy-start(bf16[2048,128]{1,0:T(8,128)(2,1)} %copy-done.17) | copy-start | bytes 1572868
  448.4 24.0 %copy-start.37 = (bf16[4,512,512]{2,1,0:T(8,128)(2,1)S(1)}, bf16[4,512,512]{2,1,0:T(8,128)(2,1)}, u32[]{:S(2)}) copy-start(bf16[4,512,512]{2,1,0:T(8,128)(2,1)} %get-tuple-element.136) | copy-start | bytes 6291460
  448.4 24.0 %copy-start.2 = (bf16[2048,1024]{1,0:T(8,128)(2,1)S(1)}, bf16[2048,1024]{1,0:T(8,128)(2,1)}, u32[]{:S(2)}) copy-start(bf16[2048,1024]{1,0:T(8,128)(2,1)} %ffn_feed.1) | copy-start | bytes 12582916
  470.4 37.9 %copy-start.21 = (bf16[2048,128]{1,0:T(8,128)(2,1)}, bf16[2048,128]{1,0:T(8,128)(2,1)S(1)}, u32[]{:S(2)}) copy-start(bf16[2048,128]{1,0:T(8,128)(2,1)S(1)} %get-tuple-element.154.grad_query) | copy-start | bytes 1572868
  470.4 37.7 %collective-permute-start.7 = (bf16[2048,256]{1,0:T(8,128)(2,1)S(1)}, bf16[2048,256]{1,0:T(8,128)(2,1)S(1)}, u32[]{:S(2)}, u32[]{:S(2)}) collective-permute-start(bf16[2048,256]{1,0:T(8,128)(2,1)S(1)} %get-tuple-element.145), channel_id=1, source_target_pairs={{4,0},{8,4},{12,8},{5,1},{9,5},{13,9},{6,2},{10,6},{14,10},{7,3},{... | collective-permute-start | bytes 3145736 | tf_op jit(solution)/shard_map/ppermute | solution.py:1316
  472.3 66.7 %collective-permute-start.10 = (bf16[4,512,512]{2,1,0:T(8,128)(2,1)S(1)}, bf16[4,512,512]{2,1,0:T(8,128)(2,1)S(1)}, u32[]{:S(2)}, u32[]{:S(2)}) collective-permute-start(bf16[4,512,512]{2,1,0:T(8,128)(2,1)S(1)} %copy-done.37), channel_id=1, source_target_pairs={{0,16},{16,0},{1,17},{17,1},{2,18},{18,2},{3,19},{19,3},{4,20},{20... | collective-permute-start | bytes 6291464 | tf_op jit(solution)/shard_map/ppermute | solution.py:1153
  476.8 60.6 %copy-start.30 = (f32[2048,256]{1,0:T(8,128)S(1)}, f32[2048,256]{1,0:T(8,128)}, u32[]{:S(2)}) copy-start(f32[2048,256]{1,0:T(8,128)} %get-tuple-element.150) | copy-start | bytes 6291460
  508.4 29.1 %collective-permute-start.9 = (bf16[2048,256]{1,0:T(8,128)(2,1)S(1)}, bf16[2048,256]{1,0:T(8,128)(2,1)S(1)}, u32[]{:S(2)}, u32[]{:S(2)}) collective-permute-start(bf16[2048,256]{1,0:T(8,128)(2,1)S(1)} %add_convert_fusion.3), channel_id=1, source_target_pairs={{4,0},{8,4},{12,8},{5,1},{9,5},{13,9},{6,2},{10,6},{14,10},{7,3},{... | collective-permute-start | bytes 3145736 | tf_op jit(solution)/shard_map/ppermute | solution.py:1316
  541.8 24.6 %collective-permute-start.8 = (bf16[512,1024]{1,0:T(8,128)(2,1)S(1)}, bf16[512,1024]{1,0:T(8,128)(2,1)S(1)}, u32[]{:S(2)}, u32[]{:S(2)}) collective-permute-start(bf16[512,1024]{1,0:T(8,128)(2,1)S(1)} %bitcast.139), channel_id=1, source_target_pairs={{0,2},{1,3},{2,0},{3,1},{4,6},{5,7},{6,4},{7,5},{8,10},{9,11},{10,... | collective-permute-start | bytes 3145736 | tf_op jit(solution)/shard_map/ppermute | solution.py:287
  543.0 23.4 %copy-start.6 = (f32[512,1024]{1,0:T(8,128)S(1)}, f32[512,1024]{1,0:T(8,128)}, u32[]{:S(2)}) copy-start(f32[512,1024]{1,0:T(8,128)} %copy-done.5) | copy-start | bytes 6291460
  568.0 112.1 %all-to-all-start = ((bf16[4,128,1024]{2,1,0:T(8,128)(2,1)}), bf16[4,128,1024]{2,1,0:T(8,128)(2,1)S(1)}, u32[]{:S(2)}, u32[]{:S(2)}) async-start(bf16[4,128,1024]{2,1,0:T(8,128)(2,1)} %bitcast.47), calls=%async_computation | async-start | bytes 2097152 | tf_op jit(solution)/shard_map/all_to_all | solution.py:33
  (23 other events, 61.9 us)
Sparse Core Ops, SparseCore 0:
  153.3 64.3 all-gather.4
  219.3 76.0 all-gather.6
  433.6 55.1 reduce-scatter.2
  541.9 61.7 reduce-scatter.4

commit v10 on v9

--- a/solution.py
+++ b/solution.py
@@ -1305,7 +1305,7 @@
             pltpu.VMEM((128, width), jnp.float32),
         ],
         compiler_params=pltpu.CompilerParams(vmem_limit_bytes=56 * 2**20),
-        cost_estimate=cost(total * width * 512, 4e6),
+        cost_estimate=cost(1e3, 1e3),
         name="project_back",
     )(rows, grads, grad_query, out_logit, projected, sigs, masks, full, full, full, full, gain, bias)
 
@@ -1532,16 +1532,19 @@
     )
     came = shift(grad_window[0], "level", -1)
     fed, beyond = pair_scatter(feed, 6, True)
+    fed_far = to_far(beyond)
     for i in range(1, reach + 1):
         if i < reach:
             came, fed = lax.optimization_barrier((came, fed))
+        else:
+            layer_out = to_home(low(middle + fed + fed_far.astype(jnp.float32)))
+            came, layer_out = lax.optimization_barrier((came, layer_out))
         grad_both = grad_window[i].astype(jnp.float32) + came.astype(jnp.float32)
         if i < reach:
             grad_keys_sent = low(grad_both)
             came = shift(grad_keys_sent, "level", -1)
     grad_both, out_came = lax.optimization_barrier((grad_both, out_came))
     ffn_out_grad = over_levels(sum_of(grad_out, out_came))
-    fed_far = to_far(beyond)
     grad_inputs, late = project_back(
         worker_in,
         grad_both,
@@ -1555,8 +1558,6 @@
         bias_row,
     )
 
-    fed_far, grad_inputs = lax.optimization_barrier((fed_far, grad_inputs))
-    layer_out = to_home(low(middle + fed + fed_far.astype(jnp.float32)))
 
     values = VEXP * DH
     layout = (

time: 702 us -> 716 us (1.020)
  waiting for transfers between devices: 103 us -> 111 us
    pallas_call x1, Pallas kernels: 102 us -> 82.2 us  [finish(): pl.pallas_call(functools.partial(finish_kernel, layout), out_shape=[jax.S...]
    pallas_call x1, Pallas kernels: 22 us -> 31.6 us  [attend_back(): pl.pallas_call(functools.partial(attend_back_kernel, parts), grid_spec=gr...]
    pallas_call x1, Pallas kernels: 16.2 us -> 23.8 us  [attend(): pl.pallas_call(functools.partial(attend_kernel, parts), grid_spec=grid_sp...]
    unnamed x86 -> x80, local copies, waits for them, and re-layouts: 21.4 us -> 22.6 us
  transfers between devices with their start and end apart: 16 -> 16, of which waited for: 5 -> 6; matrix products, arithmetic and copies ran while one was open for 7% -> 8% of each run, Pallas kernels for 60% -> 59%
where the time goes in v10:
time: 716 us; the launch traced here: 707 us
  Pallas kernels  473 us (66%)
  waiting for transfers between devices  111 us (16%)
  local copies, waits for them, and re-layouts  43.5 us (6%)
  other arithmetic  34.2 us (5%)
  starting transfers between devices  24.7 us (3%)
  between operations  14.5 us (2%)
    ppermute x4, waiting for transfers between devices, shift(): return lax.ppermute(value, axis, pairs)  101 us
    pallas_call x1, Pallas kernels, start(): pl.pallas_call(start_kernel, out_shape=shapes, in_specs=[pl.BlockSpec(mem...  89.7 us
    pallas_call x1, Pallas kernels, finish(): pl.pallas_call(functools.partial(finish_kernel, layout), out_shape=[jax.S...  82.2 us
    pallas_call x2, Pallas kernels, level_gather(): pl.pallas_call(functools.partial(gather_kernel, by_source), out_shape=jax...  59.5 us
    pallas_call x1, Pallas kernels, ffn_front(): pl.pallas_call(functools.partial(front_kernel, groups, local), grid_spec=...  36.9 us
    pallas_call x1, Pallas kernels, attend_back(): pl.pallas_call(functools.partial(attend_back_kernel, parts), grid_spec=gr...  31.6 us
    pallas_call x2, Pallas kernels, ffn_rear(): pl.pallas_call(functools.partial(rear_kernel, groups), grid_spec=pltpu.Pr...  28.2 us
    pallas_call x1, Pallas kernels, level_scatter(): pl.pallas_call(functools.partial(scatter_kernel, by_source), out_shape=ja...  27.3 us
  transfers between devices with their start and end apart: 16, of which 6 were waited for; matrix products, arithmetic and copies ran while one was open for 8% of the time, Pallas kernels for 59%

profile of v10, /device:TPU:8, one launch (start us, length us, event | category | flops | bytes accessed | tf_op | source)
XLA Modules:
  0.0 707.3 jit_solution(13600145336511024534)
XLA Ops:
  17.0 89.7 %start.1 = (bf16[4,4,4,32,1024]{4,3,2,1,0:T(8,128)(2,1)}, bf16[4,4,32,1024]{3,2,1,0:T(8,128)(2,1)}, bf16[2,4,4,32,1664]{4,3,2,1,0:T(8,128)(2,1)}, s32[4,4,512]{2...) custom-call(bf16[4,4,32,1024]{3,2,1,0:T(8,128)(2,1)} %bitcast.170, bf16[4,4,32,1024]{3,2,1,0:T(8,128)(2,1)} %bitcast.171, ...), custom_call_target="tpu_custom_call" | custom-call | bytes 200000000 | tf_op jit(solution)/shard_map/start/pallas_call | solution.py:459
  111.3 14.3 %project.1 = (bf16[2048,128]{1,0:T(8,128)(2,1)S(1)}, bf16[2048,256]{1,0:T(8,128)(2,1)S(1)}, f32[2048,640]{1,0:T(8,128)}, f32[2048,128]{1,0:T(8,128)S(1)}, f32[2048,16]{1,0:T(8,128)S(1)}) custom-call(bf16[2048,1024]{1,0:T(8,128)(2,1)} %bitcast.152, bf16[1024,1664]{1,0:T(8,128)(2,1)} %bitcast.141, bf16[1024,1664]{1,0:T(8,128)(2,1)} %bitcast.142, ...), custom_call_target="tpu_custom_call" | custom-call | flops 4294967296 | bytes 20000000 | tf_op jit(solution)/shard_map/project/pallas_call | solution.py:1211
  131.0 22.2 %collective-permute-done.1.refs_1_.refs_4_ = bf16[2048,256]{1,0:T(8,128)(2,1)} collective-permute-done((bf16[2048,256]{1,0:T(8,128)(2,1)S(1)}, bf16[2048,256]{1,0:T(8,128)(2,1)}, u32[]{:S(2)}, u32[]{:S(2)}) %collective-permute-start.1) | collective-permute-done | bytes 1048608 | tf_op jit(solution)/shard_map/ppermute | solution.py:1316
  157.6 5.6 collective-permute-start.2
  163.4 2.4 constant_dynamic-slice_fusion
  170.4 28.4 %level_gather.2 = bf16[4,4,128,1024]{3,2,1,0:T(8,128)(2,1)} custom-call(bf16[4,128,1024]{2,1,0:T(8,128)(2,1)} %bitcast.120), custom_call_target="tpu_custom_call" | custom-call | bytes 90000000 | tf_op jit(solution)/shard_map/level_gather/pallas_call | solution.py:105
  198.9 16.5 %collective-permute-done.2.refs_0_.refs_3_ = bf16[2048,256]{1,0:T(8,128)(2,1)} collective-permute-done((bf16[2048,256]{1,0:T(8,128)(2,1)}, bf16[2048,256]{1,0:T(8,128)(2,1)}, u32[]{:S(2)}, u32[]{:S(2)}) %collective-permute-start.2) | collective-permute-done | bytes 1048608 | tf_op jit(solution)/shard_map/ppermute | solution.py:1316
  217.6 23.8 %attend.1 = (f32[2048,128]{1,0:T(8,128)S(1)}, f32[4,1,512]{2,1,0:T(1,128)S(1)}) custom-call(s32[4]{0:T(128)S(1)} %subtract_maximum_fusion.first, bf16[2048,128]{1,0:T(8,128)(2,1)S(1)} %copy-done.18, bf16[2048,256]{1,0:T(8,128)(2,1)} %collective-permute-done.2.refs_0_.refs_3_, bf16[2048,256]{1,0:T(8,128)(2,1)} %collective-permute-done.1.refs_1_.refs_4_, ...), custom_call_target="tpu_custom_call" | custom-call | flops 20000000000 | bytes 10000000 | tf_op jit(solution)/shard_map/attend/pallas_call | solution.py:719
  249.3 5.1 convolution_convert_fusion
  254.4 27.3 %level_scatter.1 = f32[4,128,1024]{2,1,0:T(8,128)S(1)} custom-call(bf16[4,4,128,1024]{3,2,1,0:T(8,128)(2,1)S(1)} %bitcast.119), custom_call_target="tpu_custom_call" | custom-call | bytes 80000000 | tf_op jit(solution)/shard_map/level_scatter/pallas_call | solution.py:167
  286.6 31.1 %level_gather.3 = bf16[4,4,128,1152]{3,2,1,0:T(8,128)(2,1)} custom-call(bf16[4,128,1152]{2,1,0:T(8,128)(2,1)} %bitcast.126), custom_call_target="tpu_custom_call" | custom-call | bytes 90000000 | tf_op jit(solution)/shard_map/level_gather/pallas_call | solution.py:105
  320.0 36.9 %ffn_front.1 = (bf16[2048,2048]{1,0:T(8,128)(2,1)}, bf16[2048,2048]{1,0:T(8,128)(2,1)}, bf16[2048,1152]{1,0:T(8,128)(2,1)}) custom-call(s32[2]{0:T(128)} %pad_add_fusion.1.place, bf16[2048,1152]{1,0:T(8,128)(2,1)} %bitcast.155, bf16[2048,1024]{1,0:T(8,128)(2,1)} %bitcast.157, bf16[4,2,512,512]{3,2,1,0:T(8,128)(2,1)} %bitcast.187, ...), custom_call_target="tpu_custom_call" | custom-call | flops 25769803776 | bytes 30000000 | tf_op jit(solution)/shard_map/ffn_front/pallas_call | solution.py:893
  359.2 5.8 pair_scatter.2
  367.3 14.0 %ffn_rear.2 = (bf16[4,512,512]{2,1,0:T(8,128)(2,1)}, bf16[4,512,512]{2,1,0:T(8,128)(2,1)}) custom-call(s32[2]{0:T(128)} %pad_add_fusion.1.place, bf16[2048,1152]{1,0:T(8,128)(2,1)} %bitcast.156, bf16[2048,2048]{1,0:T(8,128)(2,1)} %get-tuple-element.131.hidden_units), custom_call_target="tpu_custom_call" | custom-call | flops 1000 | bytes 1000 | tf_op jit(solution)/shard_map/ffn_rear/pallas_call | solution.py:967
  382.1 14.2 %ffn_rear.3 = (bf16[4,512,512]{2,1,0:T(8,128)(2,1)}, bf16[4,512,512]{2,1,0:T(8,128)(2,1)}) custom-call(s32[2]{0:T(128)} %pad_add_fusion.1.place, bf16[2048,1024]{1,0:T(8,128)(2,1)} %bitcast.158, bf16[2048,2048]{1,0:T(8,128)(2,1)} %get-tuple-element.134.hidden_units.active), custom_call_target="tpu_custom_call" | custom-call | flops 1000 | bytes 1000 | tf_op jit(solution)/shard_map/ffn_rear/pallas_call | solution.py:967
  397.2 7.3 %leave_ffn.1 = (f32[512,1024]{1,0:T(8,128)}, bf16[512,1024]{1,0:T(8,128)(2,1)}, bf16[1024,128]{1,0:T(8,128)(2,1)S(1)}) custom-call(f32[512,1024]{1,0:T(8,128)} %copy-done.5, f32[512,1152]{1,0:T(8,128)} %bitcast.122, bf16[512,1152]{1,0:T(8,128)(2,1)S(1)} %collective-permute-done.4.came, bf16[512,1024]{1,0:T(8,128)(2,1)S(1)} %bitcast.121, ...), custom_call_target="tpu_custom_call" | custom-call | flops 1000000000 | bytes 10000000 | tf_op jit(solution)/shard_map/leave_ffn/pallas_call | solution.py:1063
  406.7 18.2 %ffn_feed.1 = bf16[2048,1024]{1,0:T(8,128)(2,1)} custom-call(s32[2]{0:T(128)} %pad_add_fusion.1.place, bf16[2048,2048]{1,0:T(8,128)(2,1)} %get-tuple-element.134.hidden_units.active, bf16[4,512,512]{2,1,0:T(8,128)(2,1)} %bitcast.166, bf16[4,512,512]{2,1,0:T(8,128)(2,1)} %collective-permute-done.3.refs_2_.refs_1_), custom_call_target="tpu_custom_call" | custom-call | flops 1000 | bytes 1000 | tf_op jit(solution)/shard_map/ffn_feed/pallas_call | solution.py:946
  424.9 5.5 collective-permute-done.5
  430.4 6.1 pair_gather.1
  436.5 4.2 add_convert_fusion.1
  440.7 12.5 %branch_back.1 = (bf16[2048,128]{1,0:T(8,128)(2,1)S(1)}, f32[4,1,512]{2,1,0:T(1,128)S(1)}, bf16[2048,128]{1,0:T(8,128)(2,1)S(1)}, bf16[1024,640]{1,0:T(8,128)(2,1)S(1)}) custom-call(bf16[2048,1024]{1,0:T(8,128)(2,1)} %bitcast.159, bf16[1024,1664]{1,0:T(8,128)(2,1)} %bitcast.147, f32[2048,128]{1,0:T(8,128)S(1)} %get-tuple-element.115.attended, ...), custom_call_target="tpu_custom_call" | custom-call | flops 100000000 | bytes 1000000 | tf_op jit(solution)/shard_map/branch_back/pallas_call | solution.py:1122
  455.1 31.6 %attend_back.1 = (bf16[2048,128]{1,0:T(8,128)(2,1)S(1)}, bf16[2048,256]{1,0:T(8,128)(2,1)S(1)}, bf16[2048,256]{1,0:T(8,128)(2,1)S(1)}, f32[2048,256]{1,0:T(8,128)}) custom-call(s32[4]{0:T(128)S(1)} %subtract_maximum_fusion.first, bf16[2048,128]{1,0:T(8,128)(2,1)S(1)} %copy-done.19, bf16[2048,256]{1,0:T(8,128)(2,1)} %collective-permute-done.2.refs_0_.refs_3_, ...), custom_call_target="tpu_custom_call" | custom-call | flops 2000000000 | bytes 1000000 | tf_op jit(solution)/shard_map/attend_back/pallas_call | solution.py:803
  488.9 4.4 pair_scatter.3
  495.8 18.2 %collective-permute-done.7 = bf16[2048,256]{1,0:T(8,128)(2,1)S(1)} collective-permute-done((bf16[2048,256]{1,0:T(8,128)(2,1)S(1)}, bf16[2048,256]{1,0:T(8,128)(2,1)S(1)}, u32[]{:S(2)}, u32[]{:S(2)}) %collective-permute-start.7) | collective-permute-done | bytes 1048608 | tf_op jit(solution)/shard_map/ppermute | solution.py:1316
  514.0 4.5 collective-permute-done.9
  520.3 4.7 all-to-all-start
  527.2 44.1 %collective-permute-done.8 = bf16[2048,256]{1,0:T(8,128)(2,1)S(1)} collective-permute-done((bf16[2048,256]{1,0:T(8,128)(2,1)S(1)}, bf16[2048,256]{1,0:T(8,128)(2,1)S(1)}, u32[]{:S(2)}, u32[]{:S(2)}) %collective-permute-start.8) | collective-permute-done | bytes 1048608 | tf_op jit(solution)/shard_map/ppermute | solution.py:1316
  571.2 3.3 convert_add_fusion.grads
  574.5 3.6 add_convert_fusion
  578.1 23.3 %project_back.1 = (bf16[2048,1024]{1,0:T(8,128)(2,1)}, bf16[1024,1024]{1,0:T(8,128)(2,1)}) custom-call(bf16[2048,1024]{1,0:T(8,128)(2,1)} %bitcast.153, f32[2048,256]{1,0:T(8,128)} %convert_add_fusion.grads, bf16[2048,128]{1,0:T(8,128)(2,1)} %copy-done.21, bf16[2048,128]{1,0:T(8,128)(2,1)} %copy-done.20, f32[2048,640]{1,0:T(8,128)} %get-tuple-element.158.projected, ...), custom_call_target="tpu_custom_call" | custom-call | flops 1000 | bytes 1000 | tf_op jit(solution)/shard_map/project_back/pallas_call | solution.py:1291
  601.4 82.2 %finish.1 = (f32[4,4,32,1024]{3,2,1,0:T(8,128)}, f32[32,2560]{1,0:T(8,128)}, f32[32,512]{1,0:T(8,128)}, f32[32,512]{1,0:T(8,128)}, f32[4,32,128]{2,1,0:T(8,128)}...) custom-call(bf16[4,4,128,1024]{3,2,1,0:T(8,128)(2,1)} %bitcast.160, f32[4,128,1024]{2,1,0:T(8,128)} %bitcast.167, ...), custom_call_target="tpu_custom_call" | custom-call | bytes 200000000 | tf_op jit(solution)/shard_map/finish/pallas_call | solution.py:626
  694.6 3.2 copy.160
  (171 shorter events, 78.8 us)
Async XLA Ops:
  7.2 9.2 %copy-start = (s32[512,16]{0,1:T(8,128)S(1)}, s32[512,16]{0,1:T(8,128)}, u32[]{:S(2)}) copy-start(s32[512,16]{0,1:T(8,128)} %param.26) | copy-start | bytes 98308
  7.2 234.2 %all-gather.5.cloned.1.call-start = ((), (), s32[]{:S(2)}) async-start(), calls=%async_computation.5 | async-start | bytes 2621440 | tf_op jit(solution)/shard_map/all_gather | solution.py:1460
  7.2 101.0 %collective-permute-start = (bf16[512,512]{1,0:T(8,128)(2,1)}, bf16[512,512]{1,0:T(8,128)(2,1)S(1)}, u32[]{:S(2)}, u32[]{:S(2)}) collective-permute-start(bf16[512,512]{1,0:T(8,128)(2,1)} %param.38), channel_id=1, source_target_pairs={{0,16},{16,0},{1,17},{17,1},{2,18},{18,2},{3,19},{19,3},{4,20},{20... | collective-permute-start | bytes 1572872 | tf_op jit(solution)/shard_map/ppermute | solution.py:1153
  110.5 15.1 %copy-start.25 = (f32[1024]{0:T(1024)}, f32[1024]{0:T(1024)S(1)}, u32[]{:S(2)}) copy-start(f32[1024]{0:T(1024)S(1)} %get-tuple-element.252) | copy-start | bytes 12292
  110.5 15.1 %copy-start.26 = (f32[1024]{0:T(1024)}, f32[1024]{0:T(1024)S(1)}, u32[]{:S(2)}) copy-start(f32[1024]{0:T(1024)S(1)} %get-tuple-element.253) | copy-start | bytes 12292
  111.3 19.2 %copy-start.35 = (s32[1,3]{1,0:T(1,128)S(1)}, s32[1,3]{1,0:T(1,128)}, u32[]{:S(2)}) copy-start(s32[1,3]{1,0:T(1,128)} %param.23) | copy-start | bytes 40
  126.4 39.3 %copy-start.9 = (bf16[2048,256]{1,0:T(8,128)(2,1)}, bf16[2048,256]{1,0:T(8,128)(2,1)S(1)}, u32[]{:S(2)}) copy-start(bf16[2048,256]{1,0:T(8,128)(2,1)S(1)} %get-tuple-element.101.refs_2_.refs_5_) | copy-start | bytes 3145732
  126.4 314.2 %copy-start.3 = (f32[2048,128]{1,0:T(8,128)}, f32[2048,128]{1,0:T(8,128)S(1)}, u32[]{:S(2)}) copy-start(f32[2048,128]{1,0:T(8,128)S(1)} %get-tuple-element.109.sigs) | copy-start | bytes 3145732
  126.5 314.2 %copy-start.4 = (f32[2048,16]{1,0:T(8,128)}, f32[2048,16]{1,0:T(8,128)S(1)}, u32[]{:S(2)}) copy-start(f32[2048,16]{1,0:T(8,128)S(1)} %get-tuple-element.110.masks) | copy-start | bytes 393220
  126.5 29.3 %copy-start.34 = (s32[4,16,128]{2,1,0:T(8,128)S(1)}, s32[4,16,128]{2,1,0:T(8,128)}, u32[]{:S(2)}) copy-start(s32[4,16,128]{2,1,0:T(8,128)} %get-tuple-element.106) | copy-start | bytes 98308
  126.5 26.7 %collective-permute-start.1 = (bf16[2048,256]{1,0:T(8,128)(2,1)S(1)}, bf16[2048,256]{1,0:T(8,128)(2,1)}, u32[]{:S(2)}, u32[]{:S(2)}) collective-permute-start(bf16[2048,256]{1,0:T(8,128)(2,1)S(1)} %get-tuple-element.101.refs_2_.refs_5_), channel_id=1, source_target_pairs={{0,4},{4,8},{8,12},{1,5},{5,9},{9,13},{2,6},{6,10},{10,14},{3,7},{... | collective-permute-start | bytes 3145736 | tf_op jit(solution)/shard_map/ppermute | solution.py:1316
  153.2 166.7 %all-gather.7.cloned.1.call-start = ((), (), s32[]{:S(2)}) async-start(), calls=%async_computation.6 | async-start | bytes 5242880 | tf_op jit(solution)/shard_map/all_gather | solution.py:1461
  155.6 533.8 %reduce-scatter.3.cloned.1.call-start = ((), (), s32[]{:S(2)}) async-start(), calls=%async_computation.3 | async-start | bytes 2621440 | tf_op jit(solution)/shard_map/reduce_scatter | solution.py:1515
  157.6 57.8 %collective-permute-start.2 = (bf16[2048,256]{1,0:T(8,128)(2,1)}, bf16[2048,256]{1,0:T(8,128)(2,1)}, u32[]{:S(2)}, u32[]{:S(2)}) collective-permute-start(bf16[2048,256]{1,0:T(8,128)(2,1)} %collective-permute-done.1.refs_1_.refs_4_), channel_id=1, source_target_pairs={{0,4},{4,8},{8,12},{1,5},{5,9},{9,13},{2,6},{6,10},{10,14},{3,7},{... | collective-permute-start | bytes 3145736 | tf_op jit(solution)/shard_map/ppermute | solution.py:1316
  241.4 78.5 %collective-permute-start.3 = (bf16[4,512,512]{2,1,0:T(8,128)(2,1)}, bf16[4,512,512]{2,1,0:T(8,128)(2,1)}, u32[]{:S(2)}, u32[]{:S(2)}) collective-permute-start(bf16[4,512,512]{2,1,0:T(8,128)(2,1)} %bitcast.164), channel_id=1, source_target_pairs={{0,16},{16,0},{1,17},{17,1},{2,18},{18,2},{3,19},{19,3},{4,20},{20... | collective-permute-start | bytes 6291464 | tf_op jit(solution)/shard_map/ppermute | solution.py:1153
  254.4 27.3 %copy-start.14 = (bf16[4,1,4,32,1024]{4,3,2,1,0:T(8,128)(2,1)S(1)}, bf16[4,1,4,32,1024]{4,3,2,1,0:T(8,128)(2,1)}, u32[]{:S(2)}) copy-start(bf16[4,1,4,32,1024]{4,3,2,1,0:T(8,128)(2,1)} %constant_dynamic-slice_fusion) | copy-start | bytes 3145732
  254.4 27.3 %copy-start.15 = (s32[512,16]{1,0:T(8,128)S(1)}, s32[512,16]{1,0:T(8,128)}, u32[]{:S(2)}) copy-start(s32[512,16]{1,0:T(8,128)} %fusion.4.routes) | copy-start | bytes 98308
  366.4 29.8 %collective-permute-start.4 = (bf16[512,1152]{1,0:T(8,128)(2,1)}, bf16[512,1152]{1,0:T(8,128)(2,1)S(1)}, u32[]{:S(2)}, u32[]{:S(2)}) collective-permute-start(bf16[512,1152]{1,0:T(8,128)(2,1)} %bitcast.38), channel_id=1, source_target_pairs={{0,2},{1,3},{2,0},{3,1},{4,6},{5,7},{6,4},{7,5},{8,10},{9,11},{10,... | collective-permute-start | bytes 3538952 | tf_op jit(solution)/shard_map/ppermute | solution.py:287
  381.3 55.2 %collective-permute-start.6 = (bf16[4,512,512]{2,1,0:T(8,128)(2,1)}, bf16[4,512,512]{2,1,0:T(8,128)(2,1)}, u32[]{:S(2)}, u32[]{:S(2)}) collective-permute-start(bf16[4,512,512]{2,1,0:T(8,128)(2,1)} %get-tuple-element.133), channel_id=1, source_target_pairs={{0,16},{16,0},{1,17},{17,1},{2,18},{18,2},{3,19},{19,3},{4,20},{20... | collective-permute-start | bytes 6291464 | tf_op jit(solution)/shard_map/ppermute | solution.py:1153
  382.1 14.2 %copy-start.8 = (bf16[4,4,32,1024]{3,2,1,0:T(8,128)(2,1)S(1)}, bf16[4,4,32,1024]{3,2,1,0:T(8,128)(2,1)}, u32[]{:S(2)}) copy-start(bf16[4,4,32,1024]{3,2,1,0:T(8,128)(2,1)} %get-tuple-element.102) | copy-start | bytes 3145732
  382.1 14.2 %copy-start.16 = (s32[512,16]{1,0:T(8,128)S(1)}, s32[512,16]{1,0:T(8,128)}, u32[]{:S(2)}) copy-start(s32[512,16]{1,0:T(8,128)} %fusion.4.routes) | copy-start | bytes 98308
  405.2 25.2 %collective-permute-start.5 = (bf16[512,1024]{1,0:T(8,128)(2,1)}, bf16[512,1024]{1,0:T(8,128)(2,1)}, u32[]{:S(2)}, u32[]{:S(2)}) collective-permute-start(bf16[512,1024]{1,0:T(8,128)(2,1)} %get-tuple-element.139), channel_id=1, source_target_pairs={{0,2},{1,3},{2,0},{3,1},{4,6},{5,7},{6,4},{7,5},{8,10},{9,11},{10,... | collective-permute-start | bytes 3145736 | tf_op jit(solution)/shard_map/ppermute | solution.py:287
  440.7 14.4 %copy-start.19 = (bf16[2048,128]{1,0:T(8,128)(2,1)S(1)}, bf16[2048,128]{1,0:T(8,128)(2,1)}, u32[]{:S(2)}) copy-start(bf16[2048,128]{1,0:T(8,128)(2,1)} %copy-done.17) | copy-start | bytes 1572868
  455.1 33.8 %copy-start.2 = (bf16[2048,1024]{1,0:T(8,128)(2,1)S(1)}, bf16[2048,1024]{1,0:T(8,128)(2,1)}, u32[]{:S(2)}) copy-start(bf16[2048,1024]{1,0:T(8,128)(2,1)} %ffn_feed.1) | copy-start | bytes 12582916
  486.7 32.5 %copy-start.21 = (bf16[2048,128]{1,0:T(8,128)(2,1)}, bf16[2048,128]{1,0:T(8,128)(2,1)S(1)}, u32[]{:S(2)}) copy-start(bf16[2048,128]{1,0:T(8,128)(2,1)S(1)} %get-tuple-element.156.grad_query) | copy-start | bytes 1572868
  486.7 31.9 %copy-start.6 = (f32[512,1024]{1,0:T(8,128)S(1)}, f32[512,1024]{1,0:T(8,128)}, u32[]{:S(2)}) copy-start(f32[512,1024]{1,0:T(8,128)} %copy-done.5) | copy-start | bytes 6291460
  486.7 27.3 %collective-permute-start.7 = (bf16[2048,256]{1,0:T(8,128)(2,1)S(1)}, bf16[2048,256]{1,0:T(8,128)(2,1)S(1)}, u32[]{:S(2)}, u32[]{:S(2)}) collective-permute-start(bf16[2048,256]{1,0:T(8,128)(2,1)S(1)} %get-tuple-element.146), channel_id=1, source_target_pairs={{4,0},{8,4},{12,8},{5,1},{9,5},{13,9},{6,2},{10,6},{14,10},{7,3},{... | collective-permute-start | bytes 3145736 | tf_op jit(solution)/shard_map/ppermute | solution.py:1316
  493.3 25.3 %collective-permute-start.9 = (bf16[512,1024]{1,0:T(8,128)(2,1)S(1)}, bf16[512,1024]{1,0:T(8,128)(2,1)S(1)}, u32[]{:S(2)}, u32[]{:S(2)}) collective-permute-start(bf16[512,1024]{1,0:T(8,128)(2,1)S(1)} %bitcast.139), channel_id=1, source_target_pairs={{0,2},{1,3},{2,0},{3,1},{4,6},{5,7},{6,4},{7,5},{8,10},{9,11},{10,... | collective-permute-start | bytes 3145736 | tf_op jit(solution)/shard_map/ppermute | solution.py:287
  494.8 79.7 %collective-permute-start.10 = (bf16[4,512,512]{2,1,0:T(8,128)(2,1)}, bf16[4,512,512]{2,1,0:T(8,128)(2,1)}, u32[]{:S(2)}, u32[]{:S(2)}) collective-permute-start(bf16[4,512,512]{2,1,0:T(8,128)(2,1)} %get-tuple-element.136), channel_id=1, source_target_pairs={{0,16},{16,0},{1,17},{17,1},{2,18},{18,2},{3,19},{19,3},{4,20},{20... | collective-permute-start | bytes 6291464 | tf_op jit(solution)/shard_map/ppermute | solution.py:1153
  520.3 51.0 %all-to-all-start = ((bf16[4,128,1024]{2,1,0:T(8,128)(2,1)}), bf16[4,128,1024]{2,1,0:T(8,128)(2,1)S(1)}, u32[]{:S(2)}, u32[]{:S(2)}) async-start(bf16[4,128,1024]{2,1,0:T(8,128)(2,1)} %bitcast.47), calls=%async_computation | async-start | bytes 2097152 | tf_op jit(solution)/shard_map/all_to_all | solution.py:33
  525.0 166.5 %reduce-scatter.5.cloned.1.call-start = ((), (), s32[]{:S(2)}) async-start(), calls=%async_computation.4 | async-start | bytes 2621440 | tf_op jit(solution)/shard_map/reduce_scatter | solution.py:1515
  525.2 46.0 %collective-permute-start.8 = (bf16[2048,256]{1,0:T(8,128)(2,1)S(1)}, bf16[2048,256]{1,0:T(8,128)(2,1)S(1)}, u32[]{:S(2)}, u32[]{:S(2)}) collective-permute-start(bf16[2048,256]{1,0:T(8,128)(2,1)S(1)} %add_convert_fusion.3), channel_id=1, source_target_pairs={{4,0},{8,4},{12,8},{5,1},{9,5},{13,9},{6,2},{10,6},{14,10},{7,3},{... | collective-permute-start | bytes 3145736 | tf_op jit(solution)/shard_map/ppermute | solution.py:1316
  (20 other events, 43.5 us)
Sparse Core Ops, SparseCore 0:
  153.3 64.3 all-gather.4
  219.3 76.0 all-gather.6
  440.8 39.8 reduce-scatter.2
  578.2 44.0 reduce-scatter.4

commit v11 on v9

--- a/solution.py
+++ b/solution.py
@@ -662,7 +662,19 @@
     )
 
 
-def attend_kernel(parts, first, q, *refs):
+def run_blocks(step, part, parts, blocks, at, first, clear):
+    def local(block):
+        return jnp.clip(block - part * blocks, 0, blocks)
+
+    own = (parts - 1) * blocks + at
+    begin, middle, end = local(first), local(jnp.clip(clear, first, own)), local(own)
+    lax.fori_loop(begin, middle, functools.partial(step, True), 0)
+    lax.fori_loop(middle, end, functools.partial(step, False), 0)
+    if part == parts - 1:
+        step(True, at, 0)
+
+
+def attend_kernel(parts, first, clear, q, *refs):
     keys, values = refs[:parts], refs[parts : 2 * parts]
     pos_q, start_q, pos_k, out, lse, top, total, acc = refs[2 * parts :]
     at = pl.program_id(0)
@@ -676,12 +688,13 @@
 
     for part in range(parts):
 
-        def step(block, carry, k=keys[part], v=values[part], part=part):
+        def step(masked, block, carry, k=keys[part], v=values[part], part=part):
             rows = pl.ds(pl.multiple_of(block * BLOCK, BLOCK), BLOCK)
             spot = pl.ds(pl.multiple_of((part * blocks + block) * BLOCK, BLOCK), BLOCK)
             scores = dot(k[rows, :], query, 1, 1)
-            key_at = pos_k[spot, :]
-            scores = jnp.where((key_at >= row_from) & (key_at <= row_at), scores, -1e30)
+            if masked:
+                key_at = pos_k[spot, :]
+                scores = jnp.where((key_at >= row_from) & (key_at <= row_at), scores, -1e30)
             old = top[...]
             new = jnp.maximum(old, jnp.max(scores, axis=0, keepdims=True))
             shrink = jnp.exp2((old - new) * rate)
@@ -691,19 +704,17 @@
             top[...] = new
             return carry
 
-        begin = jnp.maximum(first[at] - part * blocks, 0)
-        end = at + 1 if part == parts - 1 else blocks
-        lax.fori_loop(begin, end, step, 0)
+        run_blocks(step, part, parts, blocks, at, first[at], clear[at])
     out[...] = (acc[...] / total[...]).T
     lse[0] = top[...] * rate + jnp.log2(total[...])
 
 
-def attend(first, queries, window, pos_q, start_q, pos_k):
+def attend(first, clear, queries, window, pos_q, start_q, pos_k):
     rows = queries.shape[0]
     parts = len(window)
     line = pl.BlockSpec((1, 1, BLOCK), lambda i, *_: (i, 0, 0))
     grid_spec = pltpu.PrefetchScalarGridSpec(
-        num_scalar_prefetch=1,
+        num_scalar_prefetch=2,
         grid=(rows // BLOCK,),
         in_specs=[pl.BlockSpec((BLOCK, DH), lambda i, *_: (i, 0))]
         + [pl.BlockSpec((rows, DH), lambda i, *_: (0, 0))] * parts
@@ -726,10 +737,10 @@
         compiler_params=pltpu.CompilerParams(vmem_limit_bytes=48 * 2**20),
         cost_estimate=cost(2e10, 1e7),
         name="attend",
-    )(first, queries, *window, *window, pos_q, start_q, pos_k)
-
-
-def attend_back_kernel(parts, first, q, *refs):
+    )(first, clear, queries, *window, *window, pos_q, start_q, pos_k)
+
+
+def attend_back_kernel(parts, first, clear, q, *refs):
     keys, values = refs[:parts], refs[parts : 2 * parts]
     grad, pos_q, start_q, lse, inner, pos_k, grad_q = refs[2 * parts : 2 * parts + 7]
     grads = refs[2 * parts + 7 : 3 * parts + 7]
@@ -750,14 +761,15 @@
 
     for part in range(parts):
 
-        def step(block, carry, k=keys[part], v=values[part], part=part):
+        def step(masked, block, carry, k=keys[part], v=values[part], part=part):
             rows = pl.ds(pl.multiple_of(block * BLOCK, BLOCK), BLOCK)
             spot = pl.ds(pl.multiple_of((part * blocks + block) * BLOCK, BLOCK), BLOCK)
             key, value = k[rows, :], v[rows, :]
             scores = dot(key, query, 1, 1)
-            key_at = pos_k[spot, :]
-            seen = (key_at >= row_from) & (key_at <= row_at)
-            soft = jnp.where(seen, jnp.exp2(scores * rate - row_lse), 0.0)
+            soft = jnp.exp2(scores * rate - row_lse)
+            if masked:
+                key_at = pos_k[spot, :]
+                soft = jnp.where((key_at >= row_from) & (key_at <= row_at), soft, 0.0)
             grad_soft = dot(value, grad_out, 1, 1)
             grad_scores = (soft * (grad_soft - row_inner)).astype(jnp.bfloat16)
             sum_v[spot, :] += dot(soft.astype(jnp.bfloat16), grad_out, 1, 0)
@@ -765,9 +777,7 @@
             acc[...] += dot(grad_scores, key, 0, 0)
             return carry
 
-        begin = jnp.maximum(first[at] - part * blocks, 0)
-        end = at + 1 if part == parts - 1 else blocks
-        lax.fori_loop(begin, end, step, 0)
+        run_blocks(step, part, parts, blocks, at, first[at], clear[at])
     grad_q[...] = (acc[...] * scale).astype(jnp.bfloat16)
 
     @pl.when(at == blocks - 1)
@@ -779,13 +789,13 @@
             grads[part][:, DH:] = sum_v[spot, :].astype(grads[part].dtype)
 
 
-def attend_back(first, queries, window, grads, pos_q, start_q, lse, inner, pos_k):
+def attend_back(first, clear, queries, window, grads, pos_q, start_q, lse, inner, pos_k):
     rows = queries.shape[0]
     parts = len(window)
     block = pl.BlockSpec((BLOCK, DH), lambda i, *_: (i, 0))
     line = pl.BlockSpec((1, 1, BLOCK), lambda i, *_: (i, 0, 0))
     grid_spec = pltpu.PrefetchScalarGridSpec(
-        num_scalar_prefetch=1,
+        num_scalar_prefetch=2,
         grid=(rows // BLOCK,),
         in_specs=[block]
         + [pl.BlockSpec((rows, DH), lambda i, *_: (0, 0))] * parts
@@ -808,7 +818,7 @@
         compiler_params=pltpu.CompilerParams(vmem_limit_bytes=48 * 2**20),
         cost_estimate=cost(2e9, 1e6),
         name="attend_back",
-    )(first, queries, *window, *window, grads, pos_q, start_q, lse, inner, pos_k)
+    )(first, clear, queries, *window, *window, grads, pos_q, start_q, lse, inner, pos_k)
 
 
 def columns_of(ref, group, groups, step, depth):
@@ -1439,6 +1449,8 @@
     base_block = (level - reach) * blocks
     first_block = starts_of(level * rows + jnp.arange(blocks, dtype=jnp.int32) * BLOCK) // BLOCK
     first_block = jnp.maximum(first_block - base_block, 0)
+    ends = level * rows + jnp.arange(1, blocks + 1, dtype=jnp.int32) * BLOCK - 1
+    clear_block = (starts_of(ends) + BLOCK - 1) // BLOCK - base_block
 
     own_routes = picks.reshape(levels, -1, HEADS, piece).transpose(2, 0, 3, 1).reshape(count, -1)
     own_routes = relabelled(own_routes)
@@ -1466,6 +1478,7 @@
 
     attended, log_total = attend(
         first_block,
+        clear_block,
         queries,
         window,
         lines(positions),
@@ -1521,6 +1534,7 @@
     )
     grad_queries, *grad_window = attend_back(
         first_block,
+        clear_block,
         queries,
         window,
         grad_attended,

time: 702 us -> 701 us (level)
  Pallas kernels: 476 us -> 468 us
  transfers between devices with their start and end apart: 16 -> 16, of which waited for: 5 -> 5; matrix products, arithmetic and copies ran while one was open for 7% -> 7% of each run, Pallas kernels for 60% -> 59%
where the time goes in v11:
time: 701 us; the launch traced here: 694 us
  Pallas kernels  468 us (67%)
  waiting for transfers between devices  103 us (15%)
  local copies, waits for them, and re-layouts  43 us (6%)
  other arithmetic  31.1 us (4%)
  starting transfers between devices  27.5 us (4%)
  between operations  14.8 us (2%)
    pallas_call x1, Pallas kernels, finish(): pl.pallas_call(functools.partial(finish_kernel, layout), out_shape=[jax.S...  98 us
    ppermute x4, waiting for transfers between devices, shift(): return lax.ppermute(value, axis, pairs)  97.2 us
    pallas_call x1, Pallas kernels, start(): pl.pallas_call(start_kernel, out_shape=shapes, in_specs=[pl.BlockSpec(mem...  89.7 us
    pallas_call x2, Pallas kernels, level_gather(): pl.pallas_call(functools.partial(gather_kernel, by_source), out_shape=jax...  59.4 us
    pallas_call x1, Pallas kernels, ffn_front(): pl.pallas_call(functools.partial(front_kernel, groups, local), grid_spec=...  37.2 us
    pallas_call x2, Pallas kernels, ffn_rear(): pl.pallas_call(functools.partial(rear_kernel, groups), grid_spec=pltpu.Pr...  28.1 us
    pallas_call x1, Pallas kernels, level_scatter(): pl.pallas_call(functools.partial(scatter_kernel, by_source), out_shape=ja...  27.3 us
    pallas_call x1, Pallas kernels, project_back(): pl.pallas_call(project_back_kernel, grid=(HEADS,), in_specs=[by_row(width...  23.2 us
  transfers between devices with their start and end apart: 16, of which 5 were waited for; matrix products, arithmetic and copies ran while one was open for 7% of the time, Pallas kernels for 59%

profile of v11, /device:TPU:8, one launch (start us, length us, event | category | flops | bytes accessed | tf_op | source)
XLA Modules:
  0.0 693.8 jit_solution(10675778227350381122)
XLA Ops:
  17.0 89.7 %start.1 = (bf16[4,4,4,32,1024]{4,3,2,1,0:T(8,128)(2,1)}, bf16[4,4,32,1024]{3,2,1,0:T(8,128)(2,1)}, bf16[2,4,4,32,1664]{4,3,2,1,0:T(8,128)(2,1)}, s32[4,4,512]{2...) custom-call(bf16[4,4,32,1024]{3,2,1,0:T(8,128)(2,1)} %bitcast.170, bf16[4,4,32,1024]{3,2,1,0:T(8,128)(2,1)} %bitcast.171, ...), custom_call_target="tpu_custom_call" | custom-call | bytes 200000000 | tf_op jit(solution)/shard_map/start/pallas_call | solution.py:459
  111.3 14.3 %project.1 = (bf16[2048,128]{1,0:T(8,128)(2,1)S(1)}, bf16[2048,256]{1,0:T(8,128)(2,1)S(1)}, f32[2048,640]{1,0:T(8,128)}, f32[2048,128]{1,0:T(8,128)S(1)}, f32[2048,16]{1,0:T(8,128)S(1)}) custom-call(bf16[2048,1024]{1,0:T(8,128)(2,1)} %bitcast.152, bf16[1024,1664]{1,0:T(8,128)(2,1)} %bitcast.141, bf16[1024,1664]{1,0:T(8,128)(2,1)} %bitcast.142, ...), custom_call_target="tpu_custom_call" | custom-call | flops 4294967296 | bytes 20000000 | tf_op jit(solution)/shard_map/project/pallas_call | solution.py:1221
  131.0 22.2 %collective-permute-done.1.refs_1_.refs_4_ = bf16[2048,256]{1,0:T(8,128)(2,1)} collective-permute-done((bf16[2048,256]{1,0:T(8,128)(2,1)S(1)}, bf16[2048,256]{1,0:T(8,128)(2,1)}, u32[]{:S(2)}, u32[]{:S(2)}) %collective-permute-start.1) | collective-permute-done | bytes 1048608 | tf_op jit(solution)/shard_map/ppermute | solution.py:1326
  157.6 5.3 collective-permute-start.2
  163.1 2.4 constant_dynamic-slice_fusion
  170.2 28.4 %level_gather.2 = bf16[4,4,128,1024]{3,2,1,0:T(8,128)(2,1)} custom-call(bf16[4,128,1024]{2,1,0:T(8,128)(2,1)} %bitcast.120), custom_call_target="tpu_custom_call" | custom-call | bytes 90000000 | tf_op jit(solution)/shard_map/level_gather/pallas_call | solution.py:105
  198.6 16.8 %collective-permute-done.2.refs_0_.refs_3_ = bf16[2048,256]{1,0:T(8,128)(2,1)} collective-permute-done((bf16[2048,256]{1,0:T(8,128)(2,1)}, bf16[2048,256]{1,0:T(8,128)(2,1)}, u32[]{:S(2)}, u32[]{:S(2)}) %collective-permute-start.2) | collective-permute-done | bytes 1048608 | tf_op jit(solution)/shard_map/ppermute | solution.py:1326
  217.6 14.4 %attend.1 = (f32[2048,128]{1,0:T(8,128)S(1)}, f32[4,1,512]{2,1,0:T(1,128)S(1)}) custom-call(s32[4]{0:T(128)S(1)} %get-tuple-element.263.first, s32[4]{0:T(128)S(1)} %get-tuple-element.262.clear, bf16[2048,128]{1,0:T(8,128)(2,1)S(1)} %copy-done.18, bf16[2048,256]{1,0:T(8,128)(2,1)} %collective-permute-done.2.refs_0_.refs_3_, ...), custom_call_target="tpu_custom_call" | custom-call | flops 20000000000 | bytes 10000000 | tf_op jit(solution)/shard_map/attend/pallas_call | solution.py:730
  232.1 2.4 collective-permute-start.3
  241.3 5.1 convolution_convert_fusion
  246.4 27.3 %level_scatter.1 = f32[4,128,1024]{2,1,0:T(8,128)S(1)} custom-call(bf16[4,4,128,1024]{3,2,1,0:T(8,128)(2,1)S(1)} %bitcast.119), custom_call_target="tpu_custom_call" | custom-call | bytes 80000000 | tf_op jit(solution)/shard_map/level_scatter/pallas_call | solution.py:167
  278.6 31.0 %level_gather.3 = bf16[4,4,128,1152]{3,2,1,0:T(8,128)(2,1)} custom-call(bf16[4,128,1152]{2,1,0:T(8,128)(2,1)} %bitcast.126), custom_call_target="tpu_custom_call" | custom-call | bytes 90000000 | tf_op jit(solution)/shard_map/level_gather/pallas_call | solution.py:105
  311.8 37.2 %ffn_front.1 = (bf16[2048,2048]{1,0:T(8,128)(2,1)}, bf16[2048,2048]{1,0:T(8,128)(2,1)}, bf16[2048,1152]{1,0:T(8,128)(2,1)}) custom-call(s32[2]{0:T(128)} %pad_add_fusion.1.place, bf16[2048,1152]{1,0:T(8,128)(2,1)} %bitcast.155, bf16[2048,1024]{1,0:T(8,128)(2,1)} %bitcast.157, bf16[4,2,512,512]{3,2,1,0:T(8,128)(2,1)} %bitcast.187, ...), custom_call_target="tpu_custom_call" | custom-call | flops 25769803776 | bytes 30000000 | tf_op jit(solution)/shard_map/ffn_front/pallas_call | solution.py:903
  349.0 2.3 copy-done.7
  351.3 5.8 pair_scatter.2
  359.5 14.0 %ffn_rear.2 = (bf16[4,512,512]{2,1,0:T(8,128)(2,1)}, bf16[4,512,512]{2,1,0:T(8,128)(2,1)}) custom-call(s32[2]{0:T(128)} %pad_add_fusion.1.place, bf16[2048,1152]{1,0:T(8,128)(2,1)} %bitcast.156, bf16[2048,2048]{1,0:T(8,128)(2,1)} %get-tuple-element.131.hidden_units), custom_call_target="tpu_custom_call" | custom-call | flops 1000 | bytes 1000 | tf_op jit(solution)/shard_map/ffn_rear/pallas_call | solution.py:977
  373.7 14.1 %ffn_rear.3 = (bf16[4,512,512]{2,1,0:T(8,128)(2,1)}, bf16[4,512,512]{2,1,0:T(8,128)(2,1)}) custom-call(s32[2]{0:T(128)} %pad_add_fusion.1.place, bf16[2048,1024]{1,0:T(8,128)(2,1)} %bitcast.158, bf16[2048,2048]{1,0:T(8,128)(2,1)} %get-tuple-element.134.hidden_units.active), custom_call_target="tpu_custom_call" | custom-call | flops 1000 | bytes 1000 | tf_op jit(solution)/shard_map/ffn_rear/pallas_call | solution.py:977
  388.8 7.3 %leave_ffn.1 = (f32[512,1024]{1,0:T(8,128)}, bf16[512,1024]{1,0:T(8,128)(2,1)}, bf16[1024,128]{1,0:T(8,128)(2,1)S(1)}) custom-call(f32[512,1024]{1,0:T(8,128)} %copy-done.5, f32[512,1152]{1,0:T(8,128)} %bitcast.122, bf16[512,1152]{1,0:T(8,128)(2,1)S(1)} %collective-permute-done.4.came, bf16[512,1024]{1,0:T(8,128)(2,1)S(1)} %bitcast.121, ...), custom_call_target="tpu_custom_call" | custom-call | flops 1000000000 | bytes 10000000 | tf_op jit(solution)/shard_map/leave_ffn/pallas_call | solution.py:1073
  398.0 18.2 %ffn_feed.1 = bf16[2048,1024]{1,0:T(8,128)(2,1)} custom-call(s32[2]{0:T(128)} %pad_add_fusion.1.place, bf16[2048,2048]{1,0:T(8,128)(2,1)} %get-tuple-element.134.hidden_units.active, bf16[4,512,512]{2,1,0:T(8,128)(2,1)} %bitcast.166, bf16[4,512,512]{2,1,0:T(8,128)(2,1)} %collective-permute-done.3.refs_2_.refs_1_), custom_call_target="tpu_custom_call" | custom-call | flops 1000 | bytes 1000 | tf_op jit(solution)/shard_map/ffn_feed/pallas_call | solution.py:956
  416.2 6.0 collective-permute-done.5
  422.1 6.1 pair_gather.1
  428.2 4.2 add_convert_fusion.1
  432.5 12.7 %branch_back.1 = (bf16[2048,128]{1,0:T(8,128)(2,1)S(1)}, f32[4,1,512]{2,1,0:T(1,128)S(1)}, bf16[2048,128]{1,0:T(8,128)(2,1)S(1)}, bf16[1024,640]{1,0:T(8,128)(2,1)S(1)}) custom-call(bf16[2048,1024]{1,0:T(8,128)(2,1)} %bitcast.159, bf16[1024,1664]{1,0:T(8,128)(2,1)} %bitcast.147, f32[2048,128]{1,0:T(8,128)S(1)} %get-tuple-element.115.attended, ...), custom_call_target="tpu_custom_call" | custom-call | flops 100000000 | bytes 1000000 | tf_op jit(solution)/shard_map/branch_back/pallas_call | solution.py:1132
  447.0 20.0 %attend_back.1 = (bf16[2048,128]{1,0:T(8,128)(2,1)S(1)}, bf16[2048,256]{1,0:T(8,128)(2,1)S(1)}, bf16[2048,256]{1,0:T(8,128)(2,1)S(1)}, f32[2048,256]{1,0:T(8,128)}) custom-call(s32[4]{0:T(128)S(1)} %get-tuple-element.263.first, s32[4]{0:T(128)S(1)} %get-tuple-element.262.clear, bf16[2048,128]{1,0:T(8,128)(2,1)S(1)} %copy-done.19, ...), custom_call_target="tpu_custom_call" | custom-call | flops 2000000000 | bytes 1000000 | tf_op jit(solution)/shard_map/attend_back/pallas_call | solution.py:813
  468.9 3.5 collective-permute-start.10
  472.4 4.4 pair_scatter.3
  476.8 29.3 %collective-permute-done.7 = bf16[2048,256]{1,0:T(8,128)(2,1)S(1)} collective-permute-done((bf16[2048,256]{1,0:T(8,128)(2,1)S(1)}, bf16[2048,256]{1,0:T(8,128)(2,1)S(1)}, u32[]{:S(2)}, u32[]{:S(2)}) %collective-permute-start.7) | collective-permute-done | bytes 1048608 | tf_op jit(solution)/shard_map/ppermute | solution.py:1326
  506.3 2.7 collective-permute-start.9
  509.1 29.0 %collective-permute-done.9 = bf16[2048,256]{1,0:T(8,128)(2,1)S(1)} collective-permute-done((bf16[2048,256]{1,0:T(8,128)(2,1)S(1)}, bf16[2048,256]{1,0:T(8,128)(2,1)S(1)}, u32[]{:S(2)}, u32[]{:S(2)}) %collective-permute-start.9) | collective-permute-done | bytes 1048608 | tf_op jit(solution)/shard_map/ppermute | solution.py:1326
  543.6 23.2 %project_back.1 = (bf16[2048,1024]{1,0:T(8,128)(2,1)}, bf16[1024,1024]{1,0:T(8,128)(2,1)}) custom-call(bf16[2048,1024]{1,0:T(8,128)(2,1)} %bitcast.153, f32[2048,256]{1,0:T(8,128)} %convert_add_fusion.grads, bf16[2048,128]{1,0:T(8,128)(2,1)} %copy-done.21, bf16[2048,128]{1,0:T(8,128)(2,1)} %copy-done.20, f32[2048,640]{1,0:T(8,128)} %get-tuple-element.156.projected, ...), custom_call_target="tpu_custom_call" | custom-call | flops 1073741824 | bytes 4000000 | tf_op jit(solution)/shard_map/project_back/pallas_call | solution.py:1301
  568.5 4.5 all-to-all-start
  573.0 98.0 %finish.1 = (f32[4,4,32,1024]{3,2,1,0:T(8,128)}, f32[32,2560]{1,0:T(8,128)}, f32[32,512]{1,0:T(8,128)}, f32[32,512]{1,0:T(8,128)}, f32[4,32,128]{2,1,0:T(8,128)}...) custom-call(bf16[4,4,128,1024]{3,2,1,0:T(8,128)(2,1)} %bitcast.160, f32[4,128,1024]{2,1,0:T(8,128)} %bitcast.167, ...), custom_call_target="tpu_custom_call" | custom-call | bytes 200000000 | tf_op jit(solution)/shard_map/finish/pallas_call | solution.py:626
  (179 shorter events, 77.6 us)
Async XLA Ops:
  7.2 224.9 %all-gather.5.cloned.1.call-start = ((), (), s32[]{:S(2)}) async-start(), calls=%async_computation.5 | async-start | bytes 2621440 | tf_op jit(solution)/shard_map/all_gather | solution.py:1472
  7.2 101.0 %collective-permute-start = (bf16[512,512]{1,0:T(8,128)(2,1)}, bf16[512,512]{1,0:T(8,128)(2,1)S(1)}, u32[]{:S(2)}, u32[]{:S(2)}) collective-permute-start(bf16[512,512]{1,0:T(8,128)(2,1)} %param.38), channel_id=1, source_target_pairs={{0,16},{16,0},{1,17},{17,1},{2,18},{18,2},{3,19},{19,3},{4,20},{20... | collective-permute-start | bytes 1572872 | tf_op jit(solution)/shard_map/ppermute | solution.py:1163
  110.5 15.1 %copy-start.25 = (f32[1024]{0:T(1024)}, f32[1024]{0:T(1024)S(1)}, u32[]{:S(2)}) copy-start(f32[1024]{0:T(1024)S(1)} %get-tuple-element.252) | copy-start | bytes 12292
  110.5 15.1 %copy-start.26 = (f32[1024]{0:T(1024)}, f32[1024]{0:T(1024)S(1)}, u32[]{:S(2)}) copy-start(f32[1024]{0:T(1024)S(1)} %get-tuple-element.253) | copy-start | bytes 12292
  111.3 19.2 %copy-start.38 = (s32[1,3]{1,0:T(1,128)S(1)}, s32[1,3]{1,0:T(1,128)}, u32[]{:S(2)}) copy-start(s32[1,3]{1,0:T(1,128)} %param.23) | copy-start | bytes 40
  126.4 39.0 %copy-start.9 = (bf16[2048,256]{1,0:T(8,128)(2,1)}, bf16[2048,256]{1,0:T(8,128)(2,1)S(1)}, u32[]{:S(2)}) copy-start(bf16[2048,256]{1,0:T(8,128)(2,1)S(1)} %get-tuple-element.100.refs_2_.refs_5_) | copy-start | bytes 3145732
  126.4 306.0 %copy-start.3 = (f32[2048,128]{1,0:T(8,128)}, f32[2048,128]{1,0:T(8,128)S(1)}, u32[]{:S(2)}) copy-start(f32[2048,128]{1,0:T(8,128)S(1)} %get-tuple-element.107.sigs) | copy-start | bytes 3145732
  126.4 306.0 %copy-start.4 = (f32[2048,16]{1,0:T(8,128)}, f32[2048,16]{1,0:T(8,128)S(1)}, u32[]{:S(2)}) copy-start(f32[2048,16]{1,0:T(8,128)S(1)} %get-tuple-element.108.masks) | copy-start | bytes 393220
  126.4 29.3 %copy-start.36 = (s32[4,16,128]{2,1,0:T(8,128)S(1)}, s32[4,16,128]{2,1,0:T(8,128)}, u32[]{:S(2)}) copy-start(s32[4,16,128]{2,1,0:T(8,128)} %get-tuple-element.105) | copy-start | bytes 98308
  126.5 26.7 %collective-permute-start.1 = (bf16[2048,256]{1,0:T(8,128)(2,1)S(1)}, bf16[2048,256]{1,0:T(8,128)(2,1)}, u32[]{:S(2)}, u32[]{:S(2)}) collective-permute-start(bf16[2048,256]{1,0:T(8,128)(2,1)S(1)} %get-tuple-element.100.refs_2_.refs_5_), channel_id=1, source_target_pairs={{0,4},{4,8},{8,12},{1,5},{5,9},{9,13},{2,6},{6,10},{10,14},{3,7},{... | collective-permute-start | bytes 3145736 | tf_op jit(solution)/shard_map/ppermute | solution.py:1326
  153.2 158.6 %all-gather.7.cloned.1.call-start = ((), (), s32[]{:S(2)}) async-start(), calls=%async_computation.6 | async-start | bytes 5242880 | tf_op jit(solution)/shard_map/all_gather | solution.py:1473
  155.6 521.7 %reduce-scatter.3.cloned.1.call-start = ((), (), s32[]{:S(2)}) async-start(), calls=%async_computation.3 | async-start | bytes 2621440 | tf_op jit(solution)/shard_map/reduce_scatter | solution.py:1528
  157.6 57.8 %collective-permute-start.2 = (bf16[2048,256]{1,0:T(8,128)(2,1)}, bf16[2048,256]{1,0:T(8,128)(2,1)}, u32[]{:S(2)}, u32[]{:S(2)}) collective-permute-start(bf16[2048,256]{1,0:T(8,128)(2,1)} %collective-permute-done.1.refs_1_.refs_4_), channel_id=1, source_target_pairs={{0,4},{4,8},{8,12},{1,5},{5,9},{9,13},{2,6},{6,10},{10,14},{3,7},{... | collective-permute-start | bytes 3145736 | tf_op jit(solution)/shard_map/ppermute | solution.py:1326
  232.1 79.8 %collective-permute-start.3 = (bf16[4,512,512]{2,1,0:T(8,128)(2,1)}, bf16[4,512,512]{2,1,0:T(8,128)(2,1)}, u32[]{:S(2)}, u32[]{:S(2)}) collective-permute-start(bf16[4,512,512]{2,1,0:T(8,128)(2,1)} %bitcast.164), channel_id=1, source_target_pairs={{0,16},{16,0},{1,17},{17,1},{2,18},{18,2},{3,19},{19,3},{4,20},{20... | collective-permute-start | bytes 6291464 | tf_op jit(solution)/shard_map/ppermute | solution.py:1163
  246.4 27.3 %copy-start.14 = (bf16[4,1,4,32,1024]{4,3,2,1,0:T(8,128)(2,1)S(1)}, bf16[4,1,4,32,1024]{4,3,2,1,0:T(8,128)(2,1)}, u32[]{:S(2)}) copy-start(bf16[4,1,4,32,1024]{4,3,2,1,0:T(8,128)(2,1)} %constant_dynamic-slice_fusion) | copy-start | bytes 3145732
  246.4 27.3 %copy-start.15 = (s32[512,16]{1,0:T(8,128)S(1)}, s32[512,16]{1,0:T(8,128)}, u32[]{:S(2)}) copy-start(s32[512,16]{1,0:T(8,128)} %fusion.4.routes) | copy-start | bytes 98308
  358.5 29.3 %collective-permute-start.4 = (bf16[512,1152]{1,0:T(8,128)(2,1)}, bf16[512,1152]{1,0:T(8,128)(2,1)S(1)}, u32[]{:S(2)}, u32[]{:S(2)}) collective-permute-start(bf16[512,1152]{1,0:T(8,128)(2,1)} %bitcast.38), channel_id=1, source_target_pairs={{0,2},{1,3},{2,0},{3,1},{4,6},{5,7},{6,4},{7,5},{8,10},{9,11},{10,... | collective-permute-start | bytes 3538952 | tf_op jit(solution)/shard_map/ppermute | solution.py:287
  373.5 54.7 %collective-permute-start.6 = (bf16[4,512,512]{2,1,0:T(8,128)(2,1)}, bf16[4,512,512]{2,1,0:T(8,128)(2,1)}, u32[]{:S(2)}, u32[]{:S(2)}) collective-permute-start(bf16[4,512,512]{2,1,0:T(8,128)(2,1)} %get-tuple-element.133), channel_id=1, source_target_pairs={{0,16},{16,0},{1,17},{17,1},{2,18},{18,2},{3,19},{19,3},{4,20},{20... | collective-permute-start | bytes 6291464 | tf_op jit(solution)/shard_map/ppermute | solution.py:1163
  373.7 14.2 %copy-start.16 = (s32[512,16]{1,0:T(8,128)S(1)}, s32[512,16]{1,0:T(8,128)}, u32[]{:S(2)}) copy-start(s32[512,16]{1,0:T(8,128)} %fusion.4.routes) | copy-start | bytes 98308
  396.8 25.3 %collective-permute-start.5 = (bf16[512,1024]{1,0:T(8,128)(2,1)}, bf16[512,1024]{1,0:T(8,128)(2,1)}, u32[]{:S(2)}, u32[]{:S(2)}) collective-permute-start(bf16[512,1024]{1,0:T(8,128)(2,1)} %get-tuple-element.139), channel_id=1, source_target_pairs={{0,2},{1,3},{2,0},{3,1},{4,6},{5,7},{6,4},{7,5},{8,10},{9,11},{10,... | collective-permute-start | bytes 3145736 | tf_op jit(solution)/shard_map/ppermute | solution.py:287
  432.4 247.2 %reduce-scatter.5.cloned.1.call-start = ((), (), s32[]{:S(2)}) async-start(), calls=%async_computation.4 | async-start | bytes 2621440 | tf_op jit(solution)/shard_map/reduce_scatter | solution.py:1528
  432.5 14.6 %copy-start.19 = (bf16[2048,128]{1,0:T(8,128)(2,1)S(1)}, bf16[2048,128]{1,0:T(8,128)(2,1)}, u32[]{:S(2)}) copy-start(bf16[2048,128]{1,0:T(8,128)(2,1)} %copy-done.17) | copy-start | bytes 1572868
  447.0 21.9 %copy-start.37 = (bf16[4,512,512]{2,1,0:T(8,128)(2,1)S(1)}, bf16[4,512,512]{2,1,0:T(8,128)(2,1)}, u32[]{:S(2)}) copy-start(bf16[4,512,512]{2,1,0:T(8,128)(2,1)} %get-tuple-element.136) | copy-start | bytes 6291460
  447.0 25.4 %copy-start.2 = (bf16[2048,1024]{1,0:T(8,128)(2,1)S(1)}, bf16[2048,1024]{1,0:T(8,128)(2,1)}, u32[]{:S(2)}) copy-start(bf16[2048,1024]{1,0:T(8,128)(2,1)} %ffn_feed.1) | copy-start | bytes 12582916
  467.0 39.4 %copy-start.21 = (bf16[2048,128]{1,0:T(8,128)(2,1)}, bf16[2048,128]{1,0:T(8,128)(2,1)S(1)}, u32[]{:S(2)}) copy-start(bf16[2048,128]{1,0:T(8,128)(2,1)S(1)} %get-tuple-element.154.grad_query) | copy-start | bytes 1572868
  467.0 39.1 %collective-permute-start.7 = (bf16[2048,256]{1,0:T(8,128)(2,1)S(1)}, bf16[2048,256]{1,0:T(8,128)(2,1)S(1)}, u32[]{:S(2)}, u32[]{:S(2)}) collective-permute-start(bf16[2048,256]{1,0:T(8,128)(2,1)S(1)} %get-tuple-element.145), channel_id=1, source_target_pairs={{4,0},{8,4},{12,8},{5,1},{9,5},{13,9},{6,2},{10,6},{14,10},{7,3},{... | collective-permute-start | bytes 3145736 | tf_op jit(solution)/shard_map/ppermute | solution.py:1326
  468.9 70.7 %collective-permute-start.10 = (bf16[4,512,512]{2,1,0:T(8,128)(2,1)S(1)}, bf16[4,512,512]{2,1,0:T(8,128)(2,1)S(1)}, u32[]{:S(2)}, u32[]{:S(2)}) collective-permute-start(bf16[4,512,512]{2,1,0:T(8,128)(2,1)S(1)} %copy-done.37), channel_id=1, source_target_pairs={{0,16},{16,0},{1,17},{17,1},{2,18},{18,2},{3,19},{19,3},{4,20},{20... | collective-permute-start | bytes 6291464 | tf_op jit(solution)/shard_map/ppermute | solution.py:1163
  476.8 61.3 %copy-start.30 = (f32[2048,256]{1,0:T(8,128)S(1)}, f32[2048,256]{1,0:T(8,128)}, u32[]{:S(2)}) copy-start(f32[2048,256]{1,0:T(8,128)} %get-tuple-element.150) | copy-start | bytes 6291460
  506.3 31.7 %collective-permute-start.9 = (bf16[2048,256]{1,0:T(8,128)(2,1)S(1)}, bf16[2048,256]{1,0:T(8,128)(2,1)S(1)}, u32[]{:S(2)}, u32[]{:S(2)}) collective-permute-start(bf16[2048,256]{1,0:T(8,128)(2,1)S(1)} %add_convert_fusion.3), channel_id=1, source_target_pairs={{4,0},{8,4},{12,8},{5,1},{9,5},{13,9},{6,2},{10,6},{14,10},{7,3},{... | collective-permute-start | bytes 3145736 | tf_op jit(solution)/shard_map/ppermute | solution.py:1326
  542.4 24.4 %collective-permute-start.8 = (bf16[512,1024]{1,0:T(8,128)(2,1)S(1)}, bf16[512,1024]{1,0:T(8,128)(2,1)S(1)}, u32[]{:S(2)}, u32[]{:S(2)}) collective-permute-start(bf16[512,1024]{1,0:T(8,128)(2,1)S(1)} %bitcast.139), channel_id=1, source_target_pairs={{0,2},{1,3},{2,0},{3,1},{4,6},{5,7},{6,4},{7,5},{8,10},{9,11},{10,... | collective-permute-start | bytes 3145736 | tf_op jit(solution)/shard_map/ppermute | solution.py:287
  543.6 23.2 %copy-start.6 = (f32[512,1024]{1,0:T(8,128)S(1)}, f32[512,1024]{1,0:T(8,128)}, u32[]{:S(2)}) copy-start(f32[512,1024]{1,0:T(8,128)} %copy-done.5) | copy-start | bytes 6291460
  568.5 108.8 %all-to-all-start = ((bf16[4,128,1024]{2,1,0:T(8,128)(2,1)}), bf16[4,128,1024]{2,1,0:T(8,128)(2,1)S(1)}, u32[]{:S(2)}, u32[]{:S(2)}) async-start(bf16[4,128,1024]{2,1,0:T(8,128)(2,1)} %bitcast.47), calls=%async_computation | async-start | bytes 2097152 | tf_op jit(solution)/shard_map/all_to_all | solution.py:33
  (23 other events, 61.9 us)
Sparse Core Ops, SparseCore 0:
  153.3 64.3 all-gather.4
  219.3 76.0 all-gather.6
  432.5 57.8 reduce-scatter.2
  542.5 53.0 reduce-scatter.4

commit v12 on v11

--- a/solution.py
+++ b/solution.py
@@ -381,25 +381,52 @@
         to_near.append(send(src, place, near_s.at[k], near_r.at[k], {"head": near}))
 
     share(0, tokens.at[level], level)
-    block_s, block_r = pair()
+    up_s, up_r = pair()
+    down_s, down_r = pair()
     group_s, group_r = pair()
     orders_s, orders_r = pair()
     for copy in to_mates:
         copy.wait_recv()
     own[1].wait()
-    blocks, grouped, ordered = [], [], []
-
-    def to_groups(j, source):
-        for k, to in enumerate(groups_ahead):
-            block = full.at[group, source]
-            grouped.append(
-                send(block, block, group_s.at[k, j], group_r.at[k, j], {"group": to})
-            )
-
-    for k, to in enumerate(levels_ahead):
-        block = full.at[group, level]
-        blocks.append(send(block, block, block_s.at[k], block_r.at[k], {"level": to}))
-    to_groups(0, level)
+    last = len(levels_ahead)
+    ordered = []
+
+    def to_groups(j):
+        block = full.at[group, lax.rem(level - j + last + 1, last + 1)]
+        return [
+            reach_out(block, block, group_s.at[k, j], group_r.at[k, j], {"group": to})
+            for k, to in enumerate(groups_ahead)
+        ]
+
+    def hop(k, step):
+        send_sem, recv_sem = (up_s, up_r) if step > 0 else (down_s, down_r)
+        block = full.at[group, lax.rem(level - step * k + last + 1, last + 1)]
+        to = lax.rem(level + step + last + 1, last + 1)
+        return reach_out(block, block, send_sem.at[k], recv_sem.at[k], {"level": to})
+
+    def sends(k, step):
+        return (level >= k) & (level < last) if step > 0 else (level <= last - k) & (level > 0)
+
+    def receives(k, step):
+        return level >= k + 1 if step > 0 else level <= last - k - 1
+
+    def start_hop(k, step):
+        @pl.when(sends(k, step))
+        def _():
+            hop(k, step).start()
+
+    def wait_hop(k, step):
+        @pl.when(receives(k, step))
+        def _():
+            hop(k, step).wait_recv()
+            for copy in to_groups(k + 1 if step > 0 else last - k):
+                copy.start()
+
+    for step in (1, -1):
+        start_hop(0, step)
+    for copy in to_groups(0):
+        copy.start()
+    grouped = [copy for j in range(last + 1) for copy in to_groups(j)]
     for k, to in enumerate(mates):
         table_mates.append(
             send(tables.at[to], routes.at[head], table_s.at[k], table_r.at[k], {"head": to})
@@ -414,6 +441,14 @@
     for k, to in enumerate(levels_ahead):
         block = orders.at[level]
         ordered.append(send(block, block, orders_s.at[k], orders_r.at[k], {"level": to}))
+    def finish_hop(k):
+        for step in (1, -1):
+            wait_hop(k, step)
+            if k + 1 < last:
+                start_hop(k + 1, step)
+
+    if last:
+        finish_hop(0)
     for k, source in enumerate(levels_behind):
         crossing[k].wait_recv()
         share(k + 1, rows.at[:, head, source], source)
@@ -423,9 +458,8 @@
         crossed.append(
             send(cotangents.at[to], grads.at[:, level], grad_s.at[k], grad_r.at[k], {"level": to})
         )
-    for k, source in enumerate(levels_behind):
-        blocks[k].wait_recv()
-        to_groups(k + 1, source)
+    for k in range(1, last):
+        finish_hop(k)
     passed = []
     for k, source in enumerate([level] + levels_behind):
         to_far[k].wait_recv()
@@ -433,8 +467,15 @@
         passed.append(send(place, place, pass_s.at[k], pass_r.at[k], {"head": near}))
     for copy in to_near + passed + grouped + table_mates + picking + ordered + crossed:
         copy.wait_recv()
-    for copy in started:
+    for copy in started + grouped:
         copy.wait_send()
+    for k in range(last):
+        for step in (1, -1):
+
+            @pl.when(sends(k, step))
+            def _(k=k, step=step):
+                hop(k, step).wait_send()
+
     for i in (0, 2, 3, 5):
         own[i].wait()
 
@@ -455,7 +496,7 @@
     dma = pltpu.SemaphoreType.DMA
     others, mates = (levels - 1,), (HEADS - 1,)
     counts = [others] * 2 + [mates] * 3 + [(levels,)] * 3
-    counts += [others, (groups - 1, levels), others, others]
+    counts += [others, others, (groups - 1, levels), others, others]
     return pl.pallas_call(
         start_kernel,
         out_shape=shapes,

time: 701 us -> 693 us (0.989)
  waiting for transfers between devices: 103 us -> 118 us
  Pallas kernels: 468 us -> 455 us
    ppermute x4, waiting for transfers between devices: 97.2 us -> 113 us  [shift(): return lax.ppermute(value, axis, pairs)]
    pallas_call x1, Pallas kernels: 89.7 us -> 80.1 us  [start(): pl.pallas_call(start_kernel, out_shape=shapes, in_specs=[pl.BlockSpec(mem...]
  transfers between devices with their start and end apart: 16 -> 16, of which waited for: 5 -> 5; matrix products, arithmetic and copies ran while one was open for 7% -> 8% of each run, Pallas kernels for 59% -> 58%
where the time goes in v12:
time: 693 us; the launch traced here: 690 us
  Pallas kernels  455 us (66%)
  waiting for transfers between devices  118 us (17%)
  local copies, waits for them, and re-layouts  43 us (6%)
  other arithmetic  31.1 us (4%)
  starting transfers between devices  21.5 us (3%)
  between operations  14.8 us (2%)
    ppermute x4, waiting for transfers between devices, shift(): return lax.ppermute(value, axis, pairs)  113 us
    pallas_call x1, Pallas kernels, finish(): pl.pallas_call(functools.partial(finish_kernel, layout), out_shape=[jax.S...  98 us
    pallas_call x1, Pallas kernels, start(): pl.pallas_call(start_kernel, out_shape=shapes, in_specs=[pl.BlockSpec(mem...  80.1 us
    pallas_call x2, Pallas kernels, level_gather(): pl.pallas_call(functools.partial(gather_kernel, by_source), out_shape=jax...  57.5 us
    pallas_call x1, Pallas kernels, ffn_front(): pl.pallas_call(functools.partial(front_kernel, groups, local), grid_spec=...  37.2 us
    pallas_call x2, Pallas kernels, ffn_rear(): pl.pallas_call(functools.partial(rear_kernel, groups), grid_spec=pltpu.Pr...  28.1 us
    pallas_call x1, Pallas kernels, level_scatter(): pl.pallas_call(functools.partial(scatter_kernel, by_source), out_shape=ja...  25.6 us
    pallas_call x1, Pallas kernels, project_back(): pl.pallas_call(project_back_kernel, grid=(HEADS,), in_specs=[by_row(width...  23.2 us
  transfers between devices with their start and end apart: 16, of which 5 were waited for; matrix products, arithmetic and copies ran while one was open for 8% of the time, Pallas kernels for 58%

profile of v12, /device:TPU:8, one launch (start us, length us, event | category | flops | bytes accessed | tf_op | source)
XLA Modules:
  0.0 689.5 jit_solution(10437469619893668121)
XLA Ops:
  17.0 80.1 %start.1 = (bf16[4,4,4,32,1024]{4,3,2,1,0:T(8,128)(2,1)}, bf16[4,4,32,1024]{3,2,1,0:T(8,128)(2,1)}, bf16[2,4,4,32,1664]{4,3,2,1,0:T(8,128)(2,1)}, s32[4,4,512]{2...) custom-call(bf16[4,4,32,1024]{3,2,1,0:T(8,128)(2,1)} %bitcast.170, bf16[4,4,32,1024]{3,2,1,0:T(8,128)(2,1)} %bitcast.171, ...), custom_call_target="tpu_custom_call" | custom-call | bytes 200000000 | tf_op jit(solution)/shard_map/start/pallas_call | solution.py:500
  101.7 14.3 %project.1 = (bf16[2048,128]{1,0:T(8,128)(2,1)S(1)}, bf16[2048,256]{1,0:T(8,128)(2,1)S(1)}, f32[2048,640]{1,0:T(8,128)}, f32[2048,128]{1,0:T(8,128)S(1)}, f32[2048,16]{1,0:T(8,128)S(1)}) custom-call(bf16[2048,1024]{1,0:T(8,128)(2,1)} %bitcast.152, bf16[1024,1664]{1,0:T(8,128)(2,1)} %bitcast.141, bf16[1024,1664]{1,0:T(8,128)(2,1)} %bitcast.142, ...), custom_call_target="tpu_custom_call" | custom-call | flops 4294967296 | bytes 20000000 | tf_op jit(solution)/shard_map/project/pallas_call | solution.py:1262
  121.4 29.7 %collective-permute-done.1.refs_1_.refs_4_ = bf16[2048,256]{1,0:T(8,128)(2,1)} collective-permute-done((bf16[2048,256]{1,0:T(8,128)(2,1)S(1)}, bf16[2048,256]{1,0:T(8,128)(2,1)}, u32[]{:S(2)}, u32[]{:S(2)}) %collective-permute-start.1) | collective-permute-done | bytes 1048608 | tf_op jit(solution)/shard_map/ppermute | solution.py:1367
  151.2 2.3 pad_maximum_fusion
  157.9 2.4 constant_dynamic-slice_fusion
  162.7 2.3 copy.138.refs_8_.refs_11_
  165.0 25.5 %level_gather.2 = bf16[4,4,128,1024]{3,2,1,0:T(8,128)(2,1)} custom-call(bf16[4,128,1024]{2,1,0:T(8,128)(2,1)} %bitcast.120), custom_call_target="tpu_custom_call" | custom-call | bytes 90000000 | tf_op jit(solution)/shard_map/level_gather/pallas_call | solution.py:105
  190.5 19.5 %collective-permute-done.2.refs_0_.refs_3_ = bf16[2048,256]{1,0:T(8,128)(2,1)} collective-permute-done((bf16[2048,256]{1,0:T(8,128)(2,1)}, bf16[2048,256]{1,0:T(8,128)(2,1)}, u32[]{:S(2)}, u32[]{:S(2)}) %collective-permute-start.2) | collective-permute-done | bytes 1048608 | tf_op jit(solution)/shard_map/ppermute | solution.py:1367
  212.3 14.4 %attend.1 = (f32[2048,128]{1,0:T(8,128)S(1)}, f32[4,1,512]{2,1,0:T(1,128)S(1)}) custom-call(s32[4]{0:T(128)S(1)} %get-tuple-element.263.first, s32[4]{0:T(128)S(1)} %get-tuple-element.262.clear, bf16[2048,128]{1,0:T(8,128)(2,1)S(1)} %copy-done.18, bf16[2048,256]{1,0:T(8,128)(2,1)} %collective-permute-done.2.refs_0_.refs_3_, ...), custom_call_target="tpu_custom_call" | custom-call | flops 20000000000 | bytes 10000000 | tf_op jit(solution)/shard_map/attend/pallas_call | solution.py:771
  235.1 5.1 convolution_convert_fusion
  240.2 25.6 %level_scatter.1 = f32[4,128,1024]{2,1,0:T(8,128)S(1)} custom-call(bf16[4,4,128,1024]{3,2,1,0:T(8,128)(2,1)S(1)} %bitcast.119), custom_call_target="tpu_custom_call" | custom-call | bytes 80000000 | tf_op jit(solution)/shard_map/level_scatter/pallas_call | solution.py:167
  270.7 31.9 %level_gather.3 = bf16[4,4,128,1152]{3,2,1,0:T(8,128)(2,1)} custom-call(bf16[4,128,1152]{2,1,0:T(8,128)(2,1)} %bitcast.126), custom_call_target="tpu_custom_call" | custom-call | bytes 90000000 | tf_op jit(solution)/shard_map/level_gather/pallas_call | solution.py:105
  302.7 2.2 dynamic-slice_convert_fusion.refs_3_
  304.9 37.2 %ffn_front.1 = (bf16[2048,2048]{1,0:T(8,128)(2,1)}, bf16[2048,2048]{1,0:T(8,128)(2,1)}, bf16[2048,1152]{1,0:T(8,128)(2,1)}) custom-call(s32[2]{0:T(128)} %pad_add_fusion.1.place, bf16[2048,1152]{1,0:T(8,128)(2,1)} %bitcast.155, bf16[2048,1024]{1,0:T(8,128)(2,1)} %bitcast.157, bf16[4,2,512,512]{3,2,1,0:T(8,128)(2,1)} %bitcast.187, ...), custom_call_target="tpu_custom_call" | custom-call | flops 25769803776 | bytes 30000000 | tf_op jit(solution)/shard_map/ffn_front/pallas_call | solution.py:944
  342.1 2.3 copy-done.7
  344.4 5.8 pair_scatter.2
  352.1 14.0 %ffn_rear.2 = (bf16[4,512,512]{2,1,0:T(8,128)(2,1)}, bf16[4,512,512]{2,1,0:T(8,128)(2,1)}) custom-call(s32[2]{0:T(128)} %pad_add_fusion.1.place, bf16[2048,1152]{1,0:T(8,128)(2,1)} %bitcast.156, bf16[2048,2048]{1,0:T(8,128)(2,1)} %get-tuple-element.131.hidden_units), custom_call_target="tpu_custom_call" | custom-call | flops 1000 | bytes 1000 | tf_op jit(solution)/shard_map/ffn_rear/pallas_call | solution.py:1018
  366.7 14.1 %ffn_rear.3 = (bf16[4,512,512]{2,1,0:T(8,128)(2,1)}, bf16[4,512,512]{2,1,0:T(8,128)(2,1)}) custom-call(s32[2]{0:T(128)} %pad_add_fusion.1.place, bf16[2048,1024]{1,0:T(8,128)(2,1)} %bitcast.158, bf16[2048,2048]{1,0:T(8,128)(2,1)} %get-tuple-element.134.hidden_units.active), custom_call_target="tpu_custom_call" | custom-call | flops 1000 | bytes 1000 | tf_op jit(solution)/shard_map/ffn_rear/pallas_call | solution.py:1018
  381.8 7.3 %leave_ffn.1 = (f32[512,1024]{1,0:T(8,128)}, bf16[512,1024]{1,0:T(8,128)(2,1)}, bf16[1024,128]{1,0:T(8,128)(2,1)S(1)}) custom-call(f32[512,1024]{1,0:T(8,128)} %copy-done.5, f32[512,1152]{1,0:T(8,128)} %bitcast.122, bf16[512,1152]{1,0:T(8,128)(2,1)S(1)} %collective-permute-done.4.came, bf16[512,1024]{1,0:T(8,128)(2,1)S(1)} %bitcast.121, ...), custom_call_target="tpu_custom_call" | custom-call | flops 1000000000 | bytes 10000000 | tf_op jit(solution)/shard_map/leave_ffn/pallas_call | solution.py:1114
  391.5 18.2 %ffn_feed.1 = bf16[2048,1024]{1,0:T(8,128)(2,1)} custom-call(s32[2]{0:T(128)} %pad_add_fusion.1.place, bf16[2048,2048]{1,0:T(8,128)(2,1)} %get-tuple-element.134.hidden_units.active, bf16[4,512,512]{2,1,0:T(8,128)(2,1)} %bitcast.166, bf16[4,512,512]{2,1,0:T(8,128)(2,1)} %collective-permute-done.3.refs_2_.refs_1_), custom_call_target="tpu_custom_call" | custom-call | flops 1000 | bytes 1000 | tf_op jit(solution)/shard_map/ffn_feed/pallas_call | solution.py:997
  409.7 5.3 collective-permute-done.5
  415.0 6.1 pair_gather.1
  421.1 4.2 add_convert_fusion.1
  425.4 12.7 %branch_back.1 = (bf16[2048,128]{1,0:T(8,128)(2,1)S(1)}, f32[4,1,512]{2,1,0:T(1,128)S(1)}, bf16[2048,128]{1,0:T(8,128)(2,1)S(1)}, bf16[1024,640]{1,0:T(8,128)(2,1)S(1)}) custom-call(bf16[2048,1024]{1,0:T(8,128)(2,1)} %bitcast.159, bf16[1024,1664]{1,0:T(8,128)(2,1)} %bitcast.147, f32[2048,128]{1,0:T(8,128)S(1)} %get-tuple-element.115.attended, ...), custom_call_target="tpu_custom_call" | custom-call | flops 100000000 | bytes 1000000 | tf_op jit(solution)/shard_map/branch_back/pallas_call | solution.py:1173
  439.9 20.0 %attend_back.1 = (bf16[2048,128]{1,0:T(8,128)(2,1)S(1)}, bf16[2048,256]{1,0:T(8,128)(2,1)S(1)}, bf16[2048,256]{1,0:T(8,128)(2,1)S(1)}, f32[2048,256]{1,0:T(8,128)}) custom-call(s32[4]{0:T(128)S(1)} %get-tuple-element.263.first, s32[4]{0:T(128)S(1)} %get-tuple-element.262.clear, bf16[2048,128]{1,0:T(8,128)(2,1)S(1)} %copy-done.19, ...), custom_call_target="tpu_custom_call" | custom-call | flops 2000000000 | bytes 1000000 | tf_op jit(solution)/shard_map/attend_back/pallas_call | solution.py:854
  463.3 4.4 pair_scatter.3
  467.7 39.1 %collective-permute-done.7 = bf16[2048,256]{1,0:T(8,128)(2,1)S(1)} collective-permute-done((bf16[2048,256]{1,0:T(8,128)(2,1)S(1)}, bf16[2048,256]{1,0:T(8,128)(2,1)S(1)}, u32[]{:S(2)}, u32[]{:S(2)}) %collective-permute-start.7) | collective-permute-done | bytes 1048608 | tf_op jit(solution)/shard_map/ppermute | solution.py:1367
  509.3 24.4 %collective-permute-done.9 = bf16[2048,256]{1,0:T(8,128)(2,1)S(1)} collective-permute-done((bf16[2048,256]{1,0:T(8,128)(2,1)S(1)}, bf16[2048,256]{1,0:T(8,128)(2,1)S(1)}, u32[]{:S(2)}, u32[]{:S(2)}) %collective-permute-start.9) | collective-permute-done | bytes 1048608 | tf_op jit(solution)/shard_map/ppermute | solution.py:1367
  539.7 23.2 %project_back.1 = (bf16[2048,1024]{1,0:T(8,128)(2,1)}, bf16[1024,1024]{1,0:T(8,128)(2,1)}) custom-call(bf16[2048,1024]{1,0:T(8,128)(2,1)} %bitcast.153, f32[2048,256]{1,0:T(8,128)} %convert_add_fusion.grads, bf16[2048,128]{1,0:T(8,128)(2,1)} %copy-done.21, bf16[2048,128]{1,0:T(8,128)(2,1)} %copy-done.20, f32[2048,640]{1,0:T(8,128)} %get-tuple-element.156.projected, ...), custom_call_target="tpu_custom_call" | custom-call | flops 1073741824 | bytes 4000000 | tf_op jit(solution)/shard_map/project_back/pallas_call | solution.py:1342
  564.6 4.2 all-to-all-start
  568.7 98.0 %finish.1 = (f32[4,4,32,1024]{3,2,1,0:T(8,128)}, f32[32,2560]{1,0:T(8,128)}, f32[32,512]{1,0:T(8,128)}, f32[32,512]{1,0:T(8,128)}, f32[4,32,128]{2,1,0:T(8,128)}...) custom-call(bf16[4,4,128,1024]{3,2,1,0:T(8,128)(2,1)} %bitcast.160, f32[4,128,1024]{2,1,0:T(8,128)} %bitcast.167, ...), custom_call_target="tpu_custom_call" | custom-call | bytes 200000000 | tf_op jit(solution)/shard_map/finish/pallas_call | solution.py:667
  673.1 2.3 bitcast_convert_fusion.1
  (179 shorter events, 76.7 us)
Async XLA Ops:
  7.2 219.5 %all-gather.5.cloned.1.call-start = ((), (), s32[]{:S(2)}) async-start(), calls=%async_computation.5 | async-start | bytes 2621440 | tf_op jit(solution)/shard_map/all_gather | solution.py:1513
  7.2 91.4 %collective-permute-start = (bf16[512,512]{1,0:T(8,128)(2,1)}, bf16[512,512]{1,0:T(8,128)(2,1)S(1)}, u32[]{:S(2)}, u32[]{:S(2)}) collective-permute-start(bf16[512,512]{1,0:T(8,128)(2,1)} %param.38), channel_id=1, source_target_pairs={{0,16},{16,0},{1,17},{17,1},{2,18},{18,2},{3,19},{19,3},{4,20},{20... | collective-permute-start | bytes 1572872 | tf_op jit(solution)/shard_map/ppermute | solution.py:1204
  100.9 15.1 %copy-start.25 = (f32[1024]{0:T(1024)}, f32[1024]{0:T(1024)S(1)}, u32[]{:S(2)}) copy-start(f32[1024]{0:T(1024)S(1)} %get-tuple-element.252) | copy-start | bytes 12292
  100.9 15.1 %copy-start.26 = (f32[1024]{0:T(1024)}, f32[1024]{0:T(1024)S(1)}, u32[]{:S(2)}) copy-start(f32[1024]{0:T(1024)S(1)} %get-tuple-element.253) | copy-start | bytes 12292
  101.7 19.2 %copy-start.38 = (s32[1,3]{1,0:T(1,128)S(1)}, s32[1,3]{1,0:T(1,128)}, u32[]{:S(2)}) copy-start(s32[1,3]{1,0:T(1,128)} %param.23) | copy-start | bytes 40
  116.8 43.4 %copy-start.9 = (bf16[2048,256]{1,0:T(8,128)(2,1)}, bf16[2048,256]{1,0:T(8,128)(2,1)S(1)}, u32[]{:S(2)}) copy-start(bf16[2048,256]{1,0:T(8,128)(2,1)S(1)} %get-tuple-element.100.refs_2_.refs_5_) | copy-start | bytes 3145732
  116.8 308.5 %copy-start.3 = (f32[2048,128]{1,0:T(8,128)}, f32[2048,128]{1,0:T(8,128)S(1)}, u32[]{:S(2)}) copy-start(f32[2048,128]{1,0:T(8,128)S(1)} %get-tuple-element.107.sigs) | copy-start | bytes 3145732
  116.8 308.5 %copy-start.4 = (f32[2048,16]{1,0:T(8,128)}, f32[2048,16]{1,0:T(8,128)S(1)}, u32[]{:S(2)}) copy-start(f32[2048,16]{1,0:T(8,128)S(1)} %get-tuple-element.108.masks) | copy-start | bytes 393220
  116.8 36.8 %copy-start.36 = (s32[4,16,128]{2,1,0:T(8,128)S(1)}, s32[4,16,128]{2,1,0:T(8,128)}, u32[]{:S(2)}) copy-start(s32[4,16,128]{2,1,0:T(8,128)} %get-tuple-element.105) | copy-start | bytes 98308
  116.8 34.2 %collective-permute-start.1 = (bf16[2048,256]{1,0:T(8,128)(2,1)S(1)}, bf16[2048,256]{1,0:T(8,128)(2,1)}, u32[]{:S(2)}, u32[]{:S(2)}) collective-permute-start(bf16[2048,256]{1,0:T(8,128)(2,1)S(1)} %get-tuple-element.100.refs_2_.refs_5_), channel_id=1, source_target_pairs={{0,4},{4,8},{8,12},{1,5},{5,9},{9,13},{2,6},{6,10},{10,14},{3,7},{... | collective-permute-start | bytes 3145736 | tf_op jit(solution)/shard_map/ppermute | solution.py:1367
  151.1 153.8 %all-gather.7.cloned.1.call-start = ((), (), s32[]{:S(2)}) async-start(), calls=%async_computation.6 | async-start | bytes 5242880 | tf_op jit(solution)/shard_map/all_gather | solution.py:1514
  153.5 519.6 %reduce-scatter.3.cloned.1.call-start = ((), (), s32[]{:S(2)}) async-start(), calls=%async_computation.3 | async-start | bytes 2621440 | tf_op jit(solution)/shard_map/reduce_scatter | solution.py:1569
  155.5 54.5 %collective-permute-start.2 = (bf16[2048,256]{1,0:T(8,128)(2,1)}, bf16[2048,256]{1,0:T(8,128)(2,1)}, u32[]{:S(2)}, u32[]{:S(2)}) collective-permute-start(bf16[2048,256]{1,0:T(8,128)(2,1)} %collective-permute-done.1.refs_1_.refs_4_), channel_id=1, source_target_pairs={{0,4},{4,8},{8,12},{1,5},{5,9},{9,13},{2,6},{6,10},{10,14},{3,7},{... | collective-permute-start | bytes 3145736 | tf_op jit(solution)/shard_map/ppermute | solution.py:1367
  226.7 78.3 %collective-permute-start.3 = (bf16[4,512,512]{2,1,0:T(8,128)(2,1)}, bf16[4,512,512]{2,1,0:T(8,128)(2,1)}, u32[]{:S(2)}, u32[]{:S(2)}) collective-permute-start(bf16[4,512,512]{2,1,0:T(8,128)(2,1)} %bitcast.164), channel_id=1, source_target_pairs={{0,16},{16,0},{1,17},{17,1},{2,18},{18,2},{3,19},{19,3},{4,20},{20... | collective-permute-start | bytes 6291464 | tf_op jit(solution)/shard_map/ppermute | solution.py:1204
  240.2 25.6 %copy-start.14 = (bf16[4,1,4,32,1024]{4,3,2,1,0:T(8,128)(2,1)S(1)}, bf16[4,1,4,32,1024]{4,3,2,1,0:T(8,128)(2,1)}, u32[]{:S(2)}) copy-start(bf16[4,1,4,32,1024]{4,3,2,1,0:T(8,128)(2,1)} %constant_dynamic-slice_fusion) | copy-start | bytes 3145732
  240.2 25.6 %copy-start.15 = (s32[512,16]{1,0:T(8,128)S(1)}, s32[512,16]{1,0:T(8,128)}, u32[]{:S(2)}) copy-start(s32[512,16]{1,0:T(8,128)} %fusion.4.routes) | copy-start | bytes 98308
  351.6 29.2 %collective-permute-start.4 = (bf16[512,1152]{1,0:T(8,128)(2,1)}, bf16[512,1152]{1,0:T(8,128)(2,1)S(1)}, u32[]{:S(2)}, u32[]{:S(2)}) collective-permute-start(bf16[512,1152]{1,0:T(8,128)(2,1)} %bitcast.38), channel_id=1, source_target_pairs={{0,2},{1,3},{2,0},{3,1},{4,6},{5,7},{6,4},{7,5},{8,10},{9,11},{10,... | collective-permute-start | bytes 3538952 | tf_op jit(solution)/shard_map/ppermute | solution.py:287
  366.1 55.0 %collective-permute-start.6 = (bf16[4,512,512]{2,1,0:T(8,128)(2,1)}, bf16[4,512,512]{2,1,0:T(8,128)(2,1)}, u32[]{:S(2)}, u32[]{:S(2)}) collective-permute-start(bf16[4,512,512]{2,1,0:T(8,128)(2,1)} %get-tuple-element.133), channel_id=1, source_target_pairs={{0,16},{16,0},{1,17},{17,1},{2,18},{18,2},{3,19},{19,3},{4,20},{20... | collective-permute-start | bytes 6291464 | tf_op jit(solution)/shard_map/ppermute | solution.py:1204
  366.7 14.2 %copy-start.16 = (s32[512,16]{1,0:T(8,128)S(1)}, s32[512,16]{1,0:T(8,128)}, u32[]{:S(2)}) copy-start(s32[512,16]{1,0:T(8,128)} %fusion.4.routes) | copy-start | bytes 98308
  389.8 25.2 %collective-permute-start.5 = (bf16[512,1024]{1,0:T(8,128)(2,1)}, bf16[512,1024]{1,0:T(8,128)(2,1)}, u32[]{:S(2)}, u32[]{:S(2)}) collective-permute-start(bf16[512,1024]{1,0:T(8,128)(2,1)} %get-tuple-element.139), channel_id=1, source_target_pairs={{0,2},{1,3},{2,0},{3,1},{4,6},{5,7},{6,4},{7,5},{8,10},{9,11},{10,... | collective-permute-start | bytes 3145736 | tf_op jit(solution)/shard_map/ppermute | solution.py:287
  425.3 250.1 %reduce-scatter.5.cloned.1.call-start = ((), (), s32[]{:S(2)}) async-start(), calls=%async_computation.4 | async-start | bytes 2621440 | tf_op jit(solution)/shard_map/reduce_scatter | solution.py:1569
  425.4 14.6 %copy-start.19 = (bf16[2048,128]{1,0:T(8,128)(2,1)S(1)}, bf16[2048,128]{1,0:T(8,128)(2,1)}, u32[]{:S(2)}) copy-start(bf16[2048,128]{1,0:T(8,128)(2,1)} %copy-done.17) | copy-start | bytes 1572868
  439.9 21.9 %copy-start.37 = (bf16[4,512,512]{2,1,0:T(8,128)(2,1)S(1)}, bf16[4,512,512]{2,1,0:T(8,128)(2,1)}, u32[]{:S(2)}) copy-start(bf16[4,512,512]{2,1,0:T(8,128)(2,1)} %get-tuple-element.136) | copy-start | bytes 6291460
  439.9 23.4 %copy-start.2 = (bf16[2048,1024]{1,0:T(8,128)(2,1)S(1)}, bf16[2048,1024]{1,0:T(8,128)(2,1)}, u32[]{:S(2)}) copy-start(bf16[2048,1024]{1,0:T(8,128)(2,1)} %ffn_feed.1) | copy-start | bytes 12582916
  459.9 47.2 %copy-start.21 = (bf16[2048,128]{1,0:T(8,128)(2,1)}, bf16[2048,128]{1,0:T(8,128)(2,1)S(1)}, u32[]{:S(2)}) copy-start(bf16[2048,128]{1,0:T(8,128)(2,1)S(1)} %get-tuple-element.154.grad_query) | copy-start | bytes 1572868
  459.9 46.9 %collective-permute-start.7 = (bf16[2048,256]{1,0:T(8,128)(2,1)S(1)}, bf16[2048,256]{1,0:T(8,128)(2,1)S(1)}, u32[]{:S(2)}, u32[]{:S(2)}) collective-permute-start(bf16[2048,256]{1,0:T(8,128)(2,1)S(1)} %get-tuple-element.145), channel_id=1, source_target_pairs={{4,0},{8,4},{12,8},{5,1},{9,5},{13,9},{6,2},{10,6},{14,10},{7,3},{... | collective-permute-start | bytes 3145736 | tf_op jit(solution)/shard_map/ppermute | solution.py:1367
  461.8 73.4 %collective-permute-start.10 = (bf16[4,512,512]{2,1,0:T(8,128)(2,1)S(1)}, bf16[4,512,512]{2,1,0:T(8,128)(2,1)S(1)}, u32[]{:S(2)}, u32[]{:S(2)}) collective-permute-start(bf16[4,512,512]{2,1,0:T(8,128)(2,1)S(1)} %copy-done.37), channel_id=1, source_target_pairs={{0,16},{16,0},{1,17},{17,1},{2,18},{18,2},{3,19},{19,3},{4,20},{20... | collective-permute-start | bytes 6291464 | tf_op jit(solution)/shard_map/ppermute | solution.py:1204
  467.7 66.0 %copy-start.30 = (f32[2048,256]{1,0:T(8,128)S(1)}, f32[2048,256]{1,0:T(8,128)}, u32[]{:S(2)}) copy-start(f32[2048,256]{1,0:T(8,128)} %get-tuple-element.150) | copy-start | bytes 6291460
  507.1 26.6 %collective-permute-start.9 = (bf16[2048,256]{1,0:T(8,128)(2,1)S(1)}, bf16[2048,256]{1,0:T(8,128)(2,1)S(1)}, u32[]{:S(2)}, u32[]{:S(2)}) collective-permute-start(bf16[2048,256]{1,0:T(8,128)(2,1)S(1)} %add_convert_fusion.3), channel_id=1, source_target_pairs={{4,0},{8,4},{12,8},{5,1},{9,5},{13,9},{6,2},{10,6},{14,10},{7,3},{... | collective-permute-start | bytes 3145736 | tf_op jit(solution)/shard_map/ppermute | solution.py:1367
  538.0 24.8 %collective-permute-start.8 = (bf16[512,1024]{1,0:T(8,128)(2,1)S(1)}, bf16[512,1024]{1,0:T(8,128)(2,1)S(1)}, u32[]{:S(2)}, u32[]{:S(2)}) collective-permute-start(bf16[512,1024]{1,0:T(8,128)(2,1)S(1)} %bitcast.139), channel_id=1, source_target_pairs={{0,2},{1,3},{2,0},{3,1},{4,6},{5,7},{6,4},{7,5},{8,10},{9,11},{10,... | collective-permute-start | bytes 3145736 | tf_op jit(solution)/shard_map/ppermute | solution.py:287
  539.7 23.2 %copy-start.6 = (f32[512,1024]{1,0:T(8,128)S(1)}, f32[512,1024]{1,0:T(8,128)}, u32[]{:S(2)}) copy-start(f32[512,1024]{1,0:T(8,128)} %copy-done.5) | copy-start | bytes 6291460
  564.6 108.5 %all-to-all-start = ((bf16[4,128,1024]{2,1,0:T(8,128)(2,1)}), bf16[4,128,1024]{2,1,0:T(8,128)(2,1)S(1)}, u32[]{:S(2)}, u32[]{:S(2)}) async-start(bf16[4,128,1024]{2,1,0:T(8,128)(2,1)} %bitcast.47), calls=%async_computation | async-start | bytes 2097152 | tf_op jit(solution)/shard_map/all_to_all | solution.py:33
  (23 other events, 61.9 us)
Sparse Core Ops, SparseCore 0:
  151.2 62.6 all-gather.4
  215.5 76.2 all-gather.6
  425.4 57.3 reduce-scatter.2
  538.1 52.9 reduce-scatter.4

commit v13 on v12

--- a/solution.py
+++ b/solution.py
@@ -1502,12 +1502,14 @@
     for i in range(reach):
         came = shift(window[0], "level", 1)
         if i == 0:
-            came, own_grads, pos_all, starts, ffn_out, in_rows = lax.optimization_barrier(
-                (came, own_grads, pos_all, starts, ffn_out, [ffn_in] + in_rows)
+            came, own_grads, pos_all, starts, ffn_out = lax.optimization_barrier(
+                (came, own_grads, pos_all, starts, ffn_out)
             )
             cotangent = level_gather(own_grads, 5, True)
         if i == reach - 1:
-            came, cotangent, ffn_side = lax.optimization_barrier((came, cotangent, ffn_side))
+            came, cotangent, ffn_side, in_rows = lax.optimization_barrier(
+                (came, cotangent, ffn_side, [ffn_in] + in_rows)
+            )
         window.insert(0, came)
     place = jnp.stack([head, lax.axis_index("group")])
     out_here = lax.all_gather(ffn_out, "level", axis=0)

time: 693 us -> 701 us (1.012)
  Pallas kernels: 455 us -> 477 us
  waiting for transfers between devices: 118 us -> 102 us
    ppermute x4, waiting for transfers between devices: 113 us -> 96.1 us  [shift(): return lax.ppermute(value, axis, pairs)]
    pallas_call x1, Pallas kernels: 20 us -> 29.3 us  [attend_back(): pl.pallas_call(functools.partial(attend_back_kernel, parts), grid_spec=gr...]
    pallas_call x1, Pallas kernels: 14.4 us -> 22.2 us  [attend(): pl.pallas_call(functools.partial(attend_kernel, parts), grid_spec=grid_sp...]
  transfers between devices with their start and end apart: 16 -> 16, of which waited for: 5 -> 5; matrix products, arithmetic and copies ran while one was open for 8% -> 7% of each run, Pallas kernels for 58% -> 60%
where the time goes in v13:
time: 701 us; the launch traced here: 696 us
  Pallas kernels  477 us (68%)
  waiting for transfers between devices  102 us (15%)
  local copies, waits for them, and re-layouts  43 us (6%)
  other arithmetic  31.1 us (4%)
  starting transfers between devices  22 us (3%)
  between operations  14.9 us (2%)
    pallas_call x1, Pallas kernels, finish(): pl.pallas_call(functools.partial(finish_kernel, layout), out_shape=[jax.S...  103 us
    ppermute x4, waiting for transfers between devices, shift(): return lax.ppermute(value, axis, pairs)  96.1 us
    pallas_call x1, Pallas kernels, start(): pl.pallas_call(start_kernel, out_shape=shapes, in_specs=[pl.BlockSpec(mem...  80.1 us
    pallas_call x2, Pallas kernels, level_gather(): pl.pallas_call(functools.partial(gather_kernel, by_source), out_shape=jax...  57.6 us
    pallas_call x1, Pallas kernels, ffn_front(): pl.pallas_call(functools.partial(front_kernel, groups, local), grid_spec=...  37.2 us
    pallas_call x1, Pallas kernels, attend_back(): pl.pallas_call(functools.partial(attend_back_kernel, parts), grid_spec=gr...  29.3 us
    pallas_call x2, Pallas kernels, ffn_rear(): pl.pallas_call(functools.partial(rear_kernel, groups), grid_spec=pltpu.Pr...  28.1 us
    pallas_call x1, Pallas kernels, level_scatter(): pl.pallas_call(functools.partial(scatter_kernel, by_source), out_shape=ja...  25.6 us
  transfers between devices with their start and end apart: 16, of which 5 were waited for; matrix products, arithmetic and copies ran while one was open for 7% of the time, Pallas kernels for 60%

profile of v13, /device:TPU:8, one launch (start us, length us, event | category | flops | bytes accessed | tf_op | source)
XLA Modules:
  0.0 696.2 jit_solution(1180064567273355464)
XLA Ops:
  17.0 80.1 %start.1 = (bf16[4,4,4,32,1024]{4,3,2,1,0:T(8,128)(2,1)}, bf16[4,4,32,1024]{3,2,1,0:T(8,128)(2,1)}, bf16[2,4,4,32,1664]{4,3,2,1,0:T(8,128)(2,1)}, s32[4,4,512]{2...) custom-call(bf16[4,4,32,1024]{3,2,1,0:T(8,128)(2,1)} %bitcast.170, bf16[4,4,32,1024]{3,2,1,0:T(8,128)(2,1)} %bitcast.171, ...), custom_call_target="tpu_custom_call" | custom-call | bytes 200000000 | tf_op jit(solution)/shard_map/start/pallas_call | solution.py:500
  101.7 14.4 %project.1 = (bf16[2048,128]{1,0:T(8,128)(2,1)S(1)}, bf16[2048,256]{1,0:T(8,128)(2,1)S(1)}, f32[2048,640]{1,0:T(8,128)}, f32[2048,128]{1,0:T(8,128)S(1)}, f32[2048,16]{1,0:T(8,128)S(1)}) custom-call(bf16[2048,1024]{1,0:T(8,128)(2,1)} %bitcast.152, bf16[1024,1664]{1,0:T(8,128)(2,1)} %bitcast.141, bf16[1024,1664]{1,0:T(8,128)(2,1)} %bitcast.142, ...), custom_call_target="tpu_custom_call" | custom-call | flops 4294967296 | bytes 20000000 | tf_op jit(solution)/shard_map/project/pallas_call | solution.py:1262
  121.3 29.7 %collective-permute-done.1.refs_1_.refs_4_ = bf16[2048,256]{1,0:T(8,128)(2,1)} collective-permute-done((bf16[2048,256]{1,0:T(8,128)(2,1)S(1)}, bf16[2048,256]{1,0:T(8,128)(2,1)}, u32[]{:S(2)}, u32[]{:S(2)}) %collective-permute-start.1) | collective-permute-done | bytes 1048608 | tf_op jit(solution)/shard_map/ppermute | solution.py:1367
  154.8 2.3 constant_dynamic-slice_fusion
  159.5 25.7 %level_gather.2 = bf16[4,4,128,1024]{3,2,1,0:T(8,128)(2,1)} custom-call(bf16[4,128,1024]{2,1,0:T(8,128)(2,1)} %bitcast.120), custom_call_target="tpu_custom_call" | custom-call | bytes 90000000 | tf_op jit(solution)/shard_map/level_gather/pallas_call | solution.py:105
  185.2 20.4 %collective-permute-done.2.refs_0_.refs_3_ = bf16[2048,256]{1,0:T(8,128)(2,1)} collective-permute-done((bf16[2048,256]{1,0:T(8,128)(2,1)}, bf16[2048,256]{1,0:T(8,128)(2,1)}, u32[]{:S(2)}, u32[]{:S(2)}) %collective-permute-start.2) | collective-permute-done | bytes 1048608 | tf_op jit(solution)/shard_map/ppermute | solution.py:1367
  205.6 2.3 pad_maximum_fusion
  208.6 2.3 copy.138.refs_8_.refs_11_
  213.1 22.2 %attend.1 = (f32[2048,128]{1,0:T(8,128)S(1)}, f32[4,1,512]{2,1,0:T(1,128)S(1)}) custom-call(s32[4]{0:T(128)S(1)} %get-tuple-element.263.first, s32[4]{0:T(128)S(1)} %get-tuple-element.262.clear, bf16[2048,128]{1,0:T(8,128)(2,1)S(1)} %copy-done.18, bf16[2048,256]{1,0:T(8,128)(2,1)} %collective-permute-done.2.refs_0_.refs_3_, ...), custom_call_target="tpu_custom_call" | custom-call | flops 20000000000 | bytes 10000000 | tf_op jit(solution)/shard_map/attend/pallas_call | solution.py:771
  242.2 5.1 convolution_convert_fusion
  247.3 25.6 %level_scatter.1 = f32[4,128,1024]{2,1,0:T(8,128)S(1)} custom-call(bf16[4,4,128,1024]{3,2,1,0:T(8,128)(2,1)S(1)} %bitcast.119), custom_call_target="tpu_custom_call" | custom-call | bytes 80000000 | tf_op jit(solution)/shard_map/level_scatter/pallas_call | solution.py:167
  277.9 31.9 %level_gather.3 = bf16[4,4,128,1152]{3,2,1,0:T(8,128)(2,1)} custom-call(bf16[4,128,1152]{2,1,0:T(8,128)(2,1)} %bitcast.126), custom_call_target="tpu_custom_call" | custom-call | bytes 90000000 | tf_op jit(solution)/shard_map/level_gather/pallas_call | solution.py:105
  312.1 37.2 %ffn_front.1 = (bf16[2048,2048]{1,0:T(8,128)(2,1)}, bf16[2048,2048]{1,0:T(8,128)(2,1)}, bf16[2048,1152]{1,0:T(8,128)(2,1)}) custom-call(s32[2]{0:T(128)} %pad_add_fusion.1.place, bf16[2048,1152]{1,0:T(8,128)(2,1)} %bitcast.155, bf16[2048,1024]{1,0:T(8,128)(2,1)} %bitcast.157, bf16[4,2,512,512]{3,2,1,0:T(8,128)(2,1)} %bitcast.187, ...), custom_call_target="tpu_custom_call" | custom-call | flops 25769803776 | bytes 30000000 | tf_op jit(solution)/shard_map/ffn_front/pallas_call | solution.py:944
  349.2 2.3 copy-done.7
  351.6 5.8 pair_scatter.2
  359.2 14.0 %ffn_rear.2 = (bf16[4,512,512]{2,1,0:T(8,128)(2,1)}, bf16[4,512,512]{2,1,0:T(8,128)(2,1)}) custom-call(s32[2]{0:T(128)} %pad_add_fusion.1.place, bf16[2048,1152]{1,0:T(8,128)(2,1)} %bitcast.156, bf16[2048,2048]{1,0:T(8,128)(2,1)} %get-tuple-element.131.hidden_units), custom_call_target="tpu_custom_call" | custom-call | flops 1000 | bytes 1000 | tf_op jit(solution)/shard_map/ffn_rear/pallas_call | solution.py:1018
  375.4 14.1 %ffn_rear.3 = (bf16[4,512,512]{2,1,0:T(8,128)(2,1)}, bf16[4,512,512]{2,1,0:T(8,128)(2,1)}) custom-call(s32[2]{0:T(128)} %pad_add_fusion.1.place, bf16[2048,1024]{1,0:T(8,128)(2,1)} %bitcast.158, bf16[2048,2048]{1,0:T(8,128)(2,1)} %get-tuple-element.134.hidden_units.active), custom_call_target="tpu_custom_call" | custom-call | flops 1000 | bytes 1000 | tf_op jit(solution)/shard_map/ffn_rear/pallas_call | solution.py:1018
  390.5 7.3 %leave_ffn.1 = (f32[512,1024]{1,0:T(8,128)}, bf16[512,1024]{1,0:T(8,128)(2,1)}, bf16[1024,128]{1,0:T(8,128)(2,1)S(1)}) custom-call(f32[512,1024]{1,0:T(8,128)} %copy-done.5, f32[512,1152]{1,0:T(8,128)} %bitcast.122, bf16[512,1152]{1,0:T(8,128)(2,1)S(1)} %collective-permute-done.4.came, bf16[512,1024]{1,0:T(8,128)(2,1)S(1)} %bitcast.121, ...), custom_call_target="tpu_custom_call" | custom-call | flops 1000000000 | bytes 10000000 | tf_op jit(solution)/shard_map/leave_ffn/pallas_call | solution.py:1114
  400.1 18.2 %ffn_feed.1 = bf16[2048,1024]{1,0:T(8,128)(2,1)} custom-call(s32[2]{0:T(128)} %pad_add_fusion.1.place, bf16[2048,2048]{1,0:T(8,128)(2,1)} %get-tuple-element.134.hidden_units.active, bf16[4,512,512]{2,1,0:T(8,128)(2,1)} %bitcast.166, bf16[4,512,512]{2,1,0:T(8,128)(2,1)} %collective-permute-done.3.refs_2_.refs_1_), custom_call_target="tpu_custom_call" | custom-call | flops 1000 | bytes 1000 | tf_op jit(solution)/shard_map/ffn_feed/pallas_call | solution.py:997
  418.3 5.4 collective-permute-done.5
  423.7 6.1 pair_gather.1
  429.7 4.2 add_convert_fusion.1
  434.0 12.7 %branch_back.1 = (bf16[2048,128]{1,0:T(8,128)(2,1)S(1)}, f32[4,1,512]{2,1,0:T(1,128)S(1)}, bf16[2048,128]{1,0:T(8,128)(2,1)S(1)}, bf16[1024,640]{1,0:T(8,128)(2,1)S(1)}) custom-call(bf16[2048,1024]{1,0:T(8,128)(2,1)} %bitcast.159, bf16[1024,1664]{1,0:T(8,128)(2,1)} %bitcast.147, f32[2048,128]{1,0:T(8,128)S(1)} %get-tuple-element.115.attended, ...), custom_call_target="tpu_custom_call" | custom-call | flops 100000000 | bytes 1000000 | tf_op jit(solution)/shard_map/branch_back/pallas_call | solution.py:1173
  448.6 29.3 %attend_back.1 = (bf16[2048,128]{1,0:T(8,128)(2,1)S(1)}, bf16[2048,256]{1,0:T(8,128)(2,1)S(1)}, bf16[2048,256]{1,0:T(8,128)(2,1)S(1)}, f32[2048,256]{1,0:T(8,128)}) custom-call(s32[4]{0:T(128)S(1)} %get-tuple-element.263.first, s32[4]{0:T(128)S(1)} %get-tuple-element.262.clear, bf16[2048,128]{1,0:T(8,128)(2,1)S(1)} %copy-done.19, ...), custom_call_target="tpu_custom_call" | custom-call | flops 2000000000 | bytes 1000000 | tf_op jit(solution)/shard_map/attend_back/pallas_call | solution.py:854
  479.9 4.4 pair_scatter.3
  484.3 22.0 %collective-permute-done.7 = bf16[2048,256]{1,0:T(8,128)(2,1)S(1)} collective-permute-done((bf16[2048,256]{1,0:T(8,128)(2,1)S(1)}, bf16[2048,256]{1,0:T(8,128)(2,1)S(1)}, u32[]{:S(2)}, u32[]{:S(2)}) %collective-permute-start.7) | collective-permute-done | bytes 1048608 | tf_op jit(solution)/shard_map/ppermute | solution.py:1367
  506.6 2.5 collective-permute-start.9
  509.1 24.0 %collective-permute-done.9 = bf16[2048,256]{1,0:T(8,128)(2,1)S(1)} collective-permute-done((bf16[2048,256]{1,0:T(8,128)(2,1)S(1)}, bf16[2048,256]{1,0:T(8,128)(2,1)S(1)}, u32[]{:S(2)}, u32[]{:S(2)}) %collective-permute-start.9) | collective-permute-done | bytes 1048608 | tf_op jit(solution)/shard_map/ppermute | solution.py:1367
  539.1 23.2 %project_back.1 = (bf16[2048,1024]{1,0:T(8,128)(2,1)}, bf16[1024,1024]{1,0:T(8,128)(2,1)}) custom-call(bf16[2048,1024]{1,0:T(8,128)(2,1)} %bitcast.153, f32[2048,256]{1,0:T(8,128)} %convert_add_fusion.grads, bf16[2048,128]{1,0:T(8,128)(2,1)} %copy-done.21, bf16[2048,128]{1,0:T(8,128)(2,1)} %copy-done.20, f32[2048,640]{1,0:T(8,128)} %get-tuple-element.156.projected, ...), custom_call_target="tpu_custom_call" | custom-call | flops 1073741824 | bytes 4000000 | tf_op jit(solution)/shard_map/project_back/pallas_call | solution.py:1342
  564.0 6.0 all-to-all-start
  570.0 103.4 %finish.1 = (f32[4,4,32,1024]{3,2,1,0:T(8,128)}, f32[32,2560]{1,0:T(8,128)}, f32[32,512]{1,0:T(8,128)}, f32[32,512]{1,0:T(8,128)}, f32[4,32,128]{2,1,0:T(8,128)}...) custom-call(bf16[4,4,128,1024]{3,2,1,0:T(8,128)(2,1)} %bitcast.160, f32[4,128,1024]{2,1,0:T(8,128)} %bitcast.167, ...), custom_call_target="tpu_custom_call" | custom-call | bytes 200000000 | tf_op jit(solution)/shard_map/finish/pallas_call | solution.py:667
  679.7 2.3 bitcast_convert_fusion.1
  (179 shorter events, 75.2 us)
Async XLA Ops:
  7.2 228.1 %all-gather.5.cloned.1.call-start = ((), (), s32[]{:S(2)}) async-start(), calls=%async_computation.5 | async-start | bytes 2621440 | tf_op jit(solution)/shard_map/all_gather | solution.py:1515
  7.2 91.4 %collective-permute-start = (bf16[512,512]{1,0:T(8,128)(2,1)}, bf16[512,512]{1,0:T(8,128)(2,1)S(1)}, u32[]{:S(2)}, u32[]{:S(2)}) collective-permute-start(bf16[512,512]{1,0:T(8,128)(2,1)} %param.38), channel_id=1, source_target_pairs={{0,16},{16,0},{1,17},{17,1},{2,18},{18,2},{3,19},{19,3},{4,20},{20... | collective-permute-start | bytes 1572872 | tf_op jit(solution)/shard_map/ppermute | solution.py:1204
  100.9 15.2 %copy-start.25 = (f32[1024]{0:T(1024)}, f32[1024]{0:T(1024)S(1)}, u32[]{:S(2)}) copy-start(f32[1024]{0:T(1024)S(1)} %get-tuple-element.252) | copy-start | bytes 12292
  100.9 15.1 %copy-start.26 = (f32[1024]{0:T(1024)}, f32[1024]{0:T(1024)S(1)}, u32[]{:S(2)}) copy-start(f32[1024]{0:T(1024)S(1)} %get-tuple-element.253) | copy-start | bytes 12292
  101.7 19.1 %copy-start.38 = (s32[1,3]{1,0:T(1,128)S(1)}, s32[1,3]{1,0:T(1,128)}, u32[]{:S(2)}) copy-start(s32[1,3]{1,0:T(1,128)} %param.23) | copy-start | bytes 40
  101.7 51.3 %copy-start.36 = (s32[4,16,128]{2,1,0:T(8,128)S(1)}, s32[4,16,128]{2,1,0:T(8,128)}, u32[]{:S(2)}) copy-start(s32[4,16,128]{2,1,0:T(8,128)} %get-tuple-element.104) | copy-start | bytes 98308
  116.9 68.4 %copy-start.9 = (bf16[2048,256]{1,0:T(8,128)(2,1)}, bf16[2048,256]{1,0:T(8,128)(2,1)S(1)}, u32[]{:S(2)}) copy-start(bf16[2048,256]{1,0:T(8,128)(2,1)S(1)} %get-tuple-element.100.refs_2_.refs_5_) | copy-start | bytes 3145732
  116.9 317.1 %copy-start.3 = (f32[2048,128]{1,0:T(8,128)}, f32[2048,128]{1,0:T(8,128)S(1)}, u32[]{:S(2)}) copy-start(f32[2048,128]{1,0:T(8,128)S(1)} %get-tuple-element.107.sigs) | copy-start | bytes 3145732
  116.9 317.1 %copy-start.4 = (f32[2048,16]{1,0:T(8,128)}, f32[2048,16]{1,0:T(8,128)S(1)}, u32[]{:S(2)}) copy-start(f32[2048,16]{1,0:T(8,128)S(1)} %get-tuple-element.108.masks) | copy-start | bytes 393220
  116.9 34.1 %collective-permute-start.1 = (bf16[2048,256]{1,0:T(8,128)(2,1)S(1)}, bf16[2048,256]{1,0:T(8,128)(2,1)}, u32[]{:S(2)}, u32[]{:S(2)}) collective-permute-start(bf16[2048,256]{1,0:T(8,128)(2,1)S(1)} %get-tuple-element.100.refs_2_.refs_5_), channel_id=1, source_target_pairs={{0,4},{4,8},{8,12},{1,5},{5,9},{9,13},{2,6},{6,10},{10,14},{3,7},{... | collective-permute-start | bytes 3145736 | tf_op jit(solution)/shard_map/ppermute | solution.py:1367
  151.0 161.1 %all-gather.7.cloned.1.call-start = ((), (), s32[]{:S(2)}) async-start(), calls=%async_computation.6 | async-start | bytes 5242880 | tf_op jit(solution)/shard_map/all_gather | solution.py:1516
  151.0 54.6 %collective-permute-start.2 = (bf16[2048,256]{1,0:T(8,128)(2,1)}, bf16[2048,256]{1,0:T(8,128)(2,1)}, u32[]{:S(2)}, u32[]{:S(2)}) collective-permute-start(bf16[2048,256]{1,0:T(8,128)(2,1)} %collective-permute-done.1.refs_1_.refs_4_), channel_id=1, source_target_pairs={{0,4},{4,8},{8,12},{1,5},{5,9},{9,13},{2,6},{6,10},{10,14},{3,7},{... | collective-permute-start | bytes 3145736 | tf_op jit(solution)/shard_map/ppermute | solution.py:1367
  207.9 471.8 %reduce-scatter.3.cloned.1.call-start = ((), (), s32[]{:S(2)}) async-start(), calls=%async_computation.3 | async-start | bytes 2621440 | tf_op jit(solution)/shard_map/reduce_scatter | solution.py:1571
  235.3 76.7 %collective-permute-start.3 = (bf16[4,512,512]{2,1,0:T(8,128)(2,1)}, bf16[4,512,512]{2,1,0:T(8,128)(2,1)}, u32[]{:S(2)}, u32[]{:S(2)}) collective-permute-start(bf16[4,512,512]{2,1,0:T(8,128)(2,1)} %bitcast.164), channel_id=1, source_target_pairs={{0,16},{16,0},{1,17},{17,1},{2,18},{18,2},{3,19},{19,3},{4,20},{20... | collective-permute-start | bytes 6291464 | tf_op jit(solution)/shard_map/ppermute | solution.py:1204
  247.3 25.6 %copy-start.14 = (bf16[4,1,4,32,1024]{4,3,2,1,0:T(8,128)(2,1)S(1)}, bf16[4,1,4,32,1024]{4,3,2,1,0:T(8,128)(2,1)}, u32[]{:S(2)}) copy-start(bf16[4,1,4,32,1024]{4,3,2,1,0:T(8,128)(2,1)} %constant_dynamic-slice_fusion) | copy-start | bytes 3145732
  247.3 25.6 %copy-start.15 = (s32[512,16]{1,0:T(8,128)S(1)}, s32[512,16]{1,0:T(8,128)}, u32[]{:S(2)}) copy-start(s32[512,16]{1,0:T(8,128)} %fusion.4.routes) | copy-start | bytes 98308
  358.8 30.7 %collective-permute-start.4 = (bf16[512,1152]{1,0:T(8,128)(2,1)}, bf16[512,1152]{1,0:T(8,128)(2,1)S(1)}, u32[]{:S(2)}, u32[]{:S(2)}) collective-permute-start(bf16[512,1152]{1,0:T(8,128)(2,1)} %bitcast.38), channel_id=1, source_target_pairs={{0,2},{1,3},{2,0},{3,1},{4,6},{5,7},{6,4},{7,5},{8,10},{9,11},{10,... | collective-permute-start | bytes 3538952 | tf_op jit(solution)/shard_map/ppermute | solution.py:287
  373.2 56.5 %collective-permute-start.6 = (bf16[4,512,512]{2,1,0:T(8,128)(2,1)}, bf16[4,512,512]{2,1,0:T(8,128)(2,1)}, u32[]{:S(2)}, u32[]{:S(2)}) collective-permute-start(bf16[4,512,512]{2,1,0:T(8,128)(2,1)} %get-tuple-element.133), channel_id=1, source_target_pairs={{0,16},{16,0},{1,17},{17,1},{2,18},{18,2},{3,19},{19,3},{4,20},{20... | collective-permute-start | bytes 6291464 | tf_op jit(solution)/shard_map/ppermute | solution.py:1204
  375.3 14.2 %copy-start.16 = (s32[512,16]{1,0:T(8,128)S(1)}, s32[512,16]{1,0:T(8,128)}, u32[]{:S(2)}) copy-start(s32[512,16]{1,0:T(8,128)} %fusion.4.routes) | copy-start | bytes 98308
  398.5 25.2 %collective-permute-start.5 = (bf16[512,1024]{1,0:T(8,128)(2,1)}, bf16[512,1024]{1,0:T(8,128)(2,1)}, u32[]{:S(2)}, u32[]{:S(2)}) collective-permute-start(bf16[512,1024]{1,0:T(8,128)(2,1)} %get-tuple-element.139), channel_id=1, source_target_pairs={{0,2},{1,3},{2,0},{3,1},{4,6},{5,7},{6,4},{7,5},{8,10},{9,11},{10,... | collective-permute-start | bytes 3145736 | tf_op jit(solution)/shard_map/ppermute | solution.py:287
  433.9 248.1 %reduce-scatter.5.cloned.1.call-start = ((), (), s32[]{:S(2)}) async-start(), calls=%async_computation.4 | async-start | bytes 2621440 | tf_op jit(solution)/shard_map/reduce_scatter | solution.py:1571
  434.0 14.6 %copy-start.19 = (bf16[2048,128]{1,0:T(8,128)(2,1)S(1)}, bf16[2048,128]{1,0:T(8,128)(2,1)}, u32[]{:S(2)}) copy-start(bf16[2048,128]{1,0:T(8,128)(2,1)} %copy-done.17) | copy-start | bytes 1572868
  448.6 31.2 %copy-start.37 = (bf16[4,512,512]{2,1,0:T(8,128)(2,1)S(1)}, bf16[4,512,512]{2,1,0:T(8,128)(2,1)}, u32[]{:S(2)}) copy-start(bf16[4,512,512]{2,1,0:T(8,128)(2,1)} %get-tuple-element.136) | copy-start | bytes 6291460
  448.6 31.3 %copy-start.2 = (bf16[2048,1024]{1,0:T(8,128)(2,1)S(1)}, bf16[2048,1024]{1,0:T(8,128)(2,1)}, u32[]{:S(2)}) copy-start(bf16[2048,1024]{1,0:T(8,128)(2,1)} %ffn_feed.1) | copy-start | bytes 12582916
  477.9 28.8 %copy-start.21 = (bf16[2048,128]{1,0:T(8,128)(2,1)}, bf16[2048,128]{1,0:T(8,128)(2,1)S(1)}, u32[]{:S(2)}) copy-start(bf16[2048,128]{1,0:T(8,128)(2,1)S(1)} %get-tuple-element.154.grad_query) | copy-start | bytes 1572868
  477.9 28.5 %collective-permute-start.7 = (bf16[2048,256]{1,0:T(8,128)(2,1)S(1)}, bf16[2048,256]{1,0:T(8,128)(2,1)S(1)}, u32[]{:S(2)}, u32[]{:S(2)}) collective-permute-start(bf16[2048,256]{1,0:T(8,128)(2,1)S(1)} %get-tuple-element.145), channel_id=1, source_target_pairs={{4,0},{8,4},{12,8},{5,1},{9,5},{13,9},{6,2},{10,6},{14,10},{7,3},{... | collective-permute-start | bytes 3145736 | tf_op jit(solution)/shard_map/ppermute | solution.py:1367
  479.8 54.9 %collective-permute-start.10 = (bf16[4,512,512]{2,1,0:T(8,128)(2,1)S(1)}, bf16[4,512,512]{2,1,0:T(8,128)(2,1)S(1)}, u32[]{:S(2)}, u32[]{:S(2)}) collective-permute-start(bf16[4,512,512]{2,1,0:T(8,128)(2,1)S(1)} %copy-done.37), channel_id=1, source_target_pairs={{0,16},{16,0},{1,17},{17,1},{2,18},{18,2},{3,19},{19,3},{4,20},{20... | collective-permute-start | bytes 6291464 | tf_op jit(solution)/shard_map/ppermute | solution.py:1204
  484.3 48.8 %copy-start.30 = (f32[2048,256]{1,0:T(8,128)S(1)}, f32[2048,256]{1,0:T(8,128)}, u32[]{:S(2)}) copy-start(f32[2048,256]{1,0:T(8,128)} %get-tuple-element.150) | copy-start | bytes 6291460
  506.6 26.5 %collective-permute-start.9 = (bf16[2048,256]{1,0:T(8,128)(2,1)S(1)}, bf16[2048,256]{1,0:T(8,128)(2,1)S(1)}, u32[]{:S(2)}, u32[]{:S(2)}) collective-permute-start(bf16[2048,256]{1,0:T(8,128)(2,1)S(1)} %add_convert_fusion.3), channel_id=1, source_target_pairs={{4,0},{8,4},{12,8},{5,1},{9,5},{13,9},{6,2},{10,6},{14,10},{7,3},{... | collective-permute-start | bytes 3145736 | tf_op jit(solution)/shard_map/ppermute | solution.py:1367
  537.5 24.9 %collective-permute-start.8 = (bf16[512,1024]{1,0:T(8,128)(2,1)S(1)}, bf16[512,1024]{1,0:T(8,128)(2,1)S(1)}, u32[]{:S(2)}, u32[]{:S(2)}) collective-permute-start(bf16[512,1024]{1,0:T(8,128)(2,1)S(1)} %bitcast.139), channel_id=1, source_target_pairs={{0,2},{1,3},{2,0},{3,1},{4,6},{5,7},{6,4},{7,5},{8,10},{9,11},{10,... | collective-permute-start | bytes 3145736 | tf_op jit(solution)/shard_map/ppermute | solution.py:287
  539.1 23.2 %copy-start.6 = (f32[512,1024]{1,0:T(8,128)S(1)}, f32[512,1024]{1,0:T(8,128)}, u32[]{:S(2)}) copy-start(f32[512,1024]{1,0:T(8,128)} %copy-done.5) | copy-start | bytes 6291460
  564.0 115.7 %all-to-all-start = ((bf16[4,128,1024]{2,1,0:T(8,128)(2,1)}), bf16[4,128,1024]{2,1,0:T(8,128)(2,1)S(1)}, u32[]{:S(2)}, u32[]{:S(2)}) async-start(bf16[4,128,1024]{2,1,0:T(8,128)(2,1)} %bitcast.47), calls=%async_computation | async-start | bytes 2097152 | tf_op jit(solution)/shard_map/all_to_all | solution.py:33
  (23 other events, 61.9 us)
Sparse Core Ops, SparseCore 0:
  151.1 58.3 all-gather.4
  211.1 76.2 all-gather.6
  434.0 45.1 reduce-scatter.2
  537.6 87.7 reduce-scatter.4
